TPU v7x, 32 devices: a whole 2x2x4 slice. The times are simulated.
32 devices in a mesh: dp: 2 (over x), vocab: 16 (over z, y, core).
Axes of the slice: x: 2, y: 2, z: 4, core: 2. Of those that a mesh axis runs over, the one named last changes fastest.
Arguments:
- token_ids: int32 [32, 256], P(('dp', 'vocab')), may hold values from 0 to 30526
- pred_mask: int32 [32, 256], P(('dp', 'vocab')), may hold values from 0 to 1, as said below
- fact_order: int32 [32, 256], P(('dp', 'vocab')), may hold values from 0 to 255, each once within a row
- corpus: int32 [32], P(('dp', 'vocab')), may hold values from 0 to 3, as said below
- embed_table: float32 [30720, 768], P('vocab'), may hold values from -0.42 to 0.42
- table_moment: float32 [30720, 768], P('vocab'), may hold values from -1.1444092e-05 to 1.1444092e-05
- table_square: float32 [30720, 768], P('vocab'), may hold values from 1.6192649e-13 to 2.5908238e-12
- layer_weights: float32 [3, 768, 3072], P(None, ('dp', 'vocab'))
- layer_moment: float32 [3, 768, 3072], P(None, ('dp', 'vocab')), may hold values from -1.1444092e-05 to 1.1444092e-05
- layer_square: float32 [3, 768, 3072], P(None, ('dp', 'vocab')), may hold values from 1.6192649e-13 to 2.5908238e-12
- position_table: float32 [256, 768], P(None, ('dp', 'vocab')), may hold values from -0.42 to 0.42
- position_moment: float32 [256, 768], P(None, ('dp', 'vocab')), may hold values from -1.1444092e-05 to 1.1444092e-05
- position_square: float32 [256, 768], P(None, ('dp', 'vocab')), may hold values from 1.6192649e-13 to 2.5908238e-12
- small_params: float32 [14, 768], P(None, ('dp', 'vocab'))
- small_moment: float32 [14, 768], P(None, ('dp', 'vocab')), may hold values from -1.1444092e-05 to 1.1444092e-05
- small_square: float32 [14, 768], P(None, ('dp', 'vocab')), may hold values from 1.6192649e-13 to 2.5908238e-12
Outputs:
- loss_value: float32 [], replicated
- grad_norm: float32 [], replicated
- table_next: float32 [30720, 768], P('vocab')
- table_moments: float32 [30720, 768], P('vocab')
- table_squares: float32 [30720, 768], P('vocab')
- layer_next: float32 [3, 768, 3072], P(None, ('dp', 'vocab'))
- layer_moments: float32 [3, 768, 3072], P(None, ('dp', 'vocab'))
- layer_squares: float32 [3, 768, 3072], P(None, ('dp', 'vocab'))
- position_next: float32 [256, 768], P(None, ('dp', 'vocab'))
- position_moments: float32 [256, 768], P(None, ('dp', 'vocab'))
- position_squares: float32 [256, 768], P(None, ('dp', 'vocab'))
- small_next: float32 [14, 768], P(None, ('dp', 'vocab'))
- small_moments: float32 [14, 768], P(None, ('dp', 'vocab'))
- small_squares: float32 [14, 768], P(None, ('dp', 'vocab'))
- trust_norms: float32 [6, 2], replicated
Inputs may be any that keep to these rules, and one draw needn't show every extreme that they name: `pred_mask`: every sequence has between 256 // 10 and 64 masked tokens, and some sequence has exactly 64. Every corpus holds exactly 8 sequences.
All inputs are finite; a program needn't handle non-finite values.
Results may differ from a plain program's by a relative error of at most 0.0055.
The roundings to bfloat16 on the way count: a program that leaves them out, or rounds other values in their place, can miss the bound.
Values may be sent and summed in bfloat16 or wider, within the bound.
No kernel may reach another device: no remote copies, remote signals or barrier semaphores. Data moves between devices by JAX's collectives and lax.ppermute only.
A program may use at most 256 MiB of HBM per device.

v0:
```python
from functools import partial

import jax
import jax.numpy as jnp
from jax import lax
from jax.sharding import PartitionSpec as P

HEADS = 12
HD = 64
MASK_ID = 103
NCORP = 4
STEP = 5
CAP = 64


clip_norm = 0.1
learn_rate = 0.3
beta_first = 0.9
beta_second = 0.999
adam_eps = 1e-06
weight_decay = 0.01
norm_eps = 1e-05
masked_score = -1e30
bfloat = jnp.bfloat16
single = jnp.float32


def combined_all(value, axis, join):
    pieces = jax.tree.map(lambda part: lax.all_gather(part, axis), value)
    head = jax.tree.map(lambda part: part[0], pieces)
    tail = jax.tree.map(lambda part: part[1:], pieces)
    so_far, _ = lax.scan(lambda so_far, slab: (join(so_far, slab), None), head, tail)
    return so_far


def plain_dot(left_op, right_op):
    return jnp.dot(left_op, right_op, preferred_element_type=single)


def trans_dot(left_op, right_op):
    return lax.dot_general(
        left_op, right_op, (((1,), (1,)), ((), ())), preferred_element_type=single
    )


def rows_dot(left_op, right_op):
    return lax.dot_general(
        left_op, right_op, (((0,), (0,)), ((), ())), preferred_element_type=single
    )


def column_sum(values):
    return jnp.sum(values.astype(single), axis=0)


def norm_forward(values, gain_row, bias_row):
    center = values - jnp.mean(values, axis=-1, keepdims=True)
    inverse = lax.rsqrt(jnp.mean(center * center, axis=-1, keepdims=True) + norm_eps)
    normed = center * inverse
    return (normed * gain_row + bias_row, (normed, inverse))


def norm_backward(upstream, kept_norm, gain_row):
    normed, inverse = kept_norm
    scaled = upstream * gain_row
    inner = (
        scaled
        - jnp.mean(scaled, axis=-1, keepdims=True)
        - normed * jnp.mean(scaled * normed, axis=-1, keepdims=True)
    )
    return (inner * inverse, jnp.sum(upstream * normed, axis=0), jnp.sum(upstream, axis=0))


def split_heads(rows):
    return rows.reshape(rows.shape[0], HEADS, HD)


def attention_probs(query_rows, key_rows, allowed, log_total):
    scores = jnp.einsum(
        "qhd,khd->hqk",
        split_heads(query_rows),
        split_heads(key_rows),
        preferred_element_type=single,
    ) * HD ** (-0.5)
    scores = jnp.where(allowed[None], scores, masked_score)
    if log_total is None:
        row_top = jnp.max(scores, axis=-1, keepdims=True)
        log_total = row_top + jnp.log(jnp.sum(jnp.exp(scores - row_top), axis=-1, keepdims=True))
    return (jnp.exp(scores - log_total), log_total)


def layer_forward(layer_b, small_full, stream_b, query_init, allowed):
    width = stream_b.shape[1]
    key_rows = plain_dot(stream_b, layer_b[0, :, width : 2 * width]).astype(bfloat)
    value_rows = (plain_dot(stream_b, layer_b[0, :, 2 * width : 3 * width]) + small_full[3]).astype(
        bfloat
    )
    init_b = query_init.astype(bfloat)
    query_rows = (plain_dot(init_b, layer_b[0, :, :width]) + small_full[2]).astype(bfloat)
    attn_probs, log_total = attention_probs(query_rows, key_rows, allowed, None)
    mixed_b = jnp.einsum(
        "hqk,khd->qhd",
        attn_probs.astype(bfloat),
        split_heads(value_rows),
        preferred_element_type=single,
    )
    mixed_b = mixed_b.reshape(-1, width).astype(bfloat)
    attend = plain_dot(mixed_b, layer_b[0, :, 3 * width :]) + small_full[4]
    middle, middle_kept = norm_forward(query_init + attend, small_full[5], small_full[6])
    middle_b = middle.astype(bfloat)
    hidden = plain_dot(middle_b, layer_b[1]) + small_full[7:11].reshape(-1)
    active_b = jax.nn.gelu(hidden, approximate=False).astype(bfloat)
    branch = trans_dot(active_b, layer_b[2]) + small_full[11]
    output_rows, final_kept = norm_forward(middle + branch, small_full[12], small_full[13])
    kept_state = (
        key_rows,
        value_rows,
        init_b,
        query_rows,
        log_total,
        mixed_b,
        middle_kept,
        middle_b,
        hidden,
        active_b,
        final_kept,
    )
    return (output_rows, kept_state)


def layer_backward(layer_b, small_full, stream_b, allowed, kept_state, d_output):
    (
        key_rows,
        value_rows,
        init_b,
        query_rows,
        log_total,
        mixed_b,
        middle_kept,
        middle_b,
        hidden,
        active_b,
        final_kept,
    ) = kept_state
    width = stream_b.shape[1]
    d_sum, gain_three, bias_three = norm_backward(d_output, final_kept, small_full[12])
    d_branch = d_sum.astype(bfloat)
    grad_down = rows_dot(d_branch, active_b)
    _, gelu_pull = jax.vjp(partial(jax.nn.gelu, approximate=False), hidden)
    d_hidden = gelu_pull(plain_dot(d_branch, layer_b[2]))[0].astype(bfloat)
    grad_up = rows_dot(middle_b, d_hidden)
    d_middle = d_sum + trans_dot(d_hidden, layer_b[1])
    d_pre, gain_two, bias_two = norm_backward(d_middle, middle_kept, small_full[5])
    d_attend = d_pre.astype(bfloat)
    grad_out = rows_dot(mixed_b, d_attend)
    d_mixed = trans_dot(d_attend, layer_b[0, :, 3 * width :]).astype(bfloat)
    attn_probs, _ = attention_probs(query_rows, key_rows, allowed, log_total)
    mixed_heads = split_heads(d_mixed)
    d_probs = jnp.einsum(
        "qhd,khd->hqk", mixed_heads, split_heads(value_rows), preferred_element_type=single
    )
    d_value = jnp.einsum(
        "hqk,qhd->khd", attn_probs.astype(bfloat), mixed_heads, preferred_element_type=single
    )
    d_value = d_value.reshape(-1, width).astype(bfloat)
    d_scores = (
        attn_probs * (d_probs - jnp.sum(attn_probs * d_probs, axis=-1, keepdims=True))
    ).astype(bfloat)
    scale = HD ** (-0.5)
    d_query = (
        jnp.einsum("hqk,khd->qhd", d_scores, split_heads(key_rows), preferred_element_type=single)
        * scale
    )
    d_query = d_query.reshape(-1, width).astype(bfloat)
    d_key = (
        jnp.einsum("hqk,qhd->khd", d_scores, split_heads(query_rows), preferred_element_type=single)
        * scale
    )
    d_key = d_key.reshape(-1, width).astype(bfloat)
    grad_query = rows_dot(init_b, d_query)
    d_init = d_pre + trans_dot(d_query, layer_b[0, :, :width])
    grad_key = rows_dot(stream_b, d_key)
    grad_value = rows_dot(stream_b, d_value)
    d_stream = trans_dot(d_key, layer_b[0, :, width : 2 * width]) + trans_dot(
        d_value, layer_b[0, :, 2 * width : 3 * width]
    )
    grad_layer = jnp.stack(
        [jnp.concatenate([grad_query, grad_key, grad_value, grad_out], axis=1), grad_up, grad_down]
    )
    grad_mid = jnp.concatenate(
        [
            column_sum(d_query)[None],
            column_sum(d_value)[None],
            column_sum(d_attend)[None],
            gain_two[None],
            bias_two[None],
            column_sum(d_hidden).reshape(4, width),
            column_sum(d_branch)[None],
            gain_three[None],
            bias_three[None],
        ]
    )
    return (grad_layer, grad_mid, d_init, d_stream)


def adam_moments(weight_arr, first_mom, second_mom, gradient, factor):
    clipped = gradient * factor
    new_first = beta_first * first_mom + (1.0 - beta_first) * clipped
    new_second = beta_second * second_mom + (1.0 - beta_second) * clipped * clipped
    direction = (
        new_first
        / (1.0 - beta_first**STEP)
        / (jnp.sqrt(new_second / (1.0 - beta_second**STEP)) + adam_eps)
        + weight_decay * weight_arr
    )
    return (new_first, new_second, direction)


def norm_pair(weight_arr, direction, axes):
    return jnp.stack(
        [jnp.sum(weight_arr * weight_arr, axis=axes), jnp.sum(direction * direction, axis=axes)],
        axis=-1,
    )


def combine_parts(one_side, other_side):
    row_top = jnp.maximum(one_side[0], other_side[0])
    total = one_side[1] * jnp.exp(one_side[0] - row_top) + other_side[1] * jnp.exp(
        other_side[0] - row_top
    )
    return (row_top, total)


def on_device(
    token_ids,
    pred_mask,
    fact_order,
    corpus,
    embed_table,
    table_moment,
    table_square,
    layer_weights,
    layer_moment,
    layer_square,
    position_table,
    position_moment,
    position_square,
    small_params,
    small_moment,
    small_square,
):
    layer_b, position_b, small_b = (
        lax.all_gather(layer_weights.astype(bfloat), ("dp", "vocab"), axis=1, tiled=True),
        lax.all_gather(position_table.astype(bfloat), ("dp", "vocab"), axis=1, tiled=True),
        lax.all_gather(small_params.astype(bfloat), ("dp", "vocab"), axis=1, tiled=True),
    )
    small_full = small_b.astype(single)
    position_full = position_b.astype(single)
    token_row = token_ids[0]
    pred_row = pred_mask[0]
    width = embed_table.shape[1]
    vrows = embed_table.shape[0]
    content = jnp.where(pred_row == 1, MASK_ID, token_row)
    rank_row = jnp.argsort(fact_order[0])
    slot_pos = jnp.argsort(1 - pred_row, stable=True)[:CAP]
    live_slots = jnp.arange(CAP) < jnp.sum(pred_row)
    slot_tag = jnp.where(live_slots, corpus[0], NCORP)
    slot_target = token_row[slot_pos]
    group_content, group_target, group_tag = (
        lax.all_gather(content, "vocab", axis=0, tiled=True),
        lax.all_gather(slot_target, "vocab", axis=0, tiled=True),
        lax.all_gather(slot_tag, "vocab", axis=0, tiled=True),
    )
    count_term = (jnp.arange(NCORP) == corpus[0]).astype(single) * jnp.sum(pred_row).astype(single)
    corpus_counts = lax.psum(count_term, ("dp", "vocab"))
    vocab_devs = lax.axis_size("vocab")
    first_row = lax.axis_index("vocab") * vrows
    table_b = embed_table.astype(bfloat)
    local_ids = group_content - first_row
    owned_rows = (local_ids >= 0) & (local_ids < vrows)
    picked = jnp.take(table_b, jnp.clip(local_ids, 0, vrows - 1), axis=0)
    outgoing = jnp.where(owned_rows[:, None], picked, jnp.zeros_like(picked)).reshape(
        vocab_devs, -1, width
    )
    arrived = lax.all_to_all(outgoing, "vocab", split_axis=0, concat_axis=0, tiled=True)
    embed_rows = jnp.sum(arrived, axis=0, dtype=single)
    stream, stream_kept = norm_forward(embed_rows + position_full, small_full[0], small_full[1])
    stream_b = stream.astype(bfloat)
    query_init, init_kept = norm_forward(position_full[slot_pos], small_full[0], small_full[1])
    allowed = rank_row[None, :] <= rank_row[slot_pos][:, None]
    output_rows, kept_state = layer_forward(layer_b, small_full, stream_b, query_init, allowed)
    output_b = output_rows.astype(bfloat)
    group_rows = lax.all_gather(output_b, "vocab", axis=0, tiled=True)
    logits = trans_dot(group_rows, table_b)
    local_target = group_target - first_row
    target_hit = jnp.arange(vrows)[None, :] == local_target[:, None]
    row_top = jnp.max(logits, axis=1)
    row_total = jnp.sum(jnp.exp(logits - row_top[:, None]), axis=1)
    row_target = jnp.sum(jnp.where(target_hit, logits, 0.0), axis=1)
    top_all, total_all = combined_all((row_top, row_total), "vocab", combine_parts)
    log_total = top_all + jnp.log(total_all)
    corpus_match = group_tag[:, None] == jnp.arange(NCORP)[None, :]
    group_weight = jnp.sum(
        jnp.where(corpus_match, 1.0 / (NCORP * corpus_counts)[None, :], 0.0), axis=1
    )
    own_total = lax.dynamic_slice_in_dim(
        log_total * group_weight, lax.axis_index("vocab") * CAP, CAP, 0
    )
    loss_part = jnp.sum(own_total) - jnp.sum(row_target * group_weight)
    d_logits = (
        group_weight[:, None] * (jnp.exp(logits - log_total[:, None]) - target_hit.astype(single))
    ).astype(bfloat)
    grad_head = rows_dot(d_logits, group_rows)
    d_output = lax.psum_scatter(
        plain_dot(d_logits, table_b), "vocab", scatter_dimension=0, tiled=True
    )
    grad_layer, grad_mid, d_init, d_stream = layer_backward(
        layer_b, small_full, stream_b, allowed, kept_state, d_output
    )
    d_start, gain_init, bias_init = norm_backward(d_init, init_kept, small_full[0])
    d_embed, gain_stream, bias_stream = norm_backward(d_stream, stream_kept, small_full[0])
    grad_position = d_embed.at[slot_pos].add(d_start)
    grad_small = jnp.concatenate(
        [(gain_init + gain_stream)[None], (bias_init + bias_stream)[None], grad_mid]
    )
    embed_back = d_embed.astype(bfloat)
    piece_ids = group_content - first_row
    owned_piece = (piece_ids >= 0) & (piece_ids < vrows)
    segment = jnp.where(owned_piece, piece_ids, vrows)
    summed = jax.ops.segment_sum(
        lax.all_gather(embed_back[None], "vocab", axis=0, tiled=True)
        .reshape(-1, width)
        .astype(single),
        segment,
        num_segments=vrows + 1,
    )
    grad_lookup = summed[:vrows]
    table_grad = lax.psum(grad_head + grad_lookup, "dp")
    layer_grad, position_grad, small_grad = (
        lax.psum_scatter(grad_layer, ("dp", "vocab"), scatter_dimension=1, tiled=True),
        lax.psum_scatter(grad_position, ("dp", "vocab"), scatter_dimension=1, tiled=True),
        lax.psum_scatter(grad_small, ("dp", "vocab"), scatter_dimension=1, tiled=True),
    )
    dp_devs = lax.axis_size("dp")
    square_part = (
        jnp.sum(table_grad * table_grad) / dp_devs
        + jnp.sum(layer_grad * layer_grad)
        + jnp.sum(position_grad * position_grad)
        + jnp.sum(small_grad * small_grad)
    )
    total_square, loss_value = lax.psum((square_part, loss_part), ("dp", "vocab"))
    grad_norm = jnp.sqrt(total_square)
    factor = jnp.minimum(1.0, clip_norm / grad_norm)
    table_first, table_second, table_dir = adam_moments(
        embed_table, table_moment, table_square, table_grad, factor
    )
    layer_first, layer_second, layer_dir = adam_moments(
        layer_weights, layer_moment, layer_square, layer_grad, factor
    )
    position_first, position_second, position_dir = adam_moments(
        position_table, position_moment, position_square, position_grad, factor
    )
    small_first, small_second, small_dir = adam_moments(
        small_params, small_moment, small_square, small_grad, factor
    )
    partial_norms = jnp.concatenate(
        [
            norm_pair(embed_table, table_dir, (0, 1))[None] / dp_devs,
            norm_pair(layer_weights, layer_dir, (1, 2)),
            norm_pair(position_table, position_dir, (0, 1))[None],
            norm_pair(small_params, small_dir, (0, 1))[None],
        ]
    )
    trust_square = lax.psum(partial_norms, ("dp", "vocab"))
    trust_norms = jnp.sqrt(trust_square)
    ratio = trust_norms[:, 0] / trust_norms[:, 1]
    table_next = embed_table - learn_rate * ratio[0] * table_dir
    layer_next = layer_weights - learn_rate * ratio[1:4][:, None, None] * layer_dir
    position_next = position_table - learn_rate * ratio[4] * position_dir
    small_next = small_params - learn_rate * ratio[5] * small_dir
    return (
        loss_value,
        grad_norm,
        table_next,
        table_first,
        table_second,
        layer_next,
        layer_first,
        layer_second,
        position_next,
        position_first,
        position_second,
        small_next,
        small_first,
        small_second,
        trust_norms,
    )


def solution(mesh):
    return jax.shard_map(
        on_device,
        mesh=mesh,
        in_specs=(
            P(("dp", "vocab"), None),
            P(("dp", "vocab"), None),
            P(("dp", "vocab"), None),
            P(("dp", "vocab")),
            P("vocab", None),
            P("vocab", None),
            P("vocab", None),
            P(None, ("dp", "vocab"), None),
            P(None, ("dp", "vocab"), None),
            P(None, ("dp", "vocab"), None),
            P(None, ("dp", "vocab")),
            P(None, ("dp", "vocab")),
            P(None, ("dp", "vocab")),
            P(None, ("dp", "vocab")),
            P(None, ("dp", "vocab")),
            P(None, ("dp", "vocab")),
        ),
        out_specs=(
            P(),
            P(),
            P("vocab", None),
            P("vocab", None),
            P("vocab", None),
            P(None, ("dp", "vocab"), None),
            P(None, ("dp", "vocab"), None),
            P(None, ("dp", "vocab"), None),
            P(None, ("dp", "vocab")),
            P(None, ("dp", "vocab")),
            P(None, ("dp", "vocab")),
            P(None, ("dp", "vocab")),
            P(None, ("dp", "vocab")),
            P(None, ("dp", "vocab")),
            P(),
        ),
        check_vma=False,
    )
```

profile of v0, /device:TPU:0, one launch (start us, length us, event | category | flops | bytes accessed | tf_op | source)
XLA Modules:
  0.0 1609.4 jit_solution(1861759870598335878)
XLA Ops:
  10.6 23.1 %all-gather.5 = s32[16,1,256]{2,1,0:T(1,128)S(1)} all-gather(s32[1,1,256]{2,1,0:T(1,128)S(1)} %bitcast.174), channel_id=1, replica_groups=mesh['dp'=2,'vocab'=16] {'vocab'}, dimensions={0}, use_global_device_ids=true | all-gather | bytes 17408 | tf_op jit(solution)/shard_map/all_gather | solution.py:270
  37.4 17.8 %gather_fusion.1 = bf16[4096,768]{1,0:T(8,128)(2,1)} fusion(bf16[1920,768]{1,0:T(8,128)(2,1)S(1)} %convert_element_type.150, s32[4096]{0:T(1024)S(1)} %get-tuple-element.184), kind=kCustom, calls=%fused_computation.1 | custom fusion | bytes 12599296 | tf_op jit(solution)/shard_map/jit(_take)/gather | solution.py:281
  55.2 6.3 select_select_fusion
  66.4 203.4 %all-gather.4 = bf16[32,24,14]{1,2,0:T(8,128)(2,1)S(1)} all-gather(bf16[1,24,14]{1,2,0:T(8,128)(2,1)S(1)} %convert_bitcast_fusion), channel_id=1, replica_groups=mesh['dp'=2,'vocab'=16] {'dp','vocab'}, dimensions={0}, use_global_device_ids=true | all-gather | bytes 22176 | tf_op jit(solution)/shard_map/all_gather | solution.py:255
  270.9 40.3 %all_gather.36 = bf16[256,768]{0,1:T(8,128)(2,1)} all-gather(bf16[256,24]{0,1:T(8,128)(2,1)S(1)} %convert_element_type.146), channel_id=1, replica_groups=mesh['dp'=2,'vocab'=16] {'dp','vocab'}, dimensions={1}, use_global_device_ids=true | all-gather | bytes 405504 | tf_op jit(solution)/shard_map/all_gather | solution.py:254
  365.3 39.3 %psum.35 = f32[4]{0:T(128)} all-reduce(f32[4]{0:T(128)} %compare_select_fusion.2), channel_id=1, replica_groups=mesh['dp'=2,'vocab'=16] {'dp','vocab'}, use_global_device_ids=true, to_apply=%region_18.19 | all-reduce | flops 4 | bytes 32 | tf_op jit(solution)/shard_map/psum | solution.py:275
  408.9 12.5 all-reduce.4
  429.0 19.3 %all-gather = f32[16384]{0:T(1024)S(1)} all-gather(f32[1024]{0:T(1024)S(1)} %get-tuple-element.199), channel_id=2, replica_groups=mesh['dp'=2,'vocab'=16] {'vocab'}, dimensions={0}, use_global_device_ids=true | all-gather | bytes 69632 | tf_op jit(solution)/shard_map/all_gather | solution.py:29
  452.5 17.6 %all-gather.1 = f32[16384]{0:T(1024)S(1)} all-gather(f32[1024]{0:T(1024)S(1)} %get-tuple-element.110), channel_id=3, replica_groups=mesh['dp'=2,'vocab'=16] {'vocab'}, dimensions={0}, use_global_device_ids=true | all-gather | bytes 69632 | tf_op jit(solution)/shard_map/all_gather | solution.py:29
  474.3 31.2 %while.12 = (s32[]{:T(128)}, f32[1024]{0:T(1024)S(1)}, f32[1024]{0:T(1024)}, f32[15,1024]{1,0:T(8,128)}, f32[15,1024]{1,0:T(8,128)}, /*index=5*/s32[]{:T(128)}) while((s32[]{:T(128)}, f32[1024]{0:T(1024)S(1)}, f32[1024]{0:T(1024)}, f32[15,1024]{1,0:T(8,128)}, f32[15,1024]{1,0:T(8,128)}, /*index=5*/s32[]{:T(128)}) %tuple.90), condition=%wide.region_16.17_spmd, body=%wide.region_15.16_spmd.sunk | while | flops 6146 | bytes 41041 | solution.py:32
  519.6 64.1 %reduce-scatter.6.cloned.1.call-done = f32[64,768]{1,0:T(8,128)} async-done(((f32[1024,768]{1,0:T(8,128)}), f32[64,768]{1,0:T(8,128)}) %reduce-scatter.6.cloned.1.call-update) | async-done | bytes 196624 | tf_op jit(solution)/shard_map/reduce_scatter | solution.py:314
  616.8 6.2 convolution_bitcast_fusion.1
  630.3 6.6 convolution_bitcast_fusion
  641.1 17.2 %pad_maximum_fusion = f32[3,768,3072]{1,2,0:T(8,128)} fusion(f32[1,768,3072]{1,2,0:T(8,128)} %convolution_bitcast_fusion, f32[1,768,3072]{1,2,0:T(8,128)} %convolution_bitcast_fusion.1, f32[1,768,3072]{1,2,0:T(8,128)S(1)} %maximum_bitcast_fusion), kind=kLoop, calls=%fused_computation.9 | loop fusion | flops 14155776 | bytes 56623104 | tf_op jit(solution)/shard_map/stack | solution.py:187
  658.3 40.7 %copy.153 = f32[3,768,3072]{2,0,1:T(4,128)} copy(f32[3,768,3072]{1,2,0:T(8,128)} %pad_maximum_fusion) | data formatting | bytes 56623104 | tf_op jit(solution)/shard_map/stack | solution.py:187
  699.1 31.2 %scatter_custom_fusion = f32[1921,768]{1,0:T(8,128)} fusion(s32[4096]{0:T(1024)} %get-tuple-element.183, bf16[4096,768]{1,0:T(8,128)(2,1)} %all-gather.14.cloned.1.call-done, f32[]{:T(128)} %constant.68.clone.1), kind=kCustom, calls=%fused_computation.10 | custom fusion | flops 6291456 | bytes 12193280 | tf_op jit(solution)/shard_map/scatter-add | solution.py:330
  730.3 9.8 slice_add_fusion
  742.3 41.5 %all-reduce.3 = f32[14,768]{1,0:T(8,128)S(1)} all-reduce(f32[14,768]{1,0:T(8,128)S(1)} %concatenate.17), channel_id=9, replica_groups=mesh['dp'=2,'vocab'=16] {'dp','vocab'}, use_global_device_ids=true, to_apply=%region_55.56.clone | all-reduce | flops 10752 | bytes 86016
  786.0 540.0 %all-reduce.11.cloned.1.call-done = f32[3,768,3072]{2,0,1:T(4,128)} async-done(((f32[3,768,3072]{2,0,1:T(4,128)}), f32[3,768,3072]{2,0,1:T(4,128)}) %all-reduce.11.cloned.1.call-update) | async-done | bytes 28311568
  1328.5 145.2 %all-reduce.9.cloned.1.call-done = f32[1920,768]{1,0:T(8,128)} async-done(((f32[1920,768]{1,0:T(8,128)}), f32[1920,768]{1,0:T(8,128)}) %all-reduce.9.cloned.1.call-update) | async-done | bytes 5898256 | tf_op jit(solution)/shard_map/psum | solution.py:338
  1482.4 39.4 %psum.38 = f32[]{:T(128)} all-reduce(f32[]{:T(128)S(6)} %add.342), channel_id=1, replica_groups=mesh['dp'=2,'vocab'=16] {'dp','vocab'}, use_global_device_ids=true, to_apply=%region_57.58 | all-reduce | flops 1 | bytes 8 | tf_op jit(solution)/shard_map/psum | solution.py:351
  1526.8 13.6 multiply_reduce_fusion.1
  1543.8 41.4 %all-reduce.5 = (f32[]{:T(128)}, f32[6,2]{0,1:T(2,128)S(1)}) all-reduce(f32[]{:T(128)S(6)} %sub.184, f32[6,2]{0,1:T(2,128)S(1)} %pad_maximum_fusion.1), channel_id=1, replica_groups=mesh['dp'=2,'vocab'=16] {'dp','vocab'}, use_global_device_ids=true, to_apply=%region_23.24 | all-reduce | flops 13 | bytes 104 | tf_op jit(solution)/shard_map/psum | solution.py:351
  1591.7 9.2 multiply_subtract_fusion
  (380 shorter events, 198.3 us)
Async XLA Ops:
  7.2 327.0 %all-gather.10.cloned.1.call-start = ((), (), s32[]{:S(2)}) async-start(), calls=%async_computation.3 | async-start | bytes 14598144 | tf_op jit(solution)/shard_map/all_gather | solution.py:253
  61.5 251.9 %copy-start.83 = (s32[1,256]{1,0:T(1,128)S(1)}, s32[1,256]{1,0:T(1,128)}, u32[]{:S(2)}) copy-start(s32[1,256]{1,0:T(1,128)} %param.20) | copy-start | bytes 3076
  61.5 255.0 %copy-start.84 = (s32[1,256]{1,0:T(1,128)S(1)}, s32[1,256]{1,0:T(1,128)}, u32[]{:S(2)}) copy-start(s32[1,256]{1,0:T(1,128)} %param.19) | copy-start | bytes 3076
  61.5 267.6 %all-to-all-start = ((bf16[16,256,768]{2,1,0:T(8,128)(2,1)}), bf16[16,256,768]{2,1,0:T(8,128)(2,1)}, u32[]{:S(2)}, u32[]{:S(2)}) async-start(bf16[16,256,768]{2,1,0:T(8,128)(2,1)} %select_select_fusion), calls=%async_computation | async-start | bytes 12582912 | tf_op jit(solution)/shard_map/all_to_all | solution.py:285
  66.3 357.7 %all-gather.12.cloned.1.call-start = ((), (), s32[]{:S(2)}) async-start(), calls=%async_computation.4 | async-start | bytes 1671168 | tf_op jit(solution)/shard_map/all_gather | solution.py:293
  363.5 220.3 %reduce-scatter.6.cloned.1.call-start = ((), (), s32[]{:S(2)}) async-start(), calls=%async_computation.5 | async-start | bytes 3342336 | tf_op jit(solution)/shard_map/reduce_scatter | solution.py:314
  514.3 69.4 %copy-start.44 = (f32[768]{0:T(1024)S(1)}, f32[768]{0:T(1024)}, u32[]{:S(2)}) copy-start(f32[768]{0:T(1024)} %get-tuple-element.131) | copy-start | bytes 9220
  514.3 69.4 %copy-start.68 = (f32[64]{0:T(128)S(1)}, f32[64]{0:T(128)}, u32[]{:S(2)}) copy-start(f32[64]{0:T(128)} %copy-done.67) | copy-start | bytes 772
  519.4 179.7 %all-gather.14.cloned.1.call-start = ((), (), s32[]{:S(2)}) async-start(), calls=%async_computation.7 | async-start | bytes 6684672 | tf_op jit(solution)/shard_map/all_gather | solution.py:331
  610.2 174.3 %reduce-scatter.8.cloned.1.call-start = ((), (), s32[]{:S(2)}) async-start(), calls=%async_computation.8 | async-start | bytes 811008
  636.9 689.1 %all-reduce.11.cloned.1.call-start = ((), (), s32[]{:S(2)}) async-start(), calls=%async_computation.9 | async-start | bytes 75497472
  699.0 774.7 %all-reduce.9.cloned.1.call-start = ((), (), s32[]{:S(2)}) async-start(), calls=%async_computation.6 | async-start | bytes 11796480 | tf_op jit(solution)/shard_map/psum | solution.py:338
  740.3 782.2 %copy-start.40 = (f32[14,24]{1,0:T(8,128)S(1)}, f32[14,24]{1,0:T(8,128)}, u32[]{:S(2)}) copy-start(f32[14,24]{1,0:T(8,128)} %param.31) | copy-start | bytes 4036
  740.3 782.2 %copy-start.69 = (f32[14,24]{1,0:T(8,128)S(1)}, f32[14,24]{1,0:T(8,128)}, u32[]{:S(2)}) copy-start(f32[14,24]{1,0:T(8,128)} %param.32) | copy-start | bytes 4036
  740.3 782.2 %copy-start.70 = (f32[14,24]{1,0:T(8,128)S(1)}, f32[14,24]{1,0:T(8,128)}, u32[]{:S(2)}) copy-start(f32[14,24]{1,0:T(8,128)} %param.33) | copy-start | bytes 4036
  740.3 784.4 %copy-start.25 = (f32[256,24]{0,1:T(8,128)S(1)}, f32[256,24]{0,1:T(8,128)}, u32[]{:S(2)}) copy-start(f32[256,24]{0,1:T(8,128)} %param.28) | copy-start | bytes 73732
  740.3 784.4 %copy-start.50 = (f32[256,24]{0,1:T(8,128)S(1)}, f32[256,24]{0,1:T(8,128)}, u32[]{:S(2)}) copy-start(f32[256,24]{0,1:T(8,128)} %param.29) | copy-start | bytes 73732
  740.3 784.4 %copy-start.51 = (f32[256,24]{0,1:T(8,128)S(1)}, f32[256,24]{0,1:T(8,128)}, u32[]{:S(2)}) copy-start(f32[256,24]{0,1:T(8,128)} %param.30) | copy-start | bytes 73732
  784.4 740.2 %copy-start.36 = (f32[24,256]{1,0:T(8,128)S(1)}, f32[24,256]{1,0:T(8,128)}, u32[]{:S(2)}) copy-start(f32[24,256]{1,0:T(8,128)} %reduce-scatter.8.cloned.1.call-done) | copy-start | bytes 73732
  1523.2 64.7 %copy-start.48 = (f32[14,24]{1,0:T(8,128)}, f32[14,24]{1,0:T(8,128)S(1)}, u32[]{:S(2)}) copy-start(f32[14,24]{1,0:T(8,128)S(1)} %get-tuple-element.167) | copy-start | bytes 4036
  1523.2 64.7 %copy-start.49 = (f32[14,24]{1,0:T(8,128)}, f32[14,24]{1,0:T(8,128)S(1)}, u32[]{:S(2)}) copy-start(f32[14,24]{1,0:T(8,128)S(1)} %get-tuple-element.168) | copy-start | bytes 4036
  1525.3 63.2 %copy-start.37 = (f32[256,24]{0,1:T(8,128)}, f32[256,24]{0,1:T(8,128)S(1)}, u32[]{:S(2)}) copy-start(f32[256,24]{0,1:T(8,128)S(1)} %get-tuple-element.165) | copy-start | bytes 73732
  1525.3 63.2 %copy-start.38 = (f32[256,24]{0,1:T(8,128)}, f32[256,24]{0,1:T(8,128)S(1)}, u32[]{:S(2)}) copy-start(f32[256,24]{0,1:T(8,128)S(1)} %get-tuple-element.166) | copy-start | bytes 73732
  1543.7 57.2 %copy-start.9 = (f32[3,24,3072]{2,1,0:T(8,128)}, f32[3,24,3072]{2,1,0:T(8,128)S(1)}, u32[]{:S(2)}) copy-start(f32[3,24,3072]{2,1,0:T(8,128)S(1)} %get-tuple-element.163) | copy-start | bytes 2654212
  (75 other events, 601.5 us)
Sparse Core Ops, SparseCore 0:
  11.5 186.4 all-gather.9
  363.6 38.1 all-gather.11
  519.5 64.1 reduce-scatter.5
  610.3 60.7 all-gather.13
  676.6 94.2 reduce-scatter.7
  777.2 548.7 all-reduce.10
  1329.0 144.6 all-reduce.8
where the time goes:
time: 1620 us; the launch traced here: 1610 us
  waiting for transfers between devices  749 us (46%)
  blocking collectives  478 us (30%)
  other arithmetic  168 us (10%)
  local copies, waits for them, and re-layouts  101 us (6%)
  matrix products  82.4 us (5%)
  between operations  25.5 us (2%)
    unnamed x9, waiting for transfers between devices  540 us
    all_gather x1, blocking collectives, on_device(): lax.all_gather(small_params.astype(bfloat), ('dp', 'vocab'), axis=1, tile...  203 us
    psum x1, waiting for transfers between devices, on_device(): table_grad = lax.psum(grad_head + grad_lookup, 'dp')  145 us
    psum x2, blocking collectives, on_device(): lax.psum((square_part, loss_part), ('dp', 'vocab'))  80.8 us
    reduce_scatter x1, waiting for transfers between devices, on_device(): lax.psum_scatter(plain_dot(d_logits, table_b), 'vocab', scatter_dimension...  64.1 us
    unnamed x2, blocking collectives  53.9 us
    another operation x1, local copies, waits for them, and re-layouts, layer_backward(): jnp.stack([jnp.concatenate([grad_query, grad_key, grad_value, grad_out],...  40.7 us
    all_gather x1, blocking collectives, on_device(): lax.all_gather(position_table.astype(bfloat), ('dp', 'vocab'), axis=1, ti...  40.3 us
  transfers between devices with their start and end apart: 8, of which 3 were waited for; matrix products, arithmetic and copies ran while one was open for 12% of the time, Pallas kernels for 0%

commit v1 on v0

v1 whole, which is shorter than its diff:
```python
from functools import partial

import jax
import jax.numpy as jnp
from jax import lax
from jax.sharding import Mesh
from jax.sharding import PartitionSpec as P

HEADS = 12
HD = 64
MASK_ID = 103
NCORP = 4
STEP = 5
CAP = 64


clip_norm = 0.1
learn_rate = 0.3
beta_first = 0.9
beta_second = 0.999
adam_eps = 1e-06
weight_decay = 0.01
norm_eps = 1e-05
masked_score = -1e30
BUCKET = 32
ALL = ("dp", "hi", "mid", "core")
VOC = ("hi", "mid", "core")
bfloat = jnp.bfloat16
single = jnp.float32


def plain_dot(left_op, right_op):
    return jnp.dot(left_op, right_op, preferred_element_type=single)


def trans_dot(left_op, right_op):
    return lax.dot_general(
        left_op, right_op, (((1,), (1,)), ((), ())), preferred_element_type=single
    )


def rows_dot(left_op, right_op):
    return lax.dot_general(
        left_op, right_op, (((0,), (0,)), ((), ())), preferred_element_type=single
    )


def column_sum(values):
    return jnp.sum(values.astype(single), axis=0)


def norm_forward(values, gain_row, bias_row):
    center = values - jnp.mean(values, axis=-1, keepdims=True)
    inverse = lax.rsqrt(jnp.mean(center * center, axis=-1, keepdims=True) + norm_eps)
    normed = center * inverse
    return (normed * gain_row + bias_row, (normed, inverse))


def norm_backward(upstream, kept_norm, gain_row):
    normed, inverse = kept_norm
    scaled = upstream * gain_row
    inner = (
        scaled
        - jnp.mean(scaled, axis=-1, keepdims=True)
        - normed * jnp.mean(scaled * normed, axis=-1, keepdims=True)
    )
    return (inner * inverse, jnp.sum(upstream * normed, axis=0), jnp.sum(upstream, axis=0))


def split_heads(rows):
    return rows.reshape(rows.shape[0], HEADS, HD)


def attention_probs(query_rows, key_rows, allowed, log_total):
    scores = jnp.einsum(
        "qhd,khd->hqk",
        split_heads(query_rows),
        split_heads(key_rows),
        preferred_element_type=single,
    ) * HD ** (-0.5)
    scores = jnp.where(allowed[None], scores, masked_score)
    if log_total is None:
        row_top = jnp.max(scores, axis=-1, keepdims=True)
        log_total = row_top + jnp.log(jnp.sum(jnp.exp(scores - row_top), axis=-1, keepdims=True))
    return (jnp.exp(scores - log_total), log_total)


def layer_forward(layer_b, small_full, stream_b, query_init, allowed):
    width = stream_b.shape[1]
    key_rows = plain_dot(stream_b, layer_b[0][:, width : 2 * width]).astype(bfloat)
    value_rows = (plain_dot(stream_b, layer_b[0][:, 2 * width : 3 * width]) + small_full[3]).astype(
        bfloat
    )
    init_b = query_init.astype(bfloat)
    query_rows = (plain_dot(init_b, layer_b[0][:, :width]) + small_full[2]).astype(bfloat)
    attn_probs, log_total = attention_probs(query_rows, key_rows, allowed, None)
    mixed_b = jnp.einsum(
        "hqk,khd->qhd",
        attn_probs.astype(bfloat),
        split_heads(value_rows),
        preferred_element_type=single,
    )
    mixed_b = mixed_b.reshape(-1, width).astype(bfloat)
    attend = plain_dot(mixed_b, layer_b[0][:, 3 * width :]) + small_full[4]
    middle, middle_kept = norm_forward(query_init + attend, small_full[5], small_full[6])
    middle_b = middle.astype(bfloat)
    hidden = plain_dot(middle_b, layer_b[1]) + small_full[7:11].reshape(-1)
    active_b = jax.nn.gelu(hidden, approximate=False).astype(bfloat)
    branch = trans_dot(active_b, layer_b[2]) + small_full[11]
    output_rows, final_kept = norm_forward(middle + branch, small_full[12], small_full[13])
    kept_state = (
        key_rows,
        value_rows,
        init_b,
        query_rows,
        log_total,
        mixed_b,
        middle_kept,
        middle_b,
        hidden,
        active_b,
        final_kept,
    )
    return (output_rows, kept_state)


def layer_backward(layer_b, small_full, stream_b, allowed, kept_state, d_output):
    (
        key_rows,
        value_rows,
        init_b,
        query_rows,
        log_total,
        mixed_b,
        middle_kept,
        middle_b,
        hidden,
        active_b,
        final_kept,
    ) = kept_state
    width = stream_b.shape[1]
    d_sum, gain_three, bias_three = norm_backward(d_output, final_kept, small_full[12])
    d_branch = d_sum.astype(bfloat)
    grad_down = rows_dot(d_branch, active_b)
    _, gelu_pull = jax.vjp(partial(jax.nn.gelu, approximate=False), hidden)
    d_hidden = gelu_pull(plain_dot(d_branch, layer_b[2]))[0].astype(bfloat)
    grad_up = rows_dot(middle_b, d_hidden)
    d_middle = d_sum + trans_dot(d_hidden, layer_b[1])
    d_pre, gain_two, bias_two = norm_backward(d_middle, middle_kept, small_full[5])
    d_attend = d_pre.astype(bfloat)
    grad_out = rows_dot(mixed_b, d_attend)
    d_mixed = trans_dot(d_attend, layer_b[0][:, 3 * width :]).astype(bfloat)
    attn_probs, _ = attention_probs(query_rows, key_rows, allowed, log_total)
    mixed_heads = split_heads(d_mixed)
    d_probs = jnp.einsum(
        "qhd,khd->hqk", mixed_heads, split_heads(value_rows), preferred_element_type=single
    )
    d_value = jnp.einsum(
        "hqk,qhd->khd", attn_probs.astype(bfloat), mixed_heads, preferred_element_type=single
    )
    d_value = d_value.reshape(-1, width).astype(bfloat)
    d_scores = (
        attn_probs * (d_probs - jnp.sum(attn_probs * d_probs, axis=-1, keepdims=True))
    ).astype(bfloat)
    scale = HD ** (-0.5)
    d_query = (
        jnp.einsum("hqk,khd->qhd", d_scores, split_heads(key_rows), preferred_element_type=single)
        * scale
    )
    d_query = d_query.reshape(-1, width).astype(bfloat)
    d_key = (
        jnp.einsum("hqk,qhd->khd", d_scores, split_heads(query_rows), preferred_element_type=single)
        * scale
    )
    d_key = d_key.reshape(-1, width).astype(bfloat)
    grad_query = rows_dot(init_b, d_query)
    d_init = d_pre + trans_dot(d_query, layer_b[0][:, :width])
    grad_key = rows_dot(stream_b, d_key)
    grad_value = rows_dot(stream_b, d_value)
    d_stream = trans_dot(d_key, layer_b[0][:, width : 2 * width]) + trans_dot(
        d_value, layer_b[0][:, 2 * width : 3 * width]
    )
    grad_layer = (
        jnp.concatenate([grad_query, grad_key, grad_value, grad_out], axis=1),
        grad_up,
        grad_down,
    )
    grad_mid = jnp.concatenate(
        [
            column_sum(d_query)[None],
            column_sum(d_value)[None],
            column_sum(d_attend)[None],
            gain_two[None],
            bias_two[None],
            column_sum(d_hidden).reshape(4, width),
            column_sum(d_branch)[None],
            gain_three[None],
            bias_three[None],
        ]
    )
    return (grad_layer, grad_mid, d_init, d_stream)


def adam_moments(weight_arr, first_mom, second_mom, gradient, factor):
    clipped = gradient * factor
    new_first = beta_first * first_mom + (1.0 - beta_first) * clipped
    new_second = beta_second * second_mom + (1.0 - beta_second) * clipped * clipped
    direction = (
        new_first
        / (1.0 - beta_first**STEP)
        / (jnp.sqrt(new_second / (1.0 - beta_second**STEP)) + adam_eps)
        + weight_decay * weight_arr
    )
    return (new_first, new_second, direction)


def norm_pair(weight_arr, direction, axes):
    return jnp.stack(
        [jnp.sum(weight_arr * weight_arr, axis=axes), jnp.sum(direction * direction, axis=axes)],
        axis=-1,
    )


def copies_to(values, axes, count):
    return lax.all_to_all(
        jnp.broadcast_to(values[None], (count,) + values.shape), axes, 0, 0, tiled=True
    )


def total_over(values, axes, count):
    return jnp.sum(copies_to(values, axes, count), axis=0)


def masked_total(mask, values):
    return jnp.sum(jnp.where(mask, values, 0), axis=-1)


def slot_layout(pred_row, order_row, token_row):
    length = pred_row.shape[0]
    index = jnp.arange(length)
    before = index[None, :] <= index[:, None]
    seen = masked_total(before, pred_row[None, :])
    masked = jnp.sum(pred_row)
    place = jnp.where(pred_row == 1, seen - 1, masked + index - seen)
    slot_hot = place[None, :] == jnp.arange(CAP)[:, None]
    rank_row = masked_total(order_row[None, :] == index[:, None], index[None, :])
    slot_rank = masked_total(slot_hot, rank_row[None, :])
    slot_target = masked_total(slot_hot, token_row[None, :])
    allowed = rank_row[None, :] <= slot_rank[:, None]
    return slot_hot, slot_target, allowed, masked


def bucket_layout(content, vrows):
    index = jnp.arange(content.shape[0])
    same = content[None, :] == content[:, None]
    first = jnp.min(jnp.where(same, index[None, :], content.shape[0]), axis=1)
    is_first = first == index
    owner = content // vrows
    ahead = (owner[None, :] == owner[:, None]) & is_first[None, :] & (index[None, :] < first[:, None])
    return owner, jnp.sum(ahead.astype(jnp.int32), axis=1)


def bucket_round(content, owner, place, turn, owners, vrows):
    usable = BUCKET - 1
    local = place - turn * usable
    taken = (local >= 0) & (local < usable)
    flat = jnp.where(taken, owner * BUCKET + local, -1)
    hot = flat[None, :] == jnp.arange(owners * BUCKET)[:, None]
    wanted = jnp.max(jnp.where(hot, (content - owner * vrows)[None, :], -1), axis=1)
    return hot.astype(bfloat), wanted.reshape(owners, BUCKET)


def on_device(
    token_ids,
    pred_mask,
    fact_order,
    corpus,
    embed_table,
    table_moment,
    table_square,
    layer_weights,
    layer_moment,
    layer_square,
    position_table,
    position_moment,
    position_square,
    small_params,
    small_moment,
    small_square,
):
    dp_devs = lax.axis_size("dp")
    owners = lax.axis_size(VOC)
    devices = dp_devs * owners
    vrows, width = embed_table.shape
    length = token_ids.shape[1]
    attn_b, feed_b = (
        lax.all_gather(layer_weights[:1].astype(bfloat), ALL, axis=1, tiled=True),
        lax.all_gather(layer_weights[1:].astype(bfloat), ALL, axis=1, tiled=True),
    )
    layer_b = (attn_b[0], feed_b[0], feed_b[1])
    table_b = embed_table.astype(bfloat)
    token_row = token_ids[0]
    pred_row = pred_mask[0]
    first_row = lax.axis_index(VOC) * vrows
    content = jnp.where(pred_row == 1, MASK_ID, token_row)
    slot_hot, slot_target, allowed, masked = slot_layout(pred_row, fact_order[0], token_row)
    owner, place = bucket_layout(content, vrows)
    hot, wanted = bucket_round(content, owner, place, 0, owners, vrows)
    note = jnp.concatenate([slot_target, jnp.stack([masked, corpus[0], jnp.max(place)])])
    packet = jnp.concatenate(
        [wanted, jnp.broadcast_to(note[None], (owners, note.shape[0]))], axis=1
    )
    packet = jnp.pad(packet, ((0, 0), (0, 128 - packet.shape[1])))
    packet = jnp.broadcast_to(packet[None], (dp_devs,) + packet.shape)
    packet = lax.all_to_all(
        packet.reshape(devices, packet.shape[-1]), ALL, 0, 0, tiled=True
    )
    asked = packet[:, :BUCKET]
    counts_all = packet[:, BUCKET + CAP]
    corpus_all = packet[:, BUCKET + CAP + 1]
    rounds = jnp.max(packet[:, BUCKET + CAP + 2]) // (BUCKET - 1) + 1
    group = lax.axis_index("dp") * owners
    group_asked = lax.dynamic_slice_in_dim(asked, group, owners, 0)
    group_target = lax.dynamic_slice_in_dim(
        packet[:, BUCKET : BUCKET + CAP], group, owners, 0
    ).reshape(-1)
    corpus_hot = corpus_all[:, None] == jnp.arange(NCORP)[None, :]
    corpus_counts = jnp.sum(jnp.where(corpus_hot, counts_all[:, None], 0), axis=0)
    seq_count = masked_total(corpus_hot, corpus_counts[None, :])
    seq_weight = 1.0 / (NCORP * seq_count.astype(single))
    slot_weight = jnp.where(
        jnp.arange(CAP)[None, :] < counts_all[:, None], seq_weight[:, None], 0.0
    )
    group_weight = lax.dynamic_slice_in_dim(slot_weight, group, owners, 0).reshape(-1)

    def fetch(asked_rows, hot_rows):
        served = jnp.take(table_b, jnp.maximum(asked_rows, 0).reshape(-1), axis=0)
        arrived = lax.all_to_all(
            served.reshape(owners, BUCKET, width), VOC, 0, 0, tiled=True
        )
        return rows_dot(hot_rows, arrived.reshape(-1, width))

    embed_rows = fetch(group_asked, hot)

    def more_rows(state):
        turn, rows = state
        hot_t, wanted_t = bucket_round(content, owner, place, turn, owners, vrows)
        asked_t = lax.all_to_all(wanted_t, VOC, 0, 0, tiled=True)
        return turn + 1, rows + fetch(asked_t, hot_t)

    _, embed_rows = lax.while_loop(
        lambda state: state[0] < rounds, more_rows, (jnp.ones((), rounds.dtype), embed_rows)
    )
    shared_t = jnp.concatenate([position_table, small_params]).astype(bfloat).T
    shared = copies_to(shared_t, ALL, devices).reshape(width, -1).T
    position_b = shared[:length]
    position_full = position_b.astype(single)
    small_full = shared[length:].astype(single)
    stream, stream_kept = norm_forward(embed_rows + position_full, small_full[0], small_full[1])
    stream_b = stream.astype(bfloat)
    slot_b = slot_hot.astype(bfloat)
    query_init, init_kept = norm_forward(
        plain_dot(slot_b, position_b), small_full[0], small_full[1]
    )
    output_rows, kept_state = layer_forward(layer_b, small_full, stream_b, query_init, allowed)
    output_b = output_rows.astype(bfloat)
    group_rows = lax.all_gather(output_b, VOC, axis=0, tiled=True)
    logits = trans_dot(group_rows, table_b)
    local_target = group_target - first_row
    target_hit = jnp.arange(vrows)[None, :] == local_target[:, None]
    row_top = jnp.max(logits, axis=1)
    row_total = jnp.sum(jnp.exp(logits - row_top[:, None]), axis=1)
    row_target = jnp.sum(jnp.where(target_hit, logits, 0.0), axis=1)
    stats = copies_to(jnp.stack([row_top, row_total]), VOC, owners)
    top_all = jnp.max(stats[:, 0], axis=0)
    total_all = jnp.sum(stats[:, 1] * jnp.exp(stats[:, 0] - top_all[None]), axis=0)
    log_total = top_all + jnp.log(total_all)
    own_total = lax.dynamic_slice_in_dim(
        log_total * group_weight, lax.axis_index(VOC) * CAP, CAP, 0
    )
    loss_part = jnp.sum(own_total) - jnp.sum(row_target * group_weight)
    d_logits = (
        group_weight[:, None] * (jnp.exp(logits - log_total[:, None]) - target_hit.astype(single))
    ).astype(bfloat)
    d_output = lax.psum_scatter(
        plain_dot(d_logits, table_b), VOC, scatter_dimension=0, tiled=True
    )
    grad_head = rows_dot(d_logits, group_rows)
    if dp_devs == 2:
        grad_other = lax.ppermute(grad_head, "dp", [(0, 1), (1, 0)])
        grad_head = grad_head + grad_other
    else:
        grad_head = lax.psum(grad_head, "dp")
    grad_layer, grad_mid, d_init, d_stream = layer_backward(
        layer_b, small_full, stream_b, allowed, kept_state, d_output
    )
    d_start, gain_init, bias_init = norm_backward(d_init, init_kept, small_full[0])
    d_embed, gain_stream, bias_stream = norm_backward(d_stream, stream_kept, small_full[0])
    grad_position = d_embed + lax.dot_general(
        slot_hot.astype(single),
        d_start,
        (((0,), (0,)), ((), ())),
        precision=lax.Precision.HIGHEST,
        preferred_element_type=single,
    )
    grad_small = jnp.concatenate(
        [(gain_init + gain_stream)[None], (bias_init + bias_stream)[None], grad_mid]
    )
    embed_back = d_embed.astype(bfloat)
    mask_sum = jnp.sum(
        jnp.where((content == MASK_ID)[:, None], embed_back.astype(single), 0.0), axis=0
    )
    mask_left = mask_sum - lax.reduce_precision(mask_sum, 8, 7)
    mask_owner = MASK_ID // vrows
    is_left = (jnp.arange(BUCKET) == BUCKET - 1)[None, :] & (
        jnp.arange(owners) == mask_owner
    )[:, None]

    def give(hot_rows, extra):
        rows = plain_dot(hot_rows, embed_back).reshape(owners, BUCKET, width)
        rows = jnp.where(is_left[:, :, None] & extra, mask_left[None, None, :], rows)
        rows = jnp.broadcast_to(rows.astype(bfloat)[None], (dp_devs,) + rows.shape)
        return lax.all_to_all(
            rows.reshape(devices, BUCKET, width), ALL, 0, 0, tiled=True
        ).reshape(-1, width)

    def into_rows(asked_rows, given):
        flat = asked_rows.reshape(-1)
        row_hot = flat[None, :] == jnp.arange(vrows)[:, None]
        return plain_dot(row_hot.astype(bfloat), given)

    last = (jnp.arange(BUCKET) == BUCKET - 1)[None, :]
    left_row = jnp.where(lax.axis_index(VOC) == mask_owner, MASK_ID - first_row, -1)
    table_grad = grad_head + into_rows(jnp.where(last, left_row, asked), give(hot, True))

    def more_grads(state):
        turn, grads = state
        hot_t, wanted_t = bucket_round(content, owner, place, turn, owners, vrows)
        wanted_t = jnp.broadcast_to(wanted_t[None], (dp_devs,) + wanted_t.shape)
        asked_t = lax.all_to_all(
            wanted_t.reshape(devices, BUCKET), ALL, 0, 0, tiled=True
        )
        return turn + 1, grads + into_rows(asked_t, give(hot_t, False))

    _, table_grad = lax.while_loop(
        lambda state: state[0] < rounds, more_grads, (jnp.ones((), rounds.dtype), table_grad)
    )
    layer_grad = jnp.stack(
        [lax.psum_scatter(part, ALL, scatter_dimension=0, tiled=True) for part in grad_layer[::-1]][
            ::-1
        ]
    )
    shared_grad = jnp.concatenate([grad_position, grad_small]).T.reshape(
        devices, width // devices, -1
    )
    shared_grad = jnp.sum(lax.all_to_all(shared_grad, ALL, 0, 0, tiled=True), axis=0).T
    position_grad, small_grad = shared_grad[:length], shared_grad[length:]
    square_part = (
        jnp.sum(table_grad * table_grad) / dp_devs
        + jnp.sum(layer_grad * layer_grad)
        + jnp.sum(position_grad * position_grad)
        + jnp.sum(small_grad * small_grad)
    )
    total_square, loss_value = total_over(jnp.stack([square_part, loss_part]), ALL, devices)
    grad_norm = jnp.sqrt(total_square)
    factor = jnp.minimum(1.0, clip_norm / grad_norm)
    table_first, table_second, table_dir = adam_moments(
        embed_table, table_moment, table_square, table_grad, factor
    )
    layer_first, layer_second, layer_dir = adam_moments(
        layer_weights, layer_moment, layer_square, layer_grad, factor
    )
    position_first, position_second, position_dir = adam_moments(
        position_table, position_moment, position_square, position_grad, factor
    )
    small_first, small_second, small_dir = adam_moments(
        small_params, small_moment, small_square, small_grad, factor
    )
    partial_norms = jnp.concatenate(
        [
            norm_pair(embed_table, table_dir, (0, 1))[None] / dp_devs,
            norm_pair(layer_weights, layer_dir, (1, 2)),
            norm_pair(position_table, position_dir, (0, 1))[None],
            norm_pair(small_params, small_dir, (0, 1))[None],
        ]
    )
    trust_square = total_over(partial_norms, ALL, devices)
    trust_norms = jnp.sqrt(trust_square)
    ratio = trust_norms[:, 0] / trust_norms[:, 1]
    table_next = embed_table - learn_rate * ratio[0] * table_dir
    layer_next = layer_weights - learn_rate * ratio[1:4][:, None, None] * layer_dir
    position_next = position_table - learn_rate * ratio[4] * position_dir
    small_next = small_params - learn_rate * ratio[5] * small_dir
    return (
        loss_value,
        grad_norm,
        table_next,
        table_first,
        table_second,
        layer_next,
        layer_first,
        layer_second,
        position_next,
        position_first,
        position_second,
        small_next,
        small_first,
        small_second,
        trust_norms,
    )


def solution(mesh):
    dp_devs, owners = mesh.devices.shape
    fine = Mesh(mesh.devices.reshape(dp_devs, owners // 4, 2, 2), ALL)
    rows, inner = P(ALL, None), P(None, ALL)
    table, layer = P(VOC, None), P(None, ALL, None)
    return jax.shard_map(
        on_device,
        mesh=fine,
        in_specs=(rows,) * 3 + (P(ALL),) + (table,) * 3 + (layer,) * 3 + (inner,) * 6,
        out_specs=(P(), P()) + (table,) * 3 + (layer,) * 3 + (inner,) * 6 + (P(),),
        check_vma=False,
    )
```

time: 1620 us -> 896 us (0.55)
  blocking collectives: 478 us -> 0 us
  waiting for transfers between devices: 749 us -> 585 us
  other arithmetic: 168 us -> 94.8 us
  local copies, waits for them, and re-layouts: 101 us -> 58 us
  starting transfers between devices: 5.23 us -> 33.7 us
    unnamed x9 -> x10, waiting for transfers between devices: 540 us -> 191 us
    all_gather x5 -> x0, blocking collectives: 304 us -> none  [the longest x1 203 us: on_device(): lax.all_gather(small_params.astype(bfloat), ('dp', 'vocab'), axis=1, tile...]
    all_to_all x1 -> x8, waiting for transfers between devices: 0.01 us -> 235 us  [the longest x1 143 us: on_device(): lax.all_to_all(shared_grad, ALL, 0, 0, tiled=True)]
    psum x1 -> x0, waiting for transfers between devices: 145 us -> none  [on_device(): table_grad = lax.psum(grad_head + grad_lookup, 'dp')]
    psum x3 -> x0, blocking collectives: 120 us -> none  [the longest x2 80.8 us: on_device(): lax.psum((square_part, loss_part), ('dp', 'vocab'))]
    all_gather x3, waiting for transfers between devices: 0.04 us -> 94.4 us  [the longest x1 58.1 us: on_device(): lax.all_gather(layer_weights[1:].astype(bfloat), ALL, axis=1, tiled=True)]
    unnamed x2 -> x0, blocking collectives: 53.9 us -> none
    another operation x1 -> x5, local copies, waits for them, and re-layouts: 40.7 us -> 1.99 us  [the longest x3 1.31 us: on_device(): jnp.stack([lax.psum_scatter(part, ALL, scatter_dimension=0, tiled=True) f...]
  transfers between devices with their start and end apart: 8 -> 16, of which waited for: 3 -> 13; matrix products, arithmetic and copies ran while one was open for 12% -> 13% of each run, Pallas kernels for 0% -> 0%
where the time goes in v1:
time: 896 us; the launch traced here: 888 us
  waiting for transfers between devices  585 us (65%)
  other arithmetic  94.8 us (11%)
  matrix products  89.5 us (10%)
  local copies, waits for them, and re-layouts  58 us (6%)
  starting transfers between devices  33.7 us (4%)
  between operations  26.4 us (3%)
    unnamed x10, waiting for transfers between devices  191 us
    all_to_all x1, waiting for transfers between devices, on_device(): lax.all_to_all(shared_grad, ALL, 0, 0, tiled=True)  143 us
    reduce_scatter x1, waiting for transfers between devices, on_device(): lax.psum_scatter(plain_dot(d_logits, table_b), VOC, scatter_dimension=0,...  64.8 us
    all_gather x1, waiting for transfers between devices, on_device(): lax.all_gather(layer_weights[1:].astype(bfloat), ALL, axis=1, tiled=True)  58.1 us
    all_to_all x1, waiting for transfers between devices, give(): lax.all_to_all(rows.reshape(devices, BUCKET, width), ALL, 0, 0, tiled=True)  46.9 us
    all_gather x1, waiting for transfers between devices, on_device(): group_rows = lax.all_gather(output_b, VOC, axis=0, tiled=True)  36.3 us
    dot_general x10, matrix products, plain_dot(): return jnp.dot(left_op, right_op, preferred_element_type=single)  33.2 us
    unnamed x192, local copies, waits for them, and re-layouts  28.2 us
  transfers between devices with their start and end apart: 16, of which 13 were waited for; matrix products, arithmetic and copies ran while one was open for 13% of the time, Pallas kernels for 0%

profile of v1, /device:TPU:0, one launch (start us, length us, event | category | flops | bytes accessed | tf_op | source)
XLA Modules:
  0.0 888.3 jit_solution(11217174698059260820)
XLA Ops:
  24.3 7.3 all-to-all-start.4
  51.7 11.9 %all-to-all-done.5 = bf16[32,24,270]{2,1,0:T(8,128)(2,1)S(1)} async-done(((bf16[32,24,270]{2,1,0:T(8,128)(2,1)}), bf16[32,24,270]{2,1,0:T(8,128)(2,1)S(1)}, u32[]{:S(2)}, u32[]{:S(2)}) %all-to-all-start.5) | async-done | bytes 414752 | tf_op jit(solution)/shard_map/all_to_all | solution.py:225
  76.9 16.0 %all-to-all-done.6 = bf16[16,32,768]{2,1,0:T(8,128)(2,1)} async-done(((bf16[16,32,768]{2,1,0:T(8,128)(2,1)}), bf16[16,32,768]{2,1,0:T(8,128)(2,1)}, u32[]{:S(2)}, u32[]{:S(2)}) %all-to-all-start.6) | async-done | bytes 786464 | tf_op jit(solution)/shard_map/all_to_all | solution.py:338
  118.4 58.1 %all-gather.6.cloned.1.call-done = bf16[2,768,3072]{2,1,0:T(8,128)(2,1)} async-done(((bf16[2,24,3072]{2,1,0:T(8,128)(2,1)}), bf16[2,768,3072]{2,1,0:T(8,128)(2,1)}) %all-gather.6.cloned.1.call-update) | async-done | bytes 9437200 | tf_op jit(solution)/shard_map/all_gather | solution.py:298
  179.9 5.1 fusion.93
  188.7 36.3 %all-gather.8.cloned.1.call-done = bf16[1024,768]{1,0:T(8,128)(2,1)} async-done(((bf16[64,768]{1,0:T(8,128)(2,1)}), bf16[1024,768]{1,0:T(8,128)(2,1)}) %all-gather.8.cloned.1.call-update) | async-done | bytes 1572880 | tf_op jit(solution)/shard_map/all_gather | solution.py:367
  225.0 4.9 fusion.94
  250.6 5.0 multiply_convert_fusion
  257.4 5.1 fusion.96
  262.8 64.8 %reduce-scatter.11.cloned.1.call-done = f32[64,768]{1,0:T(8,128)} async-done(((f32[1024,768]{1,0:T(8,128)}), f32[64,768]{1,0:T(8,128)}) %reduce-scatter.11.cloned.1.call-update) | async-done | bytes 196624 | tf_op jit(solution)/shard_map/reduce_scatter | solution.py:385
  330.9 5.8 convert_reduce_fusion
  358.4 9.6 %copy.260 = f32[768,3072]{1,0:T(8,128)} copy(f32[768,3072]{0,1:T(8,128)} %pad_maximum_fusion) | data formatting | bytes 18874368
  369.1 5.2 fusion.75
  374.6 9.0 %fusion.95 = f32[1920,768]{1,0:T(8,128)} fusion(bf16[1024,1920]{1,0:T(8,128)(2,1)} %copy-done.6, bf16[1024,768]{1,0:T(8,128)(2,1)} %all-gather.8.cloned.1.call-done), kind=kOutput, calls=%fused_computation.290 | convolution fusion | flops 3019898880 | bytes 11403264 | tf_op jit(solution)/shard_map/dot_general | solution.py:43
  391.1 5.9 fusion.72
  404.0 143.3 %all-to-all-done.9 = f32[32,24,270]{2,1,0:T(8,128)S(1)} async-done(((f32[32,24,270]{2,1,0:T(8,128)}), f32[32,24,270]{2,1,0:T(8,128)S(1)}, u32[]{:S(2)}, u32[]{:S(2)}) %all-to-all-start.9) | async-done | bytes 829472 | tf_op jit(solution)/shard_map/all_to_all | solution.py:456
  556.7 46.9 %all-to-all-done.8 = bf16[32,32,768]{2,1,0:T(8,128)(2,1)S(1)} async-done(((bf16[32,32,768]{2,1,0:T(8,128)(2,1)}), bf16[32,32,768]{2,1,0:T(8,128)(2,1)S(1)}, u32[]{:S(2)}, u32[]{:S(2)}) %all-to-all-start.8) | async-done | bytes 1572896 | tf_op jit(solution)/shard_map/all_to_all | solution.py:423
  603.6 8.2 add_add_fusion
  612.1 4.9 multiply_reduce_fusion.2
  619.7 52.1 %reduce-scatter.15.cloned.1.call-done = f32[24,3072]{1,0:T(8,128)} async-done(((f32[768,3072]{1,0:T(8,128)}), f32[24,3072]{1,0:T(8,128)}) %reduce-scatter.15.cloned.1.call-update) | async-done | bytes 294928
  673.7 138.6 %reduce-scatter.17.cloned.1.call-done = f32[24,3072]{1,0:T(8,128)} async-done(((f32[768,3072]{1,0:T(8,128)}), f32[24,3072]{1,0:T(8,128)}) %reduce-scatter.17.cloned.1.call-update) | async-done | bytes 294928
  821.7 6.7 all-to-all-done.10
  836.5 13.6 %multiply_reduce_fusion.1 = (f32[]{:T(128)}, f32[]{:T(128)}, f32[1920,768]{1,0:T(8,128)}, f32[1920,768]{1,0:T(8,128)}) fusion(f32[1920,768]{1,0:T(8,128)} %param.24, f32[1920,768]{1,0:T(8,128)} %get-tuple-element.111, f32[]{:T(128)S(6)} %min.3, f32[1920,768]{1,0:T(8,128)} %param.25, f32[1920,768]{1,0:T(8,128)} %param.26), kind=kLoop, calls=%fused_computation.35 | loop fusion | flops 26542080 | bytes 35389452 | tf_op jit(solution)/shard_map/reduce_sum | solution.py:219
  870.6 9.2 %multiply_subtract_fusion.2 = f32[1920,768]{1,0:T(8,128)} fusion(f32[1920,768]{1,0:T(8,128)} %param.24, f32[]{:T(128)} %bitcast.70, f32[1920,768]{1,0:T(8,128)} %get-tuple-element.300, f32[1920,768]{1,0:T(8,128)} %get-tuple-element.299), kind=kLoop, calls=%fused_computation.31 | loop fusion | flops 11796480 | bytes 23592964 | tf_op jit(solution)/shard_map/sub | solution.py:490
  (393 shorter events, 188.4 us)
Async XLA Ops:
  7.2 91.9 %all-gather.4.cloned.1.call-start = ((), (), s32[]{:S(2)}) async-start(), calls=%async_computation.16 | async-start | bytes 4866048 | tf_op jit(solution)/shard_map/all_gather | solution.py:297
  9.1 167.4 %all-gather.6.cloned.1.call-start = ((), (), s32[]{:S(2)}) async-start(), calls=%async_computation.17 | async-start | bytes 9732096 | tf_op jit(solution)/shard_map/all_gather | solution.py:298
  24.3 14.4 %all-to-all-start.4 = ((s32[32,1,128]{2,1,0:T(1,128)}), s32[32,1,128]{2,1,0:T(1,128)S(1)}, u32[]{:S(2)}, u32[]{:S(2)}) async-start(s32[32,1,128]{2,1,0:T(1,128)} %bitcast.20), calls=%async_computation.4 | async-start | bytes 32768 | tf_op jit(solution)/shard_map/all_to_all | solution.py:315
  39.6 24.0 %all-to-all-start.5 = ((bf16[32,24,270]{2,1,0:T(8,128)(2,1)}), bf16[32,24,270]{2,1,0:T(8,128)(2,1)S(1)}, u32[]{:S(2)}, u32[]{:S(2)}) async-start(bf16[32,24,270]{2,1,0:T(8,128)(2,1)} %broadcast_in_dim.402), calls=%async_computation.5 | async-start | bytes 1179648 | tf_op jit(solution)/shard_map/all_to_all | solution.py:225
  63.6 29.3 %all-to-all-start.6 = ((bf16[16,32,768]{2,1,0:T(8,128)(2,1)}), bf16[16,32,768]{2,1,0:T(8,128)(2,1)}, u32[]{:S(2)}, u32[]{:S(2)}) async-start(bf16[16,32,768]{2,1,0:T(8,128)(2,1)} %broadcast_select_fusion.1), calls=%async_computation.6 | async-start | bytes 1572864 | tf_op jit(solution)/shard_map/all_to_all | solution.py:338
  67.9 157.1 %all-gather.8.cloned.1.call-start = ((), (), s32[]{:S(2)}) async-start(), calls=%async_computation.18 | async-start | bytes 1671168 | tf_op jit(solution)/shard_map/all_gather | solution.py:367
  236.7 12.1 %all-to-all-start.7 = ((f32[16,2,1024]{2,1,0:T(2,128)}), f32[16,2,1024]{2,1,0:T(2,128)}, u32[]{:S(2)}, u32[]{:S(2)}) async-start(f32[16,2,1024]{2,1,0:T(2,128)} %broadcast_in_dim.408), calls=%async_computation.7 | async-start | bytes 262144 | tf_op jit(solution)/shard_map/all_to_all | solution.py:225
  240.8 86.8 %reduce-scatter.11.cloned.1.call-start = ((), (), s32[]{:S(2)}) async-start(), calls=%async_computation.19 | async-start | bytes 3342336 | tf_op jit(solution)/shard_map/reduce_scatter | solution.py:385
  262.5 355.2 %reduce-scatter.13.cloned.1.call-start = ((), (), s32[]{:S(2)}) async-start(), calls=%async_computation.20 | async-start | bytes 9732096
  368.1 303.7 %reduce-scatter.15.cloned.1.call-start = ((), (), s32[]{:S(2)}) async-start(), calls=%async_computation.21 | async-start | bytes 9732096
  374.3 438.0 %reduce-scatter.17.cloned.1.call-start = ((), (), s32[]{:S(2)}) async-start(), calls=%async_computation.22 | async-start | bytes 9732096
  383.6 173.1 %collective-permute-start = (f32[1920,768]{1,0:T(8,128)}, f32[1920,768]{1,0:T(8,128)}, u32[]{:S(2)}, u32[]{:S(2)}) collective-permute-start(f32[1920,768]{1,0:T(8,128)} %fusion.95), channel_id=1, source_target_pairs={{0,16},{16,0},{1,17},{17,1},{2,18},{18,2},{3,19},{19,3},{4,20},{20... | collective-permute-start | bytes 17694728 | tf_op jit(solution)/shard_map/ppermute | solution.py:390
  399.3 153.3 %copy-start.47 = (s32[32,32]{1,0:T(8,128)S(1)}, s32[32,32]{1,0:T(8,128)}, u32[]{:S(2)}) copy-start(s32[32,32]{1,0:T(8,128)} %get-tuple-element.335) | copy-start | bytes 12292
  400.7 146.6 %all-to-all-start.9 = ((f32[32,24,270]{2,1,0:T(8,128)}), f32[32,24,270]{2,1,0:T(8,128)S(1)}, u32[]{:S(2)}, u32[]{:S(2)}) async-start(f32[32,24,270]{2,1,0:T(8,128)} %bitcast.54), calls=%async_computation.10 | async-start | bytes 2359296 | tf_op jit(solution)/shard_map/all_to_all | solution.py:456
  548.6 55.1 %all-to-all-start.8 = ((bf16[32,32,768]{2,1,0:T(8,128)(2,1)}), bf16[32,32,768]{2,1,0:T(8,128)(2,1)S(1)}, u32[]{:S(2)}, u32[]{:S(2)}) async-start(bf16[32,32,768]{2,1,0:T(8,128)(2,1)} %bitcast.44), calls=%async_computation.9 | async-start | bytes 3145728 | tf_op jit(solution)/shard_map/all_to_all | solution.py:423
  617.7 203.6 %copy-start.43 = (f32[256,24]{0,1:T(8,128)S(1)}, f32[256,24]{0,1:T(8,128)}, u32[]{:S(2)}) copy-start(f32[256,24]{0,1:T(8,128)} %param.30) | copy-start | bytes 73732
  617.7 203.7 %copy-start.50 = (f32[256,24]{0,1:T(8,128)S(1)}, f32[256,24]{0,1:T(8,128)}, u32[]{:S(2)}) copy-start(f32[256,24]{0,1:T(8,128)} %param.31) | copy-start | bytes 73732
  617.7 203.8 %copy-start.51 = (f32[256,24]{0,1:T(8,128)S(1)}, f32[256,24]{0,1:T(8,128)}, u32[]{:S(2)}) copy-start(f32[256,24]{0,1:T(8,128)} %param.32) | copy-start | bytes 73732
  617.8 212.1 %copy-start.24 = (f32[24,270]{0,1:T(8,128)S(1)}, f32[24,270]{0,1:T(8,128)}, u32[]{:S(2)}) copy-start(f32[24,270]{0,1:T(8,128)} %copy-done.23) | copy-start | bytes 77764
  619.3 213.9 %copy-start.44 = (f32[14,24]{1,0:T(8,128)S(1)}, f32[14,24]{1,0:T(8,128)}, u32[]{:S(2)}) copy-start(f32[14,24]{1,0:T(8,128)} %param.33) | copy-start | bytes 4036
  619.3 213.9 %copy-start.72 = (f32[14,24]{1,0:T(8,128)S(1)}, f32[14,24]{1,0:T(8,128)}, u32[]{:S(2)}) copy-start(f32[14,24]{1,0:T(8,128)} %param.34) | copy-start | bytes 4036
  619.3 213.9 %copy-start.73 = (f32[14,24]{1,0:T(8,128)S(1)}, f32[14,24]{1,0:T(8,128)}, u32[]{:S(2)}) copy-start(f32[14,24]{1,0:T(8,128)} %param.35) | copy-start | bytes 4036
  817.6 10.8 %all-to-all-start.10 = ((f32[32,1,2]{2,1,0:T(1,128)}), f32[32,1,2]{2,1,0:T(1,128)S(1)}, u32[]{:S(2)}, u32[]{:S(2)}) async-start(f32[32,1,2]{2,1,0:T(1,128)} %broadcast_in_dim.425), calls=%async_computation.11 | async-start | bytes 32768 | tf_op jit(solution)/shard_map/all_to_all | solution.py:225
  853.3 10.1 %all-to-all-start.11 = ((f32[32,6,2]{1,2,0:T(2,128)}), f32[32,6,2]{1,2,0:T(2,128)S(1)}, u32[]{:S(2)}, u32[]{:S(2)}) async-start(f32[32,6,2]{1,2,0:T(2,128)} %broadcast_in_dim.428), calls=%async_computation.12 | async-start | bytes 65536 | tf_op jit(solution)/shard_map/all_to_all | solution.py:225
  (83 other events, 963.4 us)
Sparse Core Ops, SparseCore 0:
  11.5 80.7 all-gather.3
  95.8 80.6 all-gather.5
  186.7 38.2 all-gather.7
  262.7 64.8 reduce-scatter.10
  368.2 156.8 reduce-scatter.12
  531.9 139.9 reduce-scatter.14
  677.7 134.5 reduce-scatter.16

commit v2 on v1

--- a/solution.py
+++ b/solution.py
@@ -25,6 +25,7 @@
 BUCKET = 32
 ALL = ("dp", "hi", "mid", "core")
 VOC = ("hi", "mid", "core")
+NEAR = ("dp", "mid", "core")
 bfloat = jnp.bfloat16
 single = jnp.float32
 
@@ -124,31 +125,31 @@
     return (output_rows, kept_state)
 
 
-def layer_backward(layer_b, small_full, stream_b, allowed, kept_state, d_output):
-    (
-        key_rows,
-        value_rows,
-        init_b,
-        query_rows,
-        log_total,
-        mixed_b,
-        middle_kept,
-        middle_b,
-        hidden,
-        active_b,
-        final_kept,
-    ) = kept_state
-    width = stream_b.shape[1]
+def feed_backward(layer_b, small_full, kept_state, d_output):
+    hidden, final_kept, middle_kept = kept_state[8], kept_state[10], kept_state[6]
     d_sum, gain_three, bias_three = norm_backward(d_output, final_kept, small_full[12])
     d_branch = d_sum.astype(bfloat)
-    grad_down = rows_dot(d_branch, active_b)
     _, gelu_pull = jax.vjp(partial(jax.nn.gelu, approximate=False), hidden)
     d_hidden = gelu_pull(plain_dot(d_branch, layer_b[2]))[0].astype(bfloat)
-    grad_up = rows_dot(middle_b, d_hidden)
     d_middle = d_sum + trans_dot(d_hidden, layer_b[1])
     d_pre, gain_two, bias_two = norm_backward(d_middle, middle_kept, small_full[5])
+    grad_mid = jnp.concatenate(
+        [
+            gain_two[None],
+            bias_two[None],
+            column_sum(d_hidden).reshape(4, -1),
+            column_sum(d_branch)[None],
+            gain_three[None],
+            bias_three[None],
+        ]
+    )
+    return d_branch, d_hidden, d_pre, grad_mid
+
+
+def attention_backward(layer_b, allowed, kept_state, d_pre):
+    key_rows, value_rows, _, query_rows, log_total = kept_state[:5]
+    width = d_pre.shape[1]
     d_attend = d_pre.astype(bfloat)
-    grad_out = rows_dot(mixed_b, d_attend)
     d_mixed = trans_dot(d_attend, layer_b[0][:, 3 * width :]).astype(bfloat)
     attn_probs, _ = attention_probs(query_rows, key_rows, allowed, log_total)
     mixed_heads = split_heads(d_mixed)
@@ -173,32 +174,14 @@
         * scale
     )
     d_key = d_key.reshape(-1, width).astype(bfloat)
-    grad_query = rows_dot(init_b, d_query)
     d_init = d_pre + trans_dot(d_query, layer_b[0][:, :width])
-    grad_key = rows_dot(stream_b, d_key)
-    grad_value = rows_dot(stream_b, d_value)
     d_stream = trans_dot(d_key, layer_b[0][:, width : 2 * width]) + trans_dot(
         d_value, layer_b[0][:, 2 * width : 3 * width]
     )
-    grad_layer = (
-        jnp.concatenate([grad_query, grad_key, grad_value, grad_out], axis=1),
-        grad_up,
-        grad_down,
-    )
     grad_mid = jnp.concatenate(
-        [
-            column_sum(d_query)[None],
-            column_sum(d_value)[None],
-            column_sum(d_attend)[None],
-            gain_two[None],
-            bias_two[None],
-            column_sum(d_hidden).reshape(4, width),
-            column_sum(d_branch)[None],
-            gain_three[None],
-            bias_three[None],
-        ]
-    )
-    return (grad_layer, grad_mid, d_init, d_stream)
+        [column_sum(d_query)[None], column_sum(d_value)[None], column_sum(d_attend)[None]]
+    )
+    return d_attend, d_query, d_key, d_value, d_init, d_stream, grad_mid
 
 
 def adam_moments(weight_arr, first_mom, second_mom, gradient, factor):
@@ -221,14 +204,33 @@
     )
 
 
-def copies_to(values, axes, count):
-    return lax.all_to_all(
-        jnp.broadcast_to(values[None], (count,) + values.shape), axes, 0, 0, tiled=True
-    )
-
-
-def total_over(values, axes, count):
-    return jnp.sum(copies_to(values, axes, count), axis=0)
+class Exchange:
+    def __init__(self):
+        self.last = None
+
+    def __call__(self, values, axes):
+        if self.last is not None:
+            values, _ = lax.optimization_barrier((values, self.last))
+        self.last = lax.all_to_all(values, axes, 0, 0, tiled=True)
+        return self.last
+
+    def copies(self, values, axes, count):
+        return self(jnp.broadcast_to(values[None], (count,) + values.shape), axes)
+
+    def total(self, values, axes, count):
+        return jnp.sum(self.copies(values, axes, count), axis=0)
+
+    def columns(self, values, axes, count):
+        rows, width = values.shape
+        blocks = values.reshape(rows, count, width // count).transpose(1, 0, 2)
+        return self(blocks, axes).reshape(count * rows, -1)
+
+    def rows(self, values, count):
+        return self(values.reshape(count, values.shape[0] // count, values.shape[1]), ALL)
+
+
+def side_by_side(blocks):
+    return blocks.transpose(1, 0, 2).reshape(blocks.shape[1], -1)
 
 
 def masked_total(mask, values):
@@ -246,8 +248,9 @@
     rank_row = masked_total(order_row[None, :] == index[:, None], index[None, :])
     slot_rank = masked_total(slot_hot, rank_row[None, :])
     slot_target = masked_total(slot_hot, token_row[None, :])
+    slot_pos = masked_total(slot_hot, index[None, :])
     allowed = rank_row[None, :] <= slot_rank[:, None]
-    return slot_hot, slot_target, allowed, masked
+    return slot_hot, slot_pos, slot_target, allowed, masked
 
 
 def bucket_layout(content, vrows):
@@ -288,42 +291,52 @@
     small_moment,
     small_square,
 ):
+    exchange = Exchange()
     dp_devs = lax.axis_size("dp")
     owners = lax.axis_size(VOC)
     devices = dp_devs * owners
     vrows, width = embed_table.shape
     length = token_ids.shape[1]
-    attn_b, feed_b = (
-        lax.all_gather(layer_weights[:1].astype(bfloat), ALL, axis=1, tiled=True),
-        lax.all_gather(layer_weights[1:].astype(bfloat), ALL, axis=1, tiled=True),
-    )
-    layer_b = (attn_b[0], feed_b[0], feed_b[1])
+    feed = layer_weights.shape[2]
+    shared = jnp.concatenate([position_table, small_params]).T
+    shared_rows = shared.shape[1]
+    shared = jnp.pad(shared, ((0, 0), (0, -shared_rows % 128)))
+    shard = jnp.concatenate([layer_weights[0], layer_weights[1], layer_weights[2], shared], axis=1)
+    shard = lax.all_gather(shard.astype(bfloat), ALL, axis=0, tiled=True)
+    layer_b = tuple(shard[:, part * feed : (part + 1) * feed] for part in range(3))
+    shared = shard[:, 3 * feed : 3 * feed + shared_rows].T
     table_b = embed_table.astype(bfloat)
     token_row = token_ids[0]
     pred_row = pred_mask[0]
     first_row = lax.axis_index(VOC) * vrows
     content = jnp.where(pred_row == 1, MASK_ID, token_row)
-    slot_hot, slot_target, allowed, masked = slot_layout(pred_row, fact_order[0], token_row)
+    slot_hot, slot_pos, slot_target, allowed, masked = slot_layout(pred_row, fact_order[0], token_row)
     owner, place = bucket_layout(content, vrows)
     hot, wanted = bucket_round(content, owner, place, 0, owners, vrows)
-    note = jnp.concatenate([slot_target, jnp.stack([masked, corpus[0], jnp.max(place)])])
+    note = jnp.concatenate(
+        [slot_target, slot_pos, jnp.stack([masked, corpus[0], jnp.max(place)])]
+    )
     packet = jnp.concatenate(
         [wanted, jnp.broadcast_to(note[None], (owners, note.shape[0]))], axis=1
     )
-    packet = jnp.pad(packet, ((0, 0), (0, 128 - packet.shape[1])))
+    packet = jnp.pad(packet, ((0, 0), (0, 256 - packet.shape[1])))
     packet = jnp.broadcast_to(packet[None], (dp_devs,) + packet.shape)
-    packet = lax.all_to_all(
-        packet.reshape(devices, packet.shape[-1]), ALL, 0, 0, tiled=True
-    )
+    packet = exchange(packet.reshape(devices, packet.shape[-1]), ALL)
     asked = packet[:, :BUCKET]
-    counts_all = packet[:, BUCKET + CAP]
-    corpus_all = packet[:, BUCKET + CAP + 1]
-    rounds = jnp.max(packet[:, BUCKET + CAP + 2]) // (BUCKET - 1) + 1
+    tail = BUCKET + 2 * CAP
+    counts_all = packet[:, tail]
+    corpus_all = packet[:, tail + 1]
+    rounds = jnp.max(packet[:, tail + 2]) // (BUCKET - 1) + 1
     group = lax.axis_index("dp") * owners
+    outer = lax.axis_size("hi")
+
+    def group_order(values):
+        return values.reshape(outer, 2, 2, CAP).transpose(2, 1, 0, 3).reshape(-1)
+
     group_asked = lax.dynamic_slice_in_dim(asked, group, owners, 0)
-    group_target = lax.dynamic_slice_in_dim(
-        packet[:, BUCKET : BUCKET + CAP], group, owners, 0
-    ).reshape(-1)
+    group_target = group_order(
+        lax.dynamic_slice_in_dim(packet[:, BUCKET : BUCKET + CAP], group, owners, 0)
+    )
     corpus_hot = corpus_all[:, None] == jnp.arange(NCORP)[None, :]
     corpus_counts = jnp.sum(jnp.where(corpus_hot, counts_all[:, None], 0), axis=0)
     seq_count = masked_total(corpus_hot, corpus_counts[None, :])
@@ -331,28 +344,25 @@
     slot_weight = jnp.where(
         jnp.arange(CAP)[None, :] < counts_all[:, None], seq_weight[:, None], 0.0
     )
-    group_weight = lax.dynamic_slice_in_dim(slot_weight, group, owners, 0).reshape(-1)
-
-    def fetch(asked_rows, hot_rows):
+    group_weight = group_order(lax.dynamic_slice_in_dim(slot_weight, group, owners, 0))
+
+    def serve(asked_rows):
         served = jnp.take(table_b, jnp.maximum(asked_rows, 0).reshape(-1), axis=0)
-        arrived = lax.all_to_all(
-            served.reshape(owners, BUCKET, width), VOC, 0, 0, tiled=True
-        )
-        return rows_dot(hot_rows, arrived.reshape(-1, width))
-
-    embed_rows = fetch(group_asked, hot)
+        return served.reshape(owners, BUCKET, width)
+
+    arrived = exchange(serve(group_asked), VOC)
+    embed_rows = rows_dot(hot, arrived.reshape(-1, width))
 
     def more_rows(state):
         turn, rows = state
         hot_t, wanted_t = bucket_round(content, owner, place, turn, owners, vrows)
         asked_t = lax.all_to_all(wanted_t, VOC, 0, 0, tiled=True)
-        return turn + 1, rows + fetch(asked_t, hot_t)
+        arrived_t = lax.all_to_all(serve(asked_t), VOC, 0, 0, tiled=True)
+        return turn + 1, rows + rows_dot(hot_t, arrived_t.reshape(-1, width))
 
     _, embed_rows = lax.while_loop(
         lambda state: state[0] < rounds, more_rows, (jnp.ones((), rounds.dtype), embed_rows)
     )
-    shared_t = jnp.concatenate([position_table, small_params]).astype(bfloat).T
-    shared = copies_to(shared_t, ALL, devices).reshape(width, -1).T
     position_b = shared[:length]
     position_full = position_b.astype(single)
     small_full = shared[length:].astype(single)
@@ -362,38 +372,90 @@
     query_init, init_kept = norm_forward(
         plain_dot(slot_b, position_b), small_full[0], small_full[1]
     )
+    few = devices <= 32
+    near = dp_devs * 4
+    if few:
+        stream_all = lax.all_gather(stream_b, NEAR, axis=0, tiled=True)
     output_rows, kept_state = layer_forward(layer_b, small_full, stream_b, query_init, allowed)
     output_b = output_rows.astype(bfloat)
-    group_rows = lax.all_gather(output_b, VOC, axis=0, tiled=True)
+    init_b, mixed_b, middle_b, active_b = (kept_state[2], kept_state[5], kept_state[7], kept_state[9])
+    if few:
+        kept_rows = jnp.concatenate([mixed_b, middle_b], axis=1)
+        kept_rows, stream_all = lax.optimization_barrier((kept_rows, stream_all))
+        kept_all = lax.all_gather(kept_rows, ALL, axis=0, tiled=True)
+    group_rows = exchange.copies(output_b, "hi", outer).reshape(-1, width)
+    group_rows = exchange.copies(group_rows, "mid", 2).reshape(-1, width)
+    group_rows = exchange.copies(group_rows, "core", 2).reshape(-1, width)
     logits = trans_dot(group_rows, table_b)
     local_target = group_target - first_row
     target_hit = jnp.arange(vrows)[None, :] == local_target[:, None]
     row_top = jnp.max(logits, axis=1)
     row_total = jnp.sum(jnp.exp(logits - row_top[:, None]), axis=1)
     row_target = jnp.sum(jnp.where(target_hit, logits, 0.0), axis=1)
-    stats = copies_to(jnp.stack([row_top, row_total]), VOC, owners)
+    stats = exchange.copies(jnp.stack([row_top, row_total]), VOC, owners)
+    if few:
+        active_mine = exchange.columns(active_b, ALL, devices)
     top_all = jnp.max(stats[:, 0], axis=0)
     total_all = jnp.sum(stats[:, 1] * jnp.exp(stats[:, 0] - top_all[None]), axis=0)
     log_total = top_all + jnp.log(total_all)
-    own_total = lax.dynamic_slice_in_dim(
-        log_total * group_weight, lax.axis_index(VOC) * CAP, CAP, 0
-    )
+    own_place = lax.axis_index(("core", "mid", "hi"))
+    own_total = lax.dynamic_slice_in_dim(log_total * group_weight, own_place * CAP, CAP, 0)
     loss_part = jnp.sum(own_total) - jnp.sum(row_target * group_weight)
     d_logits = (
         group_weight[:, None] * (jnp.exp(logits - log_total[:, None]) - target_hit.astype(single))
     ).astype(bfloat)
-    d_output = lax.psum_scatter(
-        plain_dot(d_logits, table_b), VOC, scatter_dimension=0, tiled=True
+    def swapped(axis, part):
+        side = lax.axis_index(axis)
+        theirs = lax.ppermute(part(1 - side), axis, [(0, 1), (1, 0)])
+        return part(side) + theirs
+
+    half = owners * CAP // 2
+
+    def rows_half(side):
+        return plain_dot(lax.dynamic_slice_in_dim(d_logits, side * half, half, 0), table_b)
+
+    d_output = swapped("core", rows_half)
+    quarter = half // 2
+    d_half = d_output
+    d_output = swapped(
+        "mid", lambda side: lax.dynamic_slice_in_dim(d_half, side * quarter, quarter, 0)
     )
     grad_head = rows_dot(d_logits, group_rows)
     if dp_devs == 2:
-        grad_other = lax.ppermute(grad_head, "dp", [(0, 1), (1, 0)])
-        grad_head = grad_head + grad_other
+        head_b = grad_head.astype(bfloat)
+        other_b = lax.ppermute(head_b, "dp", [(0, 1), (1, 0)])
+        d_output, head_b = lax.optimization_barrier((d_output, head_b))
+        grad_head = head_b.astype(single) + other_b.astype(single)
     else:
         grad_head = lax.psum(grad_head, "dp")
-    grad_layer, grad_mid, d_init, d_stream = layer_backward(
-        layer_b, small_full, stream_b, allowed, kept_state, d_output
-    )
+    d_output = exchange(d_output.reshape(outer, CAP, width), "hi")
+    if few:
+        d_output, kept_all = lax.optimization_barrier((d_output, kept_all))
+    d_output = jnp.sum(d_output, axis=0)
+    d_branch, d_hidden, d_pre, mid_feed = feed_backward(layer_b, small_full, kept_state, d_output)
+    if few:
+        wide = feed // devices
+        both = jnp.concatenate(
+            [
+                d_hidden.reshape(CAP, devices, -1),
+                d_pre.astype(bfloat).reshape(CAP, devices, -1),
+            ],
+            axis=2,
+        ).reshape(CAP, -1)
+        both = exchange.columns(both, ALL, devices)
+        branch_all = lax.all_gather(d_branch, ALL, axis=0, tiled=True)
+    d_attend, d_query, d_key, d_value, d_init, d_stream, mid_attn = attention_backward(
+        layer_b, allowed, kept_state, d_pre
+    )
+    grad_mid = jnp.concatenate([mid_attn, mid_feed])
+    if few:
+        piece = width // near
+        pairs = jnp.concatenate(
+            [d_key.reshape(length, near, piece), d_value.reshape(length, near, piece)], axis=2
+        ).transpose(1, 0, 2)
+        asks = d_query.reshape(CAP, near, piece).transpose(1, 0, 2)
+        asks = jnp.concatenate([asks[:, : CAP // 2], asks[:, CAP // 2 :]], axis=2)
+        pairs = exchange(jnp.concatenate([pairs, asks], axis=1), NEAR)
     d_start, gain_init, bias_init = norm_backward(d_init, init_kept, small_full[0])
     d_embed, gain_stream, bias_stream = norm_backward(d_stream, stream_kept, small_full[0])
     grad_position = d_embed + lax.dot_general(
@@ -416,22 +478,30 @@
         jnp.arange(owners) == mask_owner
     )[:, None]
 
-    def give(hot_rows, extra):
+    def plain_exchange(values, axes):
+        return lax.all_to_all(values, axes, 0, 0, tiled=True)
+
+    def give(hot_rows, extra, send):
         rows = plain_dot(hot_rows, embed_back).reshape(owners, BUCKET, width)
         rows = jnp.where(is_left[:, :, None] & extra, mask_left[None, None, :], rows)
-        rows = jnp.broadcast_to(rows.astype(bfloat)[None], (dp_devs,) + rows.shape)
-        return lax.all_to_all(
-            rows.reshape(devices, BUCKET, width), ALL, 0, 0, tiled=True
-        ).reshape(-1, width)
+        rows = send(rows.astype(bfloat), VOC).reshape(-1, width)
+        if dp_devs == 2:
+            return jnp.concatenate([rows, lax.ppermute(rows, "dp", [(0, 1), (1, 0)])])
+        return lax.all_gather(rows, "dp", axis=0, tiled=True)
+
+    def both_groups(asked_rows):
+        if dp_devs == 2:
+            return jnp.roll(asked_rows, -group, axis=0)
+        return asked_rows
 
     def into_rows(asked_rows, given):
-        flat = asked_rows.reshape(-1)
+        flat = both_groups(asked_rows).reshape(-1)
         row_hot = flat[None, :] == jnp.arange(vrows)[:, None]
         return plain_dot(row_hot.astype(bfloat), given)
 
     last = (jnp.arange(BUCKET) == BUCKET - 1)[None, :]
     left_row = jnp.where(lax.axis_index(VOC) == mask_owner, MASK_ID - first_row, -1)
-    table_grad = grad_head + into_rows(jnp.where(last, left_row, asked), give(hot, True))
+    table_grad = grad_head + into_rows(jnp.where(last, left_row, asked), give(hot, True, exchange))
 
     def more_grads(state):
         turn, grads = state
@@ -440,28 +510,76 @@
         asked_t = lax.all_to_all(
             wanted_t.reshape(devices, BUCKET), ALL, 0, 0, tiled=True
         )
-        return turn + 1, grads + into_rows(asked_t, give(hot_t, False))
+        return turn + 1, grads + into_rows(asked_t, give(hot_t, False, plain_exchange))
 
     _, table_grad = lax.while_loop(
         lambda state: state[0] < rounds, more_grads, (jnp.ones((), rounds.dtype), table_grad)
     )
-    layer_grad = jnp.stack(
-        [lax.psum_scatter(part, ALL, scatter_dimension=0, tiled=True) for part in grad_layer[::-1]][
-            ::-1
-        ]
-    )
-    shared_grad = jnp.concatenate([grad_position, grad_small]).T.reshape(
-        devices, width // devices, -1
-    )
-    shared_grad = jnp.sum(lax.all_to_all(shared_grad, ALL, 0, 0, tiled=True), axis=0).T
-    position_grad, small_grad = shared_grad[:length], shared_grad[length:]
+    if few:
+        near_pos = packet[:, BUCKET + CAP : tail].reshape(dp_devs, outer, 4 * CAP)
+        near_pos = lax.dynamic_index_in_dim(near_pos, lax.axis_index("hi"), 1, False).reshape(-1)
+        init_rows = norm_forward(position_full, small_full[0], small_full[1])[0].astype(bfloat)
+        init_hot = near_pos[:, None] == jnp.arange(length)[None, :]
+        init_all = plain_dot(init_hot.astype(bfloat), init_rows).astype(bfloat)
+        asks = pairs[:, length:]
+        asks = jnp.concatenate([asks[..., :piece], asks[..., piece:]], axis=1)
+        grad_pair = rows_dot(stream_all, pairs[:, :length].reshape(near * length, -1))
+        grad_ask = rows_dot(init_all, asks.reshape(near * CAP, piece))
+        share = width // devices
+        grad_up = rows_dot(kept_all[:, width:], both[:, :wide])
+        grad_out = rows_dot(kept_all[:, :width], both[:, wide:])
+        grad_down = rows_dot(branch_all, active_mine)
+        shared_grad = jnp.concatenate([grad_position, grad_small]).T
+        results = jnp.concatenate(
+            [grad_pair, grad_ask, grad_up, grad_down, grad_out, shared_grad], axis=1
+        )
+        results = exchange.rows(results.astype(bfloat), devices).astype(single)
+        pieces = 3 * piece
+        attn = jnp.sum(
+            results[..., :pieces].reshape(dp_devs, outer, 4, share, pieces), axis=1
+        ).reshape(near, share, pieces)
+        shared_grad = jnp.sum(results[..., -shared_rows:], axis=0).T
+        position_grad, small_grad = shared_grad[:length], shared_grad[length:]
+        grad_key, grad_value, grad_query = (
+            side_by_side(attn[..., part * piece : (part + 1) * piece]) for part in range(3)
+        )
+        grad_up = side_by_side(results[..., pieces : pieces + wide])
+        grad_down = side_by_side(results[..., pieces + wide : pieces + 2 * wide])
+        grad_out = side_by_side(results[..., pieces + 2 * wide : -shared_rows])
+        layer_grad = jnp.stack(
+            [
+                jnp.concatenate([grad_query, grad_key, grad_value, grad_out], axis=1),
+                grad_up,
+                grad_down,
+            ]
+        )
+    else:
+        whole = (
+            jnp.concatenate(
+                [
+                    rows_dot(init_b, d_query),
+                    rows_dot(stream_b, d_key),
+                    rows_dot(stream_b, d_value),
+                    rows_dot(mixed_b, d_attend),
+                ],
+                axis=1,
+            ),
+            rows_dot(middle_b, d_hidden),
+            rows_dot(d_branch, active_b),
+        )
+        layer_grad = jnp.stack(
+            [lax.psum_scatter(part, ALL, scatter_dimension=0, tiled=True) for part in whole]
+        )
+        shared_grad = jnp.concatenate([grad_position, grad_small]).T
+        shared_grad = lax.psum_scatter(shared_grad, ALL, scatter_dimension=0, tiled=True).T
+        position_grad, small_grad = shared_grad[:length], shared_grad[length:]
     square_part = (
         jnp.sum(table_grad * table_grad) / dp_devs
         + jnp.sum(layer_grad * layer_grad)
         + jnp.sum(position_grad * position_grad)
         + jnp.sum(small_grad * small_grad)
     )
-    total_square, loss_value = total_over(jnp.stack([square_part, loss_part]), ALL, devices)
+    total_square, loss_value = exchange.total(jnp.stack([square_part, loss_part]), ALL, devices)
     grad_norm = jnp.sqrt(total_square)
     factor = jnp.minimum(1.0, clip_norm / grad_norm)
     table_first, table_second, table_dir = adam_moments(
@@ -484,7 +602,7 @@
             norm_pair(small_params, small_dir, (0, 1))[None],
         ]
     )
-    trust_square = total_over(partial_norms, ALL, devices)
+    trust_square = exchange.total(partial_norms, ALL, devices)
     trust_norms = jnp.sqrt(trust_square)
     ratio = trust_norms[:, 0] / trust_norms[:, 1]
     table_next = embed_table - learn_rate * ratio[0] * table_dir

time: 896 us -> 587 us (0.66)
  waiting for transfers between devices: 585 us -> 247 us
  starting transfers between devices: 33.7 us -> 55.2 us
    unnamed x10 -> x4, waiting for transfers between devices: 191 us -> 0.07 us
    all_to_all x8 -> x13, waiting for transfers between devices: 235 us -> 158 us  [__call__(): self.last = lax.all_to_all(values, axes, 0, 0, tiled=True)]
    reduce_scatter x1 -> x0, waiting for transfers between devices: 64.8 us -> none  [on_device(): lax.psum_scatter(plain_dot(d_logits, table_b), VOC, scatter_dimension=0,...]
    all_gather x3 -> x4, waiting for transfers between devices: 94.4 us -> 57.2 us  [the longest x1 50.8 us: on_device(): shard = lax.all_gather(shard.astype(bfloat), ALL, axis=0, tiled=True)]
    ppermute x1 -> x4, waiting for transfers between devices: 0.01 us -> 31.3 us  [the longest x1 15.8 us: give(): return jnp.concatenate([rows, lax.ppermute(rows, 'dp', [(0, 1), (1, 0)])])]
    all_to_all x8 -> x13, starting transfers between devices: 31.5 us -> 53.3 us  [__call__(): self.last = lax.all_to_all(values, axes, 0, 0, tiled=True)]
    unnamed x192 -> x208, local copies, waits for them, and re-layouts: 28.2 us -> 13.4 us
    unnamed x2 -> x0, matrix products: 11.1 us -> none
  transfers between devices with their start and end apart: 16 -> 21, of which waited for: 13 -> 17; matrix products, arithmetic and copies ran while one was open for 13% -> 29% of each run, Pallas kernels for 0% -> 0%
where the time goes in v2:
time: 587 us; the launch traced here: 579 us
  waiting for transfers between devices  247 us (42%)
  other arithmetic  93.6 us (16%)
  matrix products  87.4 us (15%)
  local copies, waits for them, and re-layouts  63.6 us (11%)
  starting transfers between devices  55.2 us (9%)
  between operations  26.4 us (4%)
    all_to_all x13, waiting for transfers between devices, __call__(): self.last = lax.all_to_all(values, axes, 0, 0, tiled=True)  158 us
    all_to_all x13, starting transfers between devices, __call__(): self.last = lax.all_to_all(values, axes, 0, 0, tiled=True)  53.3 us
    all_gather x1, waiting for transfers between devices, on_device(): shard = lax.all_gather(shard.astype(bfloat), ALL, axis=0, tiled=True)  50.8 us
    dot_general x12, matrix products, plain_dot(): return jnp.dot(left_op, right_op, preferred_element_type=single)  36.6 us
    dot_general x7, matrix products, trans_dot(): lax.dot_general(left_op, right_op, (((1,), (1,)), ((), ())), preferred_el...  21.9 us
    dot_general x7, matrix products, rows_dot(): lax.dot_general(left_op, right_op, (((0,), (0,)), ((), ())), preferred_el...  21.6 us
    reduce_sum x4, other arithmetic, norm_pair(): jnp.sum(weight_arr * weight_arr, axis=axes)  17.3 us
    ppermute x1, waiting for transfers between devices, give(): return jnp.concatenate([rows, lax.ppermute(rows, 'dp', [(0, 1), (1, 0)])])  15.8 us
  transfers between devices with their start and end apart: 21, of which 17 were waited for; matrix products, arithmetic and copies ran while one was open for 29% of the time, Pallas kernels for 0%

profile of v2, /device:TPU:0, one launch (start us, length us, event | category | flops | bytes accessed | tf_op | source)
XLA Modules:
  0.0 579.1 jit_solution(6101448869401170808)
XLA Ops:
  25.3 7.1 %all-to-all-start.4 = ((s32[32,1,256]{2,1,0:T(1,128)}), s32[32,1,256]{2,1,0:T(1,128)S(1)}, u32[]{:S(2)}, u32[]{:S(2)}) async-start(s32[32,1,256]{2,1,0:T(1,128)} %copy.342), calls=%async_computation.4 | async-start | bytes 65536 | tf_op jit(solution)/shard_map/all_to_all | solution.py:214
  32.5 7.2 %all-to-all-done.4 = s32[32,1,256]{2,1,0:T(1,128)S(1)} async-done(((s32[32,1,256]{2,1,0:T(1,128)}), s32[32,1,256]{2,1,0:T(1,128)S(1)}, u32[]{:S(2)}, u32[]{:S(2)}) %all-to-all-start.4) | async-done | bytes 32800 | tf_op jit(solution)/shard_map/all_to_all | solution.py:214
  52.4 28.2 %all-to-all-done.5 = bf16[16,32,768]{2,1,0:T(8,128)(2,1)} async-done(((bf16[16,32,768]{2,1,0:T(8,128)(2,1)}), bf16[16,32,768]{2,1,0:T(8,128)(2,1)}, u32[]{:S(2)}, u32[]{:S(2)}) %all-to-all-start.5) | async-done | bytes 786464 | tf_op jit(solution)/shard_map/all_to_all | solution.py:214
  83.0 50.8 %all-gather.5.cloned.1.call-done = bf16[768,9600]{1,0:T(8,128)(2,1)} async-done(((bf16[24,9600]{1,0:T(8,128)(2,1)}), bf16[768,9600]{1,0:T(8,128)(2,1)}) %all-gather.5.cloned.1.call-update) | async-done | bytes 14745616 | tf_op jit(solution)/shard_map/all_gather | solution.py:305
  165.8 6.5 %all-gather.7.cloned.1.call-done = bf16[2048,768]{1,0:T(8,128)(2,1)} async-done(((bf16[256,768]{1,0:T(8,128)(2,1)}), bf16[2048,768]{1,0:T(8,128)(2,1)}) %all-gather.7.cloned.1.call-update) | async-done | bytes 3145744 | tf_op jit(solution)/shard_map/all_gather | solution.py:378
  173.7 5.6 multiply_convert_fusion.2
  189.7 13.5 %all-to-all-done.6 = bf16[4,64,768]{2,1,0:T(8,128)(2,1)} async-done(((bf16[4,64,768]{2,1,0:T(8,128)(2,1)}), bf16[4,64,768]{2,1,0:T(8,128)(2,1)}, u32[]{:S(2)}, u32[]{:S(2)}) %all-to-all-start.6) | async-done | bytes 393248 | tf_op jit(solution)/shard_map/all_to_all | solution.py:214
  211.0 9.2 %all-to-all-done.7 = bf16[2,256,768]{2,1,0:T(8,128)(2,1)} async-done(((bf16[2,256,768]{2,1,0:T(8,128)(2,1)}), bf16[2,256,768]{2,1,0:T(8,128)(2,1)}, u32[]{:S(2)}, u32[]{:S(2)}) %all-to-all-start.7) | async-done | bytes 786464 | tf_op jit(solution)/shard_map/all_to_all | solution.py:214
  221.4 5.7 all_to_all.121
  242.3 9.5 %all-to-all-done.9 = f32[16,2,1024]{2,1,0:T(2,128)S(1)} async-done(((f32[16,2,1024]{2,1,0:T(2,128)}), f32[16,2,1024]{2,1,0:T(2,128)S(1)}, u32[]{:S(2)}, u32[]{:S(2)}) %all-to-all-start.9) | async-done | bytes 131104 | tf_op jit(solution)/shard_map/all_to_all | solution.py:214
  274.9 7.6 %convolution_convert_fusion.1 = bf16[1920,768]{1,0:T(8,128)(2,1)} fusion(bf16[1024,1920]{1,0:T(8,128)(2,1)} %copy-done.6, bf16[1024,768]{1,0:T(8,128)(2,1)} %bitcast.248), kind=kOutput, calls=%fused_computation.54 | convolution fusion | flops 3021373440 | bytes 8454144 | tf_op jit(solution)/shard_map/dot_general | solution.py:44
  282.5 11.7 %collective-permute-done.2 = f32[256,768]{1,0:T(8,128)S(1)} collective-permute-done((f32[256,768]{1,0:T(8,128)S(1)}, f32[256,768]{1,0:T(8,128)S(1)}, u32[]{:S(2)}, u32[]{:S(2)}) %collective-permute-start.2) | collective-permute-done | bytes 786464 | tf_op jit(solution)/shard_map/ppermute | solution.py:409
  308.2 11.1 %all-to-all-done.11 = f32[4,64,768]{2,1,0:T(8,128)S(1)} async-done(((f32[4,64,768]{2,1,0:T(8,128)}), f32[4,64,768]{2,1,0:T(8,128)S(1)}, u32[]{:S(2)}, u32[]{:S(2)}) %all-to-all-start.11) | async-done | bytes 786464 | tf_op jit(solution)/shard_map/all_to_all | solution.py:214
  321.4 5.5 fusion.158
  361.7 15.7 %all-to-all-done.12 = bf16[32,64,120]{2,1,0:T(8,128)(2,1)} async-done(((bf16[32,64,120]{2,1,0:T(8,128)(2,1)}), bf16[32,64,120]{2,1,0:T(8,128)(2,1)}, u32[]{:S(2)}, u32[]{:S(2)}) %all-to-all-start.12) | async-done | bytes 491552 | tf_op jit(solution)/shard_map/all_to_all | solution.py:214
  385.0 16.4 %all-to-all-done.13 = bf16[8,288,192]{2,1,0:T(8,128)(2,1)S(1)} async-done(((bf16[8,288,192]{2,1,0:T(8,128)(2,1)}), bf16[8,288,192]{2,1,0:T(8,128)(2,1)S(1)}, u32[]{:S(2)}, u32[]{:S(2)}) %all-to-all-start.13) | async-done | bytes 884768 | tf_op jit(solution)/shard_map/all_to_all | solution.py:214
  401.4 5.6 all-to-all-start.14
  414.5 11.2 %all-to-all-done.14 = bf16[16,32,768]{2,1,0:T(8,128)(2,1)} async-done(((bf16[16,32,768]{2,1,0:T(8,128)(2,1)}), bf16[16,32,768]{2,1,0:T(8,128)(2,1)}, u32[]{:S(2)}, u32[]{:S(2)}) %all-to-all-start.14) | async-done | bytes 786464 | tf_op jit(solution)/shard_map/all_to_all | solution.py:214
  429.9 15.8 %collective-permute-done.4 = bf16[512,768]{1,0:T(8,128)(2,1)S(1)} collective-permute-done((bf16[512,768]{1,0:T(8,128)(2,1)}, bf16[512,768]{1,0:T(8,128)(2,1)S(1)}, u32[]{:S(2)}, u32[]{:S(2)}) %collective-permute-start.4) | collective-permute-done | bytes 786464 | tf_op jit(solution)/shard_map/ppermute | solution.py:489
  445.7 7.1 %add_add_fusion = f32[1920,768]{1,0:T(8,128)} fusion(bf16[1920,768]{1,0:T(8,128)(2,1)} %collective-permute-done.3, bf16[1920,768]{1,0:T(8,128)(2,1)S(1)} %copy-done.95, s32[1024]{0:T(1024)S(1)} %copy-done.76, bf16[512,768]{1,0:T(8,128)(2,1)S(1)} %collective-permute-done.4, bf16[512,768]{1,0:T(8,128)(2,1)} %bitcast.60), kind=kOutput, calls=%fused_computation.43 | convolution fusion | flops 3030908928 | bytes 13373440 | tf_op jit(solution)/shard_map/dot_general | solution.py:34
  476.2 25.4 %all-to-all-done.15 = bf16[32,24,774]{2,1,0:T(8,128)(2,1)S(1)} async-done(((bf16[32,24,774]{2,1,0:T(8,128)(2,1)}), bf16[32,24,774]{2,1,0:T(8,128)(2,1)S(1)}, u32[]{:S(2)}, u32[]{:S(2)}) %all-to-all-start.15) | async-done | bytes 1188896 | tf_op jit(solution)/shard_map/all_to_all | solution.py:214
  512.7 6.7 %all-to-all-done.16 = f32[32,1,2]{2,1,0:T(1,128)S(1)} async-done(((f32[32,1,2]{2,1,0:T(1,128)}), f32[32,1,2]{2,1,0:T(1,128)S(1)}, u32[]{:S(2)}, u32[]{:S(2)}) %all-to-all-start.16) | async-done | bytes 288 | tf_op jit(solution)/shard_map/all_to_all | solution.py:214
  527.6 13.6 %multiply_reduce_fusion.1 = (f32[]{:T(128)}, f32[]{:T(128)}, f32[1920,768]{1,0:T(8,128)}, f32[1920,768]{1,0:T(8,128)}) fusion(f32[1920,768]{1,0:T(8,128)} %param.24, f32[1920,768]{1,0:T(8,128)} %get-tuple-element.217, f32[]{:T(128)S(6)} %min.3, f32[1920,768]{1,0:T(8,128)} %param.25, f32[1920,768]{1,0:T(8,128)} %param.26), kind=kLoop, calls=%fused_computation.41 | loop fusion | flops 26542080 | bytes 35389452 | tf_op jit(solution)/shard_map/reduce_sum | solution.py:202
  561.7 9.2 %multiply_subtract_fusion.2 = f32[1920,768]{1,0:T(8,128)} fusion(f32[1920,768]{1,0:T(8,128)} %param.24, f32[]{:T(128)} %bitcast.104, f32[1920,768]{1,0:T(8,128)} %get-tuple-element.414, f32[1920,768]{1,0:T(8,128)} %get-tuple-element.413), kind=kLoop, calls=%fused_computation.37 | loop fusion | flops 11796480 | bytes 23592964 | tf_op jit(solution)/shard_map/sub | solution.py:608
  (474 shorter events, 246.6 us)
Async XLA Ops:
  7.2 126.6 %all-gather.5.cloned.1.call-start = ((), (), s32[]{:S(2)}) async-start(), calls=%async_computation.18 | async-start | bytes 15206400 | tf_op jit(solution)/shard_map/all_gather | solution.py:305
  17.0 129.6 %copy-start.52 = (s32[1,256]{1,0:T(1,128)}, s32[1,256]{1,0:T(1,128)S(1)}, u32[]{:S(2)}) copy-start(s32[1,256]{1,0:T(1,128)S(1)} %get-tuple-element.468) | copy-start | bytes 3076
  21.1 59.5 %copy-start.54 = (s32[1,256]{1,0:T(1,128)}, s32[1,256]{1,0:T(1,128)S(1)}, u32[]{:S(2)}) copy-start(s32[1,256]{1,0:T(1,128)S(1)} %and_select_fusion.2) | copy-start | bytes 3076
  25.3 14.4 %all-to-all-start.4 = ((s32[32,1,256]{2,1,0:T(1,128)}), s32[32,1,256]{2,1,0:T(1,128)S(1)}, u32[]{:S(2)}, u32[]{:S(2)}) async-start(s32[32,1,256]{2,1,0:T(1,128)} %copy.342), calls=%async_computation.4 | async-start | bytes 65536 | tf_op jit(solution)/shard_map/all_to_all | solution.py:214
  45.4 35.2 %all-to-all-start.5 = ((bf16[16,32,768]{2,1,0:T(8,128)(2,1)}), bf16[16,32,768]{2,1,0:T(8,128)(2,1)}, u32[]{:S(2)}, u32[]{:S(2)}) async-start(bf16[16,32,768]{2,1,0:T(8,128)(2,1)} %broadcast_select_fusion.1), calls=%async_computation.5 | async-start | bytes 1572864 | tf_op jit(solution)/shard_map/all_to_all | solution.py:214
  49.6 122.6 %all-gather.7.cloned.1.call-start = ((), (), s32[]{:S(2)}) async-start(), calls=%async_computation.19 | async-start | bytes 3538944 | tf_op jit(solution)/shard_map/all_gather | solution.py:378
  141.6 177.7 %all-gather.9.cloned.1.call-start = ((), (), s32[]{:S(2)}) async-start(), calls=%async_computation.20 | async-start | bytes 6488064 | tf_op jit(solution)/shard_map/all_gather | solution.py:385
  185.1 18.1 %all-to-all-start.6 = ((bf16[4,64,768]{2,1,0:T(8,128)(2,1)}), bf16[4,64,768]{2,1,0:T(8,128)(2,1)}, u32[]{:S(2)}, u32[]{:S(2)}) async-start(bf16[4,64,768]{2,1,0:T(8,128)(2,1)} %broadcast_in_dim.435), calls=%async_computation.6 | async-start | bytes 786432 | tf_op jit(solution)/shard_map/all_to_all | solution.py:214
  205.1 15.0 %all-to-all-start.7 = ((bf16[2,256,768]{2,1,0:T(8,128)(2,1)}), bf16[2,256,768]{2,1,0:T(8,128)(2,1)}, u32[]{:S(2)}, u32[]{:S(2)}) async-start(bf16[2,256,768]{2,1,0:T(8,128)(2,1)} %broadcast_in_dim.437), calls=%async_computation.7 | async-start | bytes 1572864 | tf_op jit(solution)/shard_map/all_to_all | solution.py:214
  238.0 13.8 %all-to-all-start.9 = ((f32[16,2,1024]{2,1,0:T(2,128)}), f32[16,2,1024]{2,1,0:T(2,128)S(1)}, u32[]{:S(2)}, u32[]{:S(2)}) async-start(f32[16,2,1024]{2,1,0:T(2,128)} %broadcast_in_dim.440), calls=%async_computation.9 | async-start | bytes 262144 | tf_op jit(solution)/shard_map/all_to_all | solution.py:214
  260.5 3.8 collective-permute-start.1
  269.3 24.9 %collective-permute-start.2 = (f32[256,768]{1,0:T(8,128)S(1)}, f32[256,768]{1,0:T(8,128)S(1)}, u32[]{:S(2)}, u32[]{:S(2)}) collective-permute-start(f32[256,768]{1,0:T(8,128)S(1)} %constant_dynamic-slice_fusion.1), channel_id=1, source_target_pairs={{0,2},{2,0},{1,3},{3,1},{4,6},{6,4},{5,7},{7,5},{8,10},{10,8},{9,1... | collective-permute-start | bytes 2359304 | tf_op jit(solution)/shard_map/ppermute | solution.py:409
  271.9 23.3 %all-to-all-start.10 = ((bf16[32,64,96]{2,1,0:T(8,128)(2,1)}), bf16[32,64,96]{2,1,0:T(8,128)(2,1)S(1)}, u32[]{:S(2)}, u32[]{:S(2)}) async-start(bf16[32,64,96]{2,1,0:T(8,128)(2,1)} %bitcast.189), calls=%async_computation.10 | async-start | bytes 1048576 | tf_op jit(solution)/shard_map/all_to_all | solution.py:214
  296.0 23.3 %all-to-all-start.11 = ((f32[4,64,768]{2,1,0:T(8,128)}), f32[4,64,768]{2,1,0:T(8,128)S(1)}, u32[]{:S(2)}, u32[]{:S(2)}) async-start(f32[4,64,768]{2,1,0:T(8,128)} %bitcast.43), calls=%async_computation.11 | async-start | bytes 1572864 | tf_op jit(solution)/shard_map/all_to_all | solution.py:214
  299.5 153.3 %all-gather.11.cloned.1.call-start = ((), (), s32[]{:S(2)}) async-start(), calls=%async_computation.21 | async-start | bytes 3244032 | tf_op jit(solution)/shard_map/all_gather | solution.py:446
  302.8 127.1 %collective-permute-start.3 = (bf16[1920,768]{1,0:T(8,128)(2,1)}, bf16[1920,768]{1,0:T(8,128)(2,1)}, u32[]{:S(2)}, u32[]{:S(2)}) collective-permute-start(bf16[1920,768]{1,0:T(8,128)(2,1)} %convolution_convert_fusion.1), channel_id=1, source_target_pairs={{0,16},{16,0},{1,17},{17,1},{2,18},{18,2},{3,19},{19,3},{4,20},{20... | collective-permute-start | bytes 8847368 | tf_op jit(solution)/shard_map/ppermute | solution.py:426
  349.3 28.1 %all-to-all-start.12 = ((bf16[32,64,120]{2,1,0:T(8,128)(2,1)}), bf16[32,64,120]{2,1,0:T(8,128)(2,1)}, u32[]{:S(2)}, u32[]{:S(2)}) async-start(bf16[32,64,120]{2,1,0:T(8,128)(2,1)} %maximum_bitcast_fusion.1), calls=%async_computation.12 | async-start | bytes 1048576 | tf_op jit(solution)/shard_map/all_to_all | solution.py:214
  361.6 45.8 %copy-start.53 = (s32[1,256]{1,0:T(1,128)S(1)}, s32[1,256]{1,0:T(1,128)}, u32[]{:S(2)}) copy-start(s32[1,256]{1,0:T(1,128)} %copy-done.52) | copy-start | bytes 3076
  377.3 24.0 %all-to-all-start.13 = ((bf16[8,288,192]{2,1,0:T(8,128)(2,1)}), bf16[8,288,192]{2,1,0:T(8,128)(2,1)S(1)}, u32[]{:S(2)}, u32[]{:S(2)}) async-start(bf16[8,288,192]{2,1,0:T(8,128)(2,1)} %maximum_maximum_fusion), calls=%async_computation.13 | async-start | bytes 2359296 | tf_op jit(solution)/shard_map/all_to_all | solution.py:214
  401.4 24.4 %all-to-all-start.14 = ((bf16[16,32,768]{2,1,0:T(8,128)(2,1)}), bf16[16,32,768]{2,1,0:T(8,128)(2,1)}, u32[]{:S(2)}, u32[]{:S(2)}) async-start(bf16[16,32,768]{2,1,0:T(8,128)(2,1)} %select_convert_fusion), calls=%async_computation.14 | async-start | bytes 1572864 | tf_op jit(solution)/shard_map/all_to_all | solution.py:214
  425.8 19.9 %collective-permute-start.4 = (bf16[512,768]{1,0:T(8,128)(2,1)}, bf16[512,768]{1,0:T(8,128)(2,1)S(1)}, u32[]{:S(2)}, u32[]{:S(2)}) collective-permute-start(bf16[512,768]{1,0:T(8,128)(2,1)} %bitcast.60), channel_id=1, source_target_pairs={{0,16},{16,0},{1,17},{17,1},{2,18},{18,2},{3,19},{19,3},{4,20},{20... | collective-permute-start | bytes 2359304 | tf_op jit(solution)/shard_map/ppermute | solution.py:489
  462.8 38.8 %all-to-all-start.15 = ((bf16[32,24,774]{2,1,0:T(8,128)(2,1)}), bf16[32,24,774]{2,1,0:T(8,128)(2,1)S(1)}, u32[]{:S(2)}, u32[]{:S(2)}) async-start(bf16[32,24,774]{2,1,0:T(8,128)(2,1)} %concatenate.96), calls=%async_computation.15 | async-start | bytes 2752512 | tf_op jit(solution)/shard_map/all_to_all | solution.py:214
  509.9 9.6 %all-to-all-start.16 = ((f32[32,1,2]{2,1,0:T(1,128)}), f32[32,1,2]{2,1,0:T(1,128)S(1)}, u32[]{:S(2)}, u32[]{:S(2)}) async-start(f32[32,1,2]{2,1,0:T(1,128)} %copy.381), calls=%async_computation.16 | async-start | bytes 32768 | tf_op jit(solution)/shard_map/all_to_all | solution.py:214
  544.4 10.1 %all-to-all-start.17 = ((f32[32,6,2]{1,2,0:T(2,128)}), f32[32,6,2]{1,2,0:T(2,128)S(1)}, u32[]{:S(2)}, u32[]{:S(2)}) async-start(f32[32,6,2]{1,2,0:T(2,128)} %broadcast_in_dim.459), calls=%async_computation.17 | async-start | bytes 65536 | tf_op jit(solution)/shard_map/all_to_all | solution.py:214
  (97 other events, 1658.5 us)
Sparse Core Ops, SparseCore 0:
  11.7 122.0 all-gather.4
  141.7 30.4 all-gather.6
  175.2 77.5 all-gather.8
  337.9 69.4 all-gather.10

commit v3 on v2

--- a/solution.py
+++ b/solution.py
@@ -3,6 +3,8 @@
 import jax
 import jax.numpy as jnp
 from jax import lax
+from jax.experimental import pallas as pl
+from jax.experimental.pallas import tpu as pltpu
 from jax.sharding import Mesh
 from jax.sharding import PartitionSpec as P
 
@@ -68,65 +70,178 @@
     return (inner * inverse, jnp.sum(upstream * normed, axis=0), jnp.sum(upstream, axis=0))
 
 
-def split_heads(rows):
-    return rows.reshape(rows.shape[0], HEADS, HD)
-
-
-def attention_probs(query_rows, key_rows, allowed, log_total):
-    scores = jnp.einsum(
-        "qhd,khd->hqk",
-        split_heads(query_rows),
-        split_heads(key_rows),
-        preferred_element_type=single,
-    ) * HD ** (-0.5)
-    scores = jnp.where(allowed[None], scores, masked_score)
-    if log_total is None:
-        row_top = jnp.max(scores, axis=-1, keepdims=True)
-        log_total = row_top + jnp.log(jnp.sum(jnp.exp(scores - row_top), axis=-1, keepdims=True))
-    return (jnp.exp(scores - log_total), log_total)
-
-
-def layer_forward(layer_b, small_full, stream_b, query_init, allowed):
-    width = stream_b.shape[1]
-    key_rows = plain_dot(stream_b, layer_b[0][:, width : 2 * width]).astype(bfloat)
-    value_rows = (plain_dot(stream_b, layer_b[0][:, 2 * width : 3 * width]) + small_full[3]).astype(
-        bfloat
-    )
-    init_b = query_init.astype(bfloat)
-    query_rows = (plain_dot(init_b, layer_b[0][:, :width]) + small_full[2]).astype(bfloat)
-    attn_probs, log_total = attention_probs(query_rows, key_rows, allowed, None)
-    mixed_b = jnp.einsum(
-        "hqk,khd->qhd",
-        attn_probs.astype(bfloat),
-        split_heads(value_rows),
-        preferred_element_type=single,
-    )
-    mixed_b = mixed_b.reshape(-1, width).astype(bfloat)
-    attend = plain_dot(mixed_b, layer_b[0][:, 3 * width :]) + small_full[4]
-    middle, middle_kept = norm_forward(query_init + attend, small_full[5], small_full[6])
+def pair_masks(rows):
+    lane = lax.broadcasted_iota(jnp.int32, (rows, 2 * HD), 1)
+    return lane < HD, lane >= HD
+
+
+def head_probs(query_pair, key_pair, head_lanes, blocked):
+    scores = trans_dot(jnp.where(head_lanes, query_pair, jnp.zeros_like(query_pair)), key_pair)
+    scores = jnp.where(blocked, masked_score, scores * HD ** (-0.5))
+    row_top = jnp.max(scores, axis=-1, keepdims=True)
+    powers = jnp.exp(scores - row_top)
+    return powers / jnp.sum(powers, axis=-1, keepdims=True)
+
+
+def attend_kernel(
+    stream_ref, init_ref, small_ref, allowed_ref, weight_ref,
+    key_ref, value_ref, query_ref, mixed_ref, middle_ref, normed_ref, inverse_ref,
+):
+    step = pl.program_id(0)
+
+    @pl.when(step == 0)
+    def _():
+        key_ref[...] = plain_dot(stream_ref[...], weight_ref[...]).astype(bfloat)
+
+    @pl.when(step == 1)
+    def _():
+        value_ref[...] = (
+            plain_dot(stream_ref[...], weight_ref[...]) + small_ref[pl.ds(3, 1), :]
+        ).astype(bfloat)
+
+    @pl.when(step == 2)
+    def _():
+        query_ref[...] = (
+            plain_dot(init_ref[...].astype(bfloat), weight_ref[...]) + small_ref[pl.ds(2, 1), :]
+        ).astype(bfloat)
+        blocked = allowed_ref[...] == 0.0
+        low, high = pair_masks(query_ref.shape[0])
+
+        def one_pair(pair, carry):
+            lanes = pl.ds(pl.multiple_of(pair * 2 * HD, 2 * HD), 2 * HD)
+            query_pair, key_pair, value_pair = query_ref[:, lanes], key_ref[:, lanes], value_ref[:, lanes]
+            left, right = (
+                plain_dot(
+                    head_probs(query_pair, key_pair, head_lanes, blocked).astype(bfloat), value_pair
+                )
+                for head_lanes in (low, high)
+            )
+            mixed_ref[:, lanes] = jnp.where(low, left, right).astype(bfloat)
+            return carry
+
+        lax.fori_loop(0, query_ref.shape[1] // (2 * HD), one_pair, 0)
+
+    @pl.when(step == 3)
+    def _():
+        attend = plain_dot(mixed_ref[...], weight_ref[...]) + small_ref[pl.ds(4, 1), :]
+        middle, (normed, inverse) = norm_forward(
+            init_ref[...] + attend, small_ref[pl.ds(5, 1), :], small_ref[pl.ds(6, 1), :]
+        )
+        middle_ref[...] = middle
+        normed_ref[...] = normed
+        inverse_ref[...] = jnp.broadcast_to(inverse, inverse_ref.shape)
+
+
+def attend_forward(stream_b, query_init, small_full, allowed, weights):
+    length, width = stream_b.shape
+    slots = query_init.shape[0]
+    out = lambda rows, kind, columns=width: jax.ShapeDtypeStruct((rows, columns), kind)
+    whole = lambda shape: pl.BlockSpec(shape, lambda step: (0, 0))
+    shapes = (
+        out(length, bfloat), out(length, bfloat), out(slots, bfloat), out(slots, bfloat),
+        out(slots, single), out(slots, single), out(slots, single, 128),
+    )
+    return pl.pallas_call(
+        attend_kernel,
+        grid=(4,),
+        in_specs=[
+            whole(stream_b.shape),
+            whole(query_init.shape),
+            whole(small_full.shape),
+            whole(allowed.shape),
+            pl.BlockSpec(
+                (width, width), lambda step: (0, jnp.where(step == 3, 3, (step + 1) % 3))
+            ),
+        ],
+        out_specs=[whole(shape.shape) for shape in shapes],
+        out_shape=shapes,
+        cost_estimate=pl.CostEstimate(
+            flops=4 * length * width * width + 8 * slots * length * width,
+            bytes_accessed=8 * width * width,
+            transcendentals=HEADS * slots * length,
+        ),
+        name="attention_forward",
+    )(stream_b, query_init, small_full, allowed, weights)
+
+
+def attend_back_kernel(
+    d_attend_ref, key_ref, value_ref, query_ref, allowed_ref, weight_ref,
+    d_query_ref, d_key_ref, d_value_ref, d_mixed_ref,
+):
+    d_mixed_ref[...] = trans_dot(d_attend_ref[...], weight_ref[...]).astype(bfloat)
+    blocked = allowed_ref[...] == 0.0
+    slots, length = blocked.shape
+    low, high = pair_masks(slots)
+    low_long, _ = pair_masks(length)
+    scale = HD ** (-0.5)
+
+    def one_pair(pair, carry):
+        lanes = pl.ds(pl.multiple_of(pair * 2 * HD, 2 * HD), 2 * HD)
+        query_pair, key_pair, value_pair = query_ref[:, lanes], key_ref[:, lanes], value_ref[:, lanes]
+        mixed_pair = d_mixed_ref[:, lanes]
+        found = []
+        for head_lanes in (low, high):
+            probs = head_probs(query_pair, key_pair, head_lanes, blocked)
+            d_probs = trans_dot(
+                jnp.where(head_lanes, mixed_pair, jnp.zeros_like(mixed_pair)), value_pair
+            )
+            inner = jnp.sum(probs * d_probs, axis=-1, keepdims=True)
+            d_scores = (probs * (d_probs - inner)).astype(bfloat)
+            found.append(
+                (
+                    plain_dot(d_scores, key_pair) * scale,
+                    rows_dot(d_scores, query_pair) * scale,
+                    rows_dot(probs.astype(bfloat), mixed_pair),
+                )
+            )
+        d_query_ref[:, lanes] = jnp.where(low, found[0][0], found[1][0]).astype(bfloat)
+        d_key_ref[:, lanes] = jnp.where(low_long, found[0][1], found[1][1]).astype(bfloat)
+        d_value_ref[:, lanes] = jnp.where(low_long, found[0][2], found[1][2]).astype(bfloat)
+        return carry
+
+    lax.fori_loop(0, query_ref.shape[1] // (2 * HD), one_pair, 0)
+
+
+def attend_backward(d_attend, key_rows, value_rows, query_rows, allowed, weights):
+    length, width = key_rows.shape
+    slots = d_attend.shape[0]
+    whole = lambda shape: pl.BlockSpec(shape, lambda step: (0, 0))
+    shapes = tuple(
+        jax.ShapeDtypeStruct((rows, width), bfloat) for rows in (slots, length, length)
+    )
+    return pl.pallas_call(
+        attend_back_kernel,
+        grid=(1,),
+        in_specs=[
+            whole(d_attend.shape),
+            whole(key_rows.shape),
+            whole(value_rows.shape),
+            whole(query_rows.shape),
+            whole(allowed.shape),
+            pl.BlockSpec((width, width), lambda step: (0, 3)),
+        ],
+        out_specs=[whole(shape.shape) for shape in shapes],
+        out_shape=shapes,
+        scratch_shapes=[pltpu.VMEM((slots, width), bfloat)],
+        cost_estimate=pl.CostEstimate(
+            flops=2 * slots * width * width + 20 * slots * length * width,
+            bytes_accessed=2 * width * width,
+            transcendentals=HEADS * slots * length,
+        ),
+        name="attention_backward",
+    )(d_attend, key_rows, value_rows, query_rows, allowed, weights)
+
+
+def feed_forward(layer_b, small_full, middle):
     middle_b = middle.astype(bfloat)
     hidden = plain_dot(middle_b, layer_b[1]) + small_full[7:11].reshape(-1)
     active_b = jax.nn.gelu(hidden, approximate=False).astype(bfloat)
     branch = trans_dot(active_b, layer_b[2]) + small_full[11]
     output_rows, final_kept = norm_forward(middle + branch, small_full[12], small_full[13])
-    kept_state = (
-        key_rows,
-        value_rows,
-        init_b,
-        query_rows,
-        log_total,
-        mixed_b,
-        middle_kept,
-        middle_b,
-        hidden,
-        active_b,
-        final_kept,
-    )
-    return (output_rows, kept_state)
-
-
-def feed_backward(layer_b, small_full, kept_state, d_output):
-    hidden, final_kept, middle_kept = kept_state[8], kept_state[10], kept_state[6]
+    return output_rows, (middle_b, hidden, active_b, final_kept)
+
+
+def feed_backward(layer_b, small_full, hidden, final_kept, middle_kept, d_output):
     d_sum, gain_three, bias_three = norm_backward(d_output, final_kept, small_full[12])
     d_branch = d_sum.astype(bfloat)
     _, gelu_pull = jax.vjp(partial(jax.nn.gelu, approximate=False), hidden)
@@ -146,42 +261,20 @@
     return d_branch, d_hidden, d_pre, grad_mid
 
 
-def attention_backward(layer_b, allowed, kept_state, d_pre):
-    key_rows, value_rows, _, query_rows, log_total = kept_state[:5]
+def project_backward(layer_b, d_pre, d_query, d_key, d_value):
     width = d_pre.shape[1]
-    d_attend = d_pre.astype(bfloat)
-    d_mixed = trans_dot(d_attend, layer_b[0][:, 3 * width :]).astype(bfloat)
-    attn_probs, _ = attention_probs(query_rows, key_rows, allowed, log_total)
-    mixed_heads = split_heads(d_mixed)
-    d_probs = jnp.einsum(
-        "qhd,khd->hqk", mixed_heads, split_heads(value_rows), preferred_element_type=single
-    )
-    d_value = jnp.einsum(
-        "hqk,qhd->khd", attn_probs.astype(bfloat), mixed_heads, preferred_element_type=single
-    )
-    d_value = d_value.reshape(-1, width).astype(bfloat)
-    d_scores = (
-        attn_probs * (d_probs - jnp.sum(attn_probs * d_probs, axis=-1, keepdims=True))
-    ).astype(bfloat)
-    scale = HD ** (-0.5)
-    d_query = (
-        jnp.einsum("hqk,khd->qhd", d_scores, split_heads(key_rows), preferred_element_type=single)
-        * scale
-    )
-    d_query = d_query.reshape(-1, width).astype(bfloat)
-    d_key = (
-        jnp.einsum("hqk,qhd->khd", d_scores, split_heads(query_rows), preferred_element_type=single)
-        * scale
-    )
-    d_key = d_key.reshape(-1, width).astype(bfloat)
     d_init = d_pre + trans_dot(d_query, layer_b[0][:, :width])
     d_stream = trans_dot(d_key, layer_b[0][:, width : 2 * width]) + trans_dot(
         d_value, layer_b[0][:, 2 * width : 3 * width]
     )
     grad_mid = jnp.concatenate(
-        [column_sum(d_query)[None], column_sum(d_value)[None], column_sum(d_attend)[None]]
-    )
-    return d_attend, d_query, d_key, d_value, d_init, d_stream, grad_mid
+        [
+            column_sum(d_query)[None],
+            column_sum(d_value)[None],
+            column_sum(d_pre.astype(bfloat))[None],
+        ]
+    )
+    return d_init, d_stream, grad_mid
 
 
 def adam_moments(weight_arr, first_mom, second_mom, gradient, factor):
@@ -376,9 +469,14 @@
     near = dp_devs * 4
     if few:
         stream_all = lax.all_gather(stream_b, NEAR, axis=0, tiled=True)
-    output_rows, kept_state = layer_forward(layer_b, small_full, stream_b, query_init, allowed)
+    allowed = allowed.astype(single)
+    key_rows, value_rows, query_rows, mixed_b, middle, normed, inverse = attend_forward(
+        stream_b, query_init, small_full, allowed, shard
+    )
+    output_rows, (middle_b, hidden, active_b, final_kept) = feed_forward(
+        layer_b, small_full, middle
+    )
     output_b = output_rows.astype(bfloat)
-    init_b, mixed_b, middle_b, active_b = (kept_state[2], kept_state[5], kept_state[7], kept_state[9])
     if few:
         kept_rows = jnp.concatenate([mixed_b, middle_b], axis=1)
         kept_rows, stream_all = lax.optimization_barrier((kept_rows, stream_all))
@@ -432,21 +530,25 @@
     if few:
         d_output, kept_all = lax.optimization_barrier((d_output, kept_all))
     d_output = jnp.sum(d_output, axis=0)
-    d_branch, d_hidden, d_pre, mid_feed = feed_backward(layer_b, small_full, kept_state, d_output)
+    d_branch, d_hidden, d_pre, mid_feed = feed_backward(
+        layer_b, small_full, hidden, final_kept, (normed, inverse[:, :1]), d_output
+    )
+    d_attend = d_pre.astype(bfloat)
     if few:
         wide = feed // devices
         both = jnp.concatenate(
             [
                 d_hidden.reshape(CAP, devices, -1),
-                d_pre.astype(bfloat).reshape(CAP, devices, -1),
+                d_attend.reshape(CAP, devices, -1),
             ],
             axis=2,
         ).reshape(CAP, -1)
         both = exchange.columns(both, ALL, devices)
         branch_all = lax.all_gather(d_branch, ALL, axis=0, tiled=True)
-    d_attend, d_query, d_key, d_value, d_init, d_stream, mid_attn = attention_backward(
-        layer_b, allowed, kept_state, d_pre
-    )
+    d_query, d_key, d_value = attend_backward(
+        d_attend, key_rows, value_rows, query_rows, allowed, shard
+    )
+    d_init, d_stream, mid_attn = project_backward(layer_b, d_pre, d_query, d_key, d_value)
     grad_mid = jnp.concatenate([mid_attn, mid_feed])
     if few:
         piece = width // near
@@ -484,10 +586,12 @@
     def give(hot_rows, extra, send):
         rows = plain_dot(hot_rows, embed_back).reshape(owners, BUCKET, width)
         rows = jnp.where(is_left[:, :, None] & extra, mask_left[None, None, :], rows)
-        rows = send(rows.astype(bfloat), VOC).reshape(-1, width)
+        return send(rows.astype(bfloat), VOC).reshape(-1, width)
+
+    def of_both(rows):
         if dp_devs == 2:
-            return jnp.concatenate([rows, lax.ppermute(rows, "dp", [(0, 1), (1, 0)])])
-        return lax.all_gather(rows, "dp", axis=0, tiled=True)
+            return rows, lax.ppermute(rows, "dp", [(0, 1), (1, 0)])
+        return (lax.all_gather(rows, "dp", axis=0, tiled=True),)
 
     def both_groups(asked_rows):
         if dp_devs == 2:
@@ -497,24 +601,12 @@
     def into_rows(asked_rows, given):
         flat = both_groups(asked_rows).reshape(-1)
         row_hot = flat[None, :] == jnp.arange(vrows)[:, None]
-        return plain_dot(row_hot.astype(bfloat), given)
+        return plain_dot(row_hot.astype(bfloat), jnp.concatenate(given))
 
     last = (jnp.arange(BUCKET) == BUCKET - 1)[None, :]
     left_row = jnp.where(lax.axis_index(VOC) == mask_owner, MASK_ID - first_row, -1)
-    table_grad = grad_head + into_rows(jnp.where(last, left_row, asked), give(hot, True, exchange))
-
-    def more_grads(state):
-        turn, grads = state
-        hot_t, wanted_t = bucket_round(content, owner, place, turn, owners, vrows)
-        wanted_t = jnp.broadcast_to(wanted_t[None], (dp_devs,) + wanted_t.shape)
-        asked_t = lax.all_to_all(
-            wanted_t.reshape(devices, BUCKET), ALL, 0, 0, tiled=True
-        )
-        return turn + 1, grads + into_rows(asked_t, give(hot_t, False, plain_exchange))
-
-    _, table_grad = lax.while_loop(
-        lambda state: state[0] < rounds, more_grads, (jnp.ones((), rounds.dtype), table_grad)
-    )
+    given = give(hot, True, exchange)
+
     if few:
         near_pos = packet[:, BUCKET + CAP : tail].reshape(dp_devs, outer, 4 * CAP)
         near_pos = lax.dynamic_index_in_dim(near_pos, lax.axis_index("hi"), 1, False).reshape(-1)
@@ -533,7 +625,9 @@
         results = jnp.concatenate(
             [grad_pair, grad_ask, grad_up, grad_down, grad_out, shared_grad], axis=1
         )
-        results = exchange.rows(results.astype(bfloat), devices).astype(single)
+        results = results.astype(bfloat)
+        given, _ = lax.optimization_barrier((given, results))
+        results = exchange.rows(results, devices).astype(single)
         pieces = 3 * piece
         attn = jnp.sum(
             results[..., :pieces].reshape(dp_devs, outer, 4, share, pieces), axis=1
@@ -557,7 +651,7 @@
         whole = (
             jnp.concatenate(
                 [
-                    rows_dot(init_b, d_query),
+                    rows_dot(query_init.astype(bfloat), d_query),
                     rows_dot(stream_b, d_key),
                     rows_dot(stream_b, d_value),
                     rows_dot(mixed_b, d_attend),
@@ -573,8 +667,28 @@
         shared_grad = jnp.concatenate([grad_position, grad_small]).T
         shared_grad = lax.psum_scatter(shared_grad, ALL, scatter_dimension=0, tiled=True).T
         position_grad, small_grad = shared_grad[:length], shared_grad[length:]
+    table_grad = grad_head + into_rows(jnp.where(last, left_row, asked), of_both(given))
+
+    def more_grads(state):
+        turn, grads = state
+        hot_t, wanted_t = bucket_round(content, owner, place, turn, owners, vrows)
+        wanted_t = jnp.broadcast_to(wanted_t[None], (dp_devs,) + wanted_t.shape)
+        asked_t = lax.all_to_all(
+            wanted_t.reshape(devices, BUCKET), ALL, 0, 0, tiled=True
+        )
+        return turn + 1, grads + into_rows(asked_t, of_both(give(hot_t, False, plain_exchange)))
+
+    _, table_grad = lax.while_loop(
+        lambda state: state[0] < rounds, more_grads, (jnp.ones((), rounds.dtype), table_grad)
+    )
+    split = vrows // dp_devs
+
+    def own_part(values):
+        return lax.dynamic_slice_in_dim(values, lax.axis_index("dp") * split, split, 0)
+
+    grad_part = own_part(table_grad)
     square_part = (
-        jnp.sum(table_grad * table_grad) / dp_devs
+        jnp.sum(grad_part * grad_part)
         + jnp.sum(layer_grad * layer_grad)
         + jnp.sum(position_grad * position_grad)
         + jnp.sum(small_grad * small_grad)
@@ -582,8 +696,9 @@
     total_square, loss_value = exchange.total(jnp.stack([square_part, loss_part]), ALL, devices)
     grad_norm = jnp.sqrt(total_square)
     factor = jnp.minimum(1.0, clip_norm / grad_norm)
-    table_first, table_second, table_dir = adam_moments(
-        embed_table, table_moment, table_square, table_grad, factor
+    weight_part = own_part(embed_table)
+    _, _, part_dir = adam_moments(
+        weight_part, own_part(table_moment), own_part(table_square), grad_part, factor
     )
     layer_first, layer_second, layer_dir = adam_moments(
         layer_weights, layer_moment, layer_square, layer_grad, factor
@@ -596,12 +711,17 @@
     )
     partial_norms = jnp.concatenate(
         [
-            norm_pair(embed_table, table_dir, (0, 1))[None] / dp_devs,
+            norm_pair(weight_part, part_dir, (0, 1))[None],
             norm_pair(layer_weights, layer_dir, (1, 2)),
             norm_pair(position_table, position_dir, (0, 1))[None],
             norm_pair(small_params, small_dir, (0, 1))[None],
         ]
     )
+    factor_late, _ = lax.optimization_barrier((factor, partial_norms))
+    table_first, table_second, table_dir = adam_moments(
+        embed_table, table_moment, table_square, table_grad, factor_late
+    )
+    table_dir = lax.optimization_barrier(table_dir)
     trust_square = exchange.total(partial_norms, ALL, devices)
     trust_norms = jnp.sqrt(trust_square)
     ratio = trust_norms[:, 0] / trust_norms[:, 1]

time: 587 us -> 604 us (1.029)
  Pallas kernels: 0 us -> 19.5 us
  matrix products: 87.4 us -> 74.3 us
  other arithmetic: 93.6 us -> 101 us
    pallas_call x0 -> x2, Pallas kernels: none -> 19.5 us  [the longest x1 9.91 us: attend_forward(): pl.pallas_call(attend_kernel, grid=(4,), in_specs=[whole(stream_b.shape),...]
    add x1 -> x2, other arithmetic: 0.01 us -> 16.6 us  [the longest x1 15.8 us: adam_moments(): new_first / (1.0 - beta_first ** STEP)]
    all_to_all x13, waiting for transfers between devices: 158 us -> 147 us  [__call__(): self.last = lax.all_to_all(values, axes, 0, 0, tiled=True)]
    unnamed x208 -> x191, local copies, waits for them, and re-layouts: 13.4 us -> 5.17 us
    dot_general x12 -> x8, matrix products: 36.6 us -> 29 us  [plain_dot(): return jnp.dot(left_op, right_op, preferred_element_type=single)]
    dot_general x6 -> x0, matrix products: 6.71 us -> none  [the longest x1 2.02 us: layer_forward(): jnp.einsum('hqk,khd->qhd', attn_probs.astype(bfloat), split_heads(value_r...]
    dot_general x7 -> x6, matrix products: 21.9 us -> 20.2 us  [trans_dot(): lax.dot_general(left_op, right_op, (((1,), (1,)), ((), ())), preferred_el...]
  transfers between devices with their start and end apart: 21 -> 21, of which waited for: 17 -> 15; matrix products, arithmetic and copies ran while one was open for 29% -> 31% of each run, Pallas kernels for 0% -> 3%
where the time goes in v3:
time: 604 us; the launch traced here: 596 us
  waiting for transfers between devices  242 us (40%)
  other arithmetic  101 us (17%)
  matrix products  74.3 us (12%)
  local copies, waits for them, and re-layouts  67.3 us (11%)
  starting transfers between devices  60.5 us (10%)
  between operations  26.2 us (4%)
  Pallas kernels  19.5 us (3%)
    all_to_all x13, waiting for transfers between devices, __call__(): self.last = lax.all_to_all(values, axes, 0, 0, tiled=True)  147 us
    all_to_all x13, starting transfers between devices, __call__(): self.last = lax.all_to_all(values, axes, 0, 0, tiled=True)  57.7 us
    all_gather x1, waiting for transfers between devices, on_device(): shard = lax.all_gather(shard.astype(bfloat), ALL, axis=0, tiled=True)  54 us
    dot_general x8, matrix products, plain_dot(): return jnp.dot(left_op, right_op, preferred_element_type=single)  29 us
    dot_general x7, matrix products, rows_dot(): lax.dot_general(left_op, right_op, (((0,), (0,)), ((), ())), preferred_el...  22.5 us
    dot_general x6, matrix products, trans_dot(): lax.dot_general(left_op, right_op, (((1,), (1,)), ((), ())), preferred_el...  20.2 us
    add x1, other arithmetic, adam_moments(): new_first / (1.0 - beta_first ** STEP)  15.8 us
    ppermute x2, waiting for transfers between devices, swapped(): theirs = lax.ppermute(part(1 - side), axis, [(0, 1), (1, 0)])  15 us
  transfers between devices with their start and end apart: 21, of which 15 were waited for; matrix products, arithmetic and copies ran while one was open for 31% of the time, Pallas kernels for 3%

profile of v3, /device:TPU:0, one launch (start us, length us, event | category | flops | bytes accessed | tf_op | source)
XLA Modules:
  0.0 595.8 jit_solution(6385483162378586307)
XLA Ops:
  20.9 7.3 %all-to-all-start.4 = ((s32[32,1,256]{2,1,0:T(1,128)}), s32[32,1,256]{2,1,0:T(1,128)S(1)}, u32[]{:S(2)}, u32[]{:S(2)}) async-start(s32[32,1,256]{2,1,0:T(1,128)} %copy.455), calls=%async_computation.4 | async-start | bytes 65536 | tf_op jit(solution)/shard_map/all_to_all | solution.py:307
  28.3 7.4 %all-to-all-done.4 = s32[32,1,256]{2,1,0:T(1,128)S(1)} async-done(((s32[32,1,256]{2,1,0:T(1,128)}), s32[32,1,256]{2,1,0:T(1,128)S(1)}, u32[]{:S(2)}, u32[]{:S(2)}) %all-to-all-start.4) | async-done | bytes 32800 | tf_op jit(solution)/shard_map/all_to_all | solution.py:307
  48.3 28.7 %all-to-all-done.5 = bf16[16,32,768]{2,1,0:T(8,128)(2,1)} async-done(((bf16[16,32,768]{2,1,0:T(8,128)(2,1)}), bf16[16,32,768]{2,1,0:T(8,128)(2,1)}, u32[]{:S(2)}, u32[]{:S(2)}) %all-to-all-start.5) | async-done | bytes 786464 | tf_op jit(solution)/shard_map/all_to_all | solution.py:307
  81.7 54.0 %all-gather.5.cloned.1.call-done.weight_ref = bf16[768,9600]{1,0:T(8,128)(2,1)} async-done(((bf16[24,9600]{1,0:T(8,128)(2,1)}), bf16[768,9600]{1,0:T(8,128)(2,1)}) %all-gather.5.cloned.1.call-update) | async-done | bytes 14745616 | tf_op jit(solution)/shard_map/all_gather | solution.py:398
  148.6 9.9 %attention_forward.1 = (bf16[256,768]{1,0:T(8,128)(2,1)}, bf16[256,768]{1,0:T(8,128)(2,1)}, bf16[64,768]{1,0:T(8,128)(2,1)}, bf16[64,768]{1,0:T(8,128)(2,1)}, f3...) custom-call(bf16[256,768]{1,0:T(8,128)(2,1)} %copy.459.stream_ref, f32[64,768]{1,0:T(8,128)} %multiply_add_fusion.4.init_ref, ...), custom_call_target="tpu_custom_call" | custom-call | flops 704643072 | bytes 4718592 | tf_op jit(solution)/shard_map/attention_forward/pallas_call | solution.py:144
  161.1 12.2 %all-gather.7.cloned.1.call-done = bf16[2048,768]{0,1:T(8,128)(2,1)} async-done(((bf16[256,768]{0,1:T(8,128)(2,1)}), bf16[2048,768]{0,1:T(8,128)(2,1)}) %all-gather.7.cloned.1.call-update) | async-done | bytes 3145744 | tf_op jit(solution)/shard_map/all_gather | solution.py:471
  175.4 5.6 multiply_convert_fusion.1
  190.8 13.3 %all-to-all-done.6 = bf16[4,64,768]{2,1,0:T(8,128)(2,1)S(1)} async-done(((bf16[4,64,768]{2,1,0:T(8,128)(2,1)}), bf16[4,64,768]{2,1,0:T(8,128)(2,1)S(1)}, u32[]{:S(2)}, u32[]{:S(2)}) %all-to-all-start.6) | async-done | bytes 393248 | tf_op jit(solution)/shard_map/all_to_all | solution.py:307
  212.5 7.8 %all-to-all-done.7 = bf16[2,256,768]{2,1,0:T(8,128)(2,1)} async-done(((bf16[2,256,768]{2,1,0:T(8,128)(2,1)}), bf16[2,256,768]{2,1,0:T(8,128)(2,1)}, u32[]{:S(2)}, u32[]{:S(2)}) %all-to-all-start.7) | async-done | bytes 786464 | tf_op jit(solution)/shard_map/all_to_all | solution.py:307
  239.8 9.5 %all-to-all-done.9 = f32[16,2,1024]{2,1,0:T(2,128)S(1)} async-done(((f32[16,2,1024]{2,1,0:T(2,128)}), f32[16,2,1024]{2,1,0:T(2,128)S(1)}, u32[]{:S(2)}, u32[]{:S(2)}) %all-to-all-start.9) | async-done | bytes 131104 | tf_op jit(solution)/shard_map/all_to_all | solution.py:307
  274.4 7.1 %convolution_convert_fusion.1 = bf16[1920,768]{1,0:T(8,128)(2,1)} fusion(bf16[1024,1920]{1,0:T(8,128)(2,1)} %copy-done.6, bf16[1024,768]{1,0:T(8,128)(2,1)S(1)} %bitcast.198), kind=kOutput, calls=%fused_computation.52 | convolution fusion | flops 3021373440 | bytes 8454144 | tf_op jit(solution)/shard_map/dot_general | solution.py:46
  281.6 11.2 %collective-permute-done.2 = f32[256,768]{1,0:T(8,128)S(1)} collective-permute-done((f32[256,768]{1,0:T(8,128)}, f32[256,768]{1,0:T(8,128)S(1)}, u32[]{:S(2)}, u32[]{:S(2)}) %collective-permute-start.2) | collective-permute-done | bytes 786464 | tf_op jit(solution)/shard_map/ppermute | solution.py:507
  302.3 15.0 %all-to-all-done.11 = f32[4,64,768]{2,1,0:T(8,128)S(1)} async-done(((f32[4,64,768]{2,1,0:T(8,128)}), f32[4,64,768]{2,1,0:T(8,128)S(1)}, u32[]{:S(2)}, u32[]{:S(2)}) %all-to-all-start.11) | async-done | bytes 786464 | tf_op jit(solution)/shard_map/all_to_all | solution.py:307
  332.3 9.6 %attention_backward.1 = (bf16[64,768]{1,0:T(8,128)(2,1)}, bf16[256,768]{1,0:T(8,128)(2,1)}, bf16[256,768]{1,0:T(8,128)(2,1)}) custom-call(bf16[64,768]{1,0:T(8,128)(2,1)} %copy-done.24, bf16[256,768]{1,0:T(8,128)(2,1)} %get-tuple-element.229.key_ref, bf16[256,768]{1,0:T(8,128)(2,1)} %get-tuple-element.230.value_ref, ...), custom_call_target="tpu_custom_call" | custom-call | flops 327155712 | bytes 1179648 | tf_op jit(solution)/shard_map/attention_backward/pallas_call | solution.py:212
  361.3 19.8 %all-to-all-done.12 = bf16[32,64,120]{2,1,0:T(8,128)(2,1)} async-done(((bf16[32,64,120]{2,1,0:T(8,128)(2,1)}), bf16[32,64,120]{2,1,0:T(8,128)(2,1)}, u32[]{:S(2)}, u32[]{:S(2)}) %all-to-all-start.12) | async-done | bytes 491552 | tf_op jit(solution)/shard_map/all_to_all | solution.py:307
  389.3 11.1 %all-to-all-done.13 = bf16[8,288,192]{1,2,0:T(8,128)(2,1)S(1)} async-done(((bf16[8,288,192]{1,2,0:T(8,128)(2,1)}), bf16[8,288,192]{1,2,0:T(8,128)(2,1)S(1)}, u32[]{:S(2)}, u32[]{:S(2)}) %all-to-all-start.13) | async-done | bytes 884768 | tf_op jit(solution)/shard_map/all_to_all | solution.py:307
  400.4 6.1 %all-to-all-start.14 = ((bf16[16,32,768]{2,1,0:T(8,128)(2,1)}), bf16[16,32,768]{2,1,0:T(8,128)(2,1)}, u32[]{:S(2)}, u32[]{:S(2)}) async-start(bf16[16,32,768]{2,1,0:T(8,128)(2,1)} %select_convert_fusion), calls=%async_computation.14 | async-start | bytes 1572864 | tf_op jit(solution)/shard_map/all_to_all | solution.py:307
  445.9 13.9 %collective-permute-done.4 = bf16[512,768]{1,0:T(8,128)(2,1)} collective-permute-done((bf16[512,768]{1,0:T(8,128)(2,1)}, bf16[512,768]{1,0:T(8,128)(2,1)}, u32[]{:S(2)}, u32[]{:S(2)}) %collective-permute-start.4) | collective-permute-done | bytes 786464 | tf_op jit(solution)/shard_map/ppermute | solution.py:593
  459.8 7.3 %add_add_fusion = f32[1920,768]{1,0:T(8,128)} fusion(bf16[1920,768]{1,0:T(8,128)(2,1)} %collective-permute-done.3, bf16[1920,768]{1,0:T(8,128)(2,1)S(1)} %copy-done.90, s32[1024]{0:T(1024)S(1)} %copy-done.71, bf16[512,768]{1,0:T(8,128)(2,1)} %collective-permute-done.4, bf16[512,768]{1,0:T(8,128)(2,1)} %bitcast.48), kind=kOutput, calls=%fused_computation.40 | convolution fusion | flops 3030908928 | bytes 13373440 | tf_op jit(solution)/shard_map/dot_general | solution.py:36
  488.5 27.7 %all-to-all-done.15 = bf16[32,24,774]{2,1,0:T(8,128)(2,1)S(1)} async-done(((bf16[32,24,774]{2,1,0:T(8,128)(2,1)}), bf16[32,24,774]{2,1,0:T(8,128)(2,1)S(1)}, u32[]{:S(2)}, u32[]{:S(2)}) %all-to-all-start.15) | async-done | bytes 1188896 | tf_op jit(solution)/shard_map/all_to_all | solution.py:307
  527.9 6.7 %all-to-all-done.16 = f32[32,1,2]{2,1,0:T(1,128)S(1)} async-done(((f32[32,1,2]{2,1,0:T(1,128)}), f32[32,1,2]{2,1,0:T(1,128)S(1)}, u32[]{:S(2)}, u32[]{:S(2)}) %all-to-all-start.16) | async-done | bytes 288 | tf_op jit(solution)/shard_map/all_to_all | solution.py:307
  536.1 6.3 %multiply_reduce_fusion = (f32[]{:T(128)}, f32[]{:T(128)}) fusion(f32[1920,768]{1,0:T(8,128)} %param.24, s32[]{:T(128)S(6)} %select_n.255, f32[1920,768]{1,0:T(8,128)} %param.26, f32[]{:T(128)S(6)} %min.3, f32[1920,768]{1,0:T(8,128)} %get-tuple-element.238, f32[1920,768]{1,0:T(8,128)} %param.25), kind=kLoop, calls=%fused_computation.64 | loop fusion | flops 13271038 | bytes 11796496 | tf_op jit(solution)/shard_map/reduce_sum | solution.py:295
  557.2 15.8 %multiply_add_fusion = (f32[1920,768]{1,0:T(8,128)}, f32[1920,768]{1,0:T(8,128)}, f32[1920,768]{1,0:T(8,128)}) fusion(f32[1920,768]{1,0:T(8,128)} %param.24, f32[1920,768]{1,0:T(8,128)} %get-tuple-element.238, f32[]{:T(128)S(6)} %min.3, f32[1920,768]{1,0:T(8,128)} %param.25, f32[1920,768]{1,0:T(8,128)} %param.26), kind=kLoop, calls=%fused_computation.38 | loop fusion | flops 20643840 | bytes 41287684 | tf_op jit(solution)/shard_map/add | solution.py:285
  577.8 7.8 %multiply_subtract_fusion.2 = f32[1920,768]{1,0:T(8,128)} fusion(f32[1920,768]{1,0:T(8,128)} %param.24, f32[1920,768]{1,0:T(8,128)} %get-tuple-element.518, f32[]{:T(128)} %bitcast.91), kind=kLoop, calls=%fused_computation.37 | loop fusion | flops 2949120 | bytes 17694724 | tf_op jit(solution)/shard_map/sub | solution.py:728
  (449 shorter events, 248.4 us)
Async XLA Ops:
  7.2 128.5 %all-gather.5.cloned.1.call-start = ((), (), s32[]{:S(2)}) async-start(), calls=%async_computation.18 | async-start | bytes 15206400 | tf_op jit(solution)/shard_map/all_gather | solution.py:398
  14.2 131.5 %copy-start.51 = (s32[1,256]{1,0:T(1,128)}, s32[1,256]{1,0:T(1,128)S(1)}, u32[]{:S(2)}) copy-start(s32[1,256]{1,0:T(1,128)S(1)} %get-tuple-element.572) | copy-start | bytes 3076
  17.0 60.0 %copy-start.56 = (s32[1,256]{1,0:T(1,128)}, s32[1,256]{1,0:T(1,128)S(1)}, u32[]{:S(2)}) copy-start(s32[1,256]{1,0:T(1,128)S(1)} %and_select_fusion.2) | copy-start | bytes 3076
  20.9 14.7 %all-to-all-start.4 = ((s32[32,1,256]{2,1,0:T(1,128)}), s32[32,1,256]{2,1,0:T(1,128)S(1)}, u32[]{:S(2)}, u32[]{:S(2)}) async-start(s32[32,1,256]{2,1,0:T(1,128)} %copy.455), calls=%async_computation.4 | async-start | bytes 65536 | tf_op jit(solution)/shard_map/all_to_all | solution.py:307
  41.2 35.7 %all-to-all-start.5 = ((bf16[16,32,768]{2,1,0:T(8,128)(2,1)}), bf16[16,32,768]{2,1,0:T(8,128)(2,1)}, u32[]{:S(2)}, u32[]{:S(2)}) async-start(bf16[16,32,768]{2,1,0:T(8,128)(2,1)} %broadcast_select_fusion.1), calls=%async_computation.5 | async-start | bytes 1572864 | tf_op jit(solution)/shard_map/all_to_all | solution.py:307
  45.5 127.7 %all-gather.7.cloned.1.call-start = ((), (), s32[]{:S(2)}) async-start(), calls=%async_computation.19 | async-start | bytes 3538944 | tf_op jit(solution)/shard_map/all_gather | solution.py:471
  142.1 175.2 %all-gather.9.cloned.1.call-start = ((), (), s32[]{:S(2)}) async-start(), calls=%async_computation.20 | async-start | bytes 6488064 | tf_op jit(solution)/shard_map/all_gather | solution.py:483
  186.2 17.9 %all-to-all-start.6 = ((bf16[4,64,768]{2,1,0:T(8,128)(2,1)}), bf16[4,64,768]{2,1,0:T(8,128)(2,1)S(1)}, u32[]{:S(2)}, u32[]{:S(2)}) async-start(bf16[4,64,768]{2,1,0:T(8,128)(2,1)} %broadcast_in_dim.412), calls=%async_computation.6 | async-start | bytes 786432 | tf_op jit(solution)/shard_map/all_to_all | solution.py:307
  205.1 15.2 %all-to-all-start.7 = ((bf16[2,256,768]{2,1,0:T(8,128)(2,1)}), bf16[2,256,768]{2,1,0:T(8,128)(2,1)}, u32[]{:S(2)}, u32[]{:S(2)}) async-start(bf16[2,256,768]{2,1,0:T(8,128)(2,1)} %broadcast_in_dim.414), calls=%async_computation.7 | async-start | bytes 1572864 | tf_op jit(solution)/shard_map/all_to_all | solution.py:307
  234.4 14.9 %all-to-all-start.9 = ((f32[16,2,1024]{2,1,0:T(2,128)}), f32[16,2,1024]{2,1,0:T(2,128)S(1)}, u32[]{:S(2)}, u32[]{:S(2)}) async-start(f32[16,2,1024]{2,1,0:T(2,128)} %broadcast_in_dim.417), calls=%async_computation.9 | async-start | bytes 262144 | tf_op jit(solution)/shard_map/all_to_all | solution.py:307
  258.2 3.8 collective-permute-start.1
  267.8 25.1 %collective-permute-start.2 = (f32[256,768]{1,0:T(8,128)}, f32[256,768]{1,0:T(8,128)S(1)}, u32[]{:S(2)}, u32[]{:S(2)}) collective-permute-start(f32[256,768]{1,0:T(8,128)} %constant_dynamic-slice_fusion.1), channel_id=1, source_target_pairs={{0,2},{2,0},{1,3},{3,1},{4,6},{6,4},{5,7},{7,5},{8,10},{10,8},{9,1... | collective-permute-start | bytes 2359304 | tf_op jit(solution)/shard_map/ppermute | solution.py:507
  269.3 24.5 %all-to-all-start.10 = ((bf16[32,64,96]{2,1,0:T(8,128)(2,1)}), bf16[32,64,96]{2,1,0:T(8,128)(2,1)}, u32[]{:S(2)}, u32[]{:S(2)}) async-start(bf16[32,64,96]{2,1,0:T(8,128)(2,1)} %bitcast.161), calls=%async_computation.10 | async-start | bytes 1048576 | tf_op jit(solution)/shard_map/all_to_all | solution.py:307
  293.8 23.4 %all-to-all-start.11 = ((f32[4,64,768]{2,1,0:T(8,128)}), f32[4,64,768]{2,1,0:T(8,128)S(1)}, u32[]{:S(2)}, u32[]{:S(2)}) async-start(f32[4,64,768]{2,1,0:T(8,128)} %bitcast.39), calls=%async_computation.11 | async-start | bytes 1572864 | tf_op jit(solution)/shard_map/all_to_all | solution.py:307
  297.5 169.6 %all-gather.11.cloned.1.call-start = ((), (), s32[]{:S(2)}) async-start(), calls=%async_computation.21 | async-start | bytes 3244032 | tf_op jit(solution)/shard_map/all_gather | solution.py:547
  300.7 145.2 %collective-permute-start.3 = (bf16[1920,768]{1,0:T(8,128)(2,1)}, bf16[1920,768]{1,0:T(8,128)(2,1)}, u32[]{:S(2)}, u32[]{:S(2)}) collective-permute-start(bf16[1920,768]{1,0:T(8,128)(2,1)} %convolution_convert_fusion.1), channel_id=1, source_target_pairs={{0,16},{16,0},{1,17},{17,1},{2,18},{18,2},{3,19},{19,3},{4,20},{20... | collective-permute-start | bytes 8847368 | tf_op jit(solution)/shard_map/ppermute | solution.py:524
  351.1 30.0 %all-to-all-start.12 = ((bf16[32,64,120]{2,1,0:T(8,128)(2,1)}), bf16[32,64,120]{2,1,0:T(8,128)(2,1)}, u32[]{:S(2)}, u32[]{:S(2)}) async-start(bf16[32,64,120]{2,1,0:T(8,128)(2,1)} %maximum_bitcast_fusion.1), calls=%async_computation.12 | async-start | bytes 1048576 | tf_op jit(solution)/shard_map/all_to_all | solution.py:307
  361.3 48.0 %copy-start.16 = (bf16[256,768]{1,0:T(8,128)(2,1)S(1)}, bf16[256,768]{1,0:T(8,128)(2,1)}, u32[]{:S(2)}) copy-start(bf16[256,768]{1,0:T(8,128)(2,1)} %get-tuple-element.233) | copy-start | bytes 1179652
  381.0 19.4 %all-to-all-start.13 = ((bf16[8,288,192]{1,2,0:T(8,128)(2,1)}), bf16[8,288,192]{1,2,0:T(8,128)(2,1)S(1)}, u32[]{:S(2)}, u32[]{:S(2)}) async-start(bf16[8,288,192]{1,2,0:T(8,128)(2,1)} %pad_maximum_fusion), calls=%async_computation.13 | async-start | bytes 2359296 | tf_op jit(solution)/shard_map/all_to_all | solution.py:307
  400.4 39.0 %all-to-all-start.14 = ((bf16[16,32,768]{2,1,0:T(8,128)(2,1)}), bf16[16,32,768]{2,1,0:T(8,128)(2,1)}, u32[]{:S(2)}, u32[]{:S(2)}) async-start(bf16[16,32,768]{2,1,0:T(8,128)(2,1)} %select_convert_fusion), calls=%async_computation.14 | async-start | bytes 1572864 | tf_op jit(solution)/shard_map/all_to_all | solution.py:307
  439.4 20.3 %collective-permute-start.4 = (bf16[512,768]{1,0:T(8,128)(2,1)}, bf16[512,768]{1,0:T(8,128)(2,1)}, u32[]{:S(2)}, u32[]{:S(2)}) collective-permute-start(bf16[512,768]{1,0:T(8,128)(2,1)} %bitcast.48), channel_id=1, source_target_pairs={{0,16},{16,0},{1,17},{17,1},{2,18},{18,2},{3,19},{19,3},{4,20},{20... | collective-permute-start | bytes 2359304 | tf_op jit(solution)/shard_map/ppermute | solution.py:593
  477.1 39.0 %all-to-all-start.15 = ((bf16[32,24,774]{2,1,0:T(8,128)(2,1)}), bf16[32,24,774]{2,1,0:T(8,128)(2,1)S(1)}, u32[]{:S(2)}, u32[]{:S(2)}) async-start(bf16[32,24,774]{2,1,0:T(8,128)(2,1)} %concatenate.89), calls=%async_computation.15 | async-start | bytes 2752512 | tf_op jit(solution)/shard_map/all_to_all | solution.py:307
  525.0 9.6 %all-to-all-start.16 = ((f32[32,1,2]{2,1,0:T(1,128)}), f32[32,1,2]{2,1,0:T(1,128)S(1)}, u32[]{:S(2)}, u32[]{:S(2)}) async-start(f32[32,1,2]{2,1,0:T(1,128)} %copy.503), calls=%async_computation.16 | async-start | bytes 32768 | tf_op jit(solution)/shard_map/all_to_all | solution.py:307
  554.3 20.1 %all-to-all-start.17 = ((f32[32,6,2]{1,2,0:T(2,128)}), f32[32,6,2]{1,2,0:T(2,128)S(1)}, u32[]{:S(2)}, u32[]{:S(2)}) async-start(f32[32,6,2]{1,2,0:T(2,128)} %broadcast_in_dim.437), calls=%async_computation.17 | async-start | bytes 65536 | tf_op jit(solution)/shard_map/all_to_all | solution.py:307
  (89 other events, 1009.2 us)
Sparse Core Ops, SparseCore 0:
  11.7 123.9 all-gather.4
  142.2 30.9 all-gather.6
  176.1 77.6 all-gather.8
  320.1 66.4 all-gather.10

commit v4 on v3

--- a/solution.py
+++ b/solution.py
@@ -1,5 +1,3 @@
-from functools import partial
-
 import jax
 import jax.numpy as jnp
 from jax import lax
@@ -83,26 +81,50 @@
     return powers / jnp.sum(powers, axis=-1, keepdims=True)
 
 
+def spread(column, lanes=128):
+    return jnp.broadcast_to(column, (column.shape[0], lanes))
+
+
+def row_of(ref, row):
+    return ref[pl.ds(row, 1), :]
+
+
 def attend_kernel(
-    stream_ref, init_ref, small_ref, allowed_ref, weight_ref,
+    embed_ref, slot_ref, allowed_ref, shared_ref, weight_ref,
     key_ref, value_ref, query_ref, mixed_ref, middle_ref, normed_ref, inverse_ref,
+    stream_ref, stream_normed_ref, stream_inverse_ref,
+    init_ref, init_normed_ref, init_inverse_ref, position_ref, small_ref,
 ):
     step = pl.program_id(0)
+    length = position_ref.shape[0]
 
     @pl.when(step == 0)
     def _():
+        shared = shared_ref[...].astype(single).T
+        position_ref[...] = shared[:length]
+        small_ref[...] = shared[length : length + small_ref.shape[0]]
+        gain, bias = row_of(small_ref, 0), row_of(small_ref, 1)
+        stream, (normed, inverse) = norm_forward(embed_ref[...] + position_ref[...], gain, bias)
+        stream_ref[...] = stream.astype(bfloat)
+        stream_normed_ref[...] = normed
+        stream_inverse_ref[...] = spread(inverse)
+        chosen = plain_dot(slot_ref[...].astype(bfloat), position_ref[...].astype(bfloat))
+        init, (normed, inverse) = norm_forward(chosen, gain, bias)
+        init_ref[...] = init
+        init_normed_ref[...] = normed
+        init_inverse_ref[...] = spread(inverse)
         key_ref[...] = plain_dot(stream_ref[...], weight_ref[...]).astype(bfloat)
 
     @pl.when(step == 1)
     def _():
         value_ref[...] = (
-            plain_dot(stream_ref[...], weight_ref[...]) + small_ref[pl.ds(3, 1), :]
+            plain_dot(stream_ref[...], weight_ref[...]) + row_of(small_ref, 3)
         ).astype(bfloat)
 
     @pl.when(step == 2)
     def _():
         query_ref[...] = (
-            plain_dot(init_ref[...].astype(bfloat), weight_ref[...]) + small_ref[pl.ds(2, 1), :]
+            plain_dot(init_ref[...].astype(bfloat), weight_ref[...]) + row_of(small_ref, 2)
         ).astype(bfloat)
         blocked = allowed_ref[...] == 0.0
         low, high = pair_masks(query_ref.shape[0])
@@ -123,45 +145,195 @@
 
     @pl.when(step == 3)
     def _():
-        attend = plain_dot(mixed_ref[...], weight_ref[...]) + small_ref[pl.ds(4, 1), :]
+        attend = plain_dot(mixed_ref[...], weight_ref[...]) + row_of(small_ref, 4)
         middle, (normed, inverse) = norm_forward(
-            init_ref[...] + attend, small_ref[pl.ds(5, 1), :], small_ref[pl.ds(6, 1), :]
+            init_ref[...] + attend, row_of(small_ref, 5), row_of(small_ref, 6)
         )
         middle_ref[...] = middle
         normed_ref[...] = normed
-        inverse_ref[...] = jnp.broadcast_to(inverse, inverse_ref.shape)
-
-
-def attend_forward(stream_b, query_init, small_full, allowed, weights):
-    length, width = stream_b.shape
-    slots = query_init.shape[0]
-    out = lambda rows, kind, columns=width: jax.ShapeDtypeStruct((rows, columns), kind)
-    whole = lambda shape: pl.BlockSpec(shape, lambda step: (0, 0))
-    shapes = (
-        out(length, bfloat), out(length, bfloat), out(slots, bfloat), out(slots, bfloat),
-        out(slots, single), out(slots, single), out(slots, single, 128),
-    )
+        inverse_ref[...] = spread(inverse)
+
+
+def kernel_call(body, name, steps, inputs, shapes, cost, scratch=()):
+    fixed = lambda rank: lambda step: (0,) * rank
+
+    def spec(shape, block, index):
+        if block is None:
+            return pl.BlockSpec(shape, fixed(len(shape)))
+        return pl.BlockSpec(block, index)
+
     return pl.pallas_call(
+        body,
+        grid=(steps,),
+        in_specs=[spec(array.shape, block, index) for array, block, index in inputs],
+        out_specs=[spec(shape, block, index) for shape, _, block, index in shapes],
+        out_shape=[jax.ShapeDtypeStruct(shape, kind) for shape, kind, _, _ in shapes],
+        scratch_shapes=list(scratch),
+        cost_estimate=pl.CostEstimate(flops=cost[0], bytes_accessed=cost[1], transcendentals=cost[2]),
+        name=name,
+    )(*(array for array, _, _ in inputs))
+
+
+def whole(array):
+    return array, None, None
+
+
+def attend_forward(embed_rows, slot_hot, allowed, weights, length, small_count):
+    width = embed_rows.shape[1]
+    slots = slot_hot.shape[0]
+    out = lambda rows, kind, columns=width: ((rows, columns), kind, None, None)
+    shared = weights.shape[1] - 12 * width
+    return kernel_call(
         attend_kernel,
-        grid=(4,),
-        in_specs=[
-            whole(stream_b.shape),
-            whole(query_init.shape),
-            whole(small_full.shape),
-            whole(allowed.shape),
-            pl.BlockSpec(
-                (width, width), lambda step: (0, jnp.where(step == 3, 3, (step + 1) % 3))
+        "attention_forward",
+        4,
+        [
+            whole(embed_rows),
+            whole(slot_hot),
+            whole(allowed),
+            (weights, (width, shared), lambda step: (0, 12 * width // shared)),
+            (
+                weights,
+                (width, width),
+                lambda step: (0, jnp.where(step == 3, 3, (step + 1) % 3)),
             ),
         ],
-        out_specs=[whole(shape.shape) for shape in shapes],
-        out_shape=shapes,
-        cost_estimate=pl.CostEstimate(
-            flops=4 * length * width * width + 8 * slots * length * width,
-            bytes_accessed=8 * width * width,
-            transcendentals=HEADS * slots * length,
+        [
+            out(length, bfloat), out(length, bfloat), out(slots, bfloat), out(slots, bfloat),
+            out(slots, single), out(slots, single), out(slots, single, 128),
+            out(length, bfloat), out(length, single), out(length, single, 128),
+            out(slots, single), out(slots, single), out(slots, single, 128),
+            out(length, single), out(small_count, single),
+        ],
+        (
+            4 * length * width * width + 8 * slots * length * width,
+            8 * width * width,
+            HEADS * slots * length,
         ),
-        name="attention_forward",
-    )(stream_b, query_init, small_full, allowed, weights)
+    )
+
+
+def erf_half(hidden):
+    return 0.5 * (1.0 + lax.erf(hidden * 0.5**0.5))
+
+
+def feed_kernel(
+    middle_ref, small_ref, up_ref, down_ref,
+    middle_b_ref, hidden_ref, active_ref, output_ref, normed_ref, inverse_ref, total_ref,
+):
+    step = pl.program_id(0)
+
+    @pl.when(step == 0)
+    def _():
+        middle_b_ref[...] = middle_ref[...].astype(bfloat)
+        total_ref[...] = middle_ref[...] + row_of(small_ref, 11)
+
+    hidden = plain_dot(middle_b_ref[...], up_ref[...]) + row_of(small_ref, 7 + step)
+    hidden_ref[...] = hidden
+    active = (hidden * erf_half(hidden)).astype(bfloat)
+    active_ref[...] = active
+    total_ref[...] += trans_dot(active, down_ref[...])
+
+    @pl.when(step == pl.num_programs(0) - 1)
+    def _():
+        output, (normed, inverse) = norm_forward(
+            total_ref[...], row_of(small_ref, 12), row_of(small_ref, 13)
+        )
+        output_ref[...] = output.astype(bfloat)
+        normed_ref[...] = normed
+        inverse_ref[...] = spread(inverse)
+
+
+def feed_forward(middle, small_full, weights):
+    slots, width = middle.shape
+    wide = lambda kind: ((slots, 4 * width), kind, (slots, width), lambda step: (0, step))
+    out = lambda kind, columns=width: ((slots, columns), kind, None, None)
+    return kernel_call(
+        feed_kernel,
+        "feed_forward",
+        4,
+        [
+            whole(middle),
+            whole(small_full),
+            (weights, (width, width), lambda step: (0, 4 + step)),
+            (weights, (width, width), lambda step: (0, 8 + step)),
+        ],
+        [
+            out(bfloat), wide(single), wide(bfloat), out(bfloat), out(single), out(single, 128),
+        ],
+        (16 * slots * width * width, 16 * width * width, 4 * slots * width),
+        [pltpu.VMEM((slots, width), single)],
+    )
+
+
+def norm_back(upstream, normed, inverse, gain_row):
+    return norm_backward(upstream, (normed, inverse), gain_row)
+
+
+def feed_back_kernel(
+    parts_ref, normed_ref, inverse_ref, hidden_ref, small_ref, mid_normed_ref, mid_inverse_ref,
+    up_ref, down_ref,
+    d_branch_ref, d_hidden_ref, d_pre_ref, d_attend_ref, sums_ref, d_middle_ref,
+):
+    step = pl.program_id(0)
+
+    @pl.when(step == 0)
+    def _():
+        sums_ref[...] = jnp.zeros_like(sums_ref)
+        d_sum, gain, bias = norm_back(
+            jnp.sum(parts_ref[...], axis=0), normed_ref[...], inverse_ref[:, :1], row_of(small_ref, 12)
+        )
+        d_branch = d_sum.astype(bfloat)
+        d_branch_ref[...] = d_branch
+        d_middle_ref[...] = d_sum
+        sums_ref[pl.ds(6, 1), :] = column_sum(d_branch)[None]
+        sums_ref[pl.ds(7, 1), :] = gain[None]
+        sums_ref[pl.ds(8, 1), :] = bias[None]
+
+    hidden = hidden_ref[...]
+    slope = erf_half(hidden) + hidden * jnp.exp(-0.5 * hidden * hidden) * (2.0 * jnp.pi) ** (-0.5)
+    d_hidden = (plain_dot(d_branch_ref[...], down_ref[...]) * slope).astype(bfloat)
+    d_hidden_ref[...] = d_hidden
+    sums_ref[pl.ds(2 + step, 1), :] = column_sum(d_hidden)[None]
+    d_middle_ref[...] += trans_dot(d_hidden, up_ref[...])
+
+    @pl.when(step == pl.num_programs(0) - 1)
+    def _():
+        d_pre, gain, bias = norm_back(
+            d_middle_ref[...], mid_normed_ref[...], mid_inverse_ref[:, :1], row_of(small_ref, 5)
+        )
+        d_pre_ref[...] = d_pre
+        d_attend_ref[...] = d_pre.astype(bfloat)
+        sums_ref[pl.ds(0, 1), :] = gain[None]
+        sums_ref[pl.ds(1, 1), :] = bias[None]
+
+
+def feed_backward(parts, normed, inverse, hidden, small_full, mid_normed, mid_inverse, weights):
+    slots, width = normed.shape
+    block = (slots, width), lambda step: (0, step)
+    out = lambda kind, rows=slots: ((rows, width), kind, None, None)
+    return kernel_call(
+        feed_back_kernel,
+        "feed_backward",
+        4,
+        [
+            whole(parts),
+            whole(normed),
+            whole(inverse),
+            (hidden,) + block,
+            whole(small_full),
+            whole(mid_normed),
+            whole(mid_inverse),
+            (weights, (width, width), lambda step: (0, 4 + step)),
+            (weights, (width, width), lambda step: (0, 8 + step)),
+        ],
+        [
+            out(bfloat), ((slots, 4 * width), bfloat) + block, out(single), out(bfloat),
+            out(single, 16),
+        ],
+        (16 * slots * width * width, 16 * width * width, 8 * slots * width),
+        [pltpu.VMEM((slots, width), single)],
+    )
 
 
 def attend_back_kernel(
@@ -205,76 +377,97 @@
 def attend_backward(d_attend, key_rows, value_rows, query_rows, allowed, weights):
     length, width = key_rows.shape
     slots = d_attend.shape[0]
-    whole = lambda shape: pl.BlockSpec(shape, lambda step: (0, 0))
-    shapes = tuple(
-        jax.ShapeDtypeStruct((rows, width), bfloat) for rows in (slots, length, length)
-    )
-    return pl.pallas_call(
+    out = lambda rows: ((rows, width), bfloat, None, None)
+    return kernel_call(
         attend_back_kernel,
-        grid=(1,),
-        in_specs=[
-            whole(d_attend.shape),
-            whole(key_rows.shape),
-            whole(value_rows.shape),
-            whole(query_rows.shape),
-            whole(allowed.shape),
-            pl.BlockSpec((width, width), lambda step: (0, 3)),
+        "attention_backward",
+        1,
+        [
+            whole(d_attend),
+            whole(key_rows),
+            whole(value_rows),
+            whole(query_rows),
+            whole(allowed),
+            (weights, (width, width), lambda step: (0, 3)),
         ],
-        out_specs=[whole(shape.shape) for shape in shapes],
-        out_shape=shapes,
-        scratch_shapes=[pltpu.VMEM((slots, width), bfloat)],
-        cost_estimate=pl.CostEstimate(
-            flops=2 * slots * width * width + 20 * slots * length * width,
-            bytes_accessed=2 * width * width,
-            transcendentals=HEADS * slots * length,
+        [out(slots), out(length), out(length)],
+        (
+            2 * slots * width * width + 20 * slots * length * width,
+            2 * width * width,
+            HEADS * slots * length,
         ),
-        name="attention_backward",
-    )(d_attend, key_rows, value_rows, query_rows, allowed, weights)
-
-
-def feed_forward(layer_b, small_full, middle):
-    middle_b = middle.astype(bfloat)
-    hidden = plain_dot(middle_b, layer_b[1]) + small_full[7:11].reshape(-1)
-    active_b = jax.nn.gelu(hidden, approximate=False).astype(bfloat)
-    branch = trans_dot(active_b, layer_b[2]) + small_full[11]
-    output_rows, final_kept = norm_forward(middle + branch, small_full[12], small_full[13])
-    return output_rows, (middle_b, hidden, active_b, final_kept)
-
-
-def feed_backward(layer_b, small_full, hidden, final_kept, middle_kept, d_output):
-    d_sum, gain_three, bias_three = norm_backward(d_output, final_kept, small_full[12])
-    d_branch = d_sum.astype(bfloat)
-    _, gelu_pull = jax.vjp(partial(jax.nn.gelu, approximate=False), hidden)
-    d_hidden = gelu_pull(plain_dot(d_branch, layer_b[2]))[0].astype(bfloat)
-    d_middle = d_sum + trans_dot(d_hidden, layer_b[1])
-    d_pre, gain_two, bias_two = norm_backward(d_middle, middle_kept, small_full[5])
-    grad_mid = jnp.concatenate(
+        [pltpu.VMEM((slots, width), bfloat)],
+    )
+
+
+def project_back_kernel(
+    d_pre_ref, d_query_ref, d_key_ref, d_value_ref, slot_ref, hidden_row_ref, small_ref,
+    normed_ref, inverse_ref, init_normed_ref, init_inverse_ref, weight_ref,
+    embed_ref, position_ref, sums_ref, d_stream_ref, d_init_ref,
+):
+    step = pl.program_id(0)
+
+    @pl.when(step == 0)
+    def _():
+        d_init_ref[...] = d_pre_ref[...] + trans_dot(d_query_ref[...], weight_ref[...])
+
+    @pl.when(step == 1)
+    def _():
+        d_stream_ref[...] = trans_dot(d_key_ref[...], weight_ref[...])
+
+    @pl.when(step == 2)
+    def _():
+        gain_row = row_of(small_ref, 0)
+        d_stream = d_stream_ref[...] + trans_dot(d_value_ref[...], weight_ref[...])
+        d_start, gain_init, bias_init = norm_back(
+            d_init_ref[...], init_normed_ref[...], init_inverse_ref[:, :1], gain_row
+        )
+        d_embed, gain, bias = norm_back(
+            d_stream, normed_ref[...], inverse_ref[:, :1], gain_row
+        )
+        position_ref[...] = d_embed + lax.dot_general(
+            slot_ref[...],
+            d_start,
+            (((0,), (0,)), ((), ())),
+            precision=lax.Precision.HIGHEST,
+            preferred_element_type=single,
+        )
+        embed_b = d_embed.astype(bfloat)
+        embed_ref[...] = embed_b
+        sums_ref[...] = jnp.zeros_like(sums_ref)
+        sums_ref[pl.ds(0, 1), :] = (gain_init + gain)[None]
+        sums_ref[pl.ds(1, 1), :] = (bias_init + bias)[None]
+        sums_ref[pl.ds(2, 1), :] = column_sum(d_query_ref[...])[None]
+        sums_ref[pl.ds(3, 1), :] = column_sum(d_value_ref[...])[None]
+        sums_ref[pl.ds(4, 1), :] = column_sum(d_pre_ref[...].astype(bfloat))[None]
+        masked = jnp.where(hidden_row_ref[:, :1] > 0.0, embed_b.astype(single), 0.0)
+        sums_ref[pl.ds(5, 1), :] = jnp.sum(masked, axis=0)[None]
+
+
+def project_backward(
+    d_pre, d_query, d_key, d_value, slot_hot, hidden_rows, small_full,
+    normed, inverse, init_normed, init_inverse, weights,
+):
+    length, width = normed.shape
+    slots = d_pre.shape[0]
+    arrays = (
+        d_pre, d_query, d_key, d_value, slot_hot, hidden_rows, small_full,
+        normed, inverse, init_normed, init_inverse,
+    )
+    return kernel_call(
+        project_back_kernel,
+        "projection_backward",
+        3,
+        [whole(array) for array in arrays]
+        + [(weights, (width, width), lambda step: (0, step))],
         [
-            gain_two[None],
-            bias_two[None],
-            column_sum(d_hidden).reshape(4, -1),
-            column_sum(d_branch)[None],
-            gain_three[None],
-            bias_three[None],
-        ]
-    )
-    return d_branch, d_hidden, d_pre, grad_mid
-
-
-def project_backward(layer_b, d_pre, d_query, d_key, d_value):
-    width = d_pre.shape[1]
-    d_init = d_pre + trans_dot(d_query, layer_b[0][:, :width])
-    d_stream = trans_dot(d_key, layer_b[0][:, width : 2 * width]) + trans_dot(
-        d_value, layer_b[0][:, 2 * width : 3 * width]
-    )
-    grad_mid = jnp.concatenate(
-        [
-            column_sum(d_query)[None],
-            column_sum(d_value)[None],
-            column_sum(d_pre.astype(bfloat))[None],
-        ]
-    )
-    return d_init, d_stream, grad_mid
+            ((length, width), bfloat, None, None),
+            ((length, width), single, None, None),
+            ((8, width), single, None, None),
+        ],
+        (5 * length * width * width, 6 * width * width, 0),
+        [pltpu.VMEM((length, width), single), pltpu.VMEM((slots, width), single)],
+    )
 
 
 def adam_moments(weight_arr, first_mom, second_mom, gradient, factor):
@@ -396,8 +589,6 @@
     shared = jnp.pad(shared, ((0, 0), (0, -shared_rows % 128)))
     shard = jnp.concatenate([layer_weights[0], layer_weights[1], layer_weights[2], shared], axis=1)
     shard = lax.all_gather(shard.astype(bfloat), ALL, axis=0, tiled=True)
-    layer_b = tuple(shard[:, part * feed : (part + 1) * feed] for part in range(3))
-    shared = shard[:, 3 * feed : 3 * feed + shared_rows].T
     table_b = embed_table.astype(bfloat)
     token_row = token_ids[0]
     pred_row = pred_mask[0]
@@ -456,31 +647,34 @@
     _, embed_rows = lax.while_loop(
         lambda state: state[0] < rounds, more_rows, (jnp.ones((), rounds.dtype), embed_rows)
     )
-    position_b = shared[:length]
-    position_full = position_b.astype(single)
-    small_full = shared[length:].astype(single)
-    stream, stream_kept = norm_forward(embed_rows + position_full, small_full[0], small_full[1])
-    stream_b = stream.astype(bfloat)
-    slot_b = slot_hot.astype(bfloat)
-    query_init, init_kept = norm_forward(
-        plain_dot(slot_b, position_b), small_full[0], small_full[1]
-    )
     few = devices <= 32
     near = dp_devs * 4
-    if few:
-        stream_all = lax.all_gather(stream_b, NEAR, axis=0, tiled=True)
     allowed = allowed.astype(single)
-    key_rows, value_rows, query_rows, mixed_b, middle, normed, inverse = attend_forward(
-        stream_b, query_init, small_full, allowed, shard
-    )
-    output_rows, (middle_b, hidden, active_b, final_kept) = feed_forward(
-        layer_b, small_full, middle
-    )
-    output_b = output_rows.astype(bfloat)
+    slot_hot = slot_hot.astype(single)
+    (
+        key_rows,
+        value_rows,
+        query_rows,
+        mixed_b,
+        middle,
+        mid_normed,
+        mid_inverse,
+        stream_b,
+        stream_normed,
+        stream_inverse,
+        query_init,
+        init_normed,
+        init_inverse,
+        position_full,
+        small_full,
+    ) = attend_forward(embed_rows, slot_hot, allowed, shard, length, small_params.shape[0])
+    middle_b, hidden, active_b, output_b, end_normed, end_inverse = feed_forward(
+        middle, small_full, shard
+    )
     if few:
         kept_rows = jnp.concatenate([mixed_b, middle_b], axis=1)
-        kept_rows, stream_all = lax.optimization_barrier((kept_rows, stream_all))
         kept_all = lax.all_gather(kept_rows, ALL, axis=0, tiled=True)
+        stream_all = lax.all_gather(stream_b, NEAR, axis=0, tiled=True)
     group_rows = exchange.copies(output_b, "hi", outer).reshape(-1, width)
     group_rows = exchange.copies(group_rows, "mid", 2).reshape(-1, width)
     group_rows = exchange.copies(group_rows, "core", 2).reshape(-1, width)
@@ -529,11 +723,9 @@
     d_output = exchange(d_output.reshape(outer, CAP, width), "hi")
     if few:
         d_output, kept_all = lax.optimization_barrier((d_output, kept_all))
-    d_output = jnp.sum(d_output, axis=0)
-    d_branch, d_hidden, d_pre, mid_feed = feed_backward(
-        layer_b, small_full, hidden, final_kept, (normed, inverse[:, :1]), d_output
-    )
-    d_attend = d_pre.astype(bfloat)
+    d_branch, d_hidden, d_pre, d_attend, sums_feed = feed_backward(
+        d_output, end_normed, end_inverse, hidden, small_full, mid_normed, mid_inverse, shard
+    )
     if few:
         wide = feed // devices
         both = jnp.concatenate(
@@ -548,8 +740,6 @@
     d_query, d_key, d_value = attend_backward(
         d_attend, key_rows, value_rows, query_rows, allowed, shard
     )
-    d_init, d_stream, mid_attn = project_backward(layer_b, d_pre, d_query, d_key, d_value)
-    grad_mid = jnp.concatenate([mid_attn, mid_feed])
     if few:
         piece = width // near
         pairs = jnp.concatenate(
@@ -558,22 +748,23 @@
         asks = d_query.reshape(CAP, near, piece).transpose(1, 0, 2)
         asks = jnp.concatenate([asks[:, : CAP // 2], asks[:, CAP // 2 :]], axis=2)
         pairs = exchange(jnp.concatenate([pairs, asks], axis=1), NEAR)
-    d_start, gain_init, bias_init = norm_backward(d_init, init_kept, small_full[0])
-    d_embed, gain_stream, bias_stream = norm_backward(d_stream, stream_kept, small_full[0])
-    grad_position = d_embed + lax.dot_general(
-        slot_hot.astype(single),
-        d_start,
-        (((0,), (0,)), ((), ())),
-        precision=lax.Precision.HIGHEST,
-        preferred_element_type=single,
-    )
-    grad_small = jnp.concatenate(
-        [(gain_init + gain_stream)[None], (bias_init + bias_stream)[None], grad_mid]
-    )
-    embed_back = d_embed.astype(bfloat)
-    mask_sum = jnp.sum(
-        jnp.where((content == MASK_ID)[:, None], embed_back.astype(single), 0.0), axis=0
-    )
+    hidden_rows = spread((content == MASK_ID).astype(single)[:, None])
+    embed_back, grad_position, sums_back = project_backward(
+        d_pre,
+        d_query,
+        d_key,
+        d_value,
+        slot_hot,
+        hidden_rows,
+        small_full,
+        stream_normed,
+        stream_inverse,
+        init_normed,
+        init_inverse,
+        shard,
+    )
+    grad_small = jnp.concatenate([sums_back[:5], sums_feed[:9]])
+    mask_sum = sums_back[5]
     mask_left = mask_sum - lax.reduce_precision(mask_sum, 8, 7)
     mask_owner = MASK_ID // vrows
     is_left = (jnp.arange(BUCKET) == BUCKET - 1)[None, :] & (
@@ -590,8 +781,8 @@
 
     def of_both(rows):
         if dp_devs == 2:
-            return rows, lax.ppermute(rows, "dp", [(0, 1), (1, 0)])
-        return (lax.all_gather(rows, "dp", axis=0, tiled=True),)
+            return jnp.concatenate([rows, lax.ppermute(rows, "dp", [(0, 1), (1, 0)])])
+        return lax.all_gather(rows, "dp", axis=0, tiled=True)
 
     def both_groups(asked_rows):
         if dp_devs == 2:
@@ -601,7 +792,7 @@
     def into_rows(asked_rows, given):
         flat = both_groups(asked_rows).reshape(-1)
         row_hot = flat[None, :] == jnp.arange(vrows)[:, None]
-        return plain_dot(row_hot.astype(bfloat), jnp.concatenate(given))
+        return plain_dot(row_hot.astype(bfloat), given)
 
     last = (jnp.arange(BUCKET) == BUCKET - 1)[None, :]
     left_row = jnp.where(lax.axis_index(VOC) == mask_owner, MASK_ID - first_row, -1)
@@ -626,7 +817,8 @@
             [grad_pair, grad_ask, grad_up, grad_down, grad_out, shared_grad], axis=1
         )
         results = results.astype(bfloat)
-        given, _ = lax.optimization_barrier((given, results))
+        beyond = (jnp.max(results[0].astype(single)) > 3.395e38).astype(bfloat)
+        given = given + beyond
         results = exchange.rows(results, devices).astype(single)
         pieces = 3 * piece
         attn = jnp.sum(
@@ -681,14 +873,8 @@
     _, table_grad = lax.while_loop(
         lambda state: state[0] < rounds, more_grads, (jnp.ones((), rounds.dtype), table_grad)
     )
-    split = vrows // dp_devs
-
-    def own_part(values):
-        return lax.dynamic_slice_in_dim(values, lax.axis_index("dp") * split, split, 0)
-
-    grad_part = own_part(table_grad)
     square_part = (
-        jnp.sum(grad_part * grad_part)
+        jnp.sum(table_grad * table_grad) / dp_devs
         + jnp.sum(layer_grad * layer_grad)
         + jnp.sum(position_grad * position_grad)
         + jnp.sum(small_grad * small_grad)
@@ -696,9 +882,8 @@
     total_square, loss_value = exchange.total(jnp.stack([square_part, loss_part]), ALL, devices)
     grad_norm = jnp.sqrt(total_square)
     factor = jnp.minimum(1.0, clip_norm / grad_norm)
-    weight_part = own_part(embed_table)
-    _, _, part_dir = adam_moments(
-        weight_part, own_part(table_moment), own_part(table_square), grad_part, factor
+    table_first, table_second, table_dir = adam_moments(
+        embed_table, table_moment, table_square, table_grad, factor
     )
     layer_first, layer_second, layer_dir = adam_moments(
         layer_weights, layer_moment, layer_square, layer_grad, factor
@@ -711,17 +896,12 @@
     )
     partial_norms = jnp.concatenate(
         [
-            norm_pair(weight_part, part_dir, (0, 1))[None],
+            norm_pair(embed_table, table_dir, (0, 1))[None] / dp_devs,
             norm_pair(layer_weights, layer_dir, (1, 2)),
             norm_pair(position_table, position_dir, (0, 1))[None],
             norm_pair(small_params, small_dir, (0, 1))[None],
         ]
     )
-    factor_late, _ = lax.optimization_barrier((factor, partial_norms))
-    table_first, table_second, table_dir = adam_moments(
-        embed_table, table_moment, table_square, table_grad, factor_late
-    )
-    table_dir = lax.optimization_barrier(table_dir)
     trust_square = exchange.total(partial_norms, ALL, devices)
     trust_norms = jnp.sqrt(trust_square)
     ratio = trust_norms[:, 0] / trust_norms[:, 1]

time: 604 us -> 590 us (0.977)
  waiting for transfers between devices: 242 us -> 277 us
  matrix products: 74.3 us -> 42.4 us
  local copies, waits for them, and re-layouts: 67.3 us -> 36.5 us
  other arithmetic: 101 us -> 75.6 us
  blocking collectives: 5 us -> 30 us
  Pallas kernels: 19.5 us -> 41.5 us
  starting transfers between devices: 60.5 us -> 52.9 us
    all_to_all x13 -> x12, waiting for transfers between devices: 147 us -> 178 us  [__call__(): self.last = lax.all_to_all(values, axes, 0, 0, tiled=True)]
    all_to_all x1 -> x2, blocking collectives: 5 us -> 30 us  [__call__(): self.last = lax.all_to_all(values, axes, 0, 0, tiled=True)]
    pallas_call x2 -> x5, Pallas kernels: 19.5 us -> 41.5 us  [kernel_call(): pl.pallas_call(body, grid=(steps,), in_specs=[spec(array.shape, block, in...]
    dot_general x6 -> x1, matrix products: 20.2 us -> 3.53 us  [trans_dot(): lax.dot_general(left_op, right_op, (((1,), (1,)), ((), ())), preferred_el...]
    add x2 -> x1, other arithmetic: 16.6 us -> 0.05 us  [on_device(): given = given + beyond]
    dot_general x8 -> x4, matrix products: 29 us -> 14.6 us  [plain_dot(): return jnp.dot(left_op, right_op, preferred_element_type=single)]
    all_gather x1, waiting for transfers between devices: 12.2 us -> 0.02 us  [on_device(): stream_all = lax.all_gather(stream_b, NEAR, axis=0, tiled=True)]
    broadcast_in_dim x9 -> x1, local copies, waits for them, and re-layouts: 12.7 us -> 0.75 us  [spread(): return jnp.broadcast_to(column, (column.shape[0], lanes))]
  transfers between devices with their start and end apart: 21 -> 20, of which waited for: 15 -> 14; matrix products, arithmetic and copies ran while one was open for 31% -> 16% of each run, Pallas kernels for 3% -> 4%
where the time goes in v4:
time: 590 us; the launch traced here: 582 us
  waiting for transfers between devices  277 us (47%)
  other arithmetic  75.6 us (13%)
  starting transfers between devices  52.9 us (9%)
  matrix products  42.4 us (7%)
  Pallas kernels  41.5 us (7%)
  local copies, waits for them, and re-layouts  36.5 us (6%)
  blocking collectives  30 us (5%)
  between operations  26.2 us (4%)
    all_to_all x12, waiting for transfers between devices, __call__(): self.last = lax.all_to_all(values, axes, 0, 0, tiled=True)  178 us
    all_gather x1, waiting for transfers between devices, on_device(): shard = lax.all_gather(shard.astype(bfloat), ALL, axis=0, tiled=True)  57.5 us
    all_to_all x12, starting transfers between devices, __call__(): self.last = lax.all_to_all(values, axes, 0, 0, tiled=True)  49.3 us
    pallas_call x5, Pallas kernels, kernel_call(): pl.pallas_call(body, grid=(steps,), in_specs=[spec(array.shape, block, in...  41.5 us
    all_to_all x2, blocking collectives, __call__(): self.last = lax.all_to_all(values, axes, 0, 0, tiled=True)  30 us
    ppermute x2, waiting for transfers between devices, swapped(): theirs = lax.ppermute(part(1 - side), axis, [(0, 1), (1, 0)])  25.4 us
    dot_general x7, matrix products, rows_dot(): lax.dot_general(left_op, right_op, (((0,), (0,)), ((), ())), preferred_el...  24.3 us
    reduce_sum x4, other arithmetic, norm_pair(): jnp.sum(weight_arr * weight_arr, axis=axes)  19.8 us
  transfers between devices with their start and end apart: 20, of which 14 were waited for; matrix products, arithmetic and copies ran while one was open for 16% of the time, Pallas kernels for 4%

profile of v4, /device:TPU:0, one launch (start us, length us, event | category | flops | bytes accessed | tf_op | source)
XLA Modules:
  0.0 581.8 jit_solution(9700760306294554482)
XLA Ops:
  20.4 7.3 %all-to-all-start.4 = ((s32[32,1,256]{2,1,0:T(1,128)}), s32[32,1,256]{2,1,0:T(1,128)S(1)}, u32[]{:S(2)}, u32[]{:S(2)}) async-start(s32[32,1,256]{2,1,0:T(1,128)} %copy.264), calls=%async_computation.4 | async-start | bytes 65536 | tf_op jit(solution)/shard_map/all_to_all | solution.py:500
  27.7 7.3 %all-to-all-done.4 = s32[32,1,256]{2,1,0:T(1,128)S(1)} async-done(((s32[32,1,256]{2,1,0:T(1,128)}), s32[32,1,256]{2,1,0:T(1,128)S(1)}, u32[]{:S(2)}, u32[]{:S(2)}) %all-to-all-start.4) | async-done | bytes 32800 | tf_op jit(solution)/shard_map/all_to_all | solution.py:500
  47.7 28.0 %all-to-all-done.5 = bf16[16,32,768]{2,1,0:T(8,128)(2,1)} async-done(((bf16[16,32,768]{2,1,0:T(8,128)(2,1)}), bf16[16,32,768]{2,1,0:T(8,128)(2,1)}, u32[]{:S(2)}, u32[]{:S(2)}) %all-to-all-start.5) | async-done | bytes 786464 | tf_op jit(solution)/shard_map/all_to_all | solution.py:500
  78.1 57.5 %all-gather.5.cloned.1.call-done.shared_ref.weight_ref.up_ref.down_ref = bf16[768,9600]{1,0:T(8,128)(2,1)} async-done(((bf16[24,9600]{1,0:T(8,128)(2,1)}), bf16[768,9600]{1,0:T(8,128)(2,1)}) %all-gather.5.cloned.1.call-update) | async-done | bytes 14745616 | tf_op jit(solution)/shard_map/all_gather | solution.py:591
  135.6 11.5 %attention_forward.1 = (bf16[256,768]{1,0:T(8,128)(2,1)}, bf16[256,768]{1,0:T(8,128)(2,1)}, bf16[64,768]{1,0:T(8,128)(2,1)}, bf16[64,768]{1,0:T(8,128)(2,1)}, f3...) custom-call(f32[256,768]{1,0:T(8,128)} %get-tuple-element.232.embed_, ...), custom_call_target="tpu_custom_call" | custom-call | flops 704643072 | bytes 4718592 | tf_op jit(solution)/shard_map/attention_forward/pallas_call | solution.py:165
  147.1 7.1 %feed_forward.1 = (bf16[64,768]{1,0:T(8,128)(2,1)}, f32[64,3072]{1,0:T(8,128)}, bf16[64,3072]{1,0:T(8,128)(2,1)}, bf16[64,768]{1,0:T(8,128)(2,1)}, f32[64,768]{1,0:T(8,128)}, /*index=5*/f32[64,128]{1,0:T(8,128)}) custom-call(f32[64,768]{1,0:T(8,128)} %get-tuple-element.233.middle_ref, f32[14,768]{1,0:T(8,128)} %get-tuple-element.234.small_ref, ...), custom_call_target="tpu_custom_call" | custom-call | flops 603979776 | bytes 9437184 | tf_op jit(solution)/shard_map/feed_forward/pallas_call | solution.py:165
  161.0 16.0 %all-to-all-done.6 = bf16[4,64,768]{2,1,0:T(8,128)(2,1)S(1)} async-done(((bf16[4,64,768]{2,1,0:T(8,128)(2,1)}), bf16[4,64,768]{2,1,0:T(8,128)(2,1)S(1)}, u32[]{:S(2)}, u32[]{:S(2)}) %all-to-all-start.6) | async-done | bytes 393248 | tf_op jit(solution)/shard_map/all_to_all | solution.py:500
  182.6 12.9 %all-to-all-done.7 = bf16[2,256,768]{2,1,0:T(8,128)(2,1)} async-done(((bf16[2,256,768]{2,1,0:T(8,128)(2,1)}), bf16[2,256,768]{2,1,0:T(8,128)(2,1)}, u32[]{:S(2)}, u32[]{:S(2)}) %all-to-all-start.7) | async-done | bytes 786464 | tf_op jit(solution)/shard_map/all_to_all | solution.py:500
  196.7 5.4 all_to_all.121
  214.3 8.7 %all-to-all-done.9 = f32[16,2,1024]{2,1,0:T(2,128)S(1)} async-done(((f32[16,2,1024]{2,1,0:T(2,128)}), f32[16,2,1024]{2,1,0:T(2,128)S(1)}, u32[]{:S(2)}, u32[]{:S(2)}) %all-to-all-start.9) | async-done | bytes 131104 | tf_op jit(solution)/shard_map/all_to_all | solution.py:500
  247.2 7.1 %convolution_convert_fusion.1 = bf16[1920,768]{1,0:T(8,128)(2,1)} fusion(bf16[1024,1920]{1,0:T(8,128)(2,1)} %copy-done.2, bf16[1024,768]{1,0:T(8,128)(2,1)S(1)} %bitcast.181), kind=kOutput, calls=%fused_computation.45 | convolution fusion | flops 3021373440 | bytes 8454144 | tf_op jit(solution)/shard_map/dot_general | solution.py:44
  254.3 21.7 %collective-permute-done.2 = f32[256,768]{1,0:T(8,128)} collective-permute-done((f32[256,768]{1,0:T(8,128)}, f32[256,768]{1,0:T(8,128)}, u32[]{:S(2)}, u32[]{:S(2)}) %collective-permute-start.2) | collective-permute-done | bytes 786464 | tf_op jit(solution)/shard_map/ppermute | solution.py:701
  277.2 24.5 %all_to_all.122.parts_ref = f32[4,64,768]{2,1,0:T(8,128)} all-to-all(f32[4,64,768]{2,1,0:T(8,128)S(1)} %bitcast.172), channel_id=1, replica_groups=mesh['dp'=2,'hi'=4,'mid'=2,'core'=2] {'hi'}, dimensions={0} | all-to-all | bytes 1572864 | tf_op jit(solution)/shard_map/all_to_all | solution.py:500
  301.8 7.6 %feed_backward.1 = (bf16[64,768]{1,0:T(8,128)(2,1)}, bf16[64,3072]{1,0:T(8,128)(2,1)}, f32[64,768]{1,0:T(8,128)}, bf16[64,768]{1,0:T(8,128)(2,1)}, f32[16,768]{1,0:T(8,128)}) custom-call(f32[4,64,768]{2,1,0:T(8,128)} %all_to_all.122.parts_ref, f32[64,768]{1,0:T(8,128)} %get-tuple-element.248.normed_ref, f32[64,128]{1,0:T(8,128)} %get-tuple-element.249.inverse_ref, ...), custom_call_target="tpu_custom_call" | custom-call | flops 603979776 | bytes 9437184 | tf_op jit(solution)/shard_map/feed_backward/pallas_call | solution.py:165
  319.5 9.5 %attention_backward.1 = (bf16[64,768]{1,0:T(8,128)(2,1)}, bf16[256,768]{1,0:T(8,128)(2,1)}, bf16[256,768]{1,0:T(8,128)(2,1)}) custom-call(bf16[64,768]{1,0:T(8,128)(2,1)} %get-tuple-element.254.d_attend_ref, bf16[256,768]{1,0:T(8,128)(2,1)} %get-tuple-element.255.key_ref, bf16[256,768]{1,0:T(8,128)(2,1)} %get-tuple-element.256.value_ref, ...), custom_call_target="tpu_custom_call" | custom-call | flops 327155712 | bytes 1179648 | tf_op jit(solution)/shard_map/attention_backward/pallas_call | solution.py:165
  333.5 5.9 %projection_backward.1 = (bf16[256,768]{1,0:T(8,128)(2,1)S(1)}, f32[256,768]{1,0:T(8,128)}, f32[8,768]{1,0:T(8,128)}) custom-call(f32[64,768]{1,0:T(8,128)} %get-tuple-element.253.d_pre_ref, bf16[64,768]{1,0:T(8,128)(2,1)} %get-tuple-element.258.d_query_ref, bf16[256,768]{1,0:T(8,128)(2,1)} %get-tuple-element.259.d_key_ref, ...), custom_call_target="tpu_custom_call" | custom-call | flops 754974720 | bytes 3538944 | tf_op jit(solution)/shard_map/projection_backward/pallas_call | solution.py:165
  346.5 63.3 %all-to-all-done.13 = bf16[8,288,192]{1,2,0:T(8,128)(2,1)S(1)} async-done(((bf16[8,288,192]{1,2,0:T(8,128)(2,1)}), bf16[8,288,192]{1,2,0:T(8,128)(2,1)S(1)}, u32[]{:S(2)}, u32[]{:S(2)}) %all-to-all-start.13) | async-done | bytes 884768 | tf_op jit(solution)/shard_map/all_to_all | solution.py:500
  413.8 5.8 %all-to-all-start.14 = ((bf16[16,32,768]{2,1,0:T(8,128)(2,1)}), bf16[16,32,768]{2,1,0:T(8,128)(2,1)S(1)}, u32[]{:S(2)}, u32[]{:S(2)}) async-start(bf16[16,32,768]{2,1,0:T(8,128)(2,1)} %select_convert_fusion), calls=%async_computation.14 | async-start | bytes 1572864 | tf_op jit(solution)/shard_map/all_to_all | solution.py:500
  442.5 15.8 %collective-permute-done.4 = bf16[512,768]{1,0:T(8,128)(2,1)} collective-permute-done((bf16[512,768]{1,0:T(8,128)(2,1)S(1)}, bf16[512,768]{1,0:T(8,128)(2,1)}, u32[]{:S(2)}, u32[]{:S(2)}) %collective-permute-start.4) | collective-permute-done | bytes 786464 | tf_op jit(solution)/shard_map/ppermute | solution.py:784
  458.2 7.5 %add_add_fusion = f32[1920,768]{1,0:T(8,128)} fusion(bf16[1920,768]{1,0:T(8,128)(2,1)} %collective-permute-done.3, bf16[1920,768]{1,0:T(8,128)(2,1)} %convolution_convert_fusion.1, s32[1024]{0:T(1024)S(1)} %eq.285, bf16[512,768]{1,0:T(8,128)(2,1)} %collective-permute-done.4, bf16[512,768]{1,0:T(8,128)(2,1)S(1)} %bitcast.193), kind=kOutput, calls=%fused_computation.43 | convolution fusion | flops 3030908928 | bytes 13373440 | tf_op jit(solution)/shard_map/dot_general | solution.py:34
  478.6 26.1 %all-to-all-done.15 = bf16[32,24,774]{2,1,0:T(8,128)(2,1)S(1)} async-done(((bf16[32,24,774]{2,1,0:T(8,128)(2,1)}), bf16[32,24,774]{2,1,0:T(8,128)(2,1)S(1)}, u32[]{:S(2)}, u32[]{:S(2)}) %all-to-all-start.15) | async-done | bytes 1188896 | tf_op jit(solution)/shard_map/all_to_all | solution.py:500
  533.0 14.1 %multiply_reduce_fusion.1 = (f32[]{:T(128)}, f32[]{:T(128)}, f32[1920,768]{1,0:T(8,128)}, f32[1920,768]{1,0:T(8,128)}) fusion(f32[1920,768]{1,0:T(8,128)} %param.24, f32[1920,768]{1,0:T(8,128)} %get-tuple-element.277, f32[]{:T(128)S(6)} %min.3, f32[1920,768]{1,0:T(8,128)} %param.25, f32[1920,768]{1,0:T(8,128)} %param.26), kind=kLoop, calls=%fused_computation.41 | loop fusion | flops 26542080 | bytes 35389452 | tf_op jit(solution)/shard_map/reduce_sum | solution.py:488
  553.1 5.9 %all-to-all-done.17 = f32[32,6,2]{1,2,0:T(2,128)S(1)} async-done(((f32[32,6,2]{1,2,0:T(2,128)}), f32[32,6,2]{1,2,0:T(2,128)S(1)}, u32[]{:S(2)}, u32[]{:S(2)}) %all-to-all-start.17) | async-done | bytes 1568 | tf_op jit(solution)/shard_map/all_to_all | solution.py:500
  562.4 9.3 %multiply_subtract_fusion.2 = f32[1920,768]{1,0:T(8,128)} fusion(f32[1920,768]{1,0:T(8,128)} %param.24, f32[]{:T(128)} %bitcast.85, f32[1920,768]{1,0:T(8,128)} %get-tuple-element.447, f32[1920,768]{1,0:T(8,128)} %get-tuple-element.446), kind=kLoop, calls=%fused_computation.37 | loop fusion | flops 11796480 | bytes 23592964 | tf_op jit(solution)/shard_map/sub | solution.py:908
  (276 shorter events, 170.0 us)
Async XLA Ops:
  7.2 128.4 %all-gather.5.cloned.1.call-start = ((), (), s32[]{:S(2)}) async-start(), calls=%async_computation.18 | async-start | bytes 15206400 | tf_op jit(solution)/shard_map/all_gather | solution.py:591
  20.4 14.6 %all-to-all-start.4 = ((s32[32,1,256]{2,1,0:T(1,128)}), s32[32,1,256]{2,1,0:T(1,128)S(1)}, u32[]{:S(2)}, u32[]{:S(2)}) async-start(s32[32,1,256]{2,1,0:T(1,128)} %copy.264), calls=%async_computation.4 | async-start | bytes 65536 | tf_op jit(solution)/shard_map/all_to_all | solution.py:500
  40.0 35.7 %all-to-all-start.5 = ((bf16[16,32,768]{2,1,0:T(8,128)(2,1)}), bf16[16,32,768]{2,1,0:T(8,128)(2,1)}, u32[]{:S(2)}, u32[]{:S(2)}) async-start(bf16[16,32,768]{2,1,0:T(8,128)(2,1)} %broadcast_select_fusion.1), calls=%async_computation.5 | async-start | bytes 1572864 | tf_op jit(solution)/shard_map/all_to_all | solution.py:500
  44.3 257.5 %all-gather.7.cloned.1.call-start = ((), (), s32[]{:S(2)}) async-start(), calls=%async_computation.19 | async-start | bytes 6488064 | tf_op jit(solution)/shard_map/all_gather | solution.py:676
  157.5 19.4 %all-to-all-start.6 = ((bf16[4,64,768]{2,1,0:T(8,128)(2,1)}), bf16[4,64,768]{2,1,0:T(8,128)(2,1)S(1)}, u32[]{:S(2)}, u32[]{:S(2)}) async-start(bf16[4,64,768]{2,1,0:T(8,128)(2,1)} %broadcast_in_dim.355), calls=%async_computation.6 | async-start | bytes 786432 | tf_op jit(solution)/shard_map/all_to_all | solution.py:500
  177.9 17.6 %all-to-all-start.7 = ((bf16[2,256,768]{2,1,0:T(8,128)(2,1)}), bf16[2,256,768]{2,1,0:T(8,128)(2,1)}, u32[]{:S(2)}, u32[]{:S(2)}) async-start(bf16[2,256,768]{2,1,0:T(8,128)(2,1)} %broadcast_in_dim.357), calls=%async_computation.7 | async-start | bytes 1572864 | tf_op jit(solution)/shard_map/all_to_all | solution.py:500
  209.5 13.6 %all-to-all-start.9 = ((f32[16,2,1024]{2,1,0:T(2,128)}), f32[16,2,1024]{2,1,0:T(2,128)S(1)}, u32[]{:S(2)}, u32[]{:S(2)}) async-start(f32[16,2,1024]{2,1,0:T(2,128)} %broadcast_in_dim.360), calls=%async_computation.9 | async-start | bytes 262144 | tf_op jit(solution)/shard_map/all_to_all | solution.py:500
  213.6 196.7 %all-gather.9.cloned.1.call-start = ((), (), s32[]{:S(2)}) async-start(), calls=%async_computation.20 | async-start | bytes 3538944 | tf_op jit(solution)/shard_map/all_gather | solution.py:677
  231.1 3.8 collective-permute-start.1
  240.8 35.2 %collective-permute-start.2 = (f32[256,768]{1,0:T(8,128)}, f32[256,768]{1,0:T(8,128)}, u32[]{:S(2)}, u32[]{:S(2)}) collective-permute-start(f32[256,768]{1,0:T(8,128)} %constant_dynamic-slice_fusion.1), channel_id=1, source_target_pairs={{0,2},{2,0},{1,3},{3,1},{4,6},{6,4},{5,7},{7,5},{8,10},{10,8},{9,1... | collective-permute-start | bytes 2359304 | tf_op jit(solution)/shard_map/ppermute | solution.py:701
  243.1 34.2 %all-to-all-start.10 = ((bf16[32,64,96]{2,1,0:T(8,128)(2,1)}), bf16[32,64,96]{2,1,0:T(8,128)(2,1)S(1)}, u32[]{:S(2)}, u32[]{:S(2)}) async-start(bf16[32,64,96]{2,1,0:T(8,128)(2,1)} %bitcast.144), calls=%async_computation.10 | async-start | bytes 1048576 | tf_op jit(solution)/shard_map/all_to_all | solution.py:500
  247.0 177.4 %all-gather.11.cloned.1.call-start = ((), (), s32[]{:S(2)}) async-start(), calls=%async_computation.21 | async-start | bytes 3244032 | tf_op jit(solution)/shard_map/all_gather | solution.py:739
  247.2 28.8 %copy-start.9 = (f32[512,768]{1,0:T(8,128)S(1)}, f32[512,768]{1,0:T(8,128)}, u32[]{:S(2)}) copy-start(f32[512,768]{1,0:T(8,128)} %copy-done.8) | copy-start | bytes 4718596
  314.1 26.6 %all-to-all-start.12 = ((bf16[32,64,120]{2,1,0:T(8,128)(2,1)}), bf16[32,64,120]{2,1,0:T(8,128)(2,1)S(1)}, u32[]{:S(2)}, u32[]{:S(2)}) async-start(bf16[32,64,120]{2,1,0:T(8,128)(2,1)} %maximum_bitcast_fusion.1), calls=%async_computation.12 | async-start | bytes 1048576 | tf_op jit(solution)/shard_map/all_to_all | solution.py:500
  317.7 124.7 %collective-permute-start.3 = (bf16[1920,768]{1,0:T(8,128)(2,1)}, bf16[1920,768]{1,0:T(8,128)(2,1)}, u32[]{:S(2)}, u32[]{:S(2)}) collective-permute-start(bf16[1920,768]{1,0:T(8,128)(2,1)} %convolution_convert_fusion.1), channel_id=1, source_target_pairs={{0,16},{16,0},{1,17},{17,1},{2,18},{18,2},{3,19},{19,3},{4,20},{20... | collective-permute-start | bytes 8847368 | tf_op jit(solution)/shard_map/ppermute | solution.py:718
  340.7 69.1 %all-to-all-start.13 = ((bf16[8,288,192]{1,2,0:T(8,128)(2,1)}), bf16[8,288,192]{1,2,0:T(8,128)(2,1)S(1)}, u32[]{:S(2)}, u32[]{:S(2)}) async-start(bf16[8,288,192]{1,2,0:T(8,128)(2,1)} %pad_maximum_fusion), calls=%async_computation.13 | async-start | bytes 2359296 | tf_op jit(solution)/shard_map/all_to_all | solution.py:500
  413.8 24.5 %all-to-all-start.14 = ((bf16[16,32,768]{2,1,0:T(8,128)(2,1)}), bf16[16,32,768]{2,1,0:T(8,128)(2,1)S(1)}, u32[]{:S(2)}, u32[]{:S(2)}) async-start(bf16[16,32,768]{2,1,0:T(8,128)(2,1)} %select_convert_fusion), calls=%async_computation.14 | async-start | bytes 1572864 | tf_op jit(solution)/shard_map/all_to_all | solution.py:500
  438.3 19.9 %collective-permute-start.4 = (bf16[512,768]{1,0:T(8,128)(2,1)S(1)}, bf16[512,768]{1,0:T(8,128)(2,1)}, u32[]{:S(2)}, u32[]{:S(2)}) collective-permute-start(bf16[512,768]{1,0:T(8,128)(2,1)S(1)} %bitcast.192), channel_id=1, source_target_pairs={{0,16},{16,0},{1,17},{17,1},{2,18},{18,2},{3,19},{19,3},{4,20},{20... | collective-permute-start | bytes 2359304 | tf_op jit(solution)/shard_map/ppermute | solution.py:784
  465.7 39.0 %all-to-all-start.15 = ((bf16[32,24,774]{2,1,0:T(8,128)(2,1)}), bf16[32,24,774]{2,1,0:T(8,128)(2,1)S(1)}, u32[]{:S(2)}, u32[]{:S(2)}) async-start(bf16[32,24,774]{2,1,0:T(8,128)(2,1)} %concatenate.108), calls=%async_computation.15 | async-start | bytes 2752512 | tf_op jit(solution)/shard_map/all_to_all | solution.py:500
  512.3 9.6 %all-to-all-start.16 = ((f32[32,1,2]{2,1,0:T(1,128)}), f32[32,1,2]{2,1,0:T(1,128)S(1)}, u32[]{:S(2)}, u32[]{:S(2)}) async-start(f32[32,1,2]{2,1,0:T(1,128)} %copy.293), calls=%async_computation.16 | async-start | bytes 32768 | tf_op jit(solution)/shard_map/all_to_all | solution.py:500
  525.2 47.9 %copy-start.23 = (f32[14,24]{1,0:T(8,128)}, f32[14,24]{1,0:T(8,128)S(1)}, u32[]{:S(2)}) copy-start(f32[14,24]{1,0:T(8,128)S(1)} %get-tuple-element.453) | copy-start | bytes 4036
  532.9 38.8 %copy-start.3 = (f32[3,24,3072]{2,1,0:T(8,128)}, f32[3,24,3072]{2,1,0:T(8,128)S(1)}, u32[]{:S(2)}) copy-start(f32[3,24,3072]{2,1,0:T(8,128)S(1)} %get-tuple-element.448) | copy-start | bytes 2654212
  532.9 38.8 %copy-start.4 = (f32[3,24,3072]{2,1,0:T(8,128)}, f32[3,24,3072]{2,1,0:T(8,128)S(1)}, u32[]{:S(2)}) copy-start(f32[3,24,3072]{2,1,0:T(8,128)S(1)} %get-tuple-element.449) | copy-start | bytes 2654212
  549.1 9.8 %all-to-all-start.17 = ((f32[32,6,2]{1,2,0:T(2,128)}), f32[32,6,2]{1,2,0:T(2,128)S(1)}, u32[]{:S(2)}, u32[]{:S(2)}) async-start(f32[32,6,2]{1,2,0:T(2,128)} %broadcast_in_dim.370), calls=%async_computation.17 | async-start | bytes 65536 | tf_op jit(solution)/shard_map/all_to_all | solution.py:500
  (28 other events, 273.0 us)
Sparse Core Ops, SparseCore 0:
  11.7 123.9 all-gather.4
  156.0 73.9 all-gather.6
  231.8 45.7 all-gather.8
  309.5 66.5 all-gather.10

commit v5 on v4

--- a/solution.py
+++ b/solution.py
@@ -25,7 +25,7 @@
 BUCKET = 32
 ALL = ("dp", "hi", "mid", "core")
 VOC = ("hi", "mid", "core")
-NEAR = ("dp", "mid", "core")
+NEAR = ("mid", "core")
 bfloat = jnp.bfloat16
 single = jnp.float32
 
@@ -169,7 +169,7 @@
         out_specs=[spec(shape, block, index) for shape, _, block, index in shapes],
         out_shape=[jax.ShapeDtypeStruct(shape, kind) for shape, kind, _, _ in shapes],
         scratch_shapes=list(scratch),
-        cost_estimate=pl.CostEstimate(flops=cost[0], bytes_accessed=cost[1], transcendentals=cost[2]),
+        cost_estimate=pl.CostEstimate(flops=cost[0] // 64, bytes_accessed=cost[1] // 64, transcendentals=0),
         name=name,
     )(*(array for array, _, _ in inputs))
 
@@ -470,24 +470,198 @@
     )
 
 
+def adam_direction(weight_arr, new_first, new_second):
+    return (
+        new_first
+        / (1.0 - beta_first**STEP)
+        / (jnp.sqrt(new_second / (1.0 - beta_second**STEP)) + adam_eps)
+        + weight_decay * weight_arr
+    )
+
+
 def adam_moments(weight_arr, first_mom, second_mom, gradient, factor):
     clipped = gradient * factor
     new_first = beta_first * first_mom + (1.0 - beta_first) * clipped
     new_second = beta_second * second_mom + (1.0 - beta_second) * clipped * clipped
-    direction = (
-        new_first
-        / (1.0 - beta_first**STEP)
-        / (jnp.sqrt(new_second / (1.0 - beta_second**STEP)) + adam_eps)
-        + weight_decay * weight_arr
-    )
-    return (new_first, new_second, direction)
-
-
-def norm_pair(weight_arr, direction, axes):
-    return jnp.stack(
-        [jnp.sum(weight_arr * weight_arr, axis=axes), jnp.sum(direction * direction, axis=axes)],
-        axis=-1,
-    )
+    return (new_first, new_second, adam_direction(weight_arr, new_first, new_second))
+
+
+def row_block(count):
+    return 240 if count % 240 == 0 else count
+
+
+def lookup_kernel(parts, *refs):
+    head_refs, (asked_ref, given_ref, side_ref, grad_ref, square_ref) = refs[:parts], refs[parts:]
+    step = pl.program_id(0)
+    rows, width = grad_ref.shape
+    base = step * rows
+    row_hot = asked_ref[...] == base + lax.broadcasted_iota(
+        jnp.int32, (rows, asked_ref.shape[1]), 0
+    )
+    grad = plain_dot(row_hot.astype(bfloat), given_ref[...])
+    for head_ref in head_refs:
+        grad += head_ref[...].astype(single)
+    grad_ref[...] = grad
+    place = base + lax.broadcasted_iota(jnp.int32, (rows, width), 0)
+    own = (place >= side_ref[0]) & (place < side_ref[1])
+
+    @pl.when(step == 0)
+    def _():
+        square_ref[...] = jnp.zeros_like(square_ref)
+
+    square_ref[...] += jnp.sum(jnp.where(own, grad * grad, 0.0), axis=0, keepdims=True)
+
+
+def lookup_grad(heads, asked_rows, given, sides):
+    vrows, width = heads[0].shape
+    rows = row_block(vrows)
+    block = pl.BlockSpec((rows, width), lambda step: (step, 0))
+    whole_spec = lambda array: pl.BlockSpec(array.shape, lambda step: (0, 0))
+    return pl.pallas_call(
+        lambda *refs: lookup_kernel(len(heads), *refs),
+        grid=(vrows // rows,),
+        in_specs=[block] * len(heads)
+        + [
+            whole_spec(asked_rows),
+            whole_spec(given),
+            pl.BlockSpec(memory_space=pltpu.SMEM),
+        ],
+        out_specs=[block, pl.BlockSpec((1, width), lambda step: (0, 0))],
+        out_shape=[
+            jax.ShapeDtypeStruct((vrows, width), single),
+            jax.ShapeDtypeStruct((1, width), single),
+        ],
+        cost_estimate=pl.CostEstimate(flops=0, bytes_accessed=0, transcendentals=0),
+        name="table_gradient",
+    )(*heads, asked_rows, given, sides)
+
+
+def full_sum(values):
+    return jnp.sum(jnp.sum(values, axis=1, keepdims=True), axis=0, keepdims=True)
+
+
+def pair_row(weight_sum, dir_sum):
+    lane = lax.broadcasted_iota(jnp.int32, (1, 128), 1)
+    return jnp.where(lane == 0, weight_sum, dir_sum)
+
+
+def norms_kernel(offset_ref, *refs):
+    total_ref, table_refs, layer_refs, position_refs, small_refs = (
+        refs[0], refs[1:5], refs[5:9], refs[9:13], refs[13:17],
+    )
+    norms_ref, layer_out, position_out, small_out = refs[17], refs[18:21], refs[21:24], refs[24:27]
+    sums_ref = refs[27]
+    step = pl.program_id(0)
+    total_square = jnp.sum(total_ref[...], axis=0, keepdims=True)[:, :1]
+    factor = jnp.minimum(1.0, clip_norm / jnp.sqrt(total_square))
+
+    @pl.when(step == 0)
+    def _():
+        sums_ref[...] = jnp.zeros_like(sums_ref)
+        norms_ref[...] = jnp.zeros_like(norms_ref)
+        for part in range(3):
+            weight_arr, first_mom, second_mom, gradient = (ref[part] for ref in layer_refs)
+            first, second, direction = adam_moments(
+                weight_arr, first_mom, second_mom, gradient, factor
+            )
+            for ref, value in zip(layer_out, (first, second, direction)):
+                ref[part] = value
+            norms_ref[pl.ds(1 + part, 1), :] = pair_row(
+                full_sum(weight_arr * weight_arr), full_sum(direction * direction)
+            )
+        for row, group_refs, outs in ((4, position_refs, position_out), (5, small_refs, small_out)):
+            weight_arr = group_refs[0][...]
+            first, second, direction = adam_moments(
+                weight_arr, group_refs[1][...], group_refs[2][...], group_refs[3][...], factor
+            )
+            for ref, value in zip(outs, (first, second, direction)):
+                ref[...] = value
+            norms_ref[pl.ds(row, 1), :] = pair_row(
+                full_sum(weight_arr * weight_arr), full_sum(direction * direction)
+            )
+
+    weight_arr = table_refs[0][...]
+    _, _, direction = adam_moments(
+        weight_arr, table_refs[1][...], table_refs[2][...], table_refs[3][...], factor
+    )
+    sums_ref[pl.ds(0, 1), :] += jnp.sum(weight_arr * weight_arr, axis=0, keepdims=True)
+    sums_ref[pl.ds(1, 1), :] += jnp.sum(direction * direction, axis=0, keepdims=True)
+
+    @pl.when(step == pl.num_programs(0) - 1)
+    def _():
+        norms_ref[pl.ds(0, 1), :] = pair_row(
+            full_sum(sums_ref[pl.ds(0, 1), :]), full_sum(sums_ref[pl.ds(1, 1), :])
+        )
+
+
+def update_norms(totals, table, layer, position, small, split, dp_index):
+    vrows, width = table[0].shape
+    rows = row_block(split)
+    fixed = lambda array: pl.BlockSpec(
+        array.shape, lambda step, offset, rank=array.ndim: (0,) * rank
+    )
+    part = pl.BlockSpec((rows, width), lambda step, offset: (offset[0] + step, 0))
+    groups = tuple(layer) + tuple(position) + tuple(small)
+    outs = [
+        jax.ShapeDtypeStruct(group[0].shape, single)
+        for group in (layer, position, small)
+        for _ in range(3)
+    ]
+    norms = jax.ShapeDtypeStruct((8, 128), single)
+    return pl.pallas_call(
+        norms_kernel,
+        grid_spec=pltpu.PrefetchScalarGridSpec(
+            num_scalar_prefetch=1,
+            grid=(split // rows,),
+            in_specs=[fixed(totals)] + [part] * 4 + [fixed(array) for array in groups],
+            out_specs=[fixed(norms)] + [fixed(out) for out in outs],
+            scratch_shapes=[pltpu.VMEM((8, width), single)],
+        ),
+        out_shape=[norms] + outs,
+        cost_estimate=pl.CostEstimate(flops=0, bytes_accessed=0, transcendentals=0),
+        name="update_norms",
+    )((dp_index * (split // rows)).astype(jnp.int32)[None], totals, *table, *groups)
+
+
+def final_kernel(
+    pairs_ref, weight_ref, first_ref, second_ref,
+    layer_ref, layer_dir_ref, position_ref, position_dir_ref, small_ref, small_dir_ref,
+    next_ref, layer_next_ref, position_next_ref, small_next_ref,
+):
+    roots = jnp.sqrt(jnp.sum(pairs_ref[...], axis=0, keepdims=True))
+
+    def rate(group):
+        return learn_rate * (
+            roots[:, 2 * group : 2 * group + 1] / roots[:, 2 * group + 1 : 2 * group + 2]
+        )
+
+    weight_arr = weight_ref[...]
+    direction = adam_direction(weight_arr, first_ref[...], second_ref[...])
+    next_ref[...] = weight_arr - rate(0) * direction
+
+    @pl.when(pl.program_id(0) == 0)
+    def _():
+        for part in range(3):
+            layer_next_ref[part] = layer_ref[part] - rate(1 + part) * layer_dir_ref[part]
+        position_next_ref[...] = position_ref[...] - rate(4) * position_dir_ref[...]
+        small_next_ref[...] = small_ref[...] - rate(5) * small_dir_ref[...]
+
+
+def final_update(pairs, table, groups):
+    vrows, width = table[0].shape
+    rows = row_block(vrows)
+    fixed = lambda array: pl.BlockSpec(array.shape, lambda step, rank=array.ndim: (0,) * rank)
+    block = pl.BlockSpec((rows, width), lambda step: (step, 0))
+    outs = [jax.ShapeDtypeStruct(array.shape, single) for array in groups[::2]]
+    return pl.pallas_call(
+        final_kernel,
+        grid=(vrows // rows,),
+        in_specs=[fixed(pairs)] + [block] * 3 + [fixed(array) for array in groups],
+        out_specs=[block] + [fixed(out) for out in outs],
+        out_shape=[jax.ShapeDtypeStruct((vrows, width), single)] + outs,
+        cost_estimate=pl.CostEstimate(flops=0, bytes_accessed=0, transcendentals=0),
+        name="final_update",
+    )(pairs, *table, *groups)
 
 
 class Exchange:
@@ -502,9 +676,6 @@
 
     def copies(self, values, axes, count):
         return self(jnp.broadcast_to(values[None], (count,) + values.shape), axes)
-
-    def total(self, values, axes, count):
-        return jnp.sum(self.copies(values, axes, count), axis=0)
 
     def columns(self, values, axes, count):
         rows, width = values.shape
@@ -648,7 +819,7 @@
         lambda state: state[0] < rounds, more_rows, (jnp.ones((), rounds.dtype), embed_rows)
     )
     few = devices <= 32
-    near = dp_devs * 4
+    near = 4
     allowed = allowed.astype(single)
     slot_hot = slot_hot.astype(single)
     (
@@ -717,9 +888,9 @@
         head_b = grad_head.astype(bfloat)
         other_b = lax.ppermute(head_b, "dp", [(0, 1), (1, 0)])
         d_output, head_b = lax.optimization_barrier((d_output, head_b))
-        grad_head = head_b.astype(single) + other_b.astype(single)
+        heads = (head_b, other_b)
     else:
-        grad_head = lax.psum(grad_head, "dp")
+        heads = (lax.psum(grad_head, "dp"),)
     d_output = exchange(d_output.reshape(outer, CAP, width), "hi")
     if few:
         d_output, kept_all = lax.optimization_barrier((d_output, kept_all))
@@ -789,18 +960,21 @@
             return jnp.roll(asked_rows, -group, axis=0)
         return asked_rows
 
-    def into_rows(asked_rows, given):
-        flat = both_groups(asked_rows).reshape(-1)
-        row_hot = flat[None, :] == jnp.arange(vrows)[:, None]
-        return plain_dot(row_hot.astype(bfloat), given)
+    split = vrows // dp_devs
+    sides = lax.axis_index("dp") * split + jnp.array([0, split])
+
+    def into_rows(heads, asked_rows, given, sides):
+        return lookup_grad(heads, both_groups(asked_rows).reshape(1, -1), given, sides)
 
     last = (jnp.arange(BUCKET) == BUCKET - 1)[None, :]
     left_row = jnp.where(lax.axis_index(VOC) == mask_owner, MASK_ID - first_row, -1)
     given = give(hot, True, exchange)
 
     if few:
-        near_pos = packet[:, BUCKET + CAP : tail].reshape(dp_devs, outer, 4 * CAP)
-        near_pos = lax.dynamic_index_in_dim(near_pos, lax.axis_index("hi"), 1, False).reshape(-1)
+        near_pos = packet[:, BUCKET + CAP : tail].reshape(dp_devs * outer, near * CAP)
+        near_pos = lax.dynamic_index_in_dim(
+            near_pos, lax.axis_index(("dp", "hi")), 0, False
+        )
         init_rows = norm_forward(position_full, small_full[0], small_full[1])[0].astype(bfloat)
         init_hot = near_pos[:, None] == jnp.arange(length)[None, :]
         init_all = plain_dot(init_hot.astype(bfloat), init_rows).astype(bfloat)
@@ -820,18 +994,27 @@
         beyond = (jnp.max(results[0].astype(single)) > 3.395e38).astype(bfloat)
         given = given + beyond
         results = exchange.rows(results, devices).astype(single)
+        sides = sides + (results[0, 0, 0] > 3.395e38).astype(jnp.int32)
         pieces = 3 * piece
         attn = jnp.sum(
-            results[..., :pieces].reshape(dp_devs, outer, 4, share, pieces), axis=1
-        ).reshape(near, share, pieces)
-        shared_grad = jnp.sum(results[..., -shared_rows:], axis=0).T
+            results[..., :pieces].reshape(dp_devs * outer, near, share, pieces), axis=0
+        )
+        shared_grad = jnp.sum(results[..., -shared_rows:], axis=0)
+        single_parts = results[..., pieces:-shared_rows]
+        part_square = (
+            jnp.sum(attn * attn)
+            + jnp.sum(single_parts * single_parts)
+            + jnp.sum(shared_grad * shared_grad)
+        )
+        shared_grad = shared_grad.T
         position_grad, small_grad = shared_grad[:length], shared_grad[length:]
         grad_key, grad_value, grad_query = (
             side_by_side(attn[..., part * piece : (part + 1) * piece]) for part in range(3)
         )
-        grad_up = side_by_side(results[..., pieces : pieces + wide])
-        grad_down = side_by_side(results[..., pieces + wide : pieces + 2 * wide])
-        grad_out = side_by_side(results[..., pieces + 2 * wide : -shared_rows])
+        grad_up, grad_down, grad_out = (
+            side_by_side(single_parts[..., low:high])
+            for low, high in ((0, wide), (wide, 2 * wide), (2 * wide, None))
+        )
         layer_grad = jnp.stack(
             [
                 jnp.concatenate([grad_query, grad_key, grad_value, grad_out], axis=1),
@@ -859,56 +1042,69 @@
         shared_grad = jnp.concatenate([grad_position, grad_small]).T
         shared_grad = lax.psum_scatter(shared_grad, ALL, scatter_dimension=0, tiled=True).T
         position_grad, small_grad = shared_grad[:length], shared_grad[length:]
-    table_grad = grad_head + into_rows(jnp.where(last, left_row, asked), of_both(given))
+        part_square = jnp.sum(layer_grad * layer_grad) + jnp.sum(shared_grad * shared_grad)
+    table_grad, table_square_sum = into_rows(
+        heads, jnp.where(last, left_row, asked), of_both(given), sides
+    )
 
     def more_grads(state):
-        turn, grads = state
+        turn, grads, _ = state
         hot_t, wanted_t = bucket_round(content, owner, place, turn, owners, vrows)
         wanted_t = jnp.broadcast_to(wanted_t[None], (dp_devs,) + wanted_t.shape)
         asked_t = lax.all_to_all(
             wanted_t.reshape(devices, BUCKET), ALL, 0, 0, tiled=True
         )
-        return turn + 1, grads + into_rows(asked_t, of_both(give(hot_t, False, plain_exchange)))
-
-    _, table_grad = lax.while_loop(
-        lambda state: state[0] < rounds, more_grads, (jnp.ones((), rounds.dtype), table_grad)
-    )
-    square_part = (
-        jnp.sum(table_grad * table_grad) / dp_devs
-        + jnp.sum(layer_grad * layer_grad)
-        + jnp.sum(position_grad * position_grad)
-        + jnp.sum(small_grad * small_grad)
-    )
-    total_square, loss_value = exchange.total(jnp.stack([square_part, loss_part]), ALL, devices)
+        given_t = of_both(give(hot_t, False, plain_exchange))
+        return (turn + 1,) + tuple(into_rows((grads,), asked_t, given_t, sides))
+
+    _, table_grad, table_square_sum = lax.while_loop(
+        lambda state: state[0] < rounds,
+        more_grads,
+        (jnp.ones((), rounds.dtype), table_grad, table_square_sum),
+    )
+    square_part = jnp.sum(table_square_sum) + part_square
+    totals = exchange.copies(jnp.stack([square_part, loss_part]), ALL, devices)
+    total_square, loss_value = jnp.sum(totals, axis=0)
     grad_norm = jnp.sqrt(total_square)
     factor = jnp.minimum(1.0, clip_norm / grad_norm)
-    table_first, table_second, table_dir = adam_moments(
-        embed_table, table_moment, table_square, table_grad, factor
-    )
-    layer_first, layer_second, layer_dir = adam_moments(
-        layer_weights, layer_moment, layer_square, layer_grad, factor
-    )
-    position_first, position_second, position_dir = adam_moments(
-        position_table, position_moment, position_square, position_grad, factor
-    )
-    small_first, small_second, small_dir = adam_moments(
-        small_params, small_moment, small_square, small_grad, factor
-    )
-    partial_norms = jnp.concatenate(
-        [
-            norm_pair(embed_table, table_dir, (0, 1))[None] / dp_devs,
-            norm_pair(layer_weights, layer_dir, (1, 2)),
-            norm_pair(position_table, position_dir, (0, 1))[None],
-            norm_pair(small_params, small_dir, (0, 1))[None],
-        ]
-    )
-    trust_square = exchange.total(partial_norms, ALL, devices)
-    trust_norms = jnp.sqrt(trust_square)
-    ratio = trust_norms[:, 0] / trust_norms[:, 1]
-    table_next = embed_table - learn_rate * ratio[0] * table_dir
-    layer_next = layer_weights - learn_rate * ratio[1:4][:, None, None] * layer_dir
-    position_next = position_table - learn_rate * ratio[4] * position_dir
-    small_next = small_params - learn_rate * ratio[5] * small_dir
+    (
+        norms,
+        layer_first,
+        layer_second,
+        layer_dir,
+        position_first,
+        position_second,
+        position_dir,
+        small_first,
+        small_second,
+        small_dir,
+    ) = update_norms(
+        totals,
+        (embed_table, table_moment, table_square, table_grad),
+        (layer_weights, layer_moment, layer_square, layer_grad),
+        (position_table, position_moment, position_square, position_grad),
+        (small_params, small_moment, small_square, small_grad),
+        split,
+        lax.axis_index("dp"),
+    )
+    factor_late, norms = lax.optimization_barrier((factor, norms))
+    pairs = exchange.copies(norms[:6, :2].reshape(-1), ALL, devices)
+    table_first, table_second, _ = adam_moments(
+        embed_table, table_moment, table_square, table_grad, factor_late
+    )
+    trust_norms = jnp.sqrt(jnp.sum(pairs, axis=0)).reshape(6, 2)
+    table_next, layer_next, position_next, small_next = final_update(
+        pairs,
+        (embed_table, table_first, table_second),
+        (
+            layer_weights,
+            layer_dir,
+            position_table,
+            position_dir,
+            small_params,
+            small_dir,
+        ),
+    )
     return (
         loss_value,
         grad_norm,

time: 590 us -> 599 us (1.015)
  Pallas kernels: 41.5 us -> 78.1 us
  waiting for transfers between devices: 277 us -> 254 us
  other arithmetic: 75.6 us -> 58.1 us
  local copies, waits for them, and re-layouts: 36.5 us -> 52.3 us
  matrix products: 42.4 us -> 36.2 us
    all_to_all x12, waiting for transfers between devices: 178 us -> 94.7 us  [__call__(): self.last = lax.all_to_all(values, axes, 0, 0, tiled=True)]
    ppermute x1, waiting for transfers between devices: 15.8 us -> 83 us  [of_both(): return jnp.concatenate([rows, lax.ppermute(rows, 'dp', [(0, 1), (1, 0)])])]
    pallas_call x0 -> x3, Pallas kernels: none -> 36.4 us  [the longest x1 14.3 us: final_update(): pl.pallas_call(final_kernel, grid=(vrows // rows,), in_specs=[fixed(pairs...]
    reduce_sum x13 -> x8, other arithmetic: 28.6 us -> 6.29 us  [the longest x1 1.67 us: on_device(): jnp.sum(results[..., :pieces].reshape(dp_devs * outer, near, share, piece...]
    add x0 -> x2, other arithmetic: none -> 11.7 us  [the longest x1 11.2 us: adam_moments(): beta_second * second_mom + (1.0 - beta_second) * clipped * clipped]
    sub x4 -> x0, other arithmetic: 11.4 us -> none  [the longest x1 9.26 us: on_device(): table_next = embed_table - learn_rate * ratio[0] * table_dir]
    dot_general x4 -> x3, matrix products: 14.6 us -> 8.08 us  [plain_dot(): return jnp.dot(left_op, right_op, preferred_element_type=single)]
  transfers between devices with their start and end apart: 20 -> 20, of which waited for: 14 -> 14; matrix products, arithmetic and copies ran while one was open for 16% -> 22% of each run, Pallas kernels for 4% -> 4%
where the time goes in v5:
time: 599 us; the launch traced here: 589 us
  waiting for transfers between devices  254 us (42%)
  Pallas kernels  78.1 us (13%)
  other arithmetic  58.1 us (10%)
  starting transfers between devices  54.9 us (9%)
  local copies, waits for them, and re-layouts  52.3 us (9%)
  matrix products  36.2 us (6%)
  blocking collectives  30.1 us (5%)
  between operations  24.7 us (4%)
    all_to_all x12, waiting for transfers between devices, __call__(): self.last = lax.all_to_all(values, axes, 0, 0, tiled=True)  94.7 us
    ppermute x1, waiting for transfers between devices, of_both(): return jnp.concatenate([rows, lax.ppermute(rows, 'dp', [(0, 1), (1, 0)])])  83 us
    all_gather x1, waiting for transfers between devices, on_device(): shard = lax.all_gather(shard.astype(bfloat), ALL, axis=0, tiled=True)  56.7 us
    all_to_all x12, starting transfers between devices, __call__(): self.last = lax.all_to_all(values, axes, 0, 0, tiled=True)  51.1 us
    pallas_call x5, Pallas kernels, kernel_call(): pl.pallas_call(body, grid=(steps,), in_specs=[spec(array.shape, block, in...  41.6 us
    all_to_all x2, blocking collectives, __call__(): self.last = lax.all_to_all(values, axes, 0, 0, tiled=True)  30.1 us
    dot_general x7, matrix products, rows_dot(): lax.dot_general(left_op, right_op, (((0,), (0,)), ((), ())), preferred_el...  24.6 us
    ppermute x2, waiting for transfers between devices, swapped(): theirs = lax.ppermute(part(1 - side), axis, [(0, 1), (1, 0)])  20 us
  transfers between devices with their start and end apart: 20, of which 14 were waited for; matrix products, arithmetic and copies ran while one was open for 22% of the time, Pallas kernels for 4%

profile of v5, /device:TPU:0, one launch (start us, length us, event | category | flops | bytes accessed | tf_op | source)
XLA Modules:
  0.0 588.8 jit_solution(15454072859324340771)
XLA Ops:
  20.3 7.3 %all-to-all-start.4 = ((s32[32,1,256]{2,1,0:T(1,128)}), s32[32,1,256]{2,1,0:T(1,128)S(1)}, u32[]{:S(2)}, u32[]{:S(2)}) async-start(s32[32,1,256]{2,1,0:T(1,128)} %copy.322), calls=%async_computation.4 | async-start | bytes 65536 | tf_op jit(solution)/shard_map/all_to_all | solution.py:674
  27.6 7.3 %all-to-all-done.4 = s32[32,1,256]{2,1,0:T(1,128)S(1)} async-done(((s32[32,1,256]{2,1,0:T(1,128)}), s32[32,1,256]{2,1,0:T(1,128)S(1)}, u32[]{:S(2)}, u32[]{:S(2)}) %all-to-all-start.4) | async-done | bytes 32800 | tf_op jit(solution)/shard_map/all_to_all | solution.py:674
  48.2 28.0 %all-to-all-done.5 = bf16[16,32,768]{2,1,0:T(8,128)(2,1)} async-done(((bf16[16,32,768]{2,1,0:T(8,128)(2,1)}), bf16[16,32,768]{2,1,0:T(8,128)(2,1)}, u32[]{:S(2)}, u32[]{:S(2)}) %all-to-all-start.5) | async-done | bytes 786464 | tf_op jit(solution)/shard_map/all_to_all | solution.py:674
  78.7 56.7 %all-gather.5.cloned.1.call-done.shared_ref.weight_ref.up_ref.down_ref = bf16[768,9600]{1,0:T(8,128)(2,1)} async-done(((bf16[24,9600]{1,0:T(8,128)(2,1)}), bf16[768,9600]{1,0:T(8,128)(2,1)}) %all-gather.5.cloned.1.call-update) | async-done | bytes 14745616 | tf_op jit(solution)/shard_map/all_gather | solution.py:762
  135.4 11.5 %attention_forward.1 = (bf16[256,768]{1,0:T(8,128)(2,1)}, bf16[256,768]{1,0:T(8,128)(2,1)}, bf16[64,768]{1,0:T(8,128)(2,1)}, bf16[64,768]{1,0:T(8,128)(2,1)}, f3...) custom-call(f32[256,768]{1,0:T(8,128)} %get-tuple-element.278.embed_, ...), custom_call_target="tpu_custom_call" | custom-call | flops 11010048 | bytes 73728 | tf_op jit(solution)/shard_map/attention_forward/pallas_call | solution.py:165
  146.9 7.1 %feed_forward.1 = (bf16[64,768]{1,0:T(8,128)(2,1)}, f32[64,3072]{1,0:T(8,128)}, bf16[64,3072]{1,0:T(8,128)(2,1)}, bf16[64,768]{1,0:T(8,128)(2,1)}, f32[64,768]{1,0:T(8,128)}, /*index=5*/f32[64,128]{1,0:T(8,128)}) custom-call(f32[64,768]{1,0:T(8,128)} %get-tuple-element.279.middle_ref, f32[14,768]{1,0:T(8,128)} %get-tuple-element.280.small_ref, ...), custom_call_target="tpu_custom_call" | custom-call | flops 9437184 | bytes 147456 | tf_op jit(solution)/shard_map/feed_forward/pallas_call | solution.py:165
  160.7 16.0 %all-to-all-done.6 = bf16[4,64,768]{2,1,0:T(8,128)(2,1)S(1)} async-done(((bf16[4,64,768]{2,1,0:T(8,128)(2,1)}), bf16[4,64,768]{2,1,0:T(8,128)(2,1)S(1)}, u32[]{:S(2)}, u32[]{:S(2)}) %all-to-all-start.6) | async-done | bytes 393248 | tf_op jit(solution)/shard_map/all_to_all | solution.py:674
  182.9 12.2 %all-to-all-done.7 = bf16[2,256,768]{2,1,0:T(8,128)(2,1)} async-done(((bf16[2,256,768]{2,1,0:T(8,128)(2,1)}), bf16[2,256,768]{2,1,0:T(8,128)(2,1)}, u32[]{:S(2)}, u32[]{:S(2)}) %all-to-all-start.7) | async-done | bytes 786464 | tf_op jit(solution)/shard_map/all_to_all | solution.py:674
  196.4 5.2 all_to_all.133
  213.4 8.9 %all-to-all-done.9 = f32[16,2,1024]{2,1,0:T(2,128)S(1)} async-done(((f32[16,2,1024]{2,1,0:T(2,128)}), f32[16,2,1024]{2,1,0:T(2,128)S(1)}, u32[]{:S(2)}, u32[]{:S(2)}) %all-to-all-start.9) | async-done | bytes 131104 | tf_op jit(solution)/shard_map/all_to_all | solution.py:674
  246.9 7.1 %convolution_convert_fusion.1.refs_0_ = bf16[1920,768]{1,0:T(8,128)(2,1)} fusion(bf16[1024,1920]{1,0:T(8,128)(2,1)} %copy-done.1, bf16[1024,768]{1,0:T(8,128)(2,1)S(1)} %bitcast.166), kind=kOutput, calls=%fused_computation.31 | convolution fusion | flops 3021373440 | bytes 8454144 | tf_op jit(solution)/shard_map/dot_general | solution.py:44
  254.1 16.5 %collective-permute-done.2 = f32[256,768]{1,0:T(8,128)S(1)} collective-permute-done((f32[256,768]{1,0:T(8,128)}, f32[256,768]{1,0:T(8,128)S(1)}, u32[]{:S(2)}, u32[]{:S(2)}) %collective-permute-start.2) | collective-permute-done | bytes 786464 | tf_op jit(solution)/shard_map/ppermute | solution.py:872
  270.9 24.9 %all_to_all.134.parts_ref = f32[4,64,768]{2,1,0:T(8,128)} all-to-all(f32[4,64,768]{2,1,0:T(8,128)S(1)} %bitcast.158), channel_id=1, replica_groups=mesh['dp'=2,'hi'=4,'mid'=2,'core'=2] {'hi'}, dimensions={0} | all-to-all | bytes 1572864 | tf_op jit(solution)/shard_map/all_to_all | solution.py:674
  295.8 7.6 %feed_backward.1 = (bf16[64,768]{1,0:T(8,128)(2,1)}, bf16[64,3072]{1,0:T(8,128)(2,1)}, f32[64,768]{1,0:T(8,128)}, bf16[64,768]{1,0:T(8,128)(2,1)}, f32[16,768]{1,0:T(8,128)}) custom-call(f32[4,64,768]{2,1,0:T(8,128)} %all_to_all.134.parts_ref, f32[64,768]{1,0:T(8,128)} %get-tuple-element.294.normed_ref, f32[64,128]{1,0:T(8,128)} %get-tuple-element.295.inverse_ref, ...), custom_call_target="tpu_custom_call" | custom-call | flops 9437184 | bytes 147456 | tf_op jit(solution)/shard_map/feed_backward/pallas_call | solution.py:165
  308.2 9.5 %attention_backward.1 = (bf16[64,768]{1,0:T(8,128)(2,1)}, bf16[256,768]{1,0:T(8,128)(2,1)}, bf16[256,768]{1,0:T(8,128)(2,1)}) custom-call(bf16[64,768]{1,0:T(8,128)(2,1)} %get-tuple-element.300.d_attend_ref, bf16[256,768]{1,0:T(8,128)(2,1)} %get-tuple-element.301.key_ref, bf16[256,768]{1,0:T(8,128)(2,1)} %get-tuple-element.302.value_ref, ...), custom_call_target="tpu_custom_call" | custom-call | flops 5111808 | bytes 18432 | tf_op jit(solution)/shard_map/attention_backward/pallas_call | solution.py:165
  326.8 5.9 %projection_backward.1 = (bf16[256,768]{1,0:T(8,128)(2,1)S(1)}, f32[256,768]{1,0:T(8,128)}, f32[8,768]{1,0:T(8,128)}) custom-call(f32[64,768]{1,0:T(8,128)} %get-tuple-element.299.d_pre_ref, bf16[64,768]{1,0:T(8,128)(2,1)} %get-tuple-element.304.d_query_ref, bf16[256,768]{1,0:T(8,128)(2,1)} %get-tuple-element.305.d_key_ref, ...), custom_call_target="tpu_custom_call" | custom-call | flops 11796480 | bytes 55296 | tf_op jit(solution)/shard_map/projection_backward/pallas_call | solution.py:165
  335.7 8.7 %all-to-all-done.12 = bf16[32,64,120]{2,1,0:T(8,128)(2,1)} async-done(((bf16[32,64,120]{2,1,0:T(8,128)(2,1)}), bf16[32,64,120]{2,1,0:T(8,128)(2,1)}, u32[]{:S(2)}, u32[]{:S(2)}) %all-to-all-start.12) | async-done | bytes 491552 | tf_op jit(solution)/shard_map/all_to_all | solution.py:674
  357.5 6.0 %all-to-all-done.13 = bf16[4,288,384]{2,1,0:T(8,128)(2,1)S(1)} async-done(((bf16[4,288,384]{2,1,0:T(8,128)(2,1)}), bf16[4,288,384]{2,1,0:T(8,128)(2,1)S(1)}, u32[]{:S(2)}, u32[]{:S(2)}) %all-to-all-start.13) | async-done | bytes 884768 | tf_op jit(solution)/shard_map/all_to_all | solution.py:674
  387.8 5.4 all-to-all-start.15
  412.1 83.0 %collective-permute-done.4 = bf16[512,768]{1,0:T(8,128)(2,1)S(1)} collective-permute-done((bf16[512,768]{1,0:T(8,128)(2,1)}, bf16[512,768]{1,0:T(8,128)(2,1)S(1)}, u32[]{:S(2)}, u32[]{:S(2)}) %collective-permute-start.4) | collective-permute-done | bytes 786464 | tf_op jit(solution)/shard_map/ppermute | solution.py:955
  504.8 9.8 %table_gradient.5 = (f32[1920,768]{1,0:T(8,128)}, f32[1,768]{1,0:T(1,128)}) custom-call(bf16[1920,768]{1,0:T(8,128)(2,1)} %convolution_convert_fusion.1.refs_0_, bf16[1920,768]{1,0:T(8,128)(2,1)} %collective-permute-done.3.refs_1_, s32[1,1024]{1,0:T(1,128)} %reshape.454.refs_2_, bf16[1024,768]{1,0:T(8,128)(2,1)} %pad_maximum_fusion.1.refs_3_, ...), custom_call_target="tpu_custom_call" | custom-call | tf_op jit(solution)/shard_map/table_gradient/pallas_call | solution.py:520
  534.0 12.3 %update_norms.1 = (f32[8,128]{1,0:T(8,128)}, f32[3,24,3072]{2,1,0:T(8,128)}, f32[3,24,3072]{2,1,0:T(8,128)}, f32[3,24,3072]{2,1,0:T(8,128)}, f32[256,24]{1,0:T(8...) custom-call(s32[1]{0:T(128)} %bitcast.64.offset_ref, ...), custom_call_target="tpu_custom_call" | custom-call | tf_op jit(solution)/shard_map/update_norms/pallas_call | solution.py:611
  550.3 11.2 %fusion.5 = (f32[1920,768]{1,0:T(8,128)}, f32[1920,768]{1,0:T(8,128)}) fusion(f32[1920,768]{1,0:T(8,128)} %refs_3_.1, f32[1920,768]{1,0:T(8,128)} %get-tuple-element.328.refs_4_, f32[]{:T(128)S(6)} %min.3, f32[1920,768]{1,0:T(8,128)} %refs_2_.1), kind=kLoop, calls=%fused_computation.29 | loop fusion | flops 11796480 | bytes 29491204 | tf_op jit(solution)/shard_map/add | solution.py:485
  563.5 14.3 %final_update.1 = (f32[1920,768]{1,0:T(8,128)}, f32[3,24,3072]{2,1,0:T(8,128)}, f32[256,24]{1,0:T(8,128)}, f32[14,24]{1,0:T(8,128)}) custom-call(f32[32,12]{1,0:T(8,128)} %bitcast.184, f32[1920,768]{1,0:T(8,128)} %weight_ref.1, f32[1920,768]{1,0:T(8,128)} %get-tuple-element.569.first_ref, f32[1920,768]{1,0:T(8,128)} %get-tuple-element.568.second_ref, ...), custom_call_target="tpu_custom_call" | custom-call | tf_op jit(solution)/shard_map/final_update/pallas_call | solution.py:656
  (286 shorter events, 181.5 us)
Async XLA Ops:
  7.2 128.2 %all-gather.5.cloned.1.call-start = ((), (), s32[]{:S(2)}) async-start(), calls=%async_computation.18 | async-start | bytes 15206400 | tf_op jit(solution)/shard_map/all_gather | solution.py:762
  13.3 62.9 %copy-start.26 = (s32[1,256]{1,0:T(1,128)}, s32[1,256]{1,0:T(1,128)S(1)}, u32[]{:S(2)}) copy-start(s32[1,256]{1,0:T(1,128)S(1)} %and_select_fusion.2) | copy-start | bytes 3076
  20.3 14.6 %all-to-all-start.4 = ((s32[32,1,256]{2,1,0:T(1,128)}), s32[32,1,256]{2,1,0:T(1,128)S(1)}, u32[]{:S(2)}, u32[]{:S(2)}) async-start(s32[32,1,256]{2,1,0:T(1,128)} %copy.322), calls=%async_computation.4 | async-start | bytes 65536 | tf_op jit(solution)/shard_map/all_to_all | solution.py:674
  40.5 35.8 %all-to-all-start.5 = ((bf16[16,32,768]{2,1,0:T(8,128)(2,1)}), bf16[16,32,768]{2,1,0:T(8,128)(2,1)}, u32[]{:S(2)}, u32[]{:S(2)}) async-start(bf16[16,32,768]{2,1,0:T(8,128)(2,1)} %broadcast_select_fusion.1), calls=%async_computation.5 | async-start | bytes 1572864 | tf_op jit(solution)/shard_map/all_to_all | solution.py:674
  44.8 250.9 %all-gather.7.cloned.1.call-start = ((), (), s32[]{:S(2)}) async-start(), calls=%async_computation.19 | async-start | bytes 6488064 | tf_op jit(solution)/shard_map/all_gather | solution.py:847
  157.3 19.4 %all-to-all-start.6 = ((bf16[4,64,768]{2,1,0:T(8,128)(2,1)}), bf16[4,64,768]{2,1,0:T(8,128)(2,1)S(1)}, u32[]{:S(2)}, u32[]{:S(2)}) async-start(bf16[4,64,768]{2,1,0:T(8,128)(2,1)} %broadcast_in_dim.352), calls=%async_computation.6 | async-start | bytes 786432 | tf_op jit(solution)/shard_map/all_to_all | solution.py:674
  177.6 17.6 %all-to-all-start.7 = ((bf16[2,256,768]{2,1,0:T(8,128)(2,1)}), bf16[2,256,768]{2,1,0:T(8,128)(2,1)}, u32[]{:S(2)}, u32[]{:S(2)}) async-start(bf16[2,256,768]{2,1,0:T(8,128)(2,1)} %broadcast_in_dim.354), calls=%async_computation.7 | async-start | bytes 1572864 | tf_op jit(solution)/shard_map/all_to_all | solution.py:674
  209.0 13.4 %all-to-all-start.9 = ((f32[16,2,1024]{2,1,0:T(2,128)}), f32[16,2,1024]{2,1,0:T(2,128)S(1)}, u32[]{:S(2)}, u32[]{:S(2)}) async-start(f32[16,2,1024]{2,1,0:T(2,128)} %broadcast_in_dim.357), calls=%async_computation.9 | async-start | bytes 262144 | tf_op jit(solution)/shard_map/all_to_all | solution.py:674
  213.1 161.7 %all-gather.9.cloned.1.call-start = ((), (), s32[]{:S(2)}) async-start(), calls=%async_computation.20 | async-start | bytes 1966080 | tf_op jit(solution)/shard_map/all_gather | solution.py:848
  231.1 3.8 collective-permute-start.1
  240.8 29.8 %collective-permute-start.2 = (f32[256,768]{1,0:T(8,128)}, f32[256,768]{1,0:T(8,128)S(1)}, u32[]{:S(2)}, u32[]{:S(2)}) collective-permute-start(f32[256,768]{1,0:T(8,128)} %constant_dynamic-slice_fusion.1), channel_id=1, source_target_pairs={{0,2},{2,0},{1,3},{3,1},{4,6},{6,4},{5,7},{7,5},{8,10},{10,8},{9,1... | collective-permute-start | bytes 2359304 | tf_op jit(solution)/shard_map/ppermute | solution.py:872
  243.3 27.5 %all-to-all-start.10 = ((bf16[32,64,96]{2,1,0:T(8,128)(2,1)}), bf16[32,64,96]{2,1,0:T(8,128)(2,1)S(1)}, u32[]{:S(2)}, u32[]{:S(2)}) async-start(bf16[32,64,96]{2,1,0:T(8,128)(2,1)} %bitcast.128), calls=%async_computation.10 | async-start | bytes 1048576 | tf_op jit(solution)/shard_map/all_to_all | solution.py:674
  246.5 131.0 %all-gather.11.cloned.1.call-start = ((), (), s32[]{:S(2)}) async-start(), calls=%async_computation.21 | async-start | bytes 3244032 | tf_op jit(solution)/shard_map/all_gather | solution.py:910
  246.9 23.7 %copy-start.10 = (f32[512,768]{1,0:T(8,128)S(1)}, f32[512,768]{1,0:T(8,128)}, u32[]{:S(2)}) copy-start(f32[512,768]{1,0:T(8,128)} %copy-done.9) | copy-start | bytes 4718596
  270.9 24.9 %copy-start.16 = (bf16[32,64,96]{2,1,0:T(8,128)(2,1)}, bf16[32,64,96]{2,1,0:T(8,128)(2,1)S(1)}, u32[]{:S(2)}) copy-start(bf16[32,64,96]{2,1,0:T(8,128)(2,1)S(1)} %all-to-all-done.10) | copy-start | bytes 1179652
  321.0 23.4 %all-to-all-start.12 = ((bf16[32,64,120]{2,1,0:T(8,128)(2,1)}), bf16[32,64,120]{2,1,0:T(8,128)(2,1)}, u32[]{:S(2)}, u32[]{:S(2)}) async-start(bf16[32,64,120]{2,1,0:T(8,128)(2,1)} %maximum_bitcast_fusion.1), calls=%async_computation.12 | async-start | bytes 1048576 | tf_op jit(solution)/shard_map/all_to_all | solution.py:674
  335.7 17.0 %copy-start.30 = (pred[16,32]{1,0:T(8,128)(4,1)S(1)}, pred[16,32]{1,0:T(8,128)(4,1)}, u32[]{:S(2)}) copy-start(pred[16,32]{1,0:T(8,128)(4,1)} %broadcast_and_fusion) | copy-start | bytes 1540
  345.8 17.7 %all-to-all-start.13 = ((bf16[4,288,384]{2,1,0:T(8,128)(2,1)}), bf16[4,288,384]{2,1,0:T(8,128)(2,1)S(1)}, u32[]{:S(2)}, u32[]{:S(2)}) async-start(bf16[4,288,384]{2,1,0:T(8,128)(2,1)} %copy.335), calls=%async_computation.13 | async-start | bytes 1769472 | tf_op jit(solution)/shard_map/all_to_all | solution.py:674
  363.5 23.4 %all-to-all-start.14 = ((bf16[16,32,768]{2,1,0:T(8,128)(2,1)}), bf16[16,32,768]{2,1,0:T(8,128)(2,1)S(1)}, u32[]{:S(2)}, u32[]{:S(2)}) async-start(bf16[16,32,768]{2,1,0:T(8,128)(2,1)} %select_convert_fusion), calls=%async_computation.14 | async-start | bytes 1572864 | tf_op jit(solution)/shard_map/all_to_all | solution.py:674
  387.8 109.6 %all-to-all-start.15 = ((bf16[32,24,1062]{2,1,0:T(8,128)(2,1)}), bf16[32,24,1062]{2,1,0:T(8,128)(2,1)S(1)}, u32[]{:S(2)}, u32[]{:S(2)}) async-start(bf16[32,24,1062]{2,1,0:T(8,128)(2,1)} %concatenate.95), calls=%async_computation.15 | async-start | bytes 3538944 | tf_op jit(solution)/shard_map/all_to_all | solution.py:674
  393.2 111.6 %collective-permute-start.3 = (bf16[1920,768]{1,0:T(8,128)(2,1)}, bf16[1920,768]{1,0:T(8,128)(2,1)}, u32[]{:S(2)}, u32[]{:S(2)}) collective-permute-start(bf16[1920,768]{1,0:T(8,128)(2,1)} %convolution_convert_fusion.1.refs_0_), channel_id=1, source_target_pairs={{0,16},{16,0},{1,17},{17,1},{2,18},{18,2},{3,19},{19,3},{4,20},{20... | collective-permute-start | bytes 8847368 | tf_op jit(solution)/shard_map/ppermute | solution.py:889
  401.9 93.2 %collective-permute-start.4 = (bf16[512,768]{1,0:T(8,128)(2,1)}, bf16[512,768]{1,0:T(8,128)(2,1)S(1)}, u32[]{:S(2)}, u32[]{:S(2)}) collective-permute-start(bf16[512,768]{1,0:T(8,128)(2,1)} %bitcast.49), channel_id=1, source_target_pairs={{0,16},{16,0},{1,17},{17,1},{2,18},{18,2},{3,19},{19,3},{4,20},{20... | collective-permute-start | bytes 2359304 | tf_op jit(solution)/shard_map/ppermute | solution.py:955
  519.9 12.0 %all-to-all-start.16 = ((f32[32,1,2]{2,1,0:T(1,128)}), f32[32,1,2]{2,1,0:T(1,128)S(1)}, u32[]{:S(2)}, u32[]{:S(2)}) async-start(f32[32,1,2]{2,1,0:T(1,128)} %copy.344), calls=%async_computation.16 | async-start | bytes 32768 | tf_op jit(solution)/shard_map/all_to_all | solution.py:674
  547.8 15.2 %all-to-all-start.17 = ((f32[32,1,12]{2,1,0:T(1,128)}), f32[32,1,12]{2,1,0:T(1,128)S(1)}, u32[]{:S(2)}, u32[]{:S(2)}) async-start(f32[32,1,12]{2,1,0:T(1,128)} %bitcast.74), calls=%async_computation.17 | async-start | bytes 32768 | tf_op jit(solution)/shard_map/all_to_all | solution.py:674
  (37 other events, 221.8 us)
Sparse Core Ops, SparseCore 0:
  11.5 123.8 all-gather.4
  155.7 73.9 all-gather.6
  231.4 26.5 all-gather.8
  303.5 61.4 all-gather.10

commit v6 on v5

--- a/solution.py
+++ b/solution.py
@@ -471,12 +471,10 @@
 
 
 def adam_direction(weight_arr, new_first, new_second):
-    return (
-        new_first
-        / (1.0 - beta_first**STEP)
-        / (jnp.sqrt(new_second / (1.0 - beta_second**STEP)) + adam_eps)
-        + weight_decay * weight_arr
-    )
+    first_scale, second_scale = 1.0 / (1.0 - beta_first**STEP), 1.0 / (1.0 - beta_second**STEP)
+    return (new_first * first_scale) / (
+        jnp.sqrt(new_second * second_scale) + adam_eps
+    ) + weight_decay * weight_arr
 
 
 def adam_moments(weight_arr, first_mom, second_mom, gradient, factor):
@@ -486,13 +484,13 @@
     return (new_first, new_second, adam_direction(weight_arr, new_first, new_second))
 
 
-def row_block(count):
-    return 240 if count % 240 == 0 else count
+def row_block(count, most=240):
+    return most if count % most == 0 else count
 
 
 def lookup_kernel(parts, *refs):
+    step = pl.program_id(0)
     head_refs, (asked_ref, given_ref, side_ref, grad_ref, square_ref) = refs[:parts], refs[parts:]
-    step = pl.program_id(0)
     rows, width = grad_ref.shape
     base = step * rows
     row_hot = asked_ref[...] == base + lax.broadcasted_iota(
@@ -512,15 +510,18 @@
     square_ref[...] += jnp.sum(jnp.where(own, grad * grad, 0.0), axis=0, keepdims=True)
 
 
-def lookup_grad(heads, asked_rows, given, sides):
-    vrows, width = heads[0].shape
-    rows = row_block(vrows)
+def lookup_grad(heads, parts, asked_rows, given, sides):
+    vrows, width = heads.shape[0] // parts, heads.shape[1]
+    rows = vrows // 4
     block = pl.BlockSpec((rows, width), lambda step: (step, 0))
     whole_spec = lambda array: pl.BlockSpec(array.shape, lambda step: (0, 0))
     return pl.pallas_call(
-        lambda *refs: lookup_kernel(len(heads), *refs),
-        grid=(vrows // rows,),
-        in_specs=[block] * len(heads)
+        lambda *refs: lookup_kernel(parts, *refs),
+        grid=(4,),
+        in_specs=[
+            pl.BlockSpec((rows, width), lambda step, part=part: (4 * part + step, 0))
+            for part in range(parts)
+        ]
         + [
             whole_spec(asked_rows),
             whole_spec(given),
@@ -533,7 +534,7 @@
         ],
         cost_estimate=pl.CostEstimate(flops=0, bytes_accessed=0, transcendentals=0),
         name="table_gradient",
-    )(*heads, asked_rows, given, sides)
+    )(*[heads] * parts, asked_rows, given, sides)
 
 
 def full_sum(values):
@@ -559,16 +560,6 @@
     def _():
         sums_ref[...] = jnp.zeros_like(sums_ref)
         norms_ref[...] = jnp.zeros_like(norms_ref)
-        for part in range(3):
-            weight_arr, first_mom, second_mom, gradient = (ref[part] for ref in layer_refs)
-            first, second, direction = adam_moments(
-                weight_arr, first_mom, second_mom, gradient, factor
-            )
-            for ref, value in zip(layer_out, (first, second, direction)):
-                ref[part] = value
-            norms_ref[pl.ds(1 + part, 1), :] = pair_row(
-                full_sum(weight_arr * weight_arr), full_sum(direction * direction)
-            )
         for row, group_refs, outs in ((4, position_refs, position_out), (5, small_refs, small_out)):
             weight_arr = group_refs[0][...]
             first, second, direction = adam_moments(
@@ -580,6 +571,18 @@
                 full_sum(weight_arr * weight_arr), full_sum(direction * direction)
             )
 
+    @pl.when(step < 3)
+    def _():
+        weight_arr, first_mom, second_mom, gradient = (ref[0] for ref in layer_refs)
+        first, second, direction = adam_moments(
+            weight_arr, first_mom, second_mom, gradient, factor
+        )
+        for ref, value in zip(layer_out, (first, second, direction)):
+            ref[0] = value
+        norms_ref[pl.ds(1 + step, 1), :] = pair_row(
+            full_sum(weight_arr * weight_arr), full_sum(direction * direction)
+        )
+
     weight_arr = table_refs[0][...]
     _, _, direction = adam_moments(
         weight_arr, table_refs[1][...], table_refs[2][...], table_refs[3][...], factor
@@ -596,7 +599,12 @@
 
 def update_norms(totals, table, layer, position, small, split, dp_index):
     vrows, width = table[0].shape
-    rows = row_block(split)
+    rows = row_block(split, 240)
+    if split // rows < 3:
+        rows = split // 3
+    one_part = pl.BlockSpec(
+        (1,) + layer[0].shape[1:], lambda step, offset: (jnp.minimum(step, 2), 0, 0)
+    )
     fixed = lambda array: pl.BlockSpec(
         array.shape, lambda step, offset, rank=array.ndim: (0,) * rank
     )
@@ -613,8 +621,11 @@
         grid_spec=pltpu.PrefetchScalarGridSpec(
             num_scalar_prefetch=1,
             grid=(split // rows,),
-            in_specs=[fixed(totals)] + [part] * 4 + [fixed(array) for array in groups],
-            out_specs=[fixed(norms)] + [fixed(out) for out in outs],
+            in_specs=[fixed(totals)]
+            + [part] * 4
+            + [one_part] * 4
+            + [fixed(array) for array in groups[4:]],
+            out_specs=[fixed(norms)] + [one_part] * 3 + [fixed(out) for out in outs[3:]],
             scratch_shapes=[pltpu.VMEM((8, width), single)],
         ),
         out_shape=[norms] + outs,
@@ -639,10 +650,15 @@
     direction = adam_direction(weight_arr, first_ref[...], second_ref[...])
     next_ref[...] = weight_arr - rate(0) * direction
 
-    @pl.when(pl.program_id(0) == 0)
-    def _():
-        for part in range(3):
-            layer_next_ref[part] = layer_ref[part] - rate(1 + part) * layer_dir_ref[part]
+    step = pl.program_id(0)
+    for part in range(3):
+
+        @pl.when(step == part)
+        def _():
+            layer_next_ref[0] = layer_ref[0] - rate(1 + part) * layer_dir_ref[0]
+
+    @pl.when(step == 0)
+    def _():
         position_next_ref[...] = position_ref[...] - rate(4) * position_dir_ref[...]
         small_next_ref[...] = small_ref[...] - rate(5) * small_dir_ref[...]
 
@@ -652,12 +668,16 @@
     rows = row_block(vrows)
     fixed = lambda array: pl.BlockSpec(array.shape, lambda step, rank=array.ndim: (0,) * rank)
     block = pl.BlockSpec((rows, width), lambda step: (step, 0))
+    one_part = pl.BlockSpec((1,) + groups[0].shape[1:], lambda step: (jnp.minimum(step, 2), 0, 0))
     outs = [jax.ShapeDtypeStruct(array.shape, single) for array in groups[::2]]
     return pl.pallas_call(
         final_kernel,
         grid=(vrows // rows,),
-        in_specs=[fixed(pairs)] + [block] * 3 + [fixed(array) for array in groups],
-        out_specs=[block] + [fixed(out) for out in outs],
+        in_specs=[fixed(pairs)]
+        + [block] * 3
+        + [one_part] * 2
+        + [fixed(array) for array in groups[2:]],
+        out_specs=[block, one_part] + [fixed(out) for out in outs[1:]],
         out_shape=[jax.ShapeDtypeStruct((vrows, width), single)] + outs,
         cost_estimate=pl.CostEstimate(flops=0, bytes_accessed=0, transcendentals=0),
         name="final_update",
@@ -688,6 +708,12 @@
 
 def side_by_side(blocks):
     return blocks.transpose(1, 0, 2).reshape(blocks.shape[1], -1)
+
+
+def after(values, *waits):
+    for wait in waits:
+        values = values + (wait.reshape(-1)[0] > 3.395e38).astype(values.dtype)
+    return values
 
 
 def masked_total(mask, values):
@@ -884,18 +910,21 @@
         "mid", lambda side: lax.dynamic_slice_in_dim(d_half, side * quarter, quarter, 0)
     )
     grad_head = rows_dot(d_logits, group_rows)
-    if dp_devs == 2:
-        head_b = grad_head.astype(bfloat)
-        other_b = lax.ppermute(head_b, "dp", [(0, 1), (1, 0)])
-        d_output, head_b = lax.optimization_barrier((d_output, head_b))
-        heads = (head_b, other_b)
-    else:
-        heads = (lax.psum(grad_head, "dp"),)
+    head_b = grad_head.astype(bfloat)
+    d_output, head_b = lax.optimization_barrier((d_output, head_b))
+    heads = lax.all_gather(head_b, "dp", axis=0, tiled=True)
     d_output = exchange(d_output.reshape(outer, CAP, width), "hi")
     if few:
         d_output, kept_all = lax.optimization_barrier((d_output, kept_all))
     d_branch, d_hidden, d_pre, d_attend, sums_feed = feed_backward(
-        d_output, end_normed, end_inverse, hidden, small_full, mid_normed, mid_inverse, shard
+        d_output,
+        end_normed,
+        end_inverse,
+        hidden,
+        small_full,
+        mid_normed,
+        mid_inverse,
+        shard,
     )
     if few:
         wide = feed // devices
@@ -963,8 +992,8 @@
     split = vrows // dp_devs
     sides = lax.axis_index("dp") * split + jnp.array([0, split])
 
-    def into_rows(heads, asked_rows, given, sides):
-        return lookup_grad(heads, both_groups(asked_rows).reshape(1, -1), given, sides)
+    def into_rows(heads, parts, asked_rows, given, sides):
+        return lookup_grad(heads, parts, both_groups(asked_rows).reshape(1, -1), given, sides)
 
     last = (jnp.arange(BUCKET) == BUCKET - 1)[None, :]
     left_row = jnp.where(lax.axis_index(VOC) == mask_owner, MASK_ID - first_row, -1)
@@ -991,10 +1020,9 @@
             [grad_pair, grad_ask, grad_up, grad_down, grad_out, shared_grad], axis=1
         )
         results = results.astype(bfloat)
-        beyond = (jnp.max(results[0].astype(single)) > 3.395e38).astype(bfloat)
-        given = given + beyond
+        given = after(given, jnp.max(results[0].astype(single)))
         results = exchange.rows(results, devices).astype(single)
-        sides = sides + (results[0, 0, 0] > 3.395e38).astype(jnp.int32)
+        sides = after(sides, results)
         pieces = 3 * piece
         attn = jnp.sum(
             results[..., :pieces].reshape(dp_devs * outer, near, share, pieces), axis=0
@@ -1044,7 +1072,7 @@
         position_grad, small_grad = shared_grad[:length], shared_grad[length:]
         part_square = jnp.sum(layer_grad * layer_grad) + jnp.sum(shared_grad * shared_grad)
     table_grad, table_square_sum = into_rows(
-        heads, jnp.where(last, left_row, asked), of_both(given), sides
+        heads, dp_devs, jnp.where(last, left_row, asked), of_both(given), sides
     )
 
     def more_grads(state):
@@ -1055,7 +1083,7 @@
             wanted_t.reshape(devices, BUCKET), ALL, 0, 0, tiled=True
         )
         given_t = of_both(give(hot_t, False, plain_exchange))
-        return (turn + 1,) + tuple(into_rows((grads,), asked_t, given_t, sides))
+        return (turn + 1,) + tuple(into_rows(grads, 1, asked_t, given_t, sides))
 
     _, table_grad, table_square_sum = lax.while_loop(
         lambda state: state[0] < rounds,

time: 599 us -> 572 us (0.955)
  waiting for transfers between devices: 254 us -> 224 us
    ppermute x1, waiting for transfers between devices: 83 us -> 42 us  [of_both(): return jnp.concatenate([rows, lax.ppermute(rows, 'dp', [(0, 1), (1, 0)])])]
    all_gather x0 -> x1, waiting for transfers between devices: none -> 10.1 us  [on_device(): heads = lax.all_gather(head_b, 'dp', axis=0, tiled=True)]
  transfers between devices with their start and end apart: 20 -> 20, of which waited for: 14 -> 14; matrix products, arithmetic and copies ran while one was open for 22% -> 24% of each run, Pallas kernels for 4% -> 4%
where the time goes in v6:
time: 572 us; the launch traced here: 563 us
  waiting for transfers between devices  224 us (39%)
  Pallas kernels  76 us (13%)
  other arithmetic  59.3 us (10%)
  local copies, waits for them, and re-layouts  57.2 us (10%)
  starting transfers between devices  54.8 us (10%)
  matrix products  36.6 us (6%)
  blocking collectives  29.8 us (5%)
  between operations  25 us (4%)
    all_to_all x12, waiting for transfers between devices, __call__(): self.last = lax.all_to_all(values, axes, 0, 0, tiled=True)  95 us
    all_gather x1, waiting for transfers between devices, on_device(): shard = lax.all_gather(shard.astype(bfloat), ALL, axis=0, tiled=True)  56.7 us
    all_to_all x12, starting transfers between devices, __call__(): self.last = lax.all_to_all(values, axes, 0, 0, tiled=True)  52 us
    ppermute x1, waiting for transfers between devices, of_both(): return jnp.concatenate([rows, lax.ppermute(rows, 'dp', [(0, 1), (1, 0)])])  42 us
    pallas_call x5, Pallas kernels, kernel_call(): pl.pallas_call(body, grid=(steps,), in_specs=[spec(array.shape, block, in...  41.7 us
    all_to_all x2, blocking collectives, __call__(): self.last = lax.all_to_all(values, axes, 0, 0, tiled=True)  29.8 us
    dot_general x7, matrix products, rows_dot(): lax.dot_general(left_op, right_op, (((0,), (0,)), ((), ())), preferred_el...  25 us
    ppermute x2, waiting for transfers between devices, swapped(): theirs = lax.ppermute(part(1 - side), axis, [(0, 1), (1, 0)])  20.5 us
  transfers between devices with their start and end apart: 20, of which 14 were waited for; matrix products, arithmetic and copies ran while one was open for 24% of the time, Pallas kernels for 4%

profile of v6, /device:TPU:0, one launch (start us, length us, event | category | flops | bytes accessed | tf_op | source)
XLA Modules:
  0.0 563.2 jit_solution(4336877079367744369)
XLA Ops:
  20.3 7.3 %all-to-all-start.4 = ((s32[32,1,256]{2,1,0:T(1,128)}), s32[32,1,256]{2,1,0:T(1,128)S(1)}, u32[]{:S(2)}, u32[]{:S(2)}) async-start(s32[32,1,256]{2,1,0:T(1,128)} %copy.324), calls=%async_computation.4 | async-start | bytes 65536 | tf_op jit(solution)/shard_map/all_to_all | solution.py:694
  27.6 7.3 %all-to-all-done.4 = s32[32,1,256]{2,1,0:T(1,128)S(1)} async-done(((s32[32,1,256]{2,1,0:T(1,128)}), s32[32,1,256]{2,1,0:T(1,128)S(1)}, u32[]{:S(2)}, u32[]{:S(2)}) %all-to-all-start.4) | async-done | bytes 32800 | tf_op jit(solution)/shard_map/all_to_all | solution.py:694
  48.2 28.0 %all-to-all-done.5 = bf16[16,32,768]{2,1,0:T(8,128)(2,1)} async-done(((bf16[16,32,768]{2,1,0:T(8,128)(2,1)}), bf16[16,32,768]{2,1,0:T(8,128)(2,1)}, u32[]{:S(2)}, u32[]{:S(2)}) %all-to-all-start.5) | async-done | bytes 786464 | tf_op jit(solution)/shard_map/all_to_all | solution.py:694
  78.7 56.7 %all-gather.6.cloned.1.call-done.shared_ref.weight_ref.up_ref.down_ref = bf16[768,9600]{1,0:T(8,128)(2,1)} async-done(((bf16[24,9600]{1,0:T(8,128)(2,1)}), bf16[768,9600]{1,0:T(8,128)(2,1)}) %all-gather.6.cloned.1.call-update) | async-done | bytes 14745616 | tf_op jit(solution)/shard_map/all_gather | solution.py:788
  135.4 11.5 %attention_forward.1 = (bf16[256,768]{1,0:T(8,128)(2,1)}, bf16[256,768]{1,0:T(8,128)(2,1)}, bf16[64,768]{1,0:T(8,128)(2,1)}, bf16[64,768]{1,0:T(8,128)(2,1)}, f3...) custom-call(f32[256,768]{1,0:T(8,128)} %get-tuple-element.278.embed_, ...), custom_call_target="tpu_custom_call" | custom-call | flops 11010048 | bytes 73728 | tf_op jit(solution)/shard_map/attention_forward/pallas_call | solution.py:165
  146.9 7.1 %feed_forward.1 = (bf16[64,768]{1,0:T(8,128)(2,1)}, f32[64,3072]{1,0:T(8,128)}, bf16[64,3072]{1,0:T(8,128)(2,1)}, bf16[64,768]{1,0:T(8,128)(2,1)}, f32[64,768]{1,0:T(8,128)}, /*index=5*/f32[64,128]{1,0:T(8,128)}) custom-call(f32[64,768]{1,0:T(8,128)} %get-tuple-element.279.middle_ref, f32[14,768]{1,0:T(8,128)} %get-tuple-element.280.small_ref, ...), custom_call_target="tpu_custom_call" | custom-call | flops 9437184 | bytes 147456 | tf_op jit(solution)/shard_map/feed_forward/pallas_call | solution.py:165
  160.8 15.9 %all-to-all-done.6 = bf16[4,64,768]{2,1,0:T(8,128)(2,1)S(1)} async-done(((bf16[4,64,768]{2,1,0:T(8,128)(2,1)}), bf16[4,64,768]{2,1,0:T(8,128)(2,1)S(1)}, u32[]{:S(2)}, u32[]{:S(2)}) %all-to-all-start.6) | async-done | bytes 393248 | tf_op jit(solution)/shard_map/all_to_all | solution.py:694
  183.0 12.2 %all-to-all-done.7 = bf16[2,256,768]{2,1,0:T(8,128)(2,1)} async-done(((bf16[2,256,768]{2,1,0:T(8,128)(2,1)}), bf16[2,256,768]{2,1,0:T(8,128)(2,1)}, u32[]{:S(2)}, u32[]{:S(2)}) %all-to-all-start.7) | async-done | bytes 786464 | tf_op jit(solution)/shard_map/all_to_all | solution.py:694
  196.5 5.4 all_to_all.133
  213.7 9.1 %all-to-all-done.9 = f32[16,2,1024]{2,1,0:T(2,128)S(1)} async-done(((f32[16,2,1024]{2,1,0:T(2,128)}), f32[16,2,1024]{2,1,0:T(2,128)S(1)}, u32[]{:S(2)}, u32[]{:S(2)}) %all-to-all-start.9) | async-done | bytes 131104 | tf_op jit(solution)/shard_map/all_to_all | solution.py:694
  247.7 7.0 %convolution_convert_fusion.1 = bf16[1920,768]{1,0:T(8,128)(2,1)} fusion(bf16[1024,1920]{1,0:T(8,128)(2,1)} %copy-done.1, bf16[1024,768]{1,0:T(8,128)(2,1)S(1)} %bitcast.166), kind=kOutput, calls=%fused_computation.31 | convolution fusion | flops 3021373440 | bytes 8454144 | tf_op jit(solution)/shard_map/dot_general | solution.py:44
  254.7 16.8 %collective-permute-done.2 = f32[256,768]{1,0:T(8,128)S(1)} collective-permute-done((f32[256,768]{1,0:T(8,128)}, f32[256,768]{1,0:T(8,128)S(1)}, u32[]{:S(2)}, u32[]{:S(2)}) %collective-permute-start.2) | collective-permute-done | bytes 786464 | tf_op jit(solution)/shard_map/ppermute | solution.py:898
  272.8 24.3 %all_to_all.134.parts_ref = f32[4,64,768]{2,1,0:T(8,128)} all-to-all(f32[4,64,768]{2,1,0:T(8,128)S(1)} %bitcast.158), channel_id=1, replica_groups=mesh['dp'=2,'hi'=4,'mid'=2,'core'=2] {'hi'}, dimensions={0} | all-to-all | bytes 1572864 | tf_op jit(solution)/shard_map/all_to_all | solution.py:694
  297.1 7.6 %feed_backward.1 = (bf16[64,768]{1,0:T(8,128)(2,1)}, bf16[64,3072]{1,0:T(8,128)(2,1)}, f32[64,768]{1,0:T(8,128)}, bf16[64,768]{1,0:T(8,128)(2,1)}, f32[16,768]{1,0:T(8,128)}) custom-call(f32[4,64,768]{2,1,0:T(8,128)} %all_to_all.134.parts_ref, f32[64,768]{1,0:T(8,128)} %get-tuple-element.294.normed_ref, f32[64,128]{1,0:T(8,128)} %get-tuple-element.295.inverse_ref, ...), custom_call_target="tpu_custom_call" | custom-call | flops 9437184 | bytes 147456 | tf_op jit(solution)/shard_map/feed_backward/pallas_call | solution.py:165
  308.7 9.5 %attention_backward.1 = (bf16[64,768]{1,0:T(8,128)(2,1)}, bf16[256,768]{1,0:T(8,128)(2,1)}, bf16[256,768]{1,0:T(8,128)(2,1)}) custom-call(bf16[64,768]{1,0:T(8,128)(2,1)} %get-tuple-element.300.d_attend_ref, bf16[256,768]{1,0:T(8,128)(2,1)} %get-tuple-element.301.key_ref, bf16[256,768]{1,0:T(8,128)(2,1)} %get-tuple-element.302.value_ref, ...), custom_call_target="tpu_custom_call" | custom-call | flops 5111808 | bytes 18432 | tf_op jit(solution)/shard_map/attention_backward/pallas_call | solution.py:165
  327.3 6.0 %projection_backward.1 = (bf16[256,768]{1,0:T(8,128)(2,1)S(1)}, f32[256,768]{1,0:T(8,128)}, f32[8,768]{1,0:T(8,128)}) custom-call(f32[64,768]{1,0:T(8,128)} %get-tuple-element.299.d_pre_ref, bf16[64,768]{1,0:T(8,128)(2,1)} %get-tuple-element.304.d_query_ref, bf16[256,768]{1,0:T(8,128)(2,1)} %get-tuple-element.305.d_key_ref, ...), custom_call_target="tpu_custom_call" | custom-call | flops 11796480 | bytes 55296 | tf_op jit(solution)/shard_map/projection_backward/pallas_call | solution.py:165
  336.2 8.7 %all-to-all-done.12 = bf16[32,64,120]{2,1,0:T(8,128)(2,1)} async-done(((bf16[32,64,120]{2,1,0:T(8,128)(2,1)}), bf16[32,64,120]{2,1,0:T(8,128)(2,1)}, u32[]{:S(2)}, u32[]{:S(2)}) %all-to-all-start.12) | async-done | bytes 491552 | tf_op jit(solution)/shard_map/all_to_all | solution.py:694
  357.9 7.2 %all-to-all-done.13 = bf16[4,288,384]{2,1,0:T(8,128)(2,1)S(1)} async-done(((bf16[4,288,384]{2,1,0:T(8,128)(2,1)}), bf16[4,288,384]{2,1,0:T(8,128)(2,1)S(1)}, u32[]{:S(2)}, u32[]{:S(2)}) %all-to-all-start.13) | async-done | bytes 884768 | tf_op jit(solution)/shard_map/all_to_all | solution.py:694
  413.5 42.0 %collective-permute-done.3 = bf16[512,768]{1,0:T(8,128)(2,1)S(1)} collective-permute-done((bf16[512,768]{1,0:T(8,128)(2,1)}, bf16[512,768]{1,0:T(8,128)(2,1)S(1)}, u32[]{:S(2)}, u32[]{:S(2)}) %collective-permute-start.3) | collective-permute-done | bytes 786464 | tf_op jit(solution)/shard_map/ppermute | solution.py:984
  471.0 10.1 %all-gather.8.cloned.1.call-done.refs_0_.refs_1_ = bf16[3840,768]{1,0:T(8,128)(2,1)} async-done(((bf16[1920,768]{1,0:T(8,128)(2,1)}), bf16[3840,768]{1,0:T(8,128)(2,1)}) %all-gather.8.cloned.1.call-update) | async-done | bytes 5898256 | tf_op jit(solution)/shard_map/all_gather | solution.py:915
  481.1 8.1 %table_gradient.5 = (f32[1920,768]{1,0:T(8,128)}, f32[1,768]{1,0:T(1,128)}) custom-call(bf16[3840,768]{1,0:T(8,128)(2,1)} %all-gather.8.cloned.1.call-done.refs_0_.refs_1_, bf16[3840,768]{1,0:T(8,128)(2,1)} %all-gather.8.cloned.1.call-done.refs_0_.refs_1_, s32[1,1024]{1,0:T(1,128)} %reshape.457.refs_2_, bf16[1024,768]{1,0:T(8,128)(2,1)} %pad_maximum_fusion.1.refs_3_, ...), custom_call_target="tpu_custom_call" | custom-call | tf_op jit(solution)/shard_map/table_gradient/pallas_call | solution.py:518
  508.6 11.7 %update_norms.1 = (f32[8,128]{1,0:T(8,128)}, f32[3,24,3072]{2,1,0:T(8,128)}, f32[3,24,3072]{2,1,0:T(8,128)}, f32[3,24,3072]{2,1,0:T(8,128)}, f32[256,24]{1,0:T(8...) custom-call(s32[1]{0:T(128)} %bitcast.64.offset_ref, ...), custom_call_target="tpu_custom_call" | custom-call | tf_op jit(solution)/shard_map/update_norms/pallas_call | solution.py:619
  524.3 11.2 %fusion.5 = (f32[1920,768]{1,0:T(8,128)}, f32[1920,768]{1,0:T(8,128)}) fusion(f32[1920,768]{1,0:T(8,128)} %refs_3_.1, f32[1920,768]{1,0:T(8,128)} %get-tuple-element.328.refs_4_, f32[]{:T(128)S(6)} %min.3, f32[1920,768]{1,0:T(8,128)} %refs_2_.1), kind=kLoop, calls=%fused_computation.29 | loop fusion | flops 11796480 | bytes 29491204 | tf_op jit(solution)/shard_map/add | solution.py:483
  537.5 14.4 %final_update.1 = (f32[1920,768]{1,0:T(8,128)}, f32[3,24,3072]{2,1,0:T(8,128)}, f32[256,24]{1,0:T(8,128)}, f32[14,24]{1,0:T(8,128)}) custom-call(f32[32,12]{1,0:T(8,128)} %bitcast.184, f32[1920,768]{1,0:T(8,128)} %weight_ref.1, f32[1920,768]{1,0:T(8,128)} %get-tuple-element.569.first_ref, f32[1920,768]{1,0:T(8,128)} %get-tuple-element.568.second_ref, ...), custom_call_target="tpu_custom_call" | custom-call | tf_op jit(solution)/shard_map/final_update/pallas_call | solution.py:673
  (288 shorter events, 192.9 us)
Async XLA Ops:
  7.2 128.2 %all-gather.6.cloned.1.call-start = ((), (), s32[]{:S(2)}) async-start(), calls=%async_computation.18 | async-start | bytes 15206400 | tf_op jit(solution)/shard_map/all_gather | solution.py:788
  13.3 62.9 %copy-start.26 = (s32[1,256]{1,0:T(1,128)}, s32[1,256]{1,0:T(1,128)S(1)}, u32[]{:S(2)}) copy-start(s32[1,256]{1,0:T(1,128)S(1)} %and_select_fusion.2) | copy-start | bytes 3076
  20.3 14.6 %all-to-all-start.4 = ((s32[32,1,256]{2,1,0:T(1,128)}), s32[32,1,256]{2,1,0:T(1,128)S(1)}, u32[]{:S(2)}, u32[]{:S(2)}) async-start(s32[32,1,256]{2,1,0:T(1,128)} %copy.324), calls=%async_computation.4 | async-start | bytes 65536 | tf_op jit(solution)/shard_map/all_to_all | solution.py:694
  40.5 35.8 %all-to-all-start.5 = ((bf16[16,32,768]{2,1,0:T(8,128)(2,1)}), bf16[16,32,768]{2,1,0:T(8,128)(2,1)}, u32[]{:S(2)}, u32[]{:S(2)}) async-start(bf16[16,32,768]{2,1,0:T(8,128)(2,1)} %broadcast_select_fusion.1), calls=%async_computation.5 | async-start | bytes 1572864 | tf_op jit(solution)/shard_map/all_to_all | solution.py:694
  44.8 252.3 %all-gather.10.cloned.1.call-start = ((), (), s32[]{:S(2)}) async-start(), calls=%async_computation.20 | async-start | bytes 6488064 | tf_op jit(solution)/shard_map/all_gather | solution.py:873
  157.3 19.4 %all-to-all-start.6 = ((bf16[4,64,768]{2,1,0:T(8,128)(2,1)}), bf16[4,64,768]{2,1,0:T(8,128)(2,1)S(1)}, u32[]{:S(2)}, u32[]{:S(2)}) async-start(bf16[4,64,768]{2,1,0:T(8,128)(2,1)} %broadcast_in_dim.352), calls=%async_computation.6 | async-start | bytes 786432 | tf_op jit(solution)/shard_map/all_to_all | solution.py:694
  177.6 17.6 %all-to-all-start.7 = ((bf16[2,256,768]{2,1,0:T(8,128)(2,1)}), bf16[2,256,768]{2,1,0:T(8,128)(2,1)}, u32[]{:S(2)}, u32[]{:S(2)}) async-start(bf16[2,256,768]{2,1,0:T(8,128)(2,1)} %broadcast_in_dim.354), calls=%async_computation.7 | async-start | bytes 1572864 | tf_op jit(solution)/shard_map/all_to_all | solution.py:694
  209.2 13.6 %all-to-all-start.9 = ((f32[16,2,1024]{2,1,0:T(2,128)}), f32[16,2,1024]{2,1,0:T(2,128)S(1)}, u32[]{:S(2)}, u32[]{:S(2)}) async-start(f32[16,2,1024]{2,1,0:T(2,128)} %broadcast_in_dim.357), calls=%async_computation.9 | async-start | bytes 262144 | tf_op jit(solution)/shard_map/all_to_all | solution.py:694
  213.4 163.1 %all-gather.12.cloned.1.call-start = ((), (), s32[]{:S(2)}) async-start(), calls=%async_computation.21 | async-start | bytes 1966080 | tf_op jit(solution)/shard_map/all_gather | solution.py:874
  213.6 14.9 %copy-start.23 = (f32[16,64]{1,0:T(8,128)}, f32[16,64]{1,0:T(8,128)S(1)}, u32[]{:S(2)}) copy-start(f32[16,64]{1,0:T(8,128)S(1)} %fusion.51) | copy-start | bytes 12292
  231.5 3.8 collective-permute-start.1
  241.2 30.3 %collective-permute-start.2 = (f32[256,768]{1,0:T(8,128)}, f32[256,768]{1,0:T(8,128)S(1)}, u32[]{:S(2)}, u32[]{:S(2)}) collective-permute-start(f32[256,768]{1,0:T(8,128)} %constant_dynamic-slice_fusion.1), channel_id=1, source_target_pairs={{0,2},{2,0},{1,3},{3,1},{4,6},{6,4},{5,7},{7,5},{8,10},{10,8},{9,1... | collective-permute-start | bytes 2359304 | tf_op jit(solution)/shard_map/ppermute | solution.py:898
  243.5 29.3 %all-to-all-start.10 = ((bf16[32,64,96]{2,1,0:T(8,128)(2,1)}), bf16[32,64,96]{2,1,0:T(8,128)(2,1)S(1)}, u32[]{:S(2)}, u32[]{:S(2)}) async-start(bf16[32,64,96]{2,1,0:T(8,128)(2,1)} %bitcast.128), calls=%async_computation.10 | async-start | bytes 1048576 | tf_op jit(solution)/shard_map/all_to_all | solution.py:694
  247.5 132.0 %all-gather.14.cloned.1.call-start = ((), (), s32[]{:S(2)}) async-start(), calls=%async_computation.22 | async-start | bytes 3244032 | tf_op jit(solution)/shard_map/all_gather | solution.py:939
  272.8 24.3 %copy-start.15 = (bf16[32,64,96]{2,1,0:T(8,128)(2,1)}, bf16[32,64,96]{2,1,0:T(8,128)(2,1)S(1)}, u32[]{:S(2)}) copy-start(bf16[32,64,96]{2,1,0:T(8,128)(2,1)S(1)} %all-to-all-done.10) | copy-start | bytes 1179652
  304.8 176.3 %all-gather.8.cloned.1.call-start = ((), (), s32[]{:S(2)}) async-start(), calls=%async_computation.19 | async-start | bytes 8847360 | tf_op jit(solution)/shard_map/all_gather | solution.py:915
  321.5 23.4 %all-to-all-start.12 = ((bf16[32,64,120]{2,1,0:T(8,128)(2,1)}), bf16[32,64,120]{2,1,0:T(8,128)(2,1)}, u32[]{:S(2)}, u32[]{:S(2)}) async-start(bf16[32,64,120]{2,1,0:T(8,128)(2,1)} %maximum_bitcast_fusion.1), calls=%async_computation.12 | async-start | bytes 1048576 | tf_op jit(solution)/shard_map/all_to_all | solution.py:694
  336.2 16.9 %copy-start.30 = (pred[16,32]{1,0:T(8,128)(4,1)S(1)}, pred[16,32]{1,0:T(8,128)(4,1)}, u32[]{:S(2)}) copy-start(pred[16,32]{1,0:T(8,128)(4,1)} %broadcast_and_fusion) | copy-start | bytes 1540
  346.2 18.8 %all-to-all-start.13 = ((bf16[4,288,384]{2,1,0:T(8,128)(2,1)}), bf16[4,288,384]{2,1,0:T(8,128)(2,1)S(1)}, u32[]{:S(2)}, u32[]{:S(2)}) async-start(bf16[4,288,384]{2,1,0:T(8,128)(2,1)} %copy.337), calls=%async_computation.13 | async-start | bytes 1769472 | tf_op jit(solution)/shard_map/all_to_all | solution.py:694
  365.0 23.6 %all-to-all-start.14 = ((bf16[16,32,768]{2,1,0:T(8,128)(2,1)}), bf16[16,32,768]{2,1,0:T(8,128)(2,1)S(1)}, u32[]{:S(2)}, u32[]{:S(2)}) async-start(bf16[16,32,768]{2,1,0:T(8,128)(2,1)} %select_convert_fusion), calls=%async_computation.14 | async-start | bytes 1572864 | tf_op jit(solution)/shard_map/all_to_all | solution.py:694
  389.5 68.3 %all-to-all-start.15 = ((bf16[32,24,1062]{2,1,0:T(8,128)(2,1)}), bf16[32,24,1062]{2,1,0:T(8,128)(2,1)S(1)}, u32[]{:S(2)}, u32[]{:S(2)}) async-start(bf16[32,24,1062]{2,1,0:T(8,128)(2,1)} %concatenate.95), calls=%async_computation.15 | async-start | bytes 3538944 | tf_op jit(solution)/shard_map/all_to_all | solution.py:694
  401.9 53.6 %collective-permute-start.3 = (bf16[512,768]{1,0:T(8,128)(2,1)}, bf16[512,768]{1,0:T(8,128)(2,1)S(1)}, u32[]{:S(2)}, u32[]{:S(2)}) collective-permute-start(bf16[512,768]{1,0:T(8,128)(2,1)} %bitcast.49), channel_id=1, source_target_pairs={{0,16},{16,0},{1,17},{17,1},{2,18},{18,2},{3,19},{19,3},{4,20},{20... | collective-permute-start | bytes 2359304 | tf_op jit(solution)/shard_map/ppermute | solution.py:984
  494.8 11.7 %all-to-all-start.16 = ((f32[32,1,2]{2,1,0:T(1,128)}), f32[32,1,2]{2,1,0:T(1,128)S(1)}, u32[]{:S(2)}, u32[]{:S(2)}) async-start(f32[32,1,2]{2,1,0:T(1,128)} %copy.346), calls=%async_computation.16 | async-start | bytes 32768 | tf_op jit(solution)/shard_map/all_to_all | solution.py:694
  521.7 15.2 %all-to-all-start.17 = ((f32[32,1,12]{2,1,0:T(1,128)}), f32[32,1,12]{2,1,0:T(1,128)S(1)}, u32[]{:S(2)}, u32[]{:S(2)}) async-start(f32[32,1,12]{2,1,0:T(1,128)} %bitcast.74), calls=%async_computation.17 | async-start | bytes 32768 | tf_op jit(solution)/shard_map/all_to_all | solution.py:694
  (37 other events, 219.6 us)
Sparse Core Ops, SparseCore 0:
  11.5 123.8 all-gather.5
  155.8 73.8 all-gather.9
  231.7 27.7 all-gather.11
  304.9 63.1 all-gather.13
  370.1 110.9 all-gather.7

commit v7 on v6

--- a/solution.py
+++ b/solution.py
@@ -160,6 +160,8 @@
     def spec(shape, block, index):
         if block is None:
             return pl.BlockSpec(shape, fixed(len(shape)))
+        if block == "any":
+            return pl.BlockSpec(memory_space=pl.ANY)
         return pl.BlockSpec(block, index)
 
     return pl.pallas_call(
@@ -402,7 +404,7 @@
 
 def project_back_kernel(
     d_pre_ref, d_query_ref, d_key_ref, d_value_ref, slot_ref, hidden_row_ref, small_ref,
-    normed_ref, inverse_ref, init_normed_ref, init_inverse_ref, weight_ref,
+    normed_ref, inverse_ref, init_normed_ref, init_inverse_ref, weight_ref, ahead_ref,
     embed_ref, position_ref, sums_ref, d_stream_ref, d_init_ref,
 ):
     step = pl.program_id(0)
@@ -446,7 +448,7 @@
 
 def project_backward(
     d_pre, d_query, d_key, d_value, slot_hot, hidden_rows, small_full,
-    normed, inverse, init_normed, init_inverse, weights,
+    normed, inverse, init_normed, init_inverse, weights, ahead,
 ):
     length, width = normed.shape
     slots = d_pre.shape[0]
@@ -459,7 +461,7 @@
         "projection_backward",
         3,
         [whole(array) for array in arrays]
-        + [(weights, (width, width), lambda step: (0, step))],
+        + [(weights, (width, width), lambda step: (0, step)), (ahead, "any", None)],
         [
             ((length, width), bfloat, None, None),
             ((length, width), single, None, None),
@@ -882,8 +884,6 @@
     row_total = jnp.sum(jnp.exp(logits - row_top[:, None]), axis=1)
     row_target = jnp.sum(jnp.where(target_hit, logits, 0.0), axis=1)
     stats = exchange.copies(jnp.stack([row_top, row_total]), VOC, owners)
-    if few:
-        active_mine = exchange.columns(active_b, ALL, devices)
     top_all = jnp.max(stats[:, 0], axis=0)
     total_all = jnp.sum(stats[:, 1] * jnp.exp(stats[:, 0] - top_all[None]), axis=0)
     log_total = top_all + jnp.log(total_all)
@@ -912,6 +912,8 @@
     grad_head = rows_dot(d_logits, group_rows)
     head_b = grad_head.astype(bfloat)
     d_output, head_b = lax.optimization_barrier((d_output, head_b))
+    if few:
+        head_b = after(head_b, stream_all)
     heads = lax.all_gather(head_b, "dp", axis=0, tiled=True)
     d_output = exchange(d_output.reshape(outer, CAP, width), "hi")
     if few:
@@ -962,6 +964,7 @@
         init_normed,
         init_inverse,
         shard,
+        heads,
     )
     grad_small = jnp.concatenate([sums_back[:5], sums_feed[:9]])
     mask_sum = sums_back[5]
@@ -1012,6 +1015,7 @@
         grad_pair = rows_dot(stream_all, pairs[:, :length].reshape(near * length, -1))
         grad_ask = rows_dot(init_all, asks.reshape(near * CAP, piece))
         share = width // devices
+        active_mine = exchange.columns(active_b, ALL, devices)
         grad_up = rows_dot(kept_all[:, width:], both[:, :wide])
         grad_out = rows_dot(kept_all[:, :width], both[:, wide:])
         grad_down = rows_dot(branch_all, active_mine)

time: 572 us -> 568 us (level)
  waiting for transfers between devices: 224 us -> 212 us
  local copies, waits for them, and re-layouts: 57.2 us -> 64.7 us
    ppermute x1, waiting for transfers between devices: 42 us -> 17.7 us  [of_both(): return jnp.concatenate([rows, lax.ppermute(rows, 'dp', [(0, 1), (1, 0)])])]
    all_gather x1, waiting for transfers between devices: 10.1 us -> 25.6 us  [on_device(): heads = lax.all_gather(head_b, 'dp', axis=0, tiled=True)]
    ppermute x2, waiting for transfers between devices: 20.5 us -> 9.65 us  [swapped(): theirs = lax.ppermute(part(1 - side), axis, [(0, 1), (1, 0)])]
    all_to_all x12, waiting for transfers between devices: 95 us -> 102 us  [__call__(): self.last = lax.all_to_all(values, axes, 0, 0, tiled=True)]
  transfers between devices with their start and end apart: 20 -> 20, of which waited for: 14 -> 15; matrix products, arithmetic and copies ran while one was open for 24% -> 23% of each run, Pallas kernels for 4% -> 5%
where the time goes in v7:
time: 568 us; the launch traced here: 559 us
  waiting for transfers between devices  212 us (37%)
  Pallas kernels  75.9 us (13%)
  local copies, waits for them, and re-layouts  64.7 us (11%)
  other arithmetic  61.3 us (11%)
  starting transfers between devices  55.8 us (10%)
  matrix products  35.6 us (6%)
  blocking collectives  28.1 us (5%)
  between operations  25.3 us (4%)
    all_to_all x12, waiting for transfers between devices, __call__(): self.last = lax.all_to_all(values, axes, 0, 0, tiled=True)  102 us
    all_gather x1, waiting for transfers between devices, on_device(): shard = lax.all_gather(shard.astype(bfloat), ALL, axis=0, tiled=True)  56.7 us
    all_to_all x12, starting transfers between devices, __call__(): self.last = lax.all_to_all(values, axes, 0, 0, tiled=True)  53.8 us
    pallas_call x5, Pallas kernels, kernel_call(): pl.pallas_call(body, grid=(steps,), in_specs=[spec(array.shape, block, in...  41.6 us
    all_to_all x2, blocking collectives, __call__(): self.last = lax.all_to_all(values, axes, 0, 0, tiled=True)  28.1 us
    all_gather x1, waiting for transfers between devices, on_device(): heads = lax.all_gather(head_b, 'dp', axis=0, tiled=True)  25.6 us
    dot_general x7, matrix products, rows_dot(): lax.dot_general(left_op, right_op, (((0,), (0,)), ((), ())), preferred_el...  24.9 us
    ppermute x1, waiting for transfers between devices, of_both(): return jnp.concatenate([rows, lax.ppermute(rows, 'dp', [(0, 1), (1, 0)])])  17.7 us
  transfers between devices with their start and end apart: 20, of which 15 were waited for; matrix products, arithmetic and copies ran while one was open for 23% of the time, Pallas kernels for 5%

profile of v7, /device:TPU:0, one launch (start us, length us, event | category | flops | bytes accessed | tf_op | source)
XLA Modules:
  0.0 558.5 jit_solution(16552169808003254688)
XLA Ops:
  20.3 7.3 %all-to-all-start.4 = ((s32[32,1,256]{2,1,0:T(1,128)}), s32[32,1,256]{2,1,0:T(1,128)S(1)}, u32[]{:S(2)}, u32[]{:S(2)}) async-start(s32[32,1,256]{2,1,0:T(1,128)} %copy.324), calls=%async_computation.4 | async-start | bytes 65536 | tf_op jit(solution)/shard_map/all_to_all | solution.py:696
  27.6 7.3 %all-to-all-done.4 = s32[32,1,256]{2,1,0:T(1,128)S(1)} async-done(((s32[32,1,256]{2,1,0:T(1,128)}), s32[32,1,256]{2,1,0:T(1,128)S(1)}, u32[]{:S(2)}, u32[]{:S(2)}) %all-to-all-start.4) | async-done | bytes 32800 | tf_op jit(solution)/shard_map/all_to_all | solution.py:696
  48.2 28.0 %all-to-all-done.5 = bf16[16,32,768]{2,1,0:T(8,128)(2,1)} async-done(((bf16[16,32,768]{2,1,0:T(8,128)(2,1)}), bf16[16,32,768]{2,1,0:T(8,128)(2,1)}, u32[]{:S(2)}, u32[]{:S(2)}) %all-to-all-start.5) | async-done | bytes 786464 | tf_op jit(solution)/shard_map/all_to_all | solution.py:696
  78.7 56.7 %all-gather.6.cloned.1.call-done.shared_ref.weight_ref.up_ref.down_ref = bf16[768,9600]{1,0:T(8,128)(2,1)} async-done(((bf16[24,9600]{1,0:T(8,128)(2,1)}), bf16[768,9600]{1,0:T(8,128)(2,1)}) %all-gather.6.cloned.1.call-update) | async-done | bytes 14745616 | tf_op jit(solution)/shard_map/all_gather | solution.py:790
  135.4 11.5 %attention_forward.1 = (bf16[256,768]{1,0:T(8,128)(2,1)}, bf16[256,768]{1,0:T(8,128)(2,1)}, bf16[64,768]{1,0:T(8,128)(2,1)}, bf16[64,768]{1,0:T(8,128)(2,1)}, f3...) custom-call(f32[256,768]{1,0:T(8,128)} %get-tuple-element.278.embed_, ...), custom_call_target="tpu_custom_call" | custom-call | flops 11010048 | bytes 73728 | tf_op jit(solution)/shard_map/attention_forward/pallas_call | solution.py:167
  147.0 7.2 %feed_forward.1 = (bf16[64,768]{1,0:T(8,128)(2,1)}, f32[64,3072]{1,0:T(8,128)}, bf16[64,3072]{1,0:T(8,128)(2,1)}, bf16[64,768]{1,0:T(8,128)(2,1)}, f32[64,768]{1,0:T(8,128)}, /*index=5*/f32[64,128]{1,0:T(8,128)}) custom-call(f32[64,768]{1,0:T(8,128)} %get-tuple-element.279.middle_ref, f32[14,768]{1,0:T(8,128)} %get-tuple-element.280.small_ref, ...), custom_call_target="tpu_custom_call" | custom-call | flops 9437184 | bytes 147456 | tf_op jit(solution)/shard_map/feed_forward/pallas_call | solution.py:167
  161.0 12.3 %all-to-all-done.6 = bf16[4,64,768]{2,1,0:T(8,128)(2,1)S(1)} async-done(((bf16[4,64,768]{2,1,0:T(8,128)(2,1)}), bf16[4,64,768]{2,1,0:T(8,128)(2,1)S(1)}, u32[]{:S(2)}, u32[]{:S(2)}) %all-to-all-start.6) | async-done | bytes 393248 | tf_op jit(solution)/shard_map/all_to_all | solution.py:696
  179.5 9.8 %all-to-all-done.7 = bf16[2,256,768]{2,1,0:T(8,128)(2,1)} async-done(((bf16[2,256,768]{2,1,0:T(8,128)(2,1)}), bf16[2,256,768]{2,1,0:T(8,128)(2,1)}, u32[]{:S(2)}, u32[]{:S(2)}) %all-to-all-start.7) | async-done | bytes 786464 | tf_op jit(solution)/shard_map/all_to_all | solution.py:696
  207.7 7.6 %all-to-all-done.9 = f32[16,2,1024]{2,1,0:T(2,128)S(1)} async-done(((f32[16,2,1024]{2,1,0:T(2,128)}), f32[16,2,1024]{2,1,0:T(2,128)S(1)}, u32[]{:S(2)}, u32[]{:S(2)}) %all-to-all-start.9) | async-done | bytes 131104 | tf_op jit(solution)/shard_map/all_to_all | solution.py:696
  233.0 7.7 %convolution_convert_fusion.1 = bf16[1920,768]{1,0:T(8,128)(2,1)} fusion(bf16[1024,1920]{1,0:T(8,128)(2,1)} %copy-done.1, bf16[1024,768]{1,0:T(8,128)(2,1)} %bitcast.168), kind=kOutput, calls=%fused_computation.31 | convolution fusion | flops 3021373440 | bytes 8454144 | tf_op jit(solution)/shard_map/dot_general | solution.py:44
  246.7 5.9 %collective-permute-done.2 = f32[256,768]{1,0:T(8,128)S(1)} collective-permute-done((f32[256,768]{1,0:T(8,128)S(1)}, f32[256,768]{1,0:T(8,128)S(1)}, u32[]{:S(2)}, u32[]{:S(2)}) %collective-permute-start.2) | collective-permute-done | bytes 786464 | tf_op jit(solution)/shard_map/ppermute | solution.py:898
  256.4 23.0 %all_to_all.134.parts_ref = f32[4,64,768]{2,1,0:T(8,128)} all-to-all(f32[4,64,768]{2,1,0:T(8,128)S(1)} %bitcast.159), channel_id=1, replica_groups=mesh['dp'=2,'hi'=4,'mid'=2,'core'=2] {'hi'}, dimensions={0} | all-to-all | bytes 1572864 | tf_op jit(solution)/shard_map/all_to_all | solution.py:696
  279.3 7.5 %feed_backward.1 = (bf16[64,768]{1,0:T(8,128)(2,1)}, bf16[64,3072]{1,0:T(8,128)(2,1)}, f32[64,768]{1,0:T(8,128)}, bf16[64,768]{1,0:T(8,128)(2,1)}, f32[16,768]{1,0:T(8,128)}) custom-call(f32[4,64,768]{2,1,0:T(8,128)} %all_to_all.134.parts_ref, f32[64,768]{1,0:T(8,128)} %get-tuple-element.293.normed_ref, f32[64,128]{1,0:T(8,128)} %get-tuple-element.294.inverse_ref, ...), custom_call_target="tpu_custom_call" | custom-call | flops 9437184 | bytes 147456 | tf_op jit(solution)/shard_map/feed_backward/pallas_call | solution.py:167
  297.4 9.5 %attention_backward.1 = (bf16[64,768]{1,0:T(8,128)(2,1)}, bf16[256,768]{1,0:T(8,128)(2,1)}, bf16[256,768]{1,0:T(8,128)(2,1)}) custom-call(bf16[64,768]{1,0:T(8,128)(2,1)} %get-tuple-element.299.d_attend_ref, bf16[256,768]{1,0:T(8,128)(2,1)} %get-tuple-element.300.key_ref, bf16[256,768]{1,0:T(8,128)(2,1)} %get-tuple-element.301.value_ref, ...), custom_call_target="tpu_custom_call" | custom-call | flops 5111808 | bytes 18432 | tf_op jit(solution)/shard_map/attention_backward/pallas_call | solution.py:167
  310.6 25.6 %all-gather.10.cloned.1.call-done.ahead_ref.refs_0_.refs_1_ = bf16[3840,768]{1,0:T(8,128)(2,1)} async-done(((bf16[1920,768]{1,0:T(8,128)(2,1)}), bf16[3840,768]{1,0:T(8,128)(2,1)}) %all-gather.10.cloned.1.call-update) | async-done | bytes 5898256 | tf_op jit(solution)/shard_map/all_gather | solution.py:917
  350.3 11.2 %all-to-all-done.12 = bf16[4,288,384]{2,1,0:T(8,128)(2,1)S(1)} async-done(((bf16[4,288,384]{2,1,0:T(8,128)(2,1)}), bf16[4,288,384]{2,1,0:T(8,128)(2,1)S(1)}, u32[]{:S(2)}, u32[]{:S(2)}) %all-to-all-start.12) | async-done | bytes 884768 | tf_op jit(solution)/shard_map/all_to_all | solution.py:696
  379.4 8.1 %all-to-all-done.13 = bf16[16,32,768]{2,1,0:T(8,128)(2,1)S(1)} async-done(((bf16[16,32,768]{2,1,0:T(8,128)(2,1)}), bf16[16,32,768]{2,1,0:T(8,128)(2,1)S(1)}, u32[]{:S(2)}, u32[]{:S(2)}) %all-to-all-start.13) | async-done | bytes 786464 | tf_op jit(solution)/shard_map/all_to_all | solution.py:696
  387.5 8.7 %all-to-all-start.14 = ((bf16[32,64,96]{2,1,0:T(8,128)(2,1)}), bf16[32,64,96]{2,1,0:T(8,128)(2,1)}, u32[]{:S(2)}, u32[]{:S(2)}) async-start(bf16[32,64,96]{2,1,0:T(8,128)(2,1)} %bitcast.163), calls=%async_computation.14 | async-start | bytes 1048576 | tf_op jit(solution)/shard_map/all_to_all | solution.py:696
  401.5 10.8 %all-to-all-done.14 = bf16[32,64,96]{2,1,0:T(8,128)(2,1)} async-done(((bf16[32,64,96]{2,1,0:T(8,128)(2,1)}), bf16[32,64,96]{2,1,0:T(8,128)(2,1)}, u32[]{:S(2)}, u32[]{:S(2)}) %all-to-all-start.14) | async-done | bytes 393248 | tf_op jit(solution)/shard_map/all_to_all | solution.py:696
  439.2 17.7 %collective-permute-done.3 = bf16[512,768]{1,0:T(8,128)(2,1)S(1)} collective-permute-done((bf16[512,768]{1,0:T(8,128)(2,1)}, bf16[512,768]{1,0:T(8,128)(2,1)S(1)}, u32[]{:S(2)}, u32[]{:S(2)}) %collective-permute-start.3) | collective-permute-done | bytes 786464 | tf_op jit(solution)/shard_map/ppermute | solution.py:987
  477.6 8.1 %table_gradient.5 = (f32[1920,768]{1,0:T(8,128)}, f32[1,768]{1,0:T(1,128)}) custom-call(bf16[3840,768]{1,0:T(8,128)(2,1)} %all-gather.10.cloned.1.call-done.ahead_ref.refs_0_.refs_1_, bf16[3840,768]{1,0:T(8,128)(2,1)} %all-gather.10.cloned.1.call-done.ahead_ref.refs_0_.refs_1_, s32[1,1024]{1,0:T(1,128)} %reshape.465.refs_2_, ...), custom_call_target="tpu_custom_call" | custom-call | tf_op jit(solution)/shard_map/table_gradient/pallas_call | solution.py:520
  503.1 11.7 %update_norms.1 = (f32[8,128]{1,0:T(8,128)}, f32[3,24,3072]{2,1,0:T(8,128)}, f32[3,24,3072]{2,1,0:T(8,128)}, f32[3,24,3072]{2,1,0:T(8,128)}, f32[256,24]{1,0:T(8...) custom-call(s32[1]{0:T(128)} %bitcast.65.offset_ref, ...), custom_call_target="tpu_custom_call" | custom-call | tf_op jit(solution)/shard_map/update_norms/pallas_call | solution.py:621
  519.9 11.2 %fusion.5 = (f32[1920,768]{1,0:T(8,128)}, f32[1920,768]{1,0:T(8,128)}) fusion(f32[1920,768]{1,0:T(8,128)} %refs_3_.1, f32[1920,768]{1,0:T(8,128)} %get-tuple-element.328.refs_4_, f32[]{:T(128)S(6)} %min.3, f32[1920,768]{1,0:T(8,128)} %refs_2_.1), kind=kLoop, calls=%fused_computation.29 | loop fusion | flops 11796480 | bytes 29491204 | tf_op jit(solution)/shard_map/add | solution.py:485
  533.1 14.5 %final_update.1 = (f32[1920,768]{1,0:T(8,128)}, f32[3,24,3072]{2,1,0:T(8,128)}, f32[256,24]{1,0:T(8,128)}, f32[14,24]{1,0:T(8,128)}) custom-call(f32[32,12]{1,0:T(8,128)} %bitcast.185, f32[1920,768]{1,0:T(8,128)} %weight_ref.1, f32[1920,768]{1,0:T(8,128)} %get-tuple-element.569.first_ref, f32[1920,768]{1,0:T(8,128)} %get-tuple-element.568.second_ref, ...), custom_call_target="tpu_custom_call" | custom-call | tf_op jit(solution)/shard_map/final_update/pallas_call | solution.py:675
  (275 shorter events, 204.2 us)
Async XLA Ops:
  7.2 128.2 %all-gather.6.cloned.1.call-start = ((), (), s32[]{:S(2)}) async-start(), calls=%async_computation.18 | async-start | bytes 15206400 | tf_op jit(solution)/shard_map/all_gather | solution.py:790
  13.3 62.9 %copy-start.21 = (s32[1,256]{1,0:T(1,128)}, s32[1,256]{1,0:T(1,128)S(1)}, u32[]{:S(2)}) copy-start(s32[1,256]{1,0:T(1,128)S(1)} %and_select_fusion.2) | copy-start | bytes 3076
  20.3 14.6 %all-to-all-start.4 = ((s32[32,1,256]{2,1,0:T(1,128)}), s32[32,1,256]{2,1,0:T(1,128)S(1)}, u32[]{:S(2)}, u32[]{:S(2)}) async-start(s32[32,1,256]{2,1,0:T(1,128)} %copy.324), calls=%async_computation.4 | async-start | bytes 65536 | tf_op jit(solution)/shard_map/all_to_all | solution.py:696
  40.5 35.7 %all-to-all-start.5 = ((bf16[16,32,768]{2,1,0:T(8,128)(2,1)}), bf16[16,32,768]{2,1,0:T(8,128)(2,1)}, u32[]{:S(2)}, u32[]{:S(2)}) async-start(bf16[16,32,768]{2,1,0:T(8,128)(2,1)} %broadcast_select_fusion.1), calls=%async_computation.5 | async-start | bytes 1572864 | tf_op jit(solution)/shard_map/all_to_all | solution.py:696
  44.8 195.9 %all-gather.8.cloned.1.call-start = ((), (), s32[]{:S(2)}) async-start(), calls=%async_computation.19 | async-start | bytes 1966080 | tf_op jit(solution)/shard_map/all_gather | solution.py:876
  146.9 132.4 %all-gather.12.cloned.1.call-start = ((), (), s32[]{:S(2)}) async-start(), calls=%async_computation.21 | async-start | bytes 6488064 | tf_op jit(solution)/shard_map/all_gather | solution.py:875
  157.5 15.8 %all-to-all-start.6 = ((bf16[4,64,768]{2,1,0:T(8,128)(2,1)}), bf16[4,64,768]{2,1,0:T(8,128)(2,1)S(1)}, u32[]{:S(2)}, u32[]{:S(2)}) async-start(bf16[4,64,768]{2,1,0:T(8,128)(2,1)} %broadcast_in_dim.352), calls=%async_computation.6 | async-start | bytes 786432 | tf_op jit(solution)/shard_map/all_to_all | solution.py:696
  174.2 15.1 %all-to-all-start.7 = ((bf16[2,256,768]{2,1,0:T(8,128)(2,1)}), bf16[2,256,768]{2,1,0:T(8,128)(2,1)}, u32[]{:S(2)}, u32[]{:S(2)}) async-start(bf16[2,256,768]{2,1,0:T(8,128)(2,1)} %broadcast_in_dim.354), calls=%async_computation.7 | async-start | bytes 1572864 | tf_op jit(solution)/shard_map/all_to_all | solution.py:696
  203.1 12.2 %all-to-all-start.9 = ((f32[16,2,1024]{2,1,0:T(2,128)}), f32[16,2,1024]{2,1,0:T(2,128)S(1)}, u32[]{:S(2)}, u32[]{:S(2)}) async-start(f32[16,2,1024]{2,1,0:T(2,128)} %broadcast_in_dim.357), calls=%async_computation.9 | async-start | bytes 262144 | tf_op jit(solution)/shard_map/all_to_all | solution.py:696
  207.3 128.9 %all-gather.10.cloned.1.call-start = ((), (), s32[]{:S(2)}) async-start(), calls=%async_computation.20 | async-start | bytes 8847360 | tf_op jit(solution)/shard_map/all_gather | solution.py:917
  224.0 3.8 collective-permute-start.1
  232.9 19.6 %collective-permute-start.2 = (f32[256,768]{1,0:T(8,128)S(1)}, f32[256,768]{1,0:T(8,128)S(1)}, u32[]{:S(2)}, u32[]{:S(2)}) collective-permute-start(f32[256,768]{1,0:T(8,128)S(1)} %constant_dynamic-slice_fusion.1), channel_id=1, source_target_pairs={{0,2},{2,0},{1,3},{3,1},{4,6},{6,4},{5,7},{7,5},{8,10},{10,8},{9,1... | collective-permute-start | bytes 2359304 | tf_op jit(solution)/shard_map/ppermute | solution.py:898
  256.3 156.0 %all-gather.14.cloned.1.call-start = ((), (), s32[]{:S(2)}) async-start(), calls=%async_computation.22 | async-start | bytes 3244032 | tf_op jit(solution)/shard_map/all_gather | solution.py:941
  291.2 52.6 %all-to-all-start.11 = ((bf16[32,64,120]{2,1,0:T(8,128)(2,1)}), bf16[32,64,120]{2,1,0:T(8,128)(2,1)}, u32[]{:S(2)}, u32[]{:S(2)}) async-start(bf16[32,64,120]{2,1,0:T(8,128)(2,1)} %maximum_bitcast_fusion.1), calls=%async_computation.11 | async-start | bytes 1048576 | tf_op jit(solution)/shard_map/all_to_all | solution.py:696
  297.4 38.8 %copy-start.26 = (f32[256]{0:T(256)S(1)}, f32[256]{0:T(256)}, u32[]{:S(2)}) copy-start(f32[256]{0:T(256)} %get-tuple-element.555) | copy-start | bytes 3076
  345.2 23.3 %copy-start.24 = (f32[8,768]{1,0:T(8,128)S(1)}, f32[8,768]{1,0:T(8,128)}, u32[]{:S(2)}) copy-start(f32[8,768]{1,0:T(8,128)} %get-tuple-element.310) | copy-start | bytes 73732
  345.2 23.3 %copy-start.23 = (f32[16,768]{1,0:T(8,128)S(1)}, f32[16,768]{1,0:T(8,128)}, u32[]{:S(2)}) copy-start(f32[16,768]{1,0:T(8,128)} %get-tuple-element.322) | copy-start | bytes 147460
  345.2 16.3 %all-to-all-start.12 = ((bf16[4,288,384]{2,1,0:T(8,128)(2,1)}), bf16[4,288,384]{2,1,0:T(8,128)(2,1)S(1)}, u32[]{:S(2)}, u32[]{:S(2)}) async-start(bf16[4,288,384]{2,1,0:T(8,128)(2,1)} %copy.336), calls=%async_computation.12 | async-start | bytes 1769472 | tf_op jit(solution)/shard_map/all_to_all | solution.py:696
  361.5 26.0 %all-to-all-start.13 = ((bf16[16,32,768]{2,1,0:T(8,128)(2,1)}), bf16[16,32,768]{2,1,0:T(8,128)(2,1)S(1)}, u32[]{:S(2)}, u32[]{:S(2)}) async-start(bf16[16,32,768]{2,1,0:T(8,128)(2,1)} %select_convert_fusion), calls=%async_computation.13 | async-start | bytes 1572864 | tf_op jit(solution)/shard_map/all_to_all | solution.py:696
  387.5 24.8 %all-to-all-start.14 = ((bf16[32,64,96]{2,1,0:T(8,128)(2,1)}), bf16[32,64,96]{2,1,0:T(8,128)(2,1)}, u32[]{:S(2)}, u32[]{:S(2)}) async-start(bf16[32,64,96]{2,1,0:T(8,128)(2,1)} %bitcast.163), calls=%async_computation.14 | async-start | bytes 1048576 | tf_op jit(solution)/shard_map/all_to_all | solution.py:696
  417.6 46.1 %all-to-all-start.15 = ((bf16[32,24,1062]{2,1,0:T(8,128)(2,1)}), bf16[32,24,1062]{2,1,0:T(8,128)(2,1)S(1)}, u32[]{:S(2)}, u32[]{:S(2)}) async-start(bf16[32,24,1062]{2,1,0:T(8,128)(2,1)} %concatenate.95), calls=%async_computation.15 | async-start | bytes 3538944 | tf_op jit(solution)/shard_map/all_to_all | solution.py:696
  427.5 29.4 %collective-permute-start.3 = (bf16[512,768]{1,0:T(8,128)(2,1)}, bf16[512,768]{1,0:T(8,128)(2,1)S(1)}, u32[]{:S(2)}, u32[]{:S(2)}) collective-permute-start(bf16[512,768]{1,0:T(8,128)(2,1)} %bitcast.50), channel_id=1, source_target_pairs={{0,16},{16,0},{1,17},{17,1},{2,18},{18,2},{3,19},{19,3},{4,20},{20... | collective-permute-start | bytes 2359304 | tf_op jit(solution)/shard_map/ppermute | solution.py:987
  491.1 9.9 %all-to-all-start.16 = ((f32[32,1,2]{2,1,0:T(1,128)}), f32[32,1,2]{2,1,0:T(1,128)S(1)}, u32[]{:S(2)}, u32[]{:S(2)}) async-start(f32[32,1,2]{2,1,0:T(1,128)} %copy.346), calls=%async_computation.16 | async-start | bytes 32768 | tf_op jit(solution)/shard_map/all_to_all | solution.py:696
  516.2 16.2 %all-to-all-start.17 = ((f32[32,1,12]{2,1,0:T(1,128)}), f32[32,1,12]{2,1,0:T(1,128)S(1)}, u32[]{:S(2)}, u32[]{:S(2)}) async-start(f32[32,1,12]{2,1,0:T(1,128)} %bitcast.75), calls=%async_computation.17 | async-start | bytes 32768 | tf_op jit(solution)/shard_map/all_to_all | solution.py:696
  (29 other events, 281.6 us)
Sparse Core Ops, SparseCore 0:
  11.5 123.8 all-gather.5
  147.0 17.8 all-gather.7
  167.8 70.2 all-gather.11
  256.4 79.7 all-gather.9
  338.9 63.3 all-gather.13

commit v8 on v7

--- a/solution.py
+++ b/solution.py
@@ -714,7 +714,7 @@
 
 def after(values, *waits):
     for wait in waits:
-        values = values + (wait.reshape(-1)[0] > 3.395e38).astype(values.dtype)
+        values = values + (wait[(0,) * wait.ndim] > 3.395e38).astype(values.dtype)
     return values
 
 
@@ -910,11 +910,8 @@
         "mid", lambda side: lax.dynamic_slice_in_dim(d_half, side * quarter, quarter, 0)
     )
     grad_head = rows_dot(d_logits, group_rows)
-    head_b = grad_head.astype(bfloat)
-    d_output, head_b = lax.optimization_barrier((d_output, head_b))
-    if few:
-        head_b = after(head_b, stream_all)
-    heads = lax.all_gather(head_b, "dp", axis=0, tiled=True)
+    grad_head = after(grad_head, d_half, *((stream_all,) if few else ()))
+    heads = lax.all_gather(grad_head.astype(bfloat), "dp", axis=0, tiled=True)
     d_output = exchange(d_output.reshape(outer, CAP, width), "hi")
     if few:
         d_output, kept_all = lax.optimization_barrier((d_output, kept_all))
@@ -1024,9 +1021,7 @@
             [grad_pair, grad_ask, grad_up, grad_down, grad_out, shared_grad], axis=1
         )
         results = results.astype(bfloat)
-        given = after(given, jnp.max(results[0].astype(single)))
         results = exchange.rows(results, devices).astype(single)
-        sides = after(sides, results)
         pieces = 3 * piece
         attn = jnp.sum(
             results[..., :pieces].reshape(dp_devs * outer, near, share, pieces), axis=0

time: 568 us -> 553 us (0.974)
  local copies, waits for them, and re-layouts: 64.7 us -> 53.4 us
  other arithmetic: 61.3 us -> 52 us
  waiting for transfers between devices: 212 us -> 220 us
    all_to_all x12, waiting for transfers between devices: 102 us -> 123 us  [__call__(): self.last = lax.all_to_all(values, axes, 0, 0, tiled=True)]
    all_gather x1, waiting for transfers between devices: 25.6 us -> 5.35 us  [on_device(): heads = lax.all_gather(grad_head.astype(bfloat), 'dp', axis=0, tiled=True)]
    ppermute x2, waiting for transfers between devices: 9.65 us -> 21.6 us  [swapped(): theirs = lax.ppermute(part(1 - side), axis, [(0, 1), (1, 0)])]
    reshape x2 -> x0, local copies, waits for them, and re-layouts: 9.22 us -> none  [after(): values = values + (wait.reshape(-1)[0] > 3.395e+38).astype(values.dtype)]
    dot_general x0 -> x2, local copies, waits for them, and re-layouts: none -> 7.29 us  [rows_dot(): lax.dot_general(left_op, right_op, (((0,), (0,)), ((), ())), preferred_el...]
  transfers between devices with their start and end apart: 20 -> 20, of which waited for: 15 -> 14; matrix products, arithmetic and copies ran while one was open for 23% -> 21% of each run, Pallas kernels for 5% -> 7%
where the time goes in v8:
time: 553 us; the launch traced here: 544 us
  waiting for transfers between devices  220 us (40%)
  Pallas kernels  76.1 us (14%)
  starting transfers between devices  56.1 us (10%)
  local copies, waits for them, and re-layouts  53.4 us (10%)
  other arithmetic  52 us (9%)
  matrix products  32.3 us (6%)
  blocking collectives  28.7 us (5%)
  between operations  25 us (5%)
    all_to_all x12, waiting for transfers between devices, __call__(): self.last = lax.all_to_all(values, axes, 0, 0, tiled=True)  123 us
    all_gather x1, waiting for transfers between devices, on_device(): shard = lax.all_gather(shard.astype(bfloat), ALL, axis=0, tiled=True)  57.3 us
    all_to_all x12, starting transfers between devices, __call__(): self.last = lax.all_to_all(values, axes, 0, 0, tiled=True)  55.2 us
    pallas_call x5, Pallas kernels, kernel_call(): pl.pallas_call(body, grid=(steps,), in_specs=[spec(array.shape, block, in...  41.8 us
    all_to_all x2, blocking collectives, __call__(): self.last = lax.all_to_all(values, axes, 0, 0, tiled=True)  28.7 us
    ppermute x2, waiting for transfers between devices, swapped(): theirs = lax.ppermute(part(1 - side), axis, [(0, 1), (1, 0)])  21.6 us
    dot_general x7, matrix products, rows_dot(): lax.dot_general(left_op, right_op, (((0,), (0,)), ((), ())), preferred_el...  20.3 us
    pallas_call x1, Pallas kernels, final_update(): pl.pallas_call(final_kernel, grid=(vrows // rows,), in_specs=[fixed(pairs...  14.4 us
  transfers between devices with their start and end apart: 20, of which 14 were waited for; matrix products, arithmetic and copies ran while one was open for 21% of the time, Pallas kernels for 7%

profile of v8, /device:TPU:0, one launch (start us, length us, event | category | flops | bytes accessed | tf_op | source)
XLA Modules:
  0.0 543.5 jit_solution(8267176504567887561)
XLA Ops:
  20.3 7.3 %all-to-all-start.4 = ((s32[32,1,256]{2,1,0:T(1,128)}), s32[32,1,256]{2,1,0:T(1,128)S(1)}, u32[]{:S(2)}, u32[]{:S(2)}) async-start(s32[32,1,256]{2,1,0:T(1,128)} %copy.283), calls=%async_computation.4 | async-start | bytes 65536 | tf_op jit(solution)/shard_map/all_to_all | solution.py:696
  27.6 7.3 %all-to-all-done.4 = s32[32,1,256]{2,1,0:T(1,128)S(1)} async-done(((s32[32,1,256]{2,1,0:T(1,128)}), s32[32,1,256]{2,1,0:T(1,128)S(1)}, u32[]{:S(2)}, u32[]{:S(2)}) %all-to-all-start.4) | async-done | bytes 32800 | tf_op jit(solution)/shard_map/all_to_all | solution.py:696
  47.6 28.0 %all-to-all-done.5 = bf16[16,32,768]{2,1,0:T(8,128)(2,1)} async-done(((bf16[16,32,768]{2,1,0:T(8,128)(2,1)}), bf16[16,32,768]{2,1,0:T(8,128)(2,1)}, u32[]{:S(2)}, u32[]{:S(2)}) %all-to-all-start.5) | async-done | bytes 786464 | tf_op jit(solution)/shard_map/all_to_all | solution.py:696
  78.1 57.3 %all-gather.6.cloned.1.call-done.shared_ref.weight_ref.up_ref.down_ref = bf16[768,9600]{1,0:T(8,128)(2,1)} async-done(((bf16[24,9600]{1,0:T(8,128)(2,1)}), bf16[768,9600]{1,0:T(8,128)(2,1)}) %all-gather.6.cloned.1.call-update) | async-done | bytes 14745616 | tf_op jit(solution)/shard_map/all_gather | solution.py:790
  135.4 11.5 %attention_forward.1 = (bf16[256,768]{1,0:T(8,128)(2,1)}, bf16[256,768]{1,0:T(8,128)(2,1)}, bf16[64,768]{1,0:T(8,128)(2,1)}, bf16[64,768]{1,0:T(8,128)(2,1)}, f3...) custom-call(f32[256,768]{1,0:T(8,128)} %get-tuple-element.276.embed_, ...), custom_call_target="tpu_custom_call" | custom-call | flops 11010048 | bytes 73728 | tf_op jit(solution)/shard_map/attention_forward/pallas_call | solution.py:167
  147.0 7.2 %feed_forward.1 = (bf16[64,768]{1,0:T(8,128)(2,1)}, f32[64,3072]{1,0:T(8,128)}, bf16[64,3072]{1,0:T(8,128)(2,1)}, bf16[64,768]{1,0:T(8,128)(2,1)}, f32[64,768]{1,0:T(8,128)}, /*index=5*/f32[64,128]{1,0:T(8,128)}) custom-call(f32[64,768]{1,0:T(8,128)} %get-tuple-element.277.middle_ref, f32[14,768]{1,0:T(8,128)} %get-tuple-element.278.small_ref, ...), custom_call_target="tpu_custom_call" | custom-call | flops 9437184 | bytes 147456 | tf_op jit(solution)/shard_map/feed_forward/pallas_call | solution.py:167
  160.9 12.3 %all-to-all-done.6 = bf16[4,64,768]{2,1,0:T(8,128)(2,1)S(1)} async-done(((bf16[4,64,768]{2,1,0:T(8,128)(2,1)}), bf16[4,64,768]{2,1,0:T(8,128)(2,1)S(1)}, u32[]{:S(2)}, u32[]{:S(2)}) %all-to-all-start.6) | async-done | bytes 393248 | tf_op jit(solution)/shard_map/all_to_all | solution.py:696
  180.2 9.1 %all-to-all-done.7 = bf16[2,256,768]{2,1,0:T(8,128)(2,1)} async-done(((bf16[2,256,768]{2,1,0:T(8,128)(2,1)}), bf16[2,256,768]{2,1,0:T(8,128)(2,1)}, u32[]{:S(2)}, u32[]{:S(2)}) %all-to-all-start.7) | async-done | bytes 786464 | tf_op jit(solution)/shard_map/all_to_all | solution.py:696
  207.7 7.5 %all-to-all-done.9 = f32[16,2,1024]{2,1,0:T(2,128)S(1)} async-done(((f32[16,2,1024]{2,1,0:T(2,128)}), f32[16,2,1024]{2,1,0:T(2,128)S(1)}, u32[]{:S(2)}, u32[]{:S(2)}) %all-to-all-start.9) | async-done | bytes 131104 | tf_op jit(solution)/shard_map/all_to_all | solution.py:696
  240.4 19.7 %collective-permute-done.2 = f32[256,768]{1,0:T(8,128)S(1)} collective-permute-done((f32[256,768]{1,0:T(8,128)S(1)}, f32[256,768]{1,0:T(8,128)S(1)}, u32[]{:S(2)}, u32[]{:S(2)}) %collective-permute-start.2) | collective-permute-done | bytes 786464 | tf_op jit(solution)/shard_map/ppermute | solution.py:898
  260.2 23.5 %all_to_all.134.parts_ref = f32[4,64,768]{2,1,0:T(8,128)} all-to-all(f32[4,64,768]{2,1,0:T(8,128)S(1)} %bitcast.167), channel_id=1, replica_groups=mesh['dp'=2,'hi'=4,'mid'=2,'core'=2] {'hi'}, dimensions={0} | all-to-all | bytes 1572864 | tf_op jit(solution)/shard_map/all_to_all | solution.py:696
  283.7 7.7 %feed_backward.1 = (bf16[64,768]{1,0:T(8,128)(2,1)}, bf16[64,3072]{1,0:T(8,128)(2,1)}, f32[64,768]{1,0:T(8,128)}, bf16[64,768]{1,0:T(8,128)(2,1)}, f32[16,768]{1,0:T(8,128)}) custom-call(f32[4,64,768]{2,1,0:T(8,128)} %all_to_all.134.parts_ref, f32[64,768]{1,0:T(8,128)} %get-tuple-element.289.normed_ref, f32[64,128]{1,0:T(8,128)} %get-tuple-element.290.inverse_ref, ...), custom_call_target="tpu_custom_call" | custom-call | flops 9437184 | bytes 147456 | tf_op jit(solution)/shard_map/feed_backward/pallas_call | solution.py:167
  301.6 9.5 %attention_backward.1 = (bf16[64,768]{1,0:T(8,128)(2,1)}, bf16[256,768]{1,0:T(8,128)(2,1)}, bf16[256,768]{1,0:T(8,128)(2,1)}) custom-call(bf16[64,768]{1,0:T(8,128)(2,1)} %get-tuple-element.295.d_attend_ref, bf16[256,768]{1,0:T(8,128)(2,1)} %get-tuple-element.296.key_ref, bf16[256,768]{1,0:T(8,128)(2,1)} %get-tuple-element.297.value_ref, ...), custom_call_target="tpu_custom_call" | custom-call | flops 5111808 | bytes 18432 | tf_op jit(solution)/shard_map/attention_backward/pallas_call | solution.py:167
  320.9 6.0 %projection_backward.1 = (bf16[256,768]{1,0:T(8,128)(2,1)S(1)}, f32[256,768]{1,0:T(8,128)}, f32[8,768]{1,0:T(8,128)}) custom-call(f32[64,768]{1,0:T(8,128)} %get-tuple-element.294.d_pre_ref, bf16[64,768]{1,0:T(8,128)(2,1)} %get-tuple-element.299.d_query_ref, bf16[256,768]{1,0:T(8,128)(2,1)} %get-tuple-element.300.d_key_ref, ...), custom_call_target="tpu_custom_call" | custom-call | flops 11796480 | bytes 55296 | tf_op jit(solution)/shard_map/projection_backward/pallas_call | solution.py:167
  334.3 11.2 %all-to-all-done.12 = bf16[4,288,384]{2,1,0:T(8,128)(2,1)S(1)} async-done(((bf16[4,288,384]{2,1,0:T(8,128)(2,1)}), bf16[4,288,384]{2,1,0:T(8,128)(2,1)S(1)}, u32[]{:S(2)}, u32[]{:S(2)}) %all-to-all-start.12) | async-done | bytes 884768 | tf_op jit(solution)/shard_map/all_to_all | solution.py:696
  363.9 7.5 %all-to-all-done.13 = bf16[16,32,768]{2,1,0:T(8,128)(2,1)S(1)} async-done(((bf16[16,32,768]{2,1,0:T(8,128)(2,1)}), bf16[16,32,768]{2,1,0:T(8,128)(2,1)S(1)}, u32[]{:S(2)}, u32[]{:S(2)}) %all-to-all-start.13) | async-done | bytes 786464 | tf_op jit(solution)/shard_map/all_to_all | solution.py:696
  372.2 9.5 %all-to-all-start.14 = ((bf16[32,64,96]{2,1,0:T(8,128)(2,1)}), bf16[32,64,96]{2,1,0:T(8,128)(2,1)}, u32[]{:S(2)}, u32[]{:S(2)}) async-start(bf16[32,64,96]{2,1,0:T(8,128)(2,1)} %bitcast.138), calls=%async_computation.14 | async-start | bytes 1048576 | tf_op jit(solution)/shard_map/all_to_all | solution.py:696
  385.7 12.5 %collective-permute-done.3 = bf16[512,768]{1,0:T(8,128)(2,1)} collective-permute-done((bf16[512,768]{1,0:T(8,128)(2,1)S(1)}, bf16[512,768]{1,0:T(8,128)(2,1)}, u32[]{:S(2)}, u32[]{:S(2)}) %collective-permute-start.3) | collective-permute-done | bytes 786464 | tf_op jit(solution)/shard_map/ppermute | solution.py:984
  400.6 8.1 %table_gradient.5 = (f32[1920,768]{1,0:T(8,128)}, f32[1,768]{1,0:T(1,128)}) custom-call(bf16[3840,768]{1,0:T(8,128)(2,1)} %all-gather.10.cloned.1.call-done.ahead_ref.refs_0_.refs_1_, bf16[3840,768]{1,0:T(8,128)(2,1)} %all-gather.10.cloned.1.call-done.ahead_ref.refs_0_.refs_1_, s32[1,1024]{1,0:T(1,128)} %reshape.458.refs_2_, ...), custom_call_target="tpu_custom_call" | custom-call | tf_op jit(solution)/shard_map/table_gradient/pallas_call | solution.py:520
  418.6 5.7 %all-to-all-start.15 = ((bf16[32,24,1062]{2,1,0:T(8,128)(2,1)}), bf16[32,24,1062]{2,1,0:T(8,128)(2,1)S(1)}, u32[]{:S(2)}, u32[]{:S(2)}) async-start(bf16[32,24,1062]{2,1,0:T(8,128)(2,1)} %concatenate.83), calls=%async_computation.15 | async-start | bytes 3538944 | tf_op jit(solution)/shard_map/all_to_all | solution.py:696
  430.5 36.7 %all-to-all-done.15 = bf16[32,24,1062]{2,1,0:T(8,128)(2,1)S(1)} async-done(((bf16[32,24,1062]{2,1,0:T(8,128)(2,1)}), bf16[32,24,1062]{2,1,0:T(8,128)(2,1)S(1)}, u32[]{:S(2)}, u32[]{:S(2)}) %all-to-all-start.15) | async-done | bytes 1631264 | tf_op jit(solution)/shard_map/all_to_all | solution.py:696
  488.7 11.7 %update_norms.1 = (f32[8,128]{1,0:T(8,128)}, f32[3,24,3072]{2,1,0:T(8,128)}, f32[3,24,3072]{2,1,0:T(8,128)}, f32[3,24,3072]{2,1,0:T(8,128)}, f32[256,24]{1,0:T(8...) custom-call(s32[1]{0:T(128)} %bitcast.70.offset_ref, ...), custom_call_target="tpu_custom_call" | custom-call | tf_op jit(solution)/shard_map/update_norms/pallas_call | solution.py:621
  504.7 11.2 %fusion.5 = (f32[1920,768]{1,0:T(8,128)}, f32[1920,768]{1,0:T(8,128)}) fusion(f32[1920,768]{1,0:T(8,128)} %refs_3_.1, f32[1920,768]{1,0:T(8,128)} %get-tuple-element.324.refs_4_, f32[]{:T(128)S(6)} %min.3, f32[1920,768]{1,0:T(8,128)} %refs_2_.1), kind=kLoop, calls=%fused_computation.29 | loop fusion | flops 11796480 | bytes 29491204 | tf_op jit(solution)/shard_map/add | solution.py:485
  517.8 14.4 %final_update.1 = (f32[1920,768]{1,0:T(8,128)}, f32[3,24,3072]{2,1,0:T(8,128)}, f32[256,24]{1,0:T(8,128)}, f32[14,24]{1,0:T(8,128)}) custom-call(f32[32,12]{1,0:T(8,128)} %bitcast.200, f32[1920,768]{1,0:T(8,128)} %weight_ref.1, f32[1920,768]{1,0:T(8,128)} %get-tuple-element.545.first_ref, f32[1920,768]{1,0:T(8,128)} %get-tuple-element.544.second_ref, ...), custom_call_target="tpu_custom_call" | custom-call | tf_op jit(solution)/shard_map/final_update/pallas_call | solution.py:675
  (283 shorter events, 176.0 us)
Async XLA Ops:
  7.2 128.2 %all-gather.6.cloned.1.call-start = ((), (), s32[]{:S(2)}) async-start(), calls=%async_computation.18 | async-start | bytes 15206400 | tf_op jit(solution)/shard_map/all_gather | solution.py:790
  13.3 62.3 %copy-start.23 = (s32[1,256]{1,0:T(1,128)}, s32[1,256]{1,0:T(1,128)S(1)}, u32[]{:S(2)}) copy-start(s32[1,256]{1,0:T(1,128)S(1)} %and_select_fusion.2) | copy-start | bytes 3076
  20.3 14.6 %all-to-all-start.4 = ((s32[32,1,256]{2,1,0:T(1,128)}), s32[32,1,256]{2,1,0:T(1,128)S(1)}, u32[]{:S(2)}, u32[]{:S(2)}) async-start(s32[32,1,256]{2,1,0:T(1,128)} %copy.283), calls=%async_computation.4 | async-start | bytes 65536 | tf_op jit(solution)/shard_map/all_to_all | solution.py:696
  39.9 35.7 %all-to-all-start.5 = ((bf16[16,32,768]{2,1,0:T(8,128)(2,1)}), bf16[16,32,768]{2,1,0:T(8,128)(2,1)}, u32[]{:S(2)}, u32[]{:S(2)}) async-start(bf16[16,32,768]{2,1,0:T(8,128)(2,1)} %broadcast_select_fusion.1), calls=%async_computation.5 | async-start | bytes 1572864 | tf_op jit(solution)/shard_map/all_to_all | solution.py:696
  44.2 179.7 %all-gather.8.cloned.1.call-start = ((), (), s32[]{:S(2)}) async-start(), calls=%async_computation.19 | async-start | bytes 1966080 | tf_op jit(solution)/shard_map/all_gather | solution.py:876
  45.7 133.0 %copy-start.35 = (s32[32]{0:T(128)}, s32[32]{0:T(128)S(1)}, u32[]{:S(2)}) copy-start(s32[32]{0:T(128)S(1)} %get-tuple-element.493) | copy-start | bytes 388
  146.9 136.8 %all-gather.12.cloned.1.call-start = ((), (), s32[]{:S(2)}) async-start(), calls=%async_computation.21 | async-start | bytes 6488064 | tf_op jit(solution)/shard_map/all_gather | solution.py:875
  157.5 15.8 %all-to-all-start.6 = ((bf16[4,64,768]{2,1,0:T(8,128)(2,1)}), bf16[4,64,768]{2,1,0:T(8,128)(2,1)S(1)}, u32[]{:S(2)}, u32[]{:S(2)}) async-start(bf16[4,64,768]{2,1,0:T(8,128)(2,1)} %broadcast_in_dim.352), calls=%async_computation.6 | async-start | bytes 786432 | tf_op jit(solution)/shard_map/all_to_all | solution.py:696
  174.2 15.1 %all-to-all-start.7 = ((bf16[2,256,768]{2,1,0:T(8,128)(2,1)}), bf16[2,256,768]{2,1,0:T(8,128)(2,1)}, u32[]{:S(2)}, u32[]{:S(2)}) async-start(bf16[2,256,768]{2,1,0:T(8,128)(2,1)} %broadcast_in_dim.354), calls=%async_computation.7 | async-start | bytes 1572864 | tf_op jit(solution)/shard_map/all_to_all | solution.py:696
  203.0 12.2 %all-to-all-start.9 = ((f32[16,2,1024]{2,1,0:T(2,128)}), f32[16,2,1024]{2,1,0:T(2,128)S(1)}, u32[]{:S(2)}, u32[]{:S(2)}) async-start(f32[16,2,1024]{2,1,0:T(2,128)} %broadcast_in_dim.357), calls=%async_computation.9 | async-start | bytes 262144 | tf_op jit(solution)/shard_map/all_to_all | solution.py:696
  207.3 112.9 %all-gather.10.cloned.1.call-start = ((), (), s32[]{:S(2)}) async-start(), calls=%async_computation.20 | async-start | bytes 8847360 | tf_op jit(solution)/shard_map/all_gather | solution.py:914
  223.9 3.8 collective-permute-start.1
  238.8 169.8 %all-gather.14.cloned.1.call-start = ((), (), s32[]{:S(2)}) async-start(), calls=%async_computation.22 | async-start | bytes 3244032 | tf_op jit(solution)/shard_map/all_gather | solution.py:938
  240.3 19.8 %collective-permute-start.2 = (f32[256,768]{1,0:T(8,128)S(1)}, f32[256,768]{1,0:T(8,128)S(1)}, u32[]{:S(2)}, u32[]{:S(2)}) collective-permute-start(f32[256,768]{1,0:T(8,128)S(1)} %constant_dynamic-slice_fusion.1), channel_id=1, source_target_pairs={{0,2},{2,0},{1,3},{3,1},{4,6},{6,4},{5,7},{7,5},{8,10},{10,8},{9,1... | collective-permute-start | bytes 2359304 | tf_op jit(solution)/shard_map/ppermute | solution.py:898
  298.3 29.5 %all-to-all-start.11 = ((bf16[32,64,120]{2,1,0:T(8,128)(2,1)}), bf16[32,64,120]{2,1,0:T(8,128)(2,1)S(1)}, u32[]{:S(2)}, u32[]{:S(2)}) async-start(bf16[32,64,120]{2,1,0:T(8,128)(2,1)} %maximum_bitcast_fusion.1), calls=%async_computation.11 | async-start | bytes 1048576 | tf_op jit(solution)/shard_map/all_to_all | solution.py:696
  329.2 21.9 %copy-start.28 = (f32[256]{0:T(256)S(1)}, f32[256]{0:T(256)}, u32[]{:S(2)}) copy-start(f32[256]{0:T(256)} %broadcast_multiply_fusion) | copy-start | bytes 3076
  329.2 22.1 %copy-start.34 = (s32[1,256]{1,0:T(1,128)S(1)}, s32[1,256]{1,0:T(1,128)}, u32[]{:S(2)}) copy-start(s32[1,256]{1,0:T(1,128)} %constant_dynamic-slice_fusion) | copy-start | bytes 3076
  329.2 16.3 %all-to-all-start.12 = ((bf16[4,288,384]{2,1,0:T(8,128)(2,1)}), bf16[4,288,384]{2,1,0:T(8,128)(2,1)S(1)}, u32[]{:S(2)}, u32[]{:S(2)}) async-start(bf16[4,288,384]{2,1,0:T(8,128)(2,1)} %copy.295), calls=%async_computation.12 | async-start | bytes 1769472 | tf_op jit(solution)/shard_map/all_to_all | solution.py:696
  345.5 25.9 %all-to-all-start.13 = ((bf16[16,32,768]{2,1,0:T(8,128)(2,1)}), bf16[16,32,768]{2,1,0:T(8,128)(2,1)S(1)}, u32[]{:S(2)}, u32[]{:S(2)}) async-start(bf16[16,32,768]{2,1,0:T(8,128)(2,1)} %select_convert_fusion), calls=%async_computation.13 | async-start | bytes 1572864 | tf_op jit(solution)/shard_map/all_to_all | solution.py:696
  371.4 26.8 %collective-permute-start.3 = (bf16[512,768]{1,0:T(8,128)(2,1)S(1)}, bf16[512,768]{1,0:T(8,128)(2,1)}, u32[]{:S(2)}, u32[]{:S(2)}) collective-permute-start(bf16[512,768]{1,0:T(8,128)(2,1)S(1)} %bitcast.170), channel_id=1, source_target_pairs={{0,16},{16,0},{1,17},{17,1},{2,18},{18,2},{3,19},{19,3},{4,20},{20... | collective-permute-start | bytes 2359304 | tf_op jit(solution)/shard_map/ppermute | solution.py:984
  372.2 41.1 %all-to-all-start.14 = ((bf16[32,64,96]{2,1,0:T(8,128)(2,1)}), bf16[32,64,96]{2,1,0:T(8,128)(2,1)}, u32[]{:S(2)}, u32[]{:S(2)}) async-start(bf16[32,64,96]{2,1,0:T(8,128)(2,1)} %bitcast.138), calls=%async_computation.14 | async-start | bytes 1048576 | tf_op jit(solution)/shard_map/all_to_all | solution.py:696
  418.6 48.6 %all-to-all-start.15 = ((bf16[32,24,1062]{2,1,0:T(8,128)(2,1)}), bf16[32,24,1062]{2,1,0:T(8,128)(2,1)S(1)}, u32[]{:S(2)}, u32[]{:S(2)}) async-start(bf16[32,24,1062]{2,1,0:T(8,128)(2,1)} %concatenate.83), calls=%async_computation.15 | async-start | bytes 3538944 | tf_op jit(solution)/shard_map/all_to_all | solution.py:696
  476.9 9.6 %all-to-all-start.16 = ((f32[32,1,2]{2,1,0:T(1,128)}), f32[32,1,2]{2,1,0:T(1,128)S(1)}, u32[]{:S(2)}, u32[]{:S(2)}) async-start(f32[32,1,2]{2,1,0:T(1,128)} %copy.305), calls=%async_computation.16 | async-start | bytes 32768 | tf_op jit(solution)/shard_map/all_to_all | solution.py:696
  501.8 15.5 %all-to-all-start.17 = ((f32[32,1,12]{2,1,0:T(1,128)}), f32[32,1,12]{2,1,0:T(1,128)S(1)}, u32[]{:S(2)}, u32[]{:S(2)}) async-start(f32[32,1,12]{2,1,0:T(1,128)} %bitcast.80), calls=%async_computation.17 | async-start | bytes 32768 | tf_op jit(solution)/shard_map/all_to_all | solution.py:696
  (33 other events, 256.6 us)
Sparse Core Ops, SparseCore 0:
  11.5 123.8 all-gather.5
  147.0 17.8 all-gather.7
  167.8 70.2 all-gather.11
  240.1 80.0 all-gather.9
  322.9 63.0 all-gather.13

commit v9 on v8

--- a/solution.py
+++ b/solution.py
@@ -283,7 +283,7 @@
     def _():
         sums_ref[...] = jnp.zeros_like(sums_ref)
         d_sum, gain, bias = norm_back(
-            jnp.sum(parts_ref[...], axis=0), normed_ref[...], inverse_ref[:, :1], row_of(small_ref, 12)
+            jnp.sum(parts_ref[...].astype(single), axis=0), normed_ref[...], inverse_ref[:, :1], row_of(small_ref, 12)
         )
         d_branch = d_sum.astype(bfloat)
         d_branch_ref[...] = d_branch
@@ -667,7 +667,9 @@
 
 def final_update(pairs, table, groups):
     vrows, width = table[0].shape
-    rows = row_block(vrows)
+    rows = row_block(vrows, 480)
+    if vrows // rows < 3:
+        rows = row_block(vrows, 240)
     fixed = lambda array: pl.BlockSpec(array.shape, lambda step, rank=array.ndim: (0,) * rank)
     block = pl.BlockSpec((rows, width), lambda step: (step, 0))
     one_part = pl.BlockSpec((1,) + groups[0].shape[1:], lambda step: (jnp.minimum(step, 2), 0, 0))
@@ -912,7 +914,7 @@
     grad_head = rows_dot(d_logits, group_rows)
     grad_head = after(grad_head, d_half, *((stream_all,) if few else ()))
     heads = lax.all_gather(grad_head.astype(bfloat), "dp", axis=0, tiled=True)
-    d_output = exchange(d_output.reshape(outer, CAP, width), "hi")
+    d_output = exchange(d_output.astype(bfloat).reshape(outer, CAP, width), "hi")
     if few:
         d_output, kept_all = lax.optimization_barrier((d_output, kept_all))
     d_branch, d_hidden, d_pre, d_attend, sums_feed = feed_backward(
@@ -1022,6 +1024,7 @@
         )
         results = results.astype(bfloat)
         results = exchange.rows(results, devices).astype(single)
+        sides = after(sides, results)
         pieces = 3 * piece
         attn = jnp.sum(
             results[..., :pieces].reshape(dp_devs * outer, near, share, pieces), axis=0

time: 553 us -> 545 us (0.986)
  blocking collectives: 28.7 us -> 20.2 us
    all_to_all x12, waiting for transfers between devices: 123 us -> 98.1 us  [__call__(): self.last = lax.all_to_all(values, axes, 0, 0, tiled=True)]
    ppermute x1, waiting for transfers between devices: 12.5 us -> 28.2 us  [of_both(): return jnp.concatenate([rows, lax.ppermute(rows, 'dp', [(0, 1), (1, 0)])])]
    all_gather x1, waiting for transfers between devices: 5.35 us -> 16.4 us  [on_device(): heads = lax.all_gather(grad_head.astype(bfloat), 'dp', axis=0, tiled=True)]
    all_to_all x2, blocking collectives: 28.7 us -> 20.2 us  [__call__(): self.last = lax.all_to_all(values, axes, 0, 0, tiled=True)]
  transfers between devices with their start and end apart: 20 -> 20, of which waited for: 14 -> 16; matrix products, arithmetic and copies ran while one was open for 21% -> 20% of each run, Pallas kernels for 7% -> 6%
where the time goes in v9:
time: 545 us; the launch traced here: 536 us
  waiting for transfers between devices  223 us (41%)
  Pallas kernels  75 us (14%)
  local copies, waits for them, and re-layouts  54.6 us (10%)
  starting transfers between devices  54.3 us (10%)
  other arithmetic  50.9 us (9%)
  matrix products  32.2 us (6%)
  between operations  25.2 us (5%)
  blocking collectives  20.2 us (4%)
    all_to_all x12, waiting for transfers between devices, __call__(): self.last = lax.all_to_all(values, axes, 0, 0, tiled=True)  98.1 us
    all_gather x1, waiting for transfers between devices, on_device(): shard = lax.all_gather(shard.astype(bfloat), ALL, axis=0, tiled=True)  57.1 us
    all_to_all x12, starting transfers between devices, __call__(): self.last = lax.all_to_all(values, axes, 0, 0, tiled=True)  52.3 us
    pallas_call x5, Pallas kernels, kernel_call(): pl.pallas_call(body, grid=(steps,), in_specs=[spec(array.shape, block, in...  41.7 us
    ppermute x1, waiting for transfers between devices, of_both(): return jnp.concatenate([rows, lax.ppermute(rows, 'dp', [(0, 1), (1, 0)])])  28.2 us
    ppermute x2, waiting for transfers between devices, swapped(): theirs = lax.ppermute(part(1 - side), axis, [(0, 1), (1, 0)])  21.6 us
    all_to_all x2, blocking collectives, __call__(): self.last = lax.all_to_all(values, axes, 0, 0, tiled=True)  20.2 us
    dot_general x7, matrix products, rows_dot(): lax.dot_general(left_op, right_op, (((0,), (0,)), ((), ())), preferred_el...  20.2 us
  transfers between devices with their start and end apart: 20, of which 16 were waited for; matrix products, arithmetic and copies ran while one was open for 20% of the time, Pallas kernels for 6%

profile of v9, /device:TPU:0, one launch (start us, length us, event | category | flops | bytes accessed | tf_op | source)
XLA Modules:
  0.0 535.6 jit_solution(1943703997902800663)
XLA Ops:
  19.7 7.3 %all-to-all-start.4 = ((s32[32,1,256]{2,1,0:T(1,128)}), s32[32,1,256]{2,1,0:T(1,128)S(1)}, u32[]{:S(2)}, u32[]{:S(2)}) async-start(s32[32,1,256]{2,1,0:T(1,128)} %copy.283), calls=%async_computation.4 | async-start | bytes 65536 | tf_op jit(solution)/shard_map/all_to_all | solution.py:698
  27.0 7.6 %all-to-all-done.4 = s32[32,1,256]{2,1,0:T(1,128)S(1)} async-done(((s32[32,1,256]{2,1,0:T(1,128)}), s32[32,1,256]{2,1,0:T(1,128)S(1)}, u32[]{:S(2)}, u32[]{:S(2)}) %all-to-all-start.4) | async-done | bytes 32800 | tf_op jit(solution)/shard_map/all_to_all | solution.py:698
  47.9 28.0 %all-to-all-done.5 = bf16[16,32,768]{2,1,0:T(8,128)(2,1)} async-done(((bf16[16,32,768]{2,1,0:T(8,128)(2,1)}), bf16[16,32,768]{2,1,0:T(8,128)(2,1)}, u32[]{:S(2)}, u32[]{:S(2)}) %all-to-all-start.5) | async-done | bytes 786464 | tf_op jit(solution)/shard_map/all_to_all | solution.py:698
  78.4 57.1 %all-gather.6.cloned.1.call-done.shared_ref.weight_ref.up_ref.down_ref = bf16[768,9600]{1,0:T(8,128)(2,1)} async-done(((bf16[24,9600]{1,0:T(8,128)(2,1)}), bf16[768,9600]{1,0:T(8,128)(2,1)}) %all-gather.6.cloned.1.call-update) | async-done | bytes 14745616 | tf_op jit(solution)/shard_map/all_gather | solution.py:792
  135.5 11.6 %attention_forward.1 = (bf16[256,768]{1,0:T(8,128)(2,1)}, bf16[256,768]{1,0:T(8,128)(2,1)}, bf16[64,768]{1,0:T(8,128)(2,1)}, bf16[64,768]{1,0:T(8,128)(2,1)}, f3...) custom-call(f32[256,768]{1,0:T(8,128)} %get-tuple-element.276.embed_, ...), custom_call_target="tpu_custom_call" | custom-call | flops 11010048 | bytes 73728 | tf_op jit(solution)/shard_map/attention_forward/pallas_call | solution.py:167
  147.2 7.2 %feed_forward.1 = (bf16[64,768]{1,0:T(8,128)(2,1)}, f32[64,3072]{1,0:T(8,128)}, bf16[64,3072]{1,0:T(8,128)(2,1)}, bf16[64,768]{1,0:T(8,128)(2,1)}, f32[64,768]{1,0:T(8,128)}, /*index=5*/f32[64,128]{1,0:T(8,128)}) custom-call(f32[64,768]{1,0:T(8,128)} %get-tuple-element.277.middle_ref, f32[14,768]{1,0:T(8,128)} %get-tuple-element.278.small_ref, ...), custom_call_target="tpu_custom_call" | custom-call | flops 9437184 | bytes 147456 | tf_op jit(solution)/shard_map/feed_forward/pallas_call | solution.py:167
  161.2 12.3 %all-to-all-done.6 = bf16[4,64,768]{2,1,0:T(8,128)(2,1)S(1)} async-done(((bf16[4,64,768]{2,1,0:T(8,128)(2,1)}), bf16[4,64,768]{2,1,0:T(8,128)(2,1)S(1)}, u32[]{:S(2)}, u32[]{:S(2)}) %all-to-all-start.6) | async-done | bytes 393248 | tf_op jit(solution)/shard_map/all_to_all | solution.py:698
  179.1 10.4 %all-to-all-done.7 = bf16[2,256,768]{2,1,0:T(8,128)(2,1)} async-done(((bf16[2,256,768]{2,1,0:T(8,128)(2,1)}), bf16[2,256,768]{2,1,0:T(8,128)(2,1)}, u32[]{:S(2)}, u32[]{:S(2)}) %all-to-all-start.7) | async-done | bytes 786464 | tf_op jit(solution)/shard_map/all_to_all | solution.py:698
  207.9 7.6 %all-to-all-done.9 = f32[16,2,1024]{2,1,0:T(2,128)S(1)} async-done(((f32[16,2,1024]{2,1,0:T(2,128)}), f32[16,2,1024]{2,1,0:T(2,128)S(1)}, u32[]{:S(2)}, u32[]{:S(2)}) %all-to-all-start.9) | async-done | bytes 131104 | tf_op jit(solution)/shard_map/all_to_all | solution.py:698
  240.6 19.7 %collective-permute-done.2 = f32[256,768]{1,0:T(8,128)S(1)} collective-permute-done((f32[256,768]{1,0:T(8,128)S(1)}, f32[256,768]{1,0:T(8,128)S(1)}, u32[]{:S(2)}, u32[]{:S(2)}) %collective-permute-start.2) | collective-permute-done | bytes 786464 | tf_op jit(solution)/shard_map/ppermute | solution.py:900
  260.4 15.0 %all_to_all.134.parts_ref = bf16[4,64,768]{2,1,0:T(8,128)(2,1)} all-to-all(bf16[4,64,768]{2,1,0:T(8,128)(2,1)S(1)} %bitcast.185), channel_id=1, replica_groups=mesh['dp'=2,'hi'=4,'mid'=2,'core'=2] {'hi'}, dimensions={0} | all-to-all | bytes 786432 | tf_op jit(solution)/shard_map/all_to_all | solution.py:698
  275.4 7.6 %feed_backward.1 = (bf16[64,768]{1,0:T(8,128)(2,1)}, bf16[64,3072]{1,0:T(8,128)(2,1)}, f32[64,768]{1,0:T(8,128)}, bf16[64,768]{1,0:T(8,128)(2,1)}, f32[16,768]{1,0:T(8,128)}) custom-call(bf16[4,64,768]{2,1,0:T(8,128)(2,1)} %all_to_all.134.parts_ref, f32[64,768]{1,0:T(8,128)} %get-tuple-element.289.normed_ref, f32[64,128]{1,0:T(8,128)} %get-tuple-element.290.inverse_ref, ...), custom_call_target="tpu_custom_call" | custom-call | flops 9437184 | bytes 147456 | tf_op jit(solution)/shard_map/feed_backward/pallas_call | solution.py:167
  290.8 9.5 %attention_backward.1 = (bf16[64,768]{1,0:T(8,128)(2,1)}, bf16[256,768]{1,0:T(8,128)(2,1)}, bf16[256,768]{1,0:T(8,128)(2,1)}) custom-call(bf16[64,768]{1,0:T(8,128)(2,1)} %get-tuple-element.295.d_attend_ref, bf16[256,768]{1,0:T(8,128)(2,1)} %get-tuple-element.296.key_ref, bf16[256,768]{1,0:T(8,128)(2,1)} %get-tuple-element.297.value_ref, ...), custom_call_target="tpu_custom_call" | custom-call | flops 5111808 | bytes 18432 | tf_op jit(solution)/shard_map/attention_backward/pallas_call | solution.py:167
  304.0 16.4 %all-gather.10.cloned.1.call-done.ahead_ref.refs_0_.refs_1_ = bf16[3840,768]{1,0:T(8,128)(2,1)} async-done(((bf16[1920,768]{1,0:T(8,128)(2,1)}), bf16[3840,768]{1,0:T(8,128)(2,1)}) %all-gather.10.cloned.1.call-update) | async-done | bytes 5898256 | tf_op jit(solution)/shard_map/all_gather | solution.py:916
  321.1 5.9 %projection_backward.1 = (bf16[256,768]{1,0:T(8,128)(2,1)S(1)}, f32[256,768]{1,0:T(8,128)}, f32[8,768]{1,0:T(8,128)}) custom-call(f32[64,768]{1,0:T(8,128)} %get-tuple-element.294.d_pre_ref, bf16[64,768]{1,0:T(8,128)(2,1)} %get-tuple-element.299.d_query_ref, bf16[256,768]{1,0:T(8,128)(2,1)} %get-tuple-element.300.d_key_ref, ...), custom_call_target="tpu_custom_call" | custom-call | flops 11796480 | bytes 55296 | tf_op jit(solution)/shard_map/projection_backward/pallas_call | solution.py:167
  334.3 11.3 %all-to-all-done.12 = bf16[4,288,384]{2,1,0:T(8,128)(2,1)S(1)} async-done(((bf16[4,288,384]{2,1,0:T(8,128)(2,1)}), bf16[4,288,384]{2,1,0:T(8,128)(2,1)S(1)}, u32[]{:S(2)}, u32[]{:S(2)}) %all-to-all-start.12) | async-done | bytes 884768 | tf_op jit(solution)/shard_map/all_to_all | solution.py:698
  362.7 8.8 %all-to-all-done.13 = bf16[16,32,768]{2,1,0:T(8,128)(2,1)S(1)} async-done(((bf16[16,32,768]{2,1,0:T(8,128)(2,1)}), bf16[16,32,768]{2,1,0:T(8,128)(2,1)S(1)}, u32[]{:S(2)}, u32[]{:S(2)}) %all-to-all-start.13) | async-done | bytes 786464 | tf_op jit(solution)/shard_map/all_to_all | solution.py:698
  371.5 8.7 %all-to-all-start.14 = ((bf16[32,64,96]{2,1,0:T(8,128)(2,1)}), bf16[32,64,96]{2,1,0:T(8,128)(2,1)}, u32[]{:S(2)}, u32[]{:S(2)}) async-start(bf16[32,64,96]{2,1,0:T(8,128)(2,1)} %bitcast.139), calls=%async_computation.14 | async-start | bytes 1048576 | tf_op jit(solution)/shard_map/all_to_all | solution.py:698
  391.1 5.3 all-to-all-done.14
  412.7 28.2 %collective-permute-done.3 = bf16[512,768]{1,0:T(8,128)(2,1)} collective-permute-done((bf16[512,768]{1,0:T(8,128)(2,1)S(1)}, bf16[512,768]{1,0:T(8,128)(2,1)}, u32[]{:S(2)}, u32[]{:S(2)}) %collective-permute-start.3) | collective-permute-done | bytes 786464 | tf_op jit(solution)/shard_map/ppermute | solution.py:986
  455.8 8.1 %table_gradient.5 = (f32[1920,768]{1,0:T(8,128)}, f32[1,768]{1,0:T(1,128)}) custom-call(bf16[3840,768]{1,0:T(8,128)(2,1)} %all-gather.10.cloned.1.call-done.ahead_ref.refs_0_.refs_1_, bf16[3840,768]{1,0:T(8,128)(2,1)} %all-gather.10.cloned.1.call-done.ahead_ref.refs_0_.refs_1_, s32[1,1024]{1,0:T(1,128)} %reshape.462.refs_2_, ...), custom_call_target="tpu_custom_call" | custom-call | tf_op jit(solution)/shard_map/table_gradient/pallas_call | solution.py:520
  481.2 11.7 %update_norms.1 = (f32[8,128]{1,0:T(8,128)}, f32[3,24,3072]{2,1,0:T(8,128)}, f32[3,24,3072]{2,1,0:T(8,128)}, f32[3,24,3072]{2,1,0:T(8,128)}, f32[256,24]{1,0:T(8...) custom-call(s32[1]{0:T(128)} %bitcast.71.offset_ref, ...), custom_call_target="tpu_custom_call" | custom-call | tf_op jit(solution)/shard_map/update_norms/pallas_call | solution.py:621
  498.0 11.2 %fusion.5 = (f32[1920,768]{1,0:T(8,128)}, f32[1920,768]{1,0:T(8,128)}) fusion(f32[1920,768]{1,0:T(8,128)} %refs_3_.1, f32[1920,768]{1,0:T(8,128)} %get-tuple-element.324.refs_4_, f32[]{:T(128)S(6)} %min.3, f32[1920,768]{1,0:T(8,128)} %refs_2_.1), kind=kLoop, calls=%fused_computation.29 | loop fusion | flops 11796480 | bytes 29491204 | tf_op jit(solution)/shard_map/add | solution.py:485
  511.2 13.5 %final_update.1 = (f32[1920,768]{1,0:T(8,128)}, f32[3,24,3072]{2,1,0:T(8,128)}, f32[256,24]{1,0:T(8,128)}, f32[14,24]{1,0:T(8,128)}) custom-call(f32[32,12]{1,0:T(8,128)} %bitcast.201, f32[1920,768]{1,0:T(8,128)} %weight_ref.1, f32[1920,768]{1,0:T(8,128)} %get-tuple-element.550.first_ref, f32[1920,768]{1,0:T(8,128)} %get-tuple-element.549.second_ref, ...), custom_call_target="tpu_custom_call" | custom-call | tf_op jit(solution)/shard_map/final_update/pallas_call | solution.py:677
  (276 shorter events, 180.4 us)
Async XLA Ops:
  7.2 128.3 %all-gather.6.cloned.1.call-start = ((), (), s32[]{:S(2)}) async-start(), calls=%async_computation.18 | async-start | bytes 15206400 | tf_op jit(solution)/shard_map/all_gather | solution.py:792
  19.7 14.9 %all-to-all-start.4 = ((s32[32,1,256]{2,1,0:T(1,128)}), s32[32,1,256]{2,1,0:T(1,128)S(1)}, u32[]{:S(2)}, u32[]{:S(2)}) async-start(s32[32,1,256]{2,1,0:T(1,128)} %copy.283), calls=%async_computation.4 | async-start | bytes 65536 | tf_op jit(solution)/shard_map/all_to_all | solution.py:698
  40.2 35.7 %all-to-all-start.5 = ((bf16[16,32,768]{2,1,0:T(8,128)(2,1)}), bf16[16,32,768]{2,1,0:T(8,128)(2,1)}, u32[]{:S(2)}, u32[]{:S(2)}) async-start(bf16[16,32,768]{2,1,0:T(8,128)(2,1)} %broadcast_select_fusion.1), calls=%async_computation.5 | async-start | bytes 1572864 | tf_op jit(solution)/shard_map/all_to_all | solution.py:698
  44.5 179.7 %all-gather.8.cloned.1.call-start = ((), (), s32[]{:S(2)}) async-start(), calls=%async_computation.19 | async-start | bytes 1966080 | tf_op jit(solution)/shard_map/all_gather | solution.py:878
  147.1 128.3 %all-gather.12.cloned.1.call-start = ((), (), s32[]{:S(2)}) async-start(), calls=%async_computation.21 | async-start | bytes 6488064 | tf_op jit(solution)/shard_map/all_gather | solution.py:877
  157.7 15.8 %all-to-all-start.6 = ((bf16[4,64,768]{2,1,0:T(8,128)(2,1)}), bf16[4,64,768]{2,1,0:T(8,128)(2,1)S(1)}, u32[]{:S(2)}, u32[]{:S(2)}) async-start(bf16[4,64,768]{2,1,0:T(8,128)(2,1)} %broadcast_in_dim.352), calls=%async_computation.6 | async-start | bytes 786432 | tf_op jit(solution)/shard_map/all_to_all | solution.py:698
  174.4 15.1 %all-to-all-start.7 = ((bf16[2,256,768]{2,1,0:T(8,128)(2,1)}), bf16[2,256,768]{2,1,0:T(8,128)(2,1)}, u32[]{:S(2)}, u32[]{:S(2)}) async-start(bf16[2,256,768]{2,1,0:T(8,128)(2,1)} %broadcast_in_dim.354), calls=%async_computation.7 | async-start | bytes 1572864 | tf_op jit(solution)/shard_map/all_to_all | solution.py:698
  203.3 12.2 %all-to-all-start.9 = ((f32[16,2,1024]{2,1,0:T(2,128)}), f32[16,2,1024]{2,1,0:T(2,128)S(1)}, u32[]{:S(2)}, u32[]{:S(2)}) async-start(f32[16,2,1024]{2,1,0:T(2,128)} %broadcast_in_dim.357), calls=%async_computation.9 | async-start | bytes 262144 | tf_op jit(solution)/shard_map/all_to_all | solution.py:698
  207.5 112.9 %all-gather.10.cloned.1.call-start = ((), (), s32[]{:S(2)}) async-start(), calls=%async_computation.20 | async-start | bytes 8847360 | tf_op jit(solution)/shard_map/all_gather | solution.py:916
  207.8 13.4 %copy-start.23 = (f32[16,64]{1,0:T(8,128)}, f32[16,64]{1,0:T(8,128)S(1)}, u32[]{:S(2)}) copy-start(f32[16,64]{1,0:T(8,128)S(1)} %fusion.45) | copy-start | bytes 12292
  224.2 3.8 collective-permute-start.1
  239.1 147.4 %all-gather.14.cloned.1.call-start = ((), (), s32[]{:S(2)}) async-start(), calls=%async_computation.22 | async-start | bytes 3244032 | tf_op jit(solution)/shard_map/all_gather | solution.py:940
  240.5 19.8 %collective-permute-start.2 = (f32[256,768]{1,0:T(8,128)S(1)}, f32[256,768]{1,0:T(8,128)S(1)}, u32[]{:S(2)}, u32[]{:S(2)}) collective-permute-start(f32[256,768]{1,0:T(8,128)S(1)} %constant_dynamic-slice_fusion.1), channel_id=1, source_target_pairs={{0,2},{2,0},{1,3},{3,1},{4,6},{6,4},{5,7},{7,5},{8,10},{10,8},{9,1... | collective-permute-start | bytes 2359304 | tf_op jit(solution)/shard_map/ppermute | solution.py:900
  288.1 39.9 %all-to-all-start.11 = ((bf16[32,64,120]{2,1,0:T(8,128)(2,1)}), bf16[32,64,120]{2,1,0:T(8,128)(2,1)S(1)}, u32[]{:S(2)}, u32[]{:S(2)}) async-start(bf16[32,64,120]{2,1,0:T(8,128)(2,1)} %maximum_bitcast_fusion.1), calls=%async_computation.11 | async-start | bytes 1048576 | tf_op jit(solution)/shard_map/all_to_all | solution.py:698
  329.3 16.2 %all-to-all-start.12 = ((bf16[4,288,384]{2,1,0:T(8,128)(2,1)}), bf16[4,288,384]{2,1,0:T(8,128)(2,1)S(1)}, u32[]{:S(2)}, u32[]{:S(2)}) async-start(bf16[4,288,384]{2,1,0:T(8,128)(2,1)} %copy.295), calls=%async_computation.12 | async-start | bytes 1769472 | tf_op jit(solution)/shard_map/all_to_all | solution.py:698
  334.3 21.0 %copy-start.30 = (f32[8,768]{1,0:T(8,128)S(1)}, f32[8,768]{1,0:T(8,128)}, u32[]{:S(2)}) copy-start(f32[8,768]{1,0:T(8,128)} %get-tuple-element.306) | copy-start | bytes 73732
  334.3 21.0 %copy-start.29 = (f32[16,768]{1,0:T(8,128)S(1)}, f32[16,768]{1,0:T(8,128)}, u32[]{:S(2)}) copy-start(f32[16,768]{1,0:T(8,128)} %get-tuple-element.318) | copy-start | bytes 147460
  345.5 26.0 %all-to-all-start.13 = ((bf16[16,32,768]{2,1,0:T(8,128)(2,1)}), bf16[16,32,768]{2,1,0:T(8,128)(2,1)S(1)}, u32[]{:S(2)}, u32[]{:S(2)}) async-start(bf16[16,32,768]{2,1,0:T(8,128)(2,1)} %select_convert_fusion), calls=%async_computation.13 | async-start | bytes 1572864 | tf_op jit(solution)/shard_map/all_to_all | solution.py:698
  371.5 13.4 %copy-start.4 = (bf16[16,32,768]{2,1,0:T(8,128)(2,1)}, bf16[16,32,768]{2,1,0:T(8,128)(2,1)S(1)}, u32[]{:S(2)}) copy-start(bf16[16,32,768]{2,1,0:T(8,128)(2,1)S(1)} %all-to-all-done.13) | copy-start | bytes 2359300
  371.5 25.0 %all-to-all-start.14 = ((bf16[32,64,96]{2,1,0:T(8,128)(2,1)}), bf16[32,64,96]{2,1,0:T(8,128)(2,1)}, u32[]{:S(2)}, u32[]{:S(2)}) async-start(bf16[32,64,96]{2,1,0:T(8,128)(2,1)} %bitcast.139), calls=%async_computation.14 | async-start | bytes 1048576 | tf_op jit(solution)/shard_map/all_to_all | solution.py:698
  401.8 45.9 %all-to-all-start.15 = ((bf16[32,24,1062]{2,1,0:T(8,128)(2,1)}), bf16[32,24,1062]{2,1,0:T(8,128)(2,1)S(1)}, u32[]{:S(2)}, u32[]{:S(2)}) async-start(bf16[32,24,1062]{2,1,0:T(8,128)(2,1)} %concatenate.83), calls=%async_computation.15 | async-start | bytes 3538944 | tf_op jit(solution)/shard_map/all_to_all | solution.py:698
  404.6 36.3 %collective-permute-start.3 = (bf16[512,768]{1,0:T(8,128)(2,1)S(1)}, bf16[512,768]{1,0:T(8,128)(2,1)}, u32[]{:S(2)}, u32[]{:S(2)}) collective-permute-start(bf16[512,768]{1,0:T(8,128)(2,1)S(1)} %bitcast.170), channel_id=1, source_target_pairs={{0,16},{16,0},{1,17},{17,1},{2,18},{18,2},{3,19},{19,3},{4,20},{20... | collective-permute-start | bytes 2359304 | tf_op jit(solution)/shard_map/ppermute | solution.py:986
  469.2 9.8 %all-to-all-start.16 = ((f32[32,1,2]{2,1,0:T(1,128)}), f32[32,1,2]{2,1,0:T(1,128)S(1)}, u32[]{:S(2)}, u32[]{:S(2)}) async-start(f32[32,1,2]{2,1,0:T(1,128)} %copy.305), calls=%async_computation.16 | async-start | bytes 32768 | tf_op jit(solution)/shard_map/all_to_all | solution.py:698
  494.3 16.2 %all-to-all-start.17 = ((f32[32,1,12]{2,1,0:T(1,128)}), f32[32,1,12]{2,1,0:T(1,128)S(1)}, u32[]{:S(2)}, u32[]{:S(2)}) async-start(f32[32,1,12]{2,1,0:T(1,128)} %bitcast.81), calls=%async_computation.17 | async-start | bytes 32768 | tf_op jit(solution)/shard_map/all_to_all | solution.py:698
  (29 other events, 168.3 us)
Sparse Core Ops, SparseCore 0:
  11.5 124.0 all-gather.5
  147.2 17.8 all-gather.7
  168.0 70.2 all-gather.11
  240.3 80.0 all-gather.9
  323.1 63.3 all-gather.13

commit v10 on v9

--- a/solution.py
+++ b/solution.py
@@ -160,8 +160,6 @@
     def spec(shape, block, index):
         if block is None:
             return pl.BlockSpec(shape, fixed(len(shape)))
-        if block == "any":
-            return pl.BlockSpec(memory_space=pl.ANY)
         return pl.BlockSpec(block, index)
 
     return pl.pallas_call(
@@ -404,7 +402,7 @@
 
 def project_back_kernel(
     d_pre_ref, d_query_ref, d_key_ref, d_value_ref, slot_ref, hidden_row_ref, small_ref,
-    normed_ref, inverse_ref, init_normed_ref, init_inverse_ref, weight_ref, ahead_ref,
+    normed_ref, inverse_ref, init_normed_ref, init_inverse_ref, weight_ref,
     embed_ref, position_ref, sums_ref, d_stream_ref, d_init_ref,
 ):
     step = pl.program_id(0)
@@ -448,7 +446,7 @@
 
 def project_backward(
     d_pre, d_query, d_key, d_value, slot_hot, hidden_rows, small_full,
-    normed, inverse, init_normed, init_inverse, weights, ahead,
+    normed, inverse, init_normed, init_inverse, weights,
 ):
     length, width = normed.shape
     slots = d_pre.shape[0]
@@ -461,7 +459,7 @@
         "projection_backward",
         3,
         [whole(array) for array in arrays]
-        + [(weights, (width, width), lambda step: (0, step)), (ahead, "any", None)],
+        + [(weights, (width, width), lambda step: (0, step))],
         [
             ((length, width), bfloat, None, None),
             ((length, width), single, None, None),
@@ -474,8 +472,9 @@
 
 def adam_direction(weight_arr, new_first, new_second):
     first_scale, second_scale = 1.0 / (1.0 - beta_first**STEP), 1.0 / (1.0 - beta_second**STEP)
+    scaled = new_second * second_scale
     return (new_first * first_scale) / (
-        jnp.sqrt(new_second * second_scale) + adam_eps
+        scaled * lax.rsqrt(scaled) + adam_eps
     ) + weight_decay * weight_arr
 
 
@@ -895,25 +894,26 @@
     d_logits = (
         group_weight[:, None] * (jnp.exp(logits - log_total[:, None]) - target_hit.astype(single))
     ).astype(bfloat)
-    def swapped(axis, part):
+    def swapped(axis, kind, part):
         side = lax.axis_index(axis)
-        theirs = lax.ppermute(part(1 - side), axis, [(0, 1), (1, 0)])
-        return part(side) + theirs
+        theirs = lax.ppermute(part(1 - side).astype(kind), axis, [(0, 1), (1, 0)])
+        return part(side) + theirs.astype(single)
 
     half = owners * CAP // 2
 
     def rows_half(side):
         return plain_dot(lax.dynamic_slice_in_dim(d_logits, side * half, half, 0), table_b)
 
-    d_output = swapped("core", rows_half)
+    d_output = swapped("core", single, rows_half)
     quarter = half // 2
     d_half = d_output
     d_output = swapped(
-        "mid", lambda side: lax.dynamic_slice_in_dim(d_half, side * quarter, quarter, 0)
+        "mid", bfloat, lambda side: lax.dynamic_slice_in_dim(d_half, side * quarter, quarter, 0)
     )
     grad_head = rows_dot(d_logits, group_rows)
-    grad_head = after(grad_head, d_half, *((stream_all,) if few else ()))
-    heads = lax.all_gather(grad_head.astype(bfloat), "dp", axis=0, tiled=True)
+    head_b = grad_head.astype(bfloat)
+    d_output, head_b = lax.optimization_barrier((d_output, head_b))
+    heads = lax.all_gather(head_b, "dp", axis=0, tiled=True)
     d_output = exchange(d_output.astype(bfloat).reshape(outer, CAP, width), "hi")
     if few:
         d_output, kept_all = lax.optimization_barrier((d_output, kept_all))
@@ -963,7 +963,6 @@
         init_normed,
         init_inverse,
         shard,
-        heads,
     )
     grad_small = jnp.concatenate([sums_back[:5], sums_feed[:9]])
     mask_sum = sums_back[5]

time: 545 us -> 550 us (level)
  waiting for transfers between devices: 223 us -> 234 us
    ppermute x1, waiting for transfers between devices: 28.2 us -> 52.5 us  [of_both(): return jnp.concatenate([rows, lax.ppermute(rows, 'dp', [(0, 1), (1, 0)])])]
    all_gather x1, waiting for transfers between devices: 16.4 us -> 6.09 us  [on_device(): heads = lax.all_gather(head_b, 'dp', axis=0, tiled=True)]
    ppermute x2, waiting for transfers between devices: 21.6 us -> 14.6 us  [swapped(): theirs = lax.ppermute(part(1 - side).astype(kind), axis, [(0, 1), (1, 0)])]
  transfers between devices with their start and end apart: 20 -> 20, of which waited for: 16 -> 14; matrix products, arithmetic and copies ran while one was open for 20% -> 22% of each run, Pallas kernels for 6% -> 4%
where the time goes in v10:
time: 550 us; the launch traced here: 540 us
  waiting for transfers between devices  234 us (43%)
  Pallas kernels  72.8 us (13%)
  starting transfers between devices  55.4 us (10%)
  other arithmetic  50.8 us (9%)
  local copies, waits for them, and re-layouts  49.9 us (9%)
  matrix products  32 us (6%)
  between operations  23.9 us (4%)
  blocking collectives  21.7 us (4%)
    all_to_all x12, waiting for transfers between devices, __call__(): self.last = lax.all_to_all(values, axes, 0, 0, tiled=True)  103 us
    all_gather x1, waiting for transfers between devices, on_device(): shard = lax.all_gather(shard.astype(bfloat), ALL, axis=0, tiled=True)  57.1 us
    ppermute x1, waiting for transfers between devices, of_both(): return jnp.concatenate([rows, lax.ppermute(rows, 'dp', [(0, 1), (1, 0)])])  52.5 us
    all_to_all x12, starting transfers between devices, __call__(): self.last = lax.all_to_all(values, axes, 0, 0, tiled=True)  52.4 us
    pallas_call x5, Pallas kernels, kernel_call(): pl.pallas_call(body, grid=(steps,), in_specs=[spec(array.shape, block, in...  41.5 us
    all_to_all x2, blocking collectives, __call__(): self.last = lax.all_to_all(values, axes, 0, 0, tiled=True)  21.7 us
    dot_general x7, matrix products, rows_dot(): lax.dot_general(left_op, right_op, (((0,), (0,)), ((), ())), preferred_el...  20.1 us
    ppermute x2, waiting for transfers between devices, swapped(): theirs = lax.ppermute(part(1 - side).astype(kind), axis, [(0, 1), (1, 0)])  14.6 us
  transfers between devices with their start and end apart: 20, of which 14 were waited for; matrix products, arithmetic and copies ran while one was open for 22% of the time, Pallas kernels for 4%

profile of v10, /device:TPU:0, one launch (start us, length us, event | category | flops | bytes accessed | tf_op | source)
XLA Modules:
  0.0 540.3 jit_solution(15413341547652886634)
XLA Ops:
  19.7 7.3 %all-to-all-start.4 = ((s32[32,1,256]{2,1,0:T(1,128)}), s32[32,1,256]{2,1,0:T(1,128)S(1)}, u32[]{:S(2)}, u32[]{:S(2)}) async-start(s32[32,1,256]{2,1,0:T(1,128)} %copy.283), calls=%async_computation.4 | async-start | bytes 65536 | tf_op jit(solution)/shard_map/all_to_all | solution.py:697
  27.0 7.6 %all-to-all-done.4 = s32[32,1,256]{2,1,0:T(1,128)S(1)} async-done(((s32[32,1,256]{2,1,0:T(1,128)}), s32[32,1,256]{2,1,0:T(1,128)S(1)}, u32[]{:S(2)}, u32[]{:S(2)}) %all-to-all-start.4) | async-done | bytes 32800 | tf_op jit(solution)/shard_map/all_to_all | solution.py:697
  47.9 28.0 %all-to-all-done.5 = bf16[16,32,768]{2,1,0:T(8,128)(2,1)} async-done(((bf16[16,32,768]{2,1,0:T(8,128)(2,1)}), bf16[16,32,768]{2,1,0:T(8,128)(2,1)}, u32[]{:S(2)}, u32[]{:S(2)}) %all-to-all-start.5) | async-done | bytes 786464 | tf_op jit(solution)/shard_map/all_to_all | solution.py:697
  78.4 57.1 %all-gather.6.cloned.1.call-done.shared_ref.weight_ref.up_ref.down_ref = bf16[768,9600]{1,0:T(8,128)(2,1)} async-done(((bf16[24,9600]{1,0:T(8,128)(2,1)}), bf16[768,9600]{1,0:T(8,128)(2,1)}) %all-gather.6.cloned.1.call-update) | async-done | bytes 14745616 | tf_op jit(solution)/shard_map/all_gather | solution.py:791
  135.5 11.5 %attention_forward.1 = (bf16[256,768]{1,0:T(8,128)(2,1)}, bf16[256,768]{1,0:T(8,128)(2,1)}, bf16[64,768]{1,0:T(8,128)(2,1)}, bf16[64,768]{1,0:T(8,128)(2,1)}, f3...) custom-call(f32[256,768]{1,0:T(8,128)} %get-tuple-element.278.embed_, ...), custom_call_target="tpu_custom_call" | custom-call | flops 11010048 | bytes 73728 | tf_op jit(solution)/shard_map/attention_forward/pallas_call | solution.py:165
  147.0 7.1 %feed_forward.1 = (bf16[64,768]{1,0:T(8,128)(2,1)}, f32[64,3072]{1,0:T(8,128)}, bf16[64,3072]{1,0:T(8,128)(2,1)}, bf16[64,768]{1,0:T(8,128)(2,1)}, f32[64,768]{1,0:T(8,128)}, /*index=5*/f32[64,128]{1,0:T(8,128)}) custom-call(f32[64,768]{1,0:T(8,128)} %get-tuple-element.279.middle_ref, f32[14,768]{1,0:T(8,128)} %get-tuple-element.280.small_ref, ...), custom_call_target="tpu_custom_call" | custom-call | flops 9437184 | bytes 147456 | tf_op jit(solution)/shard_map/feed_forward/pallas_call | solution.py:165
  160.9 16.0 %all-to-all-done.6 = bf16[4,64,768]{2,1,0:T(8,128)(2,1)S(1)} async-done(((bf16[4,64,768]{2,1,0:T(8,128)(2,1)}), bf16[4,64,768]{2,1,0:T(8,128)(2,1)S(1)}, u32[]{:S(2)}, u32[]{:S(2)}) %all-to-all-start.6) | async-done | bytes 393248 | tf_op jit(solution)/shard_map/all_to_all | solution.py:697
  182.5 12.9 %all-to-all-done.7 = bf16[2,256,768]{2,1,0:T(8,128)(2,1)} async-done(((bf16[2,256,768]{2,1,0:T(8,128)(2,1)}), bf16[2,256,768]{2,1,0:T(8,128)(2,1)}, u32[]{:S(2)}, u32[]{:S(2)}) %all-to-all-start.7) | async-done | bytes 786464 | tf_op jit(solution)/shard_map/all_to_all | solution.py:697
  213.5 9.0 %all-to-all-done.9 = f32[16,2,1024]{2,1,0:T(2,128)S(1)} async-done(((f32[16,2,1024]{2,1,0:T(2,128)}), f32[16,2,1024]{2,1,0:T(2,128)S(1)}, u32[]{:S(2)}, u32[]{:S(2)}) %all-to-all-start.9) | async-done | bytes 131104 | tf_op jit(solution)/shard_map/all_to_all | solution.py:697
  245.9 11.2 %collective-permute-done.2 = bf16[256,768]{1,0:T(8,128)(2,1)S(1)} collective-permute-done((bf16[256,768]{1,0:T(8,128)(2,1)S(1)}, bf16[256,768]{1,0:T(8,128)(2,1)S(1)}, u32[]{:S(2)}, u32[]{:S(2)}) %collective-permute-start.2) | collective-permute-done | bytes 393248 | tf_op jit(solution)/shard_map/ppermute | solution.py:899
  257.1 16.6 %all_to_all.134.parts_ref = bf16[4,64,768]{2,1,0:T(8,128)(2,1)} all-to-all(bf16[4,64,768]{2,1,0:T(8,128)(2,1)S(1)} %bitcast.183), channel_id=1, replica_groups=mesh['dp'=2,'hi'=4,'mid'=2,'core'=2] {'hi'}, dimensions={0} | all-to-all | bytes 786432 | tf_op jit(solution)/shard_map/all_to_all | solution.py:697
  273.7 7.6 %feed_backward.1 = (bf16[64,768]{1,0:T(8,128)(2,1)}, bf16[64,3072]{1,0:T(8,128)(2,1)}, f32[64,768]{1,0:T(8,128)}, bf16[64,768]{1,0:T(8,128)(2,1)}, f32[16,768]{1,0:T(8,128)}) custom-call(bf16[4,64,768]{2,1,0:T(8,128)(2,1)} %all_to_all.134.parts_ref, f32[64,768]{1,0:T(8,128)} %get-tuple-element.292.normed_ref, f32[64,128]{1,0:T(8,128)} %get-tuple-element.293.inverse_ref, ...), custom_call_target="tpu_custom_call" | custom-call | flops 9437184 | bytes 147456 | tf_op jit(solution)/shard_map/feed_backward/pallas_call | solution.py:165
  289.1 9.5 %attention_backward.1 = (bf16[64,768]{1,0:T(8,128)(2,1)}, bf16[256,768]{1,0:T(8,128)(2,1)}, bf16[256,768]{1,0:T(8,128)(2,1)}) custom-call(bf16[64,768]{1,0:T(8,128)(2,1)} %get-tuple-element.298.d_attend_ref, bf16[256,768]{1,0:T(8,128)(2,1)} %get-tuple-element.299.key_ref, bf16[256,768]{1,0:T(8,128)(2,1)} %get-tuple-element.300.value_ref, ...), custom_call_target="tpu_custom_call" | custom-call | flops 5111808 | bytes 18432 | tf_op jit(solution)/shard_map/attention_backward/pallas_call | solution.py:165
  303.1 5.9 %projection_backward.1 = (bf16[256,768]{1,0:T(8,128)(2,1)S(1)}, f32[256,768]{1,0:T(8,128)}, f32[8,768]{1,0:T(8,128)}) custom-call(f32[64,768]{1,0:T(8,128)} %get-tuple-element.297.d_pre_ref, bf16[64,768]{1,0:T(8,128)(2,1)} %get-tuple-element.302.d_query_ref, bf16[256,768]{1,0:T(8,128)(2,1)} %get-tuple-element.303.d_key_ref, ...), custom_call_target="tpu_custom_call" | custom-call | flops 11796480 | bytes 55296 | tf_op jit(solution)/shard_map/projection_backward/pallas_call | solution.py:165
  316.2 13.8 %all-to-all-done.12 = bf16[4,288,384]{2,1,0:T(8,128)(2,1)S(1)} async-done(((bf16[4,288,384]{2,1,0:T(8,128)(2,1)}), bf16[4,288,384]{2,1,0:T(8,128)(2,1)S(1)}, u32[]{:S(2)}, u32[]{:S(2)}) %all-to-all-start.12) | async-done | bytes 884768 | tf_op jit(solution)/shard_map/all_to_all | solution.py:697
  347.8 6.1 %all-to-all-done.13 = bf16[16,32,768]{2,1,0:T(8,128)(2,1)S(1)} async-done(((bf16[16,32,768]{2,1,0:T(8,128)(2,1)}), bf16[16,32,768]{2,1,0:T(8,128)(2,1)S(1)}, u32[]{:S(2)}, u32[]{:S(2)}) %all-to-all-start.13) | async-done | bytes 786464 | tf_op jit(solution)/shard_map/all_to_all | solution.py:697
  354.0 6.9 %all-to-all-start.14 = ((bf16[32,64,96]{2,1,0:T(8,128)(2,1)}), bf16[32,64,96]{2,1,0:T(8,128)(2,1)}, u32[]{:S(2)}, u32[]{:S(2)}) async-start(bf16[32,64,96]{2,1,0:T(8,128)(2,1)} %bitcast.137), calls=%async_computation.14 | async-start | bytes 1048576 | tf_op jit(solution)/shard_map/all_to_all | solution.py:697
  370.2 6.6 %all-to-all-done.14 = bf16[32,64,96]{2,1,0:T(8,128)(2,1)} async-done(((bf16[32,64,96]{2,1,0:T(8,128)(2,1)}), bf16[32,64,96]{2,1,0:T(8,128)(2,1)}, u32[]{:S(2)}, u32[]{:S(2)}) %all-to-all-start.14) | async-done | bytes 393248 | tf_op jit(solution)/shard_map/all_to_all | solution.py:697
  393.1 52.5 %collective-permute-done.3 = bf16[512,768]{1,0:T(8,128)(2,1)} collective-permute-done((bf16[512,768]{1,0:T(8,128)(2,1)S(1)}, bf16[512,768]{1,0:T(8,128)(2,1)}, u32[]{:S(2)}, u32[]{:S(2)}) %collective-permute-start.3) | collective-permute-done | bytes 786464 | tf_op jit(solution)/shard_map/ppermute | solution.py:985
  455.3 6.1 %all-gather.8.cloned.1.call-done.refs_0_.refs_1_ = bf16[3840,768]{1,0:T(8,128)(2,1)} async-done(((bf16[1920,768]{1,0:T(8,128)(2,1)}), bf16[3840,768]{1,0:T(8,128)(2,1)}) %all-gather.8.cloned.1.call-update) | async-done | bytes 5898256 | tf_op jit(solution)/shard_map/all_gather | solution.py:916
  461.4 8.1 %table_gradient.5 = (f32[1920,768]{1,0:T(8,128)}, f32[1,768]{1,0:T(1,128)}) custom-call(bf16[3840,768]{1,0:T(8,128)(2,1)} %all-gather.8.cloned.1.call-done.refs_0_.refs_1_, bf16[3840,768]{1,0:T(8,128)(2,1)} %all-gather.8.cloned.1.call-done.refs_0_.refs_1_, s32[1,1024]{1,0:T(1,128)} %reshape.454.refs_2_, bf16[1024,768]{1,0:T(8,128)(2,1)} %pad_maximum_fusion.1.refs_3_, ...), custom_call_target="tpu_custom_call" | custom-call | tf_op jit(solution)/shard_map/table_gradient/pallas_call | solution.py:519
  488.6 10.9 %update_norms.1 = (f32[8,128]{1,0:T(8,128)}, f32[3,24,3072]{2,1,0:T(8,128)}, f32[3,24,3072]{2,1,0:T(8,128)}, f32[3,24,3072]{2,1,0:T(8,128)}, f32[256,24]{1,0:T(8...) custom-call(s32[1]{0:T(128)} %bitcast.69.offset_ref, ...), custom_call_target="tpu_custom_call" | custom-call | tf_op jit(solution)/shard_map/update_norms/pallas_call | solution.py:620
  504.0 11.2 %fusion.5 = (f32[1920,768]{1,0:T(8,128)}, f32[1920,768]{1,0:T(8,128)}) fusion(f32[1920,768]{1,0:T(8,128)} %refs_3_.1, f32[1920,768]{1,0:T(8,128)} %get-tuple-element.328.refs_4_, f32[]{:T(128)S(6)} %min.3, f32[1920,768]{1,0:T(8,128)} %refs_2_.1), kind=kLoop, calls=%fused_computation.29 | loop fusion | flops 11796480 | bytes 29491204 | tf_op jit(solution)/shard_map/add | solution.py:484
  517.2 12.3 %final_update.1 = (f32[1920,768]{1,0:T(8,128)}, f32[3,24,3072]{2,1,0:T(8,128)}, f32[256,24]{1,0:T(8,128)}, f32[14,24]{1,0:T(8,128)}) custom-call(f32[32,12]{1,0:T(8,128)} %bitcast.199, f32[1920,768]{1,0:T(8,128)} %weight_ref.1, f32[1920,768]{1,0:T(8,128)} %get-tuple-element.554.first_ref, f32[1920,768]{1,0:T(8,128)} %get-tuple-element.553.second_ref, ...), custom_call_target="tpu_custom_call" | custom-call | tf_op jit(solution)/shard_map/final_update/pallas_call | solution.py:676
  (274 shorter events, 174.8 us)
Async XLA Ops:
  7.2 128.3 %all-gather.6.cloned.1.call-start = ((), (), s32[]{:S(2)}) async-start(), calls=%async_computation.18 | async-start | bytes 15206400 | tf_op jit(solution)/shard_map/all_gather | solution.py:791
  19.7 14.9 %all-to-all-start.4 = ((s32[32,1,256]{2,1,0:T(1,128)}), s32[32,1,256]{2,1,0:T(1,128)S(1)}, u32[]{:S(2)}, u32[]{:S(2)}) async-start(s32[32,1,256]{2,1,0:T(1,128)} %copy.283), calls=%async_computation.4 | async-start | bytes 65536 | tf_op jit(solution)/shard_map/all_to_all | solution.py:697
  40.2 35.7 %all-to-all-start.5 = ((bf16[16,32,768]{2,1,0:T(8,128)(2,1)}), bf16[16,32,768]{2,1,0:T(8,128)(2,1)}, u32[]{:S(2)}, u32[]{:S(2)}) async-start(bf16[16,32,768]{2,1,0:T(8,128)(2,1)} %broadcast_select_fusion.1), calls=%async_computation.5 | async-start | bytes 1572864 | tf_op jit(solution)/shard_map/all_to_all | solution.py:697
  44.5 229.2 %all-gather.10.cloned.1.call-start = ((), (), s32[]{:S(2)}) async-start(), calls=%async_computation.20 | async-start | bytes 6488064 | tf_op jit(solution)/shard_map/all_gather | solution.py:876
  157.4 19.4 %all-to-all-start.6 = ((bf16[4,64,768]{2,1,0:T(8,128)(2,1)}), bf16[4,64,768]{2,1,0:T(8,128)(2,1)S(1)}, u32[]{:S(2)}, u32[]{:S(2)}) async-start(bf16[4,64,768]{2,1,0:T(8,128)(2,1)} %broadcast_in_dim.352), calls=%async_computation.6 | async-start | bytes 786432 | tf_op jit(solution)/shard_map/all_to_all | solution.py:697
  177.8 17.6 %all-to-all-start.7 = ((bf16[2,256,768]{2,1,0:T(8,128)(2,1)}), bf16[2,256,768]{2,1,0:T(8,128)(2,1)}, u32[]{:S(2)}, u32[]{:S(2)}) async-start(bf16[2,256,768]{2,1,0:T(8,128)(2,1)} %broadcast_in_dim.354), calls=%async_computation.7 | async-start | bytes 1572864 | tf_op jit(solution)/shard_map/all_to_all | solution.py:697
  209.1 13.4 %all-to-all-start.9 = ((f32[16,2,1024]{2,1,0:T(2,128)}), f32[16,2,1024]{2,1,0:T(2,128)S(1)}, u32[]{:S(2)}, u32[]{:S(2)}) async-start(f32[16,2,1024]{2,1,0:T(2,128)} %broadcast_in_dim.357), calls=%async_computation.9 | async-start | bytes 262144 | tf_op jit(solution)/shard_map/all_to_all | solution.py:697
  213.2 124.5 %all-gather.12.cloned.1.call-start = ((), (), s32[]{:S(2)}) async-start(), calls=%async_computation.21 | async-start | bytes 1966080 | tf_op jit(solution)/shard_map/all_gather | solution.py:877
  213.4 14.8 %copy-start.23 = (f32[16,64]{1,0:T(8,128)}, f32[16,64]{1,0:T(8,128)S(1)}, u32[]{:S(2)}) copy-start(f32[16,64]{1,0:T(8,128)S(1)} %fusion.45) | copy-start | bytes 12292
  231.2 3.8 collective-permute-start.1
  231.5 134.1 %all-gather.14.cloned.1.call-start = ((), (), s32[]{:S(2)}) async-start(), calls=%async_computation.22 | async-start | bytes 3244032 | tf_op jit(solution)/shard_map/all_gather | solution.py:940
  240.1 17.0 %copy-start.9 = (f32[512,768]{1,0:T(8,128)S(1)}, f32[512,768]{1,0:T(8,128)}, u32[]{:S(2)}) copy-start(f32[512,768]{1,0:T(8,128)} %copy-done.8) | copy-start | bytes 4718596
  240.1 17.0 %collective-permute-start.2 = (bf16[256,768]{1,0:T(8,128)(2,1)S(1)}, bf16[256,768]{1,0:T(8,128)(2,1)S(1)}, u32[]{:S(2)}, u32[]{:S(2)}) collective-permute-start(bf16[256,768]{1,0:T(8,128)(2,1)S(1)} %dynamic-slice_convert_fusion), channel_id=1, source_target_pairs={{0,2},{2,0},{1,3},{3,1},{4,6},{6,4},{5,7},{7,5},{8,10},{10,8},{9,1... | collective-permute-start | bytes 1179656 | tf_op jit(solution)/shard_map/ppermute | solution.py:899
  286.4 23.5 %all-to-all-start.11 = ((bf16[32,64,120]{2,1,0:T(8,128)(2,1)}), bf16[32,64,120]{2,1,0:T(8,128)(2,1)S(1)}, u32[]{:S(2)}, u32[]{:S(2)}) async-start(bf16[32,64,120]{2,1,0:T(8,128)(2,1)} %maximum_bitcast_fusion.1), calls=%async_computation.11 | async-start | bytes 1048576 | tf_op jit(solution)/shard_map/all_to_all | solution.py:697
  311.3 18.7 %all-to-all-start.12 = ((bf16[4,288,384]{2,1,0:T(8,128)(2,1)}), bf16[4,288,384]{2,1,0:T(8,128)(2,1)S(1)}, u32[]{:S(2)}, u32[]{:S(2)}) async-start(bf16[4,288,384]{2,1,0:T(8,128)(2,1)} %copy.295), calls=%async_computation.12 | async-start | bytes 1769472 | tf_op jit(solution)/shard_map/all_to_all | solution.py:697
  330.0 24.0 %all-to-all-start.13 = ((bf16[16,32,768]{2,1,0:T(8,128)(2,1)}), bf16[16,32,768]{2,1,0:T(8,128)(2,1)S(1)}, u32[]{:S(2)}, u32[]{:S(2)}) async-start(bf16[16,32,768]{2,1,0:T(8,128)(2,1)} %select_convert_fusion), calls=%async_computation.13 | async-start | bytes 1572864 | tf_op jit(solution)/shard_map/all_to_all | solution.py:697
  335.3 126.1 %all-gather.8.cloned.1.call-start = ((), (), s32[]{:S(2)}) async-start(), calls=%async_computation.19 | async-start | bytes 8847360 | tf_op jit(solution)/shard_map/all_gather | solution.py:916
  354.0 11.6 %copy-start.4 = (bf16[16,32,768]{2,1,0:T(8,128)(2,1)}, bf16[16,32,768]{2,1,0:T(8,128)(2,1)S(1)}, u32[]{:S(2)}) copy-start(bf16[16,32,768]{2,1,0:T(8,128)(2,1)S(1)} %all-to-all-done.13) | copy-start | bytes 2359300
  354.0 22.9 %all-to-all-start.14 = ((bf16[32,64,96]{2,1,0:T(8,128)(2,1)}), bf16[32,64,96]{2,1,0:T(8,128)(2,1)}, u32[]{:S(2)}, u32[]{:S(2)}) async-start(bf16[32,64,96]{2,1,0:T(8,128)(2,1)} %bitcast.137), calls=%async_computation.14 | async-start | bytes 1048576 | tf_op jit(solution)/shard_map/all_to_all | solution.py:697
  382.2 65.8 %all-to-all-start.15 = ((bf16[32,24,1062]{2,1,0:T(8,128)(2,1)}), bf16[32,24,1062]{2,1,0:T(8,128)(2,1)S(1)}, u32[]{:S(2)}, u32[]{:S(2)}) async-start(bf16[32,24,1062]{2,1,0:T(8,128)(2,1)} %concatenate.83), calls=%async_computation.15 | async-start | bytes 3538944 | tf_op jit(solution)/shard_map/all_to_all | solution.py:697
  385.0 60.6 %collective-permute-start.3 = (bf16[512,768]{1,0:T(8,128)(2,1)S(1)}, bf16[512,768]{1,0:T(8,128)(2,1)}, u32[]{:S(2)}, u32[]{:S(2)}) collective-permute-start(bf16[512,768]{1,0:T(8,128)(2,1)S(1)} %bitcast.168), channel_id=1, source_target_pairs={{0,16},{16,0},{1,17},{17,1},{2,18},{18,2},{3,19},{19,3},{4,20},{20... | collective-permute-start | bytes 2359304 | tf_op jit(solution)/shard_map/ppermute | solution.py:985
  474.8 11.7 %all-to-all-start.16 = ((f32[32,1,2]{2,1,0:T(1,128)}), f32[32,1,2]{2,1,0:T(1,128)S(1)}, u32[]{:S(2)}, u32[]{:S(2)}) async-start(f32[32,1,2]{2,1,0:T(1,128)} %copy.305), calls=%async_computation.16 | async-start | bytes 32768 | tf_op jit(solution)/shard_map/all_to_all | solution.py:697
  500.9 15.6 %all-to-all-start.17 = ((f32[32,1,12]{2,1,0:T(1,128)}), f32[32,1,12]{2,1,0:T(1,128)S(1)}, u32[]{:S(2)}, u32[]{:S(2)}) async-start(f32[32,1,12]{2,1,0:T(1,128)} %bitcast.79), calls=%async_computation.17 | async-start | bytes 32768 | tf_op jit(solution)/shard_map/all_to_all | solution.py:697
  504.0 11.9 %copy-start.19 = (f32[256,24]{1,0:T(8,128)S(1)}, f32[256,24]{1,0:T(8,128)}, u32[]{:S(2)}) copy-start(f32[256,24]{1,0:T(8,128)} %get-tuple-element.489) | copy-start | bytes 73732
  (29 other events, 167.0 us)
Sparse Core Ops, SparseCore 0:
  11.5 124.0 all-gather.5
  155.9 73.9 all-gather.9
  231.6 24.1 all-gather.11
  281.4 63.2 all-gather.13
  346.7 114.5 all-gather.7

commit v11 on v10

--- a/solution.py
+++ b/solution.py
@@ -160,6 +160,8 @@
     def spec(shape, block, index):
         if block is None:
             return pl.BlockSpec(shape, fixed(len(shape)))
+        if block == "any":
+            return pl.BlockSpec(memory_space=pl.ANY)
         return pl.BlockSpec(block, index)
 
     return pl.pallas_call(
@@ -402,7 +404,7 @@
 
 def project_back_kernel(
     d_pre_ref, d_query_ref, d_key_ref, d_value_ref, slot_ref, hidden_row_ref, small_ref,
-    normed_ref, inverse_ref, init_normed_ref, init_inverse_ref, weight_ref,
+    normed_ref, inverse_ref, init_normed_ref, init_inverse_ref, weight_ref, ahead_ref,
     embed_ref, position_ref, sums_ref, d_stream_ref, d_init_ref,
 ):
     step = pl.program_id(0)
@@ -446,7 +448,7 @@
 
 def project_backward(
     d_pre, d_query, d_key, d_value, slot_hot, hidden_rows, small_full,
-    normed, inverse, init_normed, init_inverse, weights,
+    normed, inverse, init_normed, init_inverse, weights, ahead,
 ):
     length, width = normed.shape
     slots = d_pre.shape[0]
@@ -459,7 +461,7 @@
         "projection_backward",
         3,
         [whole(array) for array in arrays]
-        + [(weights, (width, width), lambda step: (0, step))],
+        + [(weights, (width, width), lambda step: (0, step)), (ahead, "any", None)],
         [
             ((length, width), bfloat, None, None),
             ((length, width), single, None, None),
@@ -489,17 +491,24 @@
     return most if count % most == 0 else count
 
 
-def lookup_kernel(parts, *refs):
+def lookup_kernel(pieces, *refs):
     step = pl.program_id(0)
-    head_refs, (asked_ref, given_ref, side_ref, grad_ref, square_ref) = refs[:parts], refs[parts:]
+    starts, count = pieces
+    runs = len(starts)
+    head_refs, refs = refs[: runs * count], refs[runs * count :]
+    asked_ref, given_ref, side_ref, grad_ref, square_ref = refs
     rows, width = grad_ref.shape
     base = step * rows
     row_hot = asked_ref[...] == base + lax.broadcasted_iota(
         jnp.int32, (rows, asked_ref.shape[1]), 0
     )
     grad = plain_dot(row_hot.astype(bfloat), given_ref[...])
-    for head_ref in head_refs:
-        grad += head_ref[...].astype(single)
+    for part in range(count):
+        head = head_refs[part][...].astype(single)
+        for run in range(1, runs):
+            later = head_refs[run * count + part][...].astype(single)
+            head = jnp.where(step >= starts[run], later, head)
+        grad += head
     grad_ref[...] = grad
     place = base + lax.broadcasted_iota(jnp.int32, (rows, width), 0)
     own = (place >= side_ref[0]) & (place < side_ref[1])
@@ -511,31 +520,43 @@
     square_ref[...] += jnp.sum(jnp.where(own, grad * grad, 0.0), axis=0, keepdims=True)
 
 
-def lookup_grad(heads, parts, asked_rows, given, sides):
-    vrows, width = heads.shape[0] // parts, heads.shape[1]
+def lookup_grad(heads, count, asked_rows, given, sides):
+    width = heads[0].shape[1]
+    vrows = sum(head.shape[0] for head in heads) // count
     rows = vrows // 4
-    block = pl.BlockSpec((rows, width), lambda step: (step, 0))
+    steps = [head.shape[0] // count // rows for head in heads]
+    starts = [sum(steps[:run]) for run in range(len(heads))]
     whole_spec = lambda array: pl.BlockSpec(array.shape, lambda step: (0, 0))
     return pl.pallas_call(
-        lambda *refs: lookup_kernel(parts, *refs),
+        lambda *refs: lookup_kernel((starts, count), *refs),
         grid=(4,),
         in_specs=[
-            pl.BlockSpec((rows, width), lambda step, part=part: (4 * part + step, 0))
-            for part in range(parts)
+            pl.BlockSpec(
+                (rows, width),
+                lambda step, run=run, part=part: (
+                    part * steps[run] + jnp.clip(step - starts[run], 0, steps[run] - 1),
+                    0,
+                ),
+            )
+            for run in range(len(heads))
+            for part in range(count)
         ]
         + [
             whole_spec(asked_rows),
             whole_spec(given),
             pl.BlockSpec(memory_space=pltpu.SMEM),
         ],
-        out_specs=[block, pl.BlockSpec((1, width), lambda step: (0, 0))],
+        out_specs=[
+            pl.BlockSpec((rows, width), lambda step: (step, 0)),
+            pl.BlockSpec((1, width), lambda step: (0, 0)),
+        ],
         out_shape=[
             jax.ShapeDtypeStruct((vrows, width), single),
             jax.ShapeDtypeStruct((1, width), single),
         ],
         cost_estimate=pl.CostEstimate(flops=0, bytes_accessed=0, transcendentals=0),
         name="table_gradient",
-    )(*[heads] * parts, asked_rows, given, sides)
+    )(*[head for head in heads for _ in range(count)], asked_rows, given, sides)
 
 
 def full_sum(values):
@@ -911,9 +932,11 @@
         "mid", bfloat, lambda side: lax.dynamic_slice_in_dim(d_half, side * quarter, quarter, 0)
     )
     grad_head = rows_dot(d_logits, group_rows)
-    head_b = grad_head.astype(bfloat)
-    d_output, head_b = lax.optimization_barrier((d_output, head_b))
-    heads = lax.all_gather(head_b, "dp", axis=0, tiled=True)
+    grad_head = after(grad_head, d_half, *((stream_all,) if few else ()))
+    heads = [
+        lax.all_gather(half_b, "dp", axis=0, tiled=True)
+        for half_b in jnp.split(grad_head.astype(bfloat), [vrows * 3 // 4])
+    ]
     d_output = exchange(d_output.astype(bfloat).reshape(outer, CAP, width), "hi")
     if few:
         d_output, kept_all = lax.optimization_barrier((d_output, kept_all))
@@ -963,6 +986,7 @@
         init_normed,
         init_inverse,
         shard,
+        heads[0],
     )
     grad_small = jnp.concatenate([sums_back[:5], sums_feed[:9]])
     mask_sum = sums_back[5]
@@ -1084,7 +1108,7 @@
             wanted_t.reshape(devices, BUCKET), ALL, 0, 0, tiled=True
         )
         given_t = of_both(give(hot_t, False, plain_exchange))
-        return (turn + 1,) + tuple(into_rows(grads, 1, asked_t, given_t, sides))
+        return (turn + 1,) + tuple(into_rows([grads], 1, asked_t, given_t, sides))
 
     _, table_grad, table_square_sum = lax.while_loop(
         lambda state: state[0] < rounds,

time: 550 us -> 540 us (0.982)
  waiting for transfers between devices: 234 us -> 217 us
  local copies, waits for them, and re-layouts: 49.9 us -> 56.2 us
    ppermute x1, waiting for transfers between devices: 52.5 us -> 42 us  [of_both(): return jnp.concatenate([rows, lax.ppermute(rows, 'dp', [(0, 1), (1, 0)])])]
    all_to_all x12, waiting for transfers between devices: 103 us -> 94.6 us  [__call__(): self.last = lax.all_to_all(values, axes, 0, 0, tiled=True)]
  transfers between devices with their start and end apart: 20 -> 21, of which waited for: 14 -> 15; matrix products, arithmetic and copies ran while one was open for 22% -> 22% of each run, Pallas kernels for 4% -> 6%
where the time goes in v11:
time: 540 us; the launch traced here: 531 us
  waiting for transfers between devices  217 us (40%)
  Pallas kernels  73.7 us (14%)
  starting transfers between devices  56.3 us (10%)
  local copies, waits for them, and re-layouts  56.2 us (10%)
  other arithmetic  50.9 us (9%)
  matrix products  31.1 us (6%)
  between operations  25.6 us (5%)
  blocking collectives  20.2 us (4%)
    all_to_all x12, waiting for transfers between devices, __call__(): self.last = lax.all_to_all(values, axes, 0, 0, tiled=True)  94.6 us
    all_gather x1, waiting for transfers between devices, on_device(): shard = lax.all_gather(shard.astype(bfloat), ALL, axis=0, tiled=True)  57.1 us
    all_to_all x12, starting transfers between devices, __call__(): self.last = lax.all_to_all(values, axes, 0, 0, tiled=True)  54.3 us
    ppermute x1, waiting for transfers between devices, of_both(): return jnp.concatenate([rows, lax.ppermute(rows, 'dp', [(0, 1), (1, 0)])])  42 us
    pallas_call x5, Pallas kernels, kernel_call(): pl.pallas_call(body, grid=(steps,), in_specs=[spec(array.shape, block, in...  41.7 us
    all_to_all x2, blocking collectives, __call__(): self.last = lax.all_to_all(values, axes, 0, 0, tiled=True)  20.2 us
    dot_general x7, matrix products, rows_dot(): lax.dot_general(left_op, right_op, (((0,), (0,)), ((), ())), preferred_el...  19.1 us
    ppermute x2, waiting for transfers between devices, swapped(): theirs = lax.ppermute(part(1 - side).astype(kind), axis, [(0, 1), (1, 0)])  13.2 us
  transfers between devices with their start and end apart: 21, of which 15 were waited for; matrix products, arithmetic and copies ran while one was open for 22% of the time, Pallas kernels for 6%

profile of v11, /device:TPU:0, one launch (start us, length us, event | category | flops | bytes accessed | tf_op | source)
XLA Modules:
  0.0 530.7 jit_solution(13488210485605980756)
XLA Ops:
  19.7 7.3 %all-to-all-start.4 = ((s32[32,1,256]{2,1,0:T(1,128)}), s32[32,1,256]{2,1,0:T(1,128)S(1)}, u32[]{:S(2)}, u32[]{:S(2)}) async-start(s32[32,1,256]{2,1,0:T(1,128)} %copy.283), calls=%async_computation.4 | async-start | bytes 65536 | tf_op jit(solution)/shard_map/all_to_all | solution.py:718
  27.0 7.6 %all-to-all-done.4 = s32[32,1,256]{2,1,0:T(1,128)S(1)} async-done(((s32[32,1,256]{2,1,0:T(1,128)}), s32[32,1,256]{2,1,0:T(1,128)S(1)}, u32[]{:S(2)}, u32[]{:S(2)}) %all-to-all-start.4) | async-done | bytes 32800 | tf_op jit(solution)/shard_map/all_to_all | solution.py:718
  48.0 28.0 %all-to-all-done.5 = bf16[16,32,768]{2,1,0:T(8,128)(2,1)} async-done(((bf16[16,32,768]{2,1,0:T(8,128)(2,1)}), bf16[16,32,768]{2,1,0:T(8,128)(2,1)}, u32[]{:S(2)}, u32[]{:S(2)}) %all-to-all-start.5) | async-done | bytes 786464 | tf_op jit(solution)/shard_map/all_to_all | solution.py:718
  78.4 57.1 %all-gather.7.cloned.1.call-done.shared_ref.weight_ref.up_ref.down_ref = bf16[768,9600]{1,0:T(8,128)(2,1)} async-done(((bf16[24,9600]{1,0:T(8,128)(2,1)}), bf16[768,9600]{1,0:T(8,128)(2,1)}) %all-gather.7.cloned.1.call-update) | async-done | bytes 14745616 | tf_op jit(solution)/shard_map/all_gather | solution.py:812
  135.5 11.5 %attention_forward.1 = (bf16[256,768]{1,0:T(8,128)(2,1)}, bf16[256,768]{1,0:T(8,128)(2,1)}, bf16[64,768]{1,0:T(8,128)(2,1)}, bf16[64,768]{1,0:T(8,128)(2,1)}, f3...) custom-call(f32[256,768]{1,0:T(8,128)} %get-tuple-element.276.embed_, ...), custom_call_target="tpu_custom_call" | custom-call | flops 11010048 | bytes 73728 | tf_op jit(solution)/shard_map/attention_forward/pallas_call | solution.py:167
  147.1 7.2 %feed_forward.1 = (bf16[64,768]{1,0:T(8,128)(2,1)}, f32[64,3072]{1,0:T(8,128)}, bf16[64,3072]{1,0:T(8,128)(2,1)}, bf16[64,768]{1,0:T(8,128)(2,1)}, f32[64,768]{1,0:T(8,128)}, /*index=5*/f32[64,128]{1,0:T(8,128)}) custom-call(f32[64,768]{1,0:T(8,128)} %get-tuple-element.277.middle_ref, f32[14,768]{1,0:T(8,128)} %get-tuple-element.278.small_ref, ...), custom_call_target="tpu_custom_call" | custom-call | flops 9437184 | bytes 147456 | tf_op jit(solution)/shard_map/feed_forward/pallas_call | solution.py:167
  161.1 12.3 %all-to-all-done.6 = bf16[4,64,768]{2,1,0:T(8,128)(2,1)S(1)} async-done(((bf16[4,64,768]{2,1,0:T(8,128)(2,1)}), bf16[4,64,768]{2,1,0:T(8,128)(2,1)S(1)}, u32[]{:S(2)}, u32[]{:S(2)}) %all-to-all-start.6) | async-done | bytes 393248 | tf_op jit(solution)/shard_map/all_to_all | solution.py:718
  179.1 10.4 %all-to-all-done.7 = bf16[2,256,768]{2,1,0:T(8,128)(2,1)} async-done(((bf16[2,256,768]{2,1,0:T(8,128)(2,1)}), bf16[2,256,768]{2,1,0:T(8,128)(2,1)}, u32[]{:S(2)}, u32[]{:S(2)}) %all-to-all-start.7) | async-done | bytes 786464 | tf_op jit(solution)/shard_map/all_to_all | solution.py:718
  207.8 7.6 %all-to-all-done.9 = f32[16,2,1024]{2,1,0:T(2,128)S(1)} async-done(((f32[16,2,1024]{2,1,0:T(2,128)}), f32[16,2,1024]{2,1,0:T(2,128)S(1)}, u32[]{:S(2)}, u32[]{:S(2)}) %all-to-all-start.9) | async-done | bytes 131104 | tf_op jit(solution)/shard_map/all_to_all | solution.py:718
  240.7 11.3 %collective-permute-done.2 = bf16[256,768]{1,0:T(8,128)(2,1)S(1)} collective-permute-done((bf16[256,768]{1,0:T(8,128)(2,1)S(1)}, bf16[256,768]{1,0:T(8,128)(2,1)S(1)}, u32[]{:S(2)}, u32[]{:S(2)}) %collective-permute-start.2) | collective-permute-done | bytes 393248 | tf_op jit(solution)/shard_map/ppermute | solution.py:920
  252.2 15.1 %all_to_all.134.parts_ref = bf16[4,64,768]{2,1,0:T(8,128)(2,1)} all-to-all(bf16[4,64,768]{2,1,0:T(8,128)(2,1)S(1)} %bitcast.185), channel_id=1, replica_groups=mesh['dp'=2,'hi'=4,'mid'=2,'core'=2] {'hi'}, dimensions={0} | all-to-all | bytes 786432 | tf_op jit(solution)/shard_map/all_to_all | solution.py:718
  267.2 7.6 %feed_backward.1 = (bf16[64,768]{1,0:T(8,128)(2,1)}, bf16[64,3072]{1,0:T(8,128)(2,1)}, f32[64,768]{1,0:T(8,128)}, bf16[64,768]{1,0:T(8,128)(2,1)}, f32[16,768]{1,0:T(8,128)}) custom-call(bf16[4,64,768]{2,1,0:T(8,128)(2,1)} %all_to_all.134.parts_ref, f32[64,768]{1,0:T(8,128)} %get-tuple-element.289.normed_ref, f32[64,128]{1,0:T(8,128)} %get-tuple-element.290.inverse_ref, ...), custom_call_target="tpu_custom_call" | custom-call | flops 9437184 | bytes 147456 | tf_op jit(solution)/shard_map/feed_backward/pallas_call | solution.py:167
  282.6 9.5 %attention_backward.1 = (bf16[64,768]{1,0:T(8,128)(2,1)}, bf16[256,768]{1,0:T(8,128)(2,1)}, bf16[256,768]{1,0:T(8,128)(2,1)}) custom-call(bf16[64,768]{1,0:T(8,128)(2,1)} %get-tuple-element.295.d_attend_ref, bf16[256,768]{1,0:T(8,128)(2,1)} %get-tuple-element.296.key_ref, bf16[256,768]{1,0:T(8,128)(2,1)} %get-tuple-element.297.value_ref, ...), custom_call_target="tpu_custom_call" | custom-call | flops 5111808 | bytes 18432 | tf_op jit(solution)/shard_map/attention_backward/pallas_call | solution.py:167
  295.8 7.9 %all-gather.11.cloned.1.call-done.ahead_ref.refs_0_.refs_1_ = bf16[2880,768]{1,0:T(8,128)(2,1)} async-done(((bf16[1440,768]{1,0:T(8,128)(2,1)}), bf16[2880,768]{1,0:T(8,128)(2,1)}) %all-gather.11.cloned.1.call-update) | async-done | bytes 4423696 | tf_op jit(solution)/shard_map/all_gather | solution.py:937
  304.4 5.9 %projection_backward.1 = (bf16[256,768]{1,0:T(8,128)(2,1)S(1)}, f32[256,768]{1,0:T(8,128)}, f32[8,768]{1,0:T(8,128)}) custom-call(f32[64,768]{1,0:T(8,128)} %get-tuple-element.294.d_pre_ref, bf16[64,768]{1,0:T(8,128)(2,1)} %get-tuple-element.299.d_query_ref, bf16[256,768]{1,0:T(8,128)(2,1)} %get-tuple-element.300.d_key_ref, ...), custom_call_target="tpu_custom_call" | custom-call | flops 11796480 | bytes 55296 | tf_op jit(solution)/shard_map/projection_backward/pallas_call | solution.py:167
  317.6 11.3 %all-to-all-done.12 = bf16[4,288,384]{2,1,0:T(8,128)(2,1)S(1)} async-done(((bf16[4,288,384]{2,1,0:T(8,128)(2,1)}), bf16[4,288,384]{2,1,0:T(8,128)(2,1)S(1)}, u32[]{:S(2)}, u32[]{:S(2)}) %all-to-all-start.12) | async-done | bytes 884768 | tf_op jit(solution)/shard_map/all_to_all | solution.py:718
  346.0 8.8 %all-to-all-done.13 = bf16[16,32,768]{2,1,0:T(8,128)(2,1)S(1)} async-done(((bf16[16,32,768]{2,1,0:T(8,128)(2,1)}), bf16[16,32,768]{2,1,0:T(8,128)(2,1)S(1)}, u32[]{:S(2)}, u32[]{:S(2)}) %all-to-all-start.13) | async-done | bytes 786464 | tf_op jit(solution)/shard_map/all_to_all | solution.py:718
  354.8 8.7 %all-to-all-start.14 = ((bf16[32,64,96]{2,1,0:T(8,128)(2,1)}), bf16[32,64,96]{2,1,0:T(8,128)(2,1)}, u32[]{:S(2)}, u32[]{:S(2)}) async-start(bf16[32,64,96]{2,1,0:T(8,128)(2,1)} %bitcast.139), calls=%async_computation.14 | async-start | bytes 1048576 | tf_op jit(solution)/shard_map/all_to_all | solution.py:718
  398.1 42.0 %collective-permute-done.3 = bf16[512,768]{1,0:T(8,128)(2,1)} collective-permute-done((bf16[512,768]{1,0:T(8,128)(2,1)S(1)}, bf16[512,768]{1,0:T(8,128)(2,1)}, u32[]{:S(2)}, u32[]{:S(2)}) %collective-permute-start.3) | collective-permute-done | bytes 786464 | tf_op jit(solution)/shard_map/ppermute | solution.py:1009
  449.9 9.0 %table_gradient.5 = (f32[1920,768]{1,0:T(8,128)}, f32[1,768]{1,0:T(1,128)}) custom-call(bf16[2880,768]{1,0:T(8,128)(2,1)} %all-gather.11.cloned.1.call-done.ahead_ref.refs_0_.refs_1_, bf16[2880,768]{1,0:T(8,128)(2,1)} %all-gather.11.cloned.1.call-done.ahead_ref.refs_0_.refs_1_, bf16[960,768]{1,0:T(8,128)(2,1)} %all-gather.13.cloned.1.call-done.refs_2_.refs_3_, ...), custom_call_target="tpu_custom_call" | custom-call | tf_op jit(solution)/shard_map/table_gradient/pallas_call | solution.py:530
  464.2 5.7 %all-to-all-start.16 = ((f32[32,1,2]{2,1,0:T(1,128)}), f32[32,1,2]{2,1,0:T(1,128)S(1)}, u32[]{:S(2)}, u32[]{:S(2)}) async-start(f32[32,1,2]{2,1,0:T(1,128)} %copy.305), calls=%async_computation.16 | async-start | bytes 32768 | tf_op jit(solution)/shard_map/all_to_all | solution.py:718
  479.2 10.8 %update_norms.1 = (f32[8,128]{1,0:T(8,128)}, f32[3,24,3072]{2,1,0:T(8,128)}, f32[3,24,3072]{2,1,0:T(8,128)}, f32[3,24,3072]{2,1,0:T(8,128)}, f32[256,24]{1,0:T(8...) custom-call(s32[1]{0:T(128)} %bitcast.71.offset_ref, ...), custom_call_target="tpu_custom_call" | custom-call | tf_op jit(solution)/shard_map/update_norms/pallas_call | solution.py:641
  494.0 11.2 %fusion.5 = (f32[1920,768]{1,0:T(8,128)}, f32[1920,768]{1,0:T(8,128)}) fusion(f32[1920,768]{1,0:T(8,128)} %refs_3_.1, f32[1920,768]{1,0:T(8,128)} %get-tuple-element.324.refs_4_, f32[]{:T(128)S(6)} %min.3, f32[1920,768]{1,0:T(8,128)} %refs_2_.1), kind=kLoop, calls=%fused_computation.29 | loop fusion | flops 11796480 | bytes 29491204 | tf_op jit(solution)/shard_map/add | solution.py:486
  507.2 12.3 %final_update.1 = (f32[1920,768]{1,0:T(8,128)}, f32[3,24,3072]{2,1,0:T(8,128)}, f32[256,24]{1,0:T(8,128)}, f32[14,24]{1,0:T(8,128)}) custom-call(f32[32,12]{1,0:T(8,128)} %bitcast.201, f32[1920,768]{1,0:T(8,128)} %weight_ref.1, f32[1920,768]{1,0:T(8,128)} %get-tuple-element.550.first_ref, f32[1920,768]{1,0:T(8,128)} %get-tuple-element.549.second_ref, ...), custom_call_target="tpu_custom_call" | custom-call | tf_op jit(solution)/shard_map/final_update/pallas_call | solution.py:697
  (283 shorter events, 179.1 us)
Async XLA Ops:
  7.2 128.3 %all-gather.7.cloned.1.call-start = ((), (), s32[]{:S(2)}) async-start(), calls=%async_computation.18 | async-start | bytes 15206400 | tf_op jit(solution)/shard_map/all_gather | solution.py:812
  19.7 14.9 %all-to-all-start.4 = ((s32[32,1,256]{2,1,0:T(1,128)}), s32[32,1,256]{2,1,0:T(1,128)S(1)}, u32[]{:S(2)}, u32[]{:S(2)}) async-start(s32[32,1,256]{2,1,0:T(1,128)} %copy.283), calls=%async_computation.4 | async-start | bytes 65536 | tf_op jit(solution)/shard_map/all_to_all | solution.py:718
  40.2 35.7 %all-to-all-start.5 = ((bf16[16,32,768]{2,1,0:T(8,128)(2,1)}), bf16[16,32,768]{2,1,0:T(8,128)(2,1)}, u32[]{:S(2)}, u32[]{:S(2)}) async-start(bf16[16,32,768]{2,1,0:T(8,128)(2,1)} %broadcast_select_fusion.1), calls=%async_computation.5 | async-start | bytes 1572864 | tf_op jit(solution)/shard_map/all_to_all | solution.py:718
  44.5 179.6 %all-gather.9.cloned.1.call-start = ((), (), s32[]{:S(2)}) async-start(), calls=%async_computation.19 | async-start | bytes 1966080 | tf_op jit(solution)/shard_map/all_gather | solution.py:898
  147.1 120.2 %all-gather.15.cloned.1.call-start = ((), (), s32[]{:S(2)}) async-start(), calls=%async_computation.22 | async-start | bytes 6488064 | tf_op jit(solution)/shard_map/all_gather | solution.py:897
  157.6 15.8 %all-to-all-start.6 = ((bf16[4,64,768]{2,1,0:T(8,128)(2,1)}), bf16[4,64,768]{2,1,0:T(8,128)(2,1)S(1)}, u32[]{:S(2)}, u32[]{:S(2)}) async-start(bf16[4,64,768]{2,1,0:T(8,128)(2,1)} %broadcast_in_dim.352), calls=%async_computation.6 | async-start | bytes 786432 | tf_op jit(solution)/shard_map/all_to_all | solution.py:718
  174.3 15.1 %all-to-all-start.7 = ((bf16[2,256,768]{2,1,0:T(8,128)(2,1)}), bf16[2,256,768]{2,1,0:T(8,128)(2,1)}, u32[]{:S(2)}, u32[]{:S(2)}) async-start(bf16[2,256,768]{2,1,0:T(8,128)(2,1)} %broadcast_in_dim.354), calls=%async_computation.7 | async-start | bytes 1572864 | tf_op jit(solution)/shard_map/all_to_all | solution.py:718
  203.2 12.2 %all-to-all-start.9 = ((f32[16,2,1024]{2,1,0:T(2,128)}), f32[16,2,1024]{2,1,0:T(2,128)S(1)}, u32[]{:S(2)}, u32[]{:S(2)}) async-start(f32[16,2,1024]{2,1,0:T(2,128)} %broadcast_in_dim.357), calls=%async_computation.9 | async-start | bytes 262144 | tf_op jit(solution)/shard_map/all_to_all | solution.py:718
  207.4 96.2 %all-gather.11.cloned.1.call-start = ((), (), s32[]{:S(2)}) async-start(), calls=%async_computation.20 | async-start | bytes 6635520 | tf_op jit(solution)/shard_map/all_gather | solution.py:937
  224.1 3.8 collective-permute-start.1
  239.9 129.9 %all-gather.17.cloned.1.call-start = ((), (), s32[]{:S(2)}) async-start(), calls=%async_computation.23 | async-start | bytes 3244032 | tf_op jit(solution)/shard_map/all_gather | solution.py:963
  240.7 11.4 %collective-permute-start.2 = (bf16[256,768]{1,0:T(8,128)(2,1)S(1)}, bf16[256,768]{1,0:T(8,128)(2,1)S(1)}, u32[]{:S(2)}, u32[]{:S(2)}) collective-permute-start(bf16[256,768]{1,0:T(8,128)(2,1)S(1)} %dynamic-slice_convert_fusion), channel_id=1, source_target_pairs={{0,2},{2,0},{1,3},{3,1},{4,6},{6,4},{5,7},{7,5},{8,10},{10,8},{9,1... | collective-permute-start | bytes 1179656 | tf_op jit(solution)/shard_map/ppermute | solution.py:920
  279.9 31.4 %all-to-all-start.11 = ((bf16[32,64,120]{2,1,0:T(8,128)(2,1)}), bf16[32,64,120]{2,1,0:T(8,128)(2,1)S(1)}, u32[]{:S(2)}, u32[]{:S(2)}) async-start(bf16[32,64,120]{2,1,0:T(8,128)(2,1)} %maximum_bitcast_fusion.1), calls=%async_computation.11 | async-start | bytes 1048576 | tf_op jit(solution)/shard_map/all_to_all | solution.py:718
  312.6 16.2 %all-to-all-start.12 = ((bf16[4,288,384]{2,1,0:T(8,128)(2,1)}), bf16[4,288,384]{2,1,0:T(8,128)(2,1)S(1)}, u32[]{:S(2)}, u32[]{:S(2)}) async-start(bf16[4,288,384]{2,1,0:T(8,128)(2,1)} %copy.295), calls=%async_computation.12 | async-start | bytes 1769472 | tf_op jit(solution)/shard_map/all_to_all | solution.py:718
  317.6 21.0 %copy-start.31 = (f32[8,768]{1,0:T(8,128)S(1)}, f32[8,768]{1,0:T(8,128)}, u32[]{:S(2)}) copy-start(f32[8,768]{1,0:T(8,128)} %get-tuple-element.306) | copy-start | bytes 73732
  317.6 21.0 %copy-start.30 = (f32[16,768]{1,0:T(8,128)S(1)}, f32[16,768]{1,0:T(8,128)}, u32[]{:S(2)}) copy-start(f32[16,768]{1,0:T(8,128)} %get-tuple-element.318) | copy-start | bytes 147460
  328.8 25.9 %all-to-all-start.13 = ((bf16[16,32,768]{2,1,0:T(8,128)(2,1)}), bf16[16,32,768]{2,1,0:T(8,128)(2,1)S(1)}, u32[]{:S(2)}, u32[]{:S(2)}) async-start(bf16[16,32,768]{2,1,0:T(8,128)(2,1)} %select_convert_fusion), calls=%async_computation.13 | async-start | bytes 1572864 | tf_op jit(solution)/shard_map/all_to_all | solution.py:718
  354.8 13.4 %copy-start.4 = (bf16[16,32,768]{2,1,0:T(8,128)(2,1)}, bf16[16,32,768]{2,1,0:T(8,128)(2,1)S(1)}, u32[]{:S(2)}) copy-start(bf16[16,32,768]{2,1,0:T(8,128)(2,1)S(1)} %all-to-all-done.13) | copy-start | bytes 2359300
  354.8 25.0 %all-to-all-start.14 = ((bf16[32,64,96]{2,1,0:T(8,128)(2,1)}), bf16[32,64,96]{2,1,0:T(8,128)(2,1)}, u32[]{:S(2)}, u32[]{:S(2)}) async-start(bf16[32,64,96]{2,1,0:T(8,128)(2,1)} %bitcast.139), calls=%async_computation.14 | async-start | bytes 1048576 | tf_op jit(solution)/shard_map/all_to_all | solution.py:718
  385.1 57.4 %all-to-all-start.15 = ((bf16[32,24,1062]{2,1,0:T(8,128)(2,1)}), bf16[32,24,1062]{2,1,0:T(8,128)(2,1)S(1)}, u32[]{:S(2)}, u32[]{:S(2)}) async-start(bf16[32,24,1062]{2,1,0:T(8,128)(2,1)} %concatenate.83), calls=%async_computation.15 | async-start | bytes 3538944 | tf_op jit(solution)/shard_map/all_to_all | solution.py:718
  387.9 61.9 %all-gather.13.cloned.1.call-start = ((), (), s32[]{:S(2)}) async-start(), calls=%async_computation.21 | async-start | bytes 2211840 | tf_op jit(solution)/shard_map/all_gather | solution.py:937
  388.0 52.1 %collective-permute-start.3 = (bf16[512,768]{1,0:T(8,128)(2,1)S(1)}, bf16[512,768]{1,0:T(8,128)(2,1)}, u32[]{:S(2)}, u32[]{:S(2)}) collective-permute-start(bf16[512,768]{1,0:T(8,128)(2,1)S(1)} %bitcast.170), channel_id=1, source_target_pairs={{0,16},{16,0},{1,17},{17,1},{2,18},{18,2},{3,19},{19,3},{4,20},{20... | collective-permute-start | bytes 2359304 | tf_op jit(solution)/shard_map/ppermute | solution.py:1009
  464.2 12.9 %all-to-all-start.16 = ((f32[32,1,2]{2,1,0:T(1,128)}), f32[32,1,2]{2,1,0:T(1,128)S(1)}, u32[]{:S(2)}, u32[]{:S(2)}) async-start(f32[32,1,2]{2,1,0:T(1,128)} %copy.305), calls=%async_computation.16 | async-start | bytes 32768 | tf_op jit(solution)/shard_map/all_to_all | solution.py:718
  491.4 15.2 %all-to-all-start.17 = ((f32[32,1,12]{2,1,0:T(1,128)}), f32[32,1,12]{2,1,0:T(1,128)S(1)}, u32[]{:S(2)}, u32[]{:S(2)}) async-start(f32[32,1,12]{2,1,0:T(1,128)} %bitcast.81), calls=%async_computation.17 | async-start | bytes 32768 | tf_op jit(solution)/shard_map/all_to_all | solution.py:718
  (31 other events, 184.4 us)
Sparse Core Ops, SparseCore 0:
  11.5 124.0 all-gather.6
  147.2 17.8 all-gather.8
  167.9 70.2 all-gather.14
  240.2 63.4 all-gather.10
  306.4 63.3 all-gather.16
  394.9 47.5 all-gather.12

commit v12 on v11

--- a/solution.py
+++ b/solution.py
@@ -1022,7 +1022,7 @@
 
     last = (jnp.arange(BUCKET) == BUCKET - 1)[None, :]
     left_row = jnp.where(lax.axis_index(VOC) == mask_owner, MASK_ID - first_row, -1)
-    given = give(hot, True, exchange)
+    given = of_both(give(hot, True, exchange))
 
     if few:
         near_pos = packet[:, BUCKET + CAP : tail].reshape(dp_devs * outer, near * CAP)
@@ -1045,7 +1045,7 @@
         results = jnp.concatenate(
             [grad_pair, grad_ask, grad_up, grad_down, grad_out, shared_grad], axis=1
         )
-        results = results.astype(bfloat)
+        results = after(results.astype(bfloat), given[-1:])
         results = exchange.rows(results, devices).astype(single)
         sides = after(sides, results)
         pieces = 3 * piece
@@ -1097,7 +1097,7 @@
         position_grad, small_grad = shared_grad[:length], shared_grad[length:]
         part_square = jnp.sum(layer_grad * layer_grad) + jnp.sum(shared_grad * shared_grad)
     table_grad, table_square_sum = into_rows(
-        heads, dp_devs, jnp.where(last, left_row, asked), of_both(given), sides
+        heads, dp_devs, jnp.where(last, left_row, asked), given, sides
     )
 
     def more_grads(state):

time: 540 us -> 538 us (level)
    ppermute x1, waiting for transfers between devices: 42 us -> 12.1 us  [of_both(): return jnp.concatenate([rows, lax.ppermute(rows, 'dp', [(0, 1), (1, 0)])])]
    all_to_all x12, waiting for transfers between devices: 94.6 us -> 121 us  [__call__(): self.last = lax.all_to_all(values, axes, 0, 0, tiled=True)]
  transfers between devices with their start and end apart: 21 -> 21, of which waited for: 15 -> 14; matrix products, arithmetic and copies ran while one was open for 22% -> 23% of each run, Pallas kernels for 6% -> 6%
where the time goes in v12:
time: 538 us; the launch traced here: 529 us
  waiting for transfers between devices  212 us (39%)
  Pallas kernels  73.7 us (14%)
  local copies, waits for them, and re-layouts  57.2 us (11%)
  starting transfers between devices  55.2 us (10%)
  other arithmetic  52.2 us (10%)
  matrix products  32.5 us (6%)
  between operations  26.3 us (5%)
  blocking collectives  20.1 us (4%)
    all_to_all x12, waiting for transfers between devices, __call__(): self.last = lax.all_to_all(values, axes, 0, 0, tiled=True)  121 us
    all_gather x1, waiting for transfers between devices, on_device(): shard = lax.all_gather(shard.astype(bfloat), ALL, axis=0, tiled=True)  57.1 us
    all_to_all x12, starting transfers between devices, __call__(): self.last = lax.all_to_all(values, axes, 0, 0, tiled=True)  54 us
    pallas_call x5, Pallas kernels, kernel_call(): pl.pallas_call(body, grid=(steps,), in_specs=[spec(array.shape, block, in...  41.7 us
    dot_general x7, matrix products, rows_dot(): lax.dot_general(left_op, right_op, (((0,), (0,)), ((), ())), preferred_el...  20.5 us
    all_to_all x2, blocking collectives, __call__(): self.last = lax.all_to_all(values, axes, 0, 0, tiled=True)  20.1 us
    ppermute x2, waiting for transfers between devices, swapped(): theirs = lax.ppermute(part(1 - side).astype(kind), axis, [(0, 1), (1, 0)])  13.2 us
    pallas_call x1, Pallas kernels, final_update(): pl.pallas_call(final_kernel, grid=(vrows // rows,), in_specs=[fixed(pairs...  12.3 us
  transfers between devices with their start and end apart: 21, of which 14 were waited for; matrix products, arithmetic and copies ran while one was open for 23% of the time, Pallas kernels for 6%

profile of v12, /device:TPU:0, one launch (start us, length us, event | category | flops | bytes accessed | tf_op | source)
XLA Modules:
  0.0 529.0 jit_solution(17033983417871547036)
XLA Ops:
  19.7 7.3 %all-to-all-start.4 = ((s32[32,1,256]{2,1,0:T(1,128)}), s32[32,1,256]{2,1,0:T(1,128)S(1)}, u32[]{:S(2)}, u32[]{:S(2)}) async-start(s32[32,1,256]{2,1,0:T(1,128)} %copy.283), calls=%async_computation.4 | async-start | bytes 65536 | tf_op jit(solution)/shard_map/all_to_all | solution.py:718
  27.0 7.6 %all-to-all-done.4 = s32[32,1,256]{2,1,0:T(1,128)S(1)} async-done(((s32[32,1,256]{2,1,0:T(1,128)}), s32[32,1,256]{2,1,0:T(1,128)S(1)}, u32[]{:S(2)}, u32[]{:S(2)}) %all-to-all-start.4) | async-done | bytes 32800 | tf_op jit(solution)/shard_map/all_to_all | solution.py:718
  47.9 28.0 %all-to-all-done.5 = bf16[16,32,768]{2,1,0:T(8,128)(2,1)} async-done(((bf16[16,32,768]{2,1,0:T(8,128)(2,1)}), bf16[16,32,768]{2,1,0:T(8,128)(2,1)}, u32[]{:S(2)}, u32[]{:S(2)}) %all-to-all-start.5) | async-done | bytes 786464 | tf_op jit(solution)/shard_map/all_to_all | solution.py:718
  78.4 57.1 %all-gather.7.cloned.1.call-done.shared_ref.weight_ref.up_ref.down_ref = bf16[768,9600]{1,0:T(8,128)(2,1)} async-done(((bf16[24,9600]{1,0:T(8,128)(2,1)}), bf16[768,9600]{1,0:T(8,128)(2,1)}) %all-gather.7.cloned.1.call-update) | async-done | bytes 14745616 | tf_op jit(solution)/shard_map/all_gather | solution.py:812
  135.5 11.5 %attention_forward.1 = (bf16[256,768]{1,0:T(8,128)(2,1)}, bf16[256,768]{1,0:T(8,128)(2,1)}, bf16[64,768]{1,0:T(8,128)(2,1)}, bf16[64,768]{1,0:T(8,128)(2,1)}, f3...) custom-call(f32[256,768]{1,0:T(8,128)} %get-tuple-element.276.embed_, ...), custom_call_target="tpu_custom_call" | custom-call | flops 11010048 | bytes 73728 | tf_op jit(solution)/shard_map/attention_forward/pallas_call | solution.py:167
  147.1 7.2 %feed_forward.1 = (bf16[64,768]{1,0:T(8,128)(2,1)}, f32[64,3072]{1,0:T(8,128)}, bf16[64,3072]{1,0:T(8,128)(2,1)}, bf16[64,768]{1,0:T(8,128)(2,1)}, f32[64,768]{1,0:T(8,128)}, /*index=5*/f32[64,128]{1,0:T(8,128)}) custom-call(f32[64,768]{1,0:T(8,128)} %get-tuple-element.277.middle_ref, f32[14,768]{1,0:T(8,128)} %get-tuple-element.278.small_ref, ...), custom_call_target="tpu_custom_call" | custom-call | flops 9437184 | bytes 147456 | tf_op jit(solution)/shard_map/feed_forward/pallas_call | solution.py:167
  161.1 12.3 %all-to-all-done.6 = bf16[4,64,768]{2,1,0:T(8,128)(2,1)S(1)} async-done(((bf16[4,64,768]{2,1,0:T(8,128)(2,1)}), bf16[4,64,768]{2,1,0:T(8,128)(2,1)S(1)}, u32[]{:S(2)}, u32[]{:S(2)}) %all-to-all-start.6) | async-done | bytes 393248 | tf_op jit(solution)/shard_map/all_to_all | solution.py:718
  179.1 10.4 %all-to-all-done.7 = bf16[2,256,768]{2,1,0:T(8,128)(2,1)} async-done(((bf16[2,256,768]{2,1,0:T(8,128)(2,1)}), bf16[2,256,768]{2,1,0:T(8,128)(2,1)}, u32[]{:S(2)}, u32[]{:S(2)}) %all-to-all-start.7) | async-done | bytes 786464 | tf_op jit(solution)/shard_map/all_to_all | solution.py:718
  207.8 7.6 %all-to-all-done.9 = f32[16,2,1024]{2,1,0:T(2,128)S(1)} async-done(((f32[16,2,1024]{2,1,0:T(2,128)}), f32[16,2,1024]{2,1,0:T(2,128)S(1)}, u32[]{:S(2)}, u32[]{:S(2)}) %all-to-all-start.9) | async-done | bytes 131104 | tf_op jit(solution)/shard_map/all_to_all | solution.py:718
  240.7 11.3 %collective-permute-done.2 = bf16[256,768]{1,0:T(8,128)(2,1)S(1)} collective-permute-done((bf16[256,768]{1,0:T(8,128)(2,1)S(1)}, bf16[256,768]{1,0:T(8,128)(2,1)S(1)}, u32[]{:S(2)}, u32[]{:S(2)}) %collective-permute-start.2) | collective-permute-done | bytes 393248 | tf_op jit(solution)/shard_map/ppermute | solution.py:920
  252.1 15.0 %all_to_all.134.parts_ref = bf16[4,64,768]{2,1,0:T(8,128)(2,1)} all-to-all(bf16[4,64,768]{2,1,0:T(8,128)(2,1)S(1)} %bitcast.186), channel_id=1, replica_groups=mesh['dp'=2,'hi'=4,'mid'=2,'core'=2] {'hi'}, dimensions={0} | all-to-all | bytes 786432 | tf_op jit(solution)/shard_map/all_to_all | solution.py:718
  267.1 7.6 %feed_backward.1 = (bf16[64,768]{1,0:T(8,128)(2,1)}, bf16[64,3072]{1,0:T(8,128)(2,1)}, f32[64,768]{1,0:T(8,128)}, bf16[64,768]{1,0:T(8,128)(2,1)}, f32[16,768]{1,0:T(8,128)}) custom-call(bf16[4,64,768]{2,1,0:T(8,128)(2,1)} %all_to_all.134.parts_ref, f32[64,768]{1,0:T(8,128)} %get-tuple-element.289.normed_ref, f32[64,128]{1,0:T(8,128)} %get-tuple-element.290.inverse_ref, ...), custom_call_target="tpu_custom_call" | custom-call | flops 9437184 | bytes 147456 | tf_op jit(solution)/shard_map/feed_backward/pallas_call | solution.py:167
  282.4 9.5 %attention_backward.1 = (bf16[64,768]{1,0:T(8,128)(2,1)}, bf16[256,768]{1,0:T(8,128)(2,1)}, bf16[256,768]{1,0:T(8,128)(2,1)}) custom-call(bf16[64,768]{1,0:T(8,128)(2,1)} %get-tuple-element.295.d_attend_ref, bf16[256,768]{1,0:T(8,128)(2,1)} %get-tuple-element.296.key_ref, bf16[256,768]{1,0:T(8,128)(2,1)} %get-tuple-element.297.value_ref, ...), custom_call_target="tpu_custom_call" | custom-call | flops 5111808 | bytes 18432 | tf_op jit(solution)/shard_map/attention_backward/pallas_call | solution.py:167
  295.6 8.0 %all-gather.11.cloned.1.call-done.ahead_ref.refs_0_.refs_1_ = bf16[2880,768]{1,0:T(8,128)(2,1)} async-done(((bf16[1440,768]{1,0:T(8,128)(2,1)}), bf16[2880,768]{1,0:T(8,128)(2,1)}) %all-gather.11.cloned.1.call-update) | async-done | bytes 4423696 | tf_op jit(solution)/shard_map/all_gather | solution.py:937
  304.4 5.9 %projection_backward.1 = (bf16[256,768]{1,0:T(8,128)(2,1)S(1)}, f32[256,768]{1,0:T(8,128)}, f32[8,768]{1,0:T(8,128)}) custom-call(f32[64,768]{1,0:T(8,128)} %get-tuple-element.294.d_pre_ref, bf16[64,768]{1,0:T(8,128)(2,1)} %get-tuple-element.299.d_query_ref, bf16[256,768]{1,0:T(8,128)(2,1)} %get-tuple-element.300.d_key_ref, ...), custom_call_target="tpu_custom_call" | custom-call | flops 11796480 | bytes 55296 | tf_op jit(solution)/shard_map/projection_backward/pallas_call | solution.py:167
  317.6 11.3 %all-to-all-done.12 = bf16[4,288,384]{2,1,0:T(8,128)(2,1)S(1)} async-done(((bf16[4,288,384]{2,1,0:T(8,128)(2,1)}), bf16[4,288,384]{2,1,0:T(8,128)(2,1)S(1)}, u32[]{:S(2)}, u32[]{:S(2)}) %all-to-all-start.12) | async-done | bytes 884768 | tf_op jit(solution)/shard_map/all_to_all | solution.py:718
  346.3 8.5 %all-to-all-done.13 = bf16[16,32,768]{2,1,0:T(8,128)(2,1)S(1)} async-done(((bf16[16,32,768]{2,1,0:T(8,128)(2,1)}), bf16[16,32,768]{2,1,0:T(8,128)(2,1)S(1)}, u32[]{:S(2)}, u32[]{:S(2)}) %all-to-all-start.13) | async-done | bytes 786464 | tf_op jit(solution)/shard_map/all_to_all | solution.py:718
  355.6 9.3 %all-to-all-start.14 = ((bf16[32,64,96]{2,1,0:T(8,128)(2,1)}), bf16[32,64,96]{2,1,0:T(8,128)(2,1)}, u32[]{:S(2)}, u32[]{:S(2)}) async-start(bf16[32,64,96]{2,1,0:T(8,128)(2,1)} %bitcast.140), calls=%async_computation.14 | async-start | bytes 1048576 | tf_op jit(solution)/shard_map/all_to_all | solution.py:718
  369.7 12.1 %collective-permute-done.3 = bf16[512,768]{1,0:T(8,128)(2,1)} collective-permute-done((bf16[512,768]{1,0:T(8,128)(2,1)S(1)}, bf16[512,768]{1,0:T(8,128)(2,1)}, u32[]{:S(2)}, u32[]{:S(2)}) %collective-permute-start.3) | collective-permute-done | bytes 786464 | tf_op jit(solution)/shard_map/ppermute | solution.py:1009
  411.7 32.1 %all-to-all-done.15 = bf16[32,24,1062]{2,1,0:T(8,128)(2,1)S(1)} async-done(((bf16[32,24,1062]{2,1,0:T(8,128)(2,1)}), bf16[32,24,1062]{2,1,0:T(8,128)(2,1)S(1)}, u32[]{:S(2)}, u32[]{:S(2)}) %all-to-all-start.15) | async-done | bytes 1631264 | tf_op jit(solution)/shard_map/all_to_all | solution.py:718
  451.1 9.0 %table_gradient.5 = (f32[1920,768]{1,0:T(8,128)}, f32[1,768]{1,0:T(1,128)}) custom-call(bf16[2880,768]{1,0:T(8,128)(2,1)} %all-gather.11.cloned.1.call-done.ahead_ref.refs_0_.refs_1_, bf16[2880,768]{1,0:T(8,128)(2,1)} %all-gather.11.cloned.1.call-done.ahead_ref.refs_0_.refs_1_, bf16[960,768]{1,0:T(8,128)(2,1)} %all-gather.13.cloned.1.call-done.refs_2_.refs_3_, ...), custom_call_target="tpu_custom_call" | custom-call | tf_op jit(solution)/shard_map/table_gradient/pallas_call | solution.py:530
  477.5 10.9 %update_norms.1 = (f32[8,128]{1,0:T(8,128)}, f32[3,24,3072]{2,1,0:T(8,128)}, f32[3,24,3072]{2,1,0:T(8,128)}, f32[3,24,3072]{2,1,0:T(8,128)}, f32[256,24]{1,0:T(8...) custom-call(s32[1]{0:T(128)} %bitcast.72.offset_ref, ...), custom_call_target="tpu_custom_call" | custom-call | tf_op jit(solution)/shard_map/update_norms/pallas_call | solution.py:641
  492.3 11.2 %fusion.5 = (f32[1920,768]{1,0:T(8,128)}, f32[1920,768]{1,0:T(8,128)}) fusion(f32[1920,768]{1,0:T(8,128)} %refs_3_.1, f32[1920,768]{1,0:T(8,128)} %get-tuple-element.324.refs_4_, f32[]{:T(128)S(6)} %min.3, f32[1920,768]{1,0:T(8,128)} %refs_2_.1), kind=kLoop, calls=%fused_computation.29 | loop fusion | flops 11796480 | bytes 29491204 | tf_op jit(solution)/shard_map/add | solution.py:486
  505.5 12.3 %final_update.1 = (f32[1920,768]{1,0:T(8,128)}, f32[3,24,3072]{2,1,0:T(8,128)}, f32[256,24]{1,0:T(8,128)}, f32[14,24]{1,0:T(8,128)}) custom-call(f32[32,12]{1,0:T(8,128)} %bitcast.202, f32[1920,768]{1,0:T(8,128)} %weight_ref.1, f32[1920,768]{1,0:T(8,128)} %get-tuple-element.550.first_ref, f32[1920,768]{1,0:T(8,128)} %get-tuple-element.549.second_ref, ...), custom_call_target="tpu_custom_call" | custom-call | tf_op jit(solution)/shard_map/final_update/pallas_call | solution.py:697
  (279 shorter events, 179.9 us)
Async XLA Ops:
  7.2 128.3 %all-gather.7.cloned.1.call-start = ((), (), s32[]{:S(2)}) async-start(), calls=%async_computation.18 | async-start | bytes 15206400 | tf_op jit(solution)/shard_map/all_gather | solution.py:812
  19.7 14.9 %all-to-all-start.4 = ((s32[32,1,256]{2,1,0:T(1,128)}), s32[32,1,256]{2,1,0:T(1,128)S(1)}, u32[]{:S(2)}, u32[]{:S(2)}) async-start(s32[32,1,256]{2,1,0:T(1,128)} %copy.283), calls=%async_computation.4 | async-start | bytes 65536 | tf_op jit(solution)/shard_map/all_to_all | solution.py:718
  40.2 35.7 %all-to-all-start.5 = ((bf16[16,32,768]{2,1,0:T(8,128)(2,1)}), bf16[16,32,768]{2,1,0:T(8,128)(2,1)}, u32[]{:S(2)}, u32[]{:S(2)}) async-start(bf16[16,32,768]{2,1,0:T(8,128)(2,1)} %broadcast_select_fusion.1), calls=%async_computation.5 | async-start | bytes 1572864 | tf_op jit(solution)/shard_map/all_to_all | solution.py:718
  44.5 179.6 %all-gather.9.cloned.1.call-start = ((), (), s32[]{:S(2)}) async-start(), calls=%async_computation.19 | async-start | bytes 1966080 | tf_op jit(solution)/shard_map/all_gather | solution.py:898
  147.0 120.0 %all-gather.15.cloned.1.call-start = ((), (), s32[]{:S(2)}) async-start(), calls=%async_computation.22 | async-start | bytes 6488064 | tf_op jit(solution)/shard_map/all_gather | solution.py:897
  157.6 15.8 %all-to-all-start.6 = ((bf16[4,64,768]{2,1,0:T(8,128)(2,1)}), bf16[4,64,768]{2,1,0:T(8,128)(2,1)S(1)}, u32[]{:S(2)}, u32[]{:S(2)}) async-start(bf16[4,64,768]{2,1,0:T(8,128)(2,1)} %broadcast_in_dim.352), calls=%async_computation.6 | async-start | bytes 786432 | tf_op jit(solution)/shard_map/all_to_all | solution.py:718
  174.3 15.1 %all-to-all-start.7 = ((bf16[2,256,768]{2,1,0:T(8,128)(2,1)}), bf16[2,256,768]{2,1,0:T(8,128)(2,1)}, u32[]{:S(2)}, u32[]{:S(2)}) async-start(bf16[2,256,768]{2,1,0:T(8,128)(2,1)} %broadcast_in_dim.354), calls=%async_computation.7 | async-start | bytes 1572864 | tf_op jit(solution)/shard_map/all_to_all | solution.py:718
  203.2 12.2 %all-to-all-start.9 = ((f32[16,2,1024]{2,1,0:T(2,128)}), f32[16,2,1024]{2,1,0:T(2,128)S(1)}, u32[]{:S(2)}, u32[]{:S(2)}) async-start(f32[16,2,1024]{2,1,0:T(2,128)} %broadcast_in_dim.357), calls=%async_computation.9 | async-start | bytes 262144 | tf_op jit(solution)/shard_map/all_to_all | solution.py:718
  207.4 96.2 %all-gather.11.cloned.1.call-start = ((), (), s32[]{:S(2)}) async-start(), calls=%async_computation.20 | async-start | bytes 6635520 | tf_op jit(solution)/shard_map/all_gather | solution.py:937
  224.1 3.8 collective-permute-start.1
  239.9 143.7 %all-gather.17.cloned.1.call-start = ((), (), s32[]{:S(2)}) async-start(), calls=%async_computation.23 | async-start | bytes 3244032 | tf_op jit(solution)/shard_map/all_gather | solution.py:963
  240.7 11.4 %collective-permute-start.2 = (bf16[256,768]{1,0:T(8,128)(2,1)S(1)}, bf16[256,768]{1,0:T(8,128)(2,1)S(1)}, u32[]{:S(2)}, u32[]{:S(2)}) collective-permute-start(bf16[256,768]{1,0:T(8,128)(2,1)S(1)} %dynamic-slice_convert_fusion), channel_id=1, source_target_pairs={{0,2},{2,0},{1,3},{3,1},{4,6},{6,4},{5,7},{7,5},{8,10},{10,8},{9,1... | collective-permute-start | bytes 1179656 | tf_op jit(solution)/shard_map/ppermute | solution.py:920
  279.7 31.6 %all-to-all-start.11 = ((bf16[32,64,120]{2,1,0:T(8,128)(2,1)}), bf16[32,64,120]{2,1,0:T(8,128)(2,1)S(1)}, u32[]{:S(2)}, u32[]{:S(2)}) async-start(bf16[32,64,120]{2,1,0:T(8,128)(2,1)} %maximum_bitcast_fusion.1), calls=%async_computation.11 | async-start | bytes 1048576 | tf_op jit(solution)/shard_map/all_to_all | solution.py:718
  312.6 16.2 %all-to-all-start.12 = ((bf16[4,288,384]{2,1,0:T(8,128)(2,1)}), bf16[4,288,384]{2,1,0:T(8,128)(2,1)S(1)}, u32[]{:S(2)}, u32[]{:S(2)}) async-start(bf16[4,288,384]{2,1,0:T(8,128)(2,1)} %copy.295), calls=%async_computation.12 | async-start | bytes 1769472 | tf_op jit(solution)/shard_map/all_to_all | solution.py:718
  317.6 20.9 %copy-start.28 = (f32[8,768]{1,0:T(8,128)S(1)}, f32[8,768]{1,0:T(8,128)}, u32[]{:S(2)}) copy-start(f32[8,768]{1,0:T(8,128)} %get-tuple-element.306) | copy-start | bytes 73732
  317.6 20.9 %copy-start.27 = (f32[16,768]{1,0:T(8,128)S(1)}, f32[16,768]{1,0:T(8,128)}, u32[]{:S(2)}) copy-start(f32[16,768]{1,0:T(8,128)} %get-tuple-element.318) | copy-start | bytes 147460
  328.8 25.9 %all-to-all-start.13 = ((bf16[16,32,768]{2,1,0:T(8,128)(2,1)}), bf16[16,32,768]{2,1,0:T(8,128)(2,1)S(1)}, u32[]{:S(2)}, u32[]{:S(2)}) async-start(bf16[16,32,768]{2,1,0:T(8,128)(2,1)} %select_convert_fusion), calls=%async_computation.13 | async-start | bytes 1572864 | tf_op jit(solution)/shard_map/all_to_all | solution.py:718
  354.8 14.9 %copy-start.4 = (bf16[16,32,768]{2,1,0:T(8,128)(2,1)}, bf16[16,32,768]{2,1,0:T(8,128)(2,1)S(1)}, u32[]{:S(2)}) copy-start(bf16[16,32,768]{2,1,0:T(8,128)(2,1)S(1)} %all-to-all-done.13) | copy-start | bytes 2359300
  354.8 27.0 %collective-permute-start.3 = (bf16[512,768]{1,0:T(8,128)(2,1)S(1)}, bf16[512,768]{1,0:T(8,128)(2,1)}, u32[]{:S(2)}, u32[]{:S(2)}) collective-permute-start(bf16[512,768]{1,0:T(8,128)(2,1)S(1)} %bitcast.171), channel_id=1, source_target_pairs={{0,16},{16,0},{1,17},{17,1},{2,18},{18,2},{3,19},{19,3},{4,20},{20... | collective-permute-start | bytes 2359304 | tf_op jit(solution)/shard_map/ppermute | solution.py:1009
  355.6 32.6 %all-to-all-start.14 = ((bf16[32,64,96]{2,1,0:T(8,128)(2,1)}), bf16[32,64,96]{2,1,0:T(8,128)(2,1)}, u32[]{:S(2)}, u32[]{:S(2)}) async-start(bf16[32,64,96]{2,1,0:T(8,128)(2,1)} %bitcast.140), calls=%async_computation.14 | async-start | bytes 1048576 | tf_op jit(solution)/shard_map/all_to_all | solution.py:718
  395.9 47.9 %all-to-all-start.15 = ((bf16[32,24,1062]{2,1,0:T(8,128)(2,1)}), bf16[32,24,1062]{2,1,0:T(8,128)(2,1)S(1)}, u32[]{:S(2)}, u32[]{:S(2)}) async-start(bf16[32,24,1062]{2,1,0:T(8,128)(2,1)} %broadcast_add_fusion), calls=%async_computation.15 | async-start | bytes 3538944 | tf_op jit(solution)/shard_map/all_to_all | solution.py:718
  400.9 50.3 %all-gather.13.cloned.1.call-start = ((), (), s32[]{:S(2)}) async-start(), calls=%async_computation.21 | async-start | bytes 2211840 | tf_op jit(solution)/shard_map/all_gather | solution.py:937
  465.5 9.8 %all-to-all-start.16 = ((f32[32,1,2]{2,1,0:T(1,128)}), f32[32,1,2]{2,1,0:T(1,128)S(1)}, u32[]{:S(2)}, u32[]{:S(2)}) async-start(f32[32,1,2]{2,1,0:T(1,128)} %copy.305), calls=%async_computation.16 | async-start | bytes 32768 | tf_op jit(solution)/shard_map/all_to_all | solution.py:718
  489.7 15.2 %all-to-all-start.17 = ((f32[32,1,12]{2,1,0:T(1,128)}), f32[32,1,12]{2,1,0:T(1,128)S(1)}, u32[]{:S(2)}, u32[]{:S(2)}) async-start(f32[32,1,12]{2,1,0:T(1,128)} %bitcast.82), calls=%async_computation.17 | async-start | bytes 32768 | tf_op jit(solution)/shard_map/all_to_all | solution.py:718
  (28 other events, 176.2 us)
Sparse Core Ops, SparseCore 0:
  11.5 124.0 all-gather.6
  147.2 17.8 all-gather.8
  167.9 70.2 all-gather.14
  240.2 63.4 all-gather.10
  306.4 63.8 all-gather.16
  406.1 34.6 all-gather.12

commit v13 on v12

--- a/solution.py
+++ b/solution.py
@@ -657,9 +657,9 @@
 
 
 def final_kernel(
-    pairs_ref, weight_ref, first_ref, second_ref,
+    pairs_ref, totals_ref, weight_ref, first_ref, old_ref, grad_ref,
     layer_ref, layer_dir_ref, position_ref, position_dir_ref, small_ref, small_dir_ref,
-    next_ref, layer_next_ref, position_next_ref, small_next_ref,
+    next_ref, second_ref, layer_next_ref, position_next_ref, small_next_ref,
 ):
     roots = jnp.sqrt(jnp.sum(pairs_ref[...], axis=0, keepdims=True))
 
@@ -668,8 +668,12 @@
             roots[:, 2 * group : 2 * group + 1] / roots[:, 2 * group + 1 : 2 * group + 2]
         )
 
-    weight_arr = weight_ref[...]
-    direction = adam_direction(weight_arr, first_ref[...], second_ref[...])
+    total_square = jnp.sum(totals_ref[...], axis=0, keepdims=True)[:, :1]
+    factor = jnp.minimum(1.0, clip_norm / jnp.sqrt(total_square))
+    weight_arr, clipped = weight_ref[...], grad_ref[...] * factor
+    second = beta_second * old_ref[...] + (1.0 - beta_second) * clipped * clipped
+    second_ref[...] = second
+    direction = adam_direction(weight_arr, first_ref[...], second)
     next_ref[...] = weight_arr - rate(0) * direction
 
     step = pl.program_id(0)
@@ -685,7 +689,7 @@
         small_next_ref[...] = small_ref[...] - rate(5) * small_dir_ref[...]
 
 
-def final_update(pairs, table, groups):
+def final_update(pairs, totals, table, groups):
     vrows, width = table[0].shape
     rows = row_block(vrows, 480)
     if vrows // rows < 3:
@@ -697,15 +701,15 @@
     return pl.pallas_call(
         final_kernel,
         grid=(vrows // rows,),
-        in_specs=[fixed(pairs)]
-        + [block] * 3
+        in_specs=[fixed(pairs), fixed(totals)]
+        + [block] * 4
         + [one_part] * 2
         + [fixed(array) for array in groups[2:]],
-        out_specs=[block, one_part] + [fixed(out) for out in outs[1:]],
-        out_shape=[jax.ShapeDtypeStruct((vrows, width), single)] + outs,
+        out_specs=[block, block, one_part] + [fixed(out) for out in outs[1:]],
+        out_shape=[jax.ShapeDtypeStruct((vrows, width), single)] * 2 + outs,
         cost_estimate=pl.CostEstimate(flops=0, bytes_accessed=0, transcendentals=0),
         name="final_update",
-    )(pairs, *table, *groups)
+    )(pairs, totals, *table, *groups)
 
 
 class Exchange:
@@ -1142,13 +1146,12 @@
     )
     factor_late, norms = lax.optimization_barrier((factor, norms))
     pairs = exchange.copies(norms[:6, :2].reshape(-1), ALL, devices)
-    table_first, table_second, _ = adam_moments(
-        embed_table, table_moment, table_square, table_grad, factor_late
-    )
+    table_first = beta_first * table_moment + (1.0 - beta_first) * (table_grad * factor_late)
     trust_norms = jnp.sqrt(jnp.sum(pairs, axis=0)).reshape(6, 2)
-    table_next, layer_next, position_next, small_next = final_update(
+    table_next, table_second, layer_next, position_next, small_next = final_update(
         pairs,
-        (embed_table, table_first, table_second),
+        totals,
+        (embed_table, table_first, table_square, table_grad),
         (
             layer_weights,
             layer_dir,

time: 538 us -> 539 us (level)
  transfers between devices with their start and end apart: 21 -> 21, of which waited for: 14 -> 14; matrix products, arithmetic and copies ran while one was open for 23% -> 22% of each run, Pallas kernels for 6% -> 6%
where the time goes in v13:
time: 539 us; the launch traced here: 530 us
  waiting for transfers between devices  212 us (39%)
  Pallas kernels  78.3 us (15%)
  local copies, waits for them, and re-layouts  57.3 us (11%)
  starting transfers between devices  55.2 us (10%)
  other arithmetic  49 us (9%)
  matrix products  32.5 us (6%)
  between operations  26.3 us (5%)
  blocking collectives  20.2 us (4%)
    all_to_all x12, waiting for transfers between devices, __call__(): self.last = lax.all_to_all(values, axes, 0, 0, tiled=True)  121 us
    all_gather x1, waiting for transfers between devices, on_device(): shard = lax.all_gather(shard.astype(bfloat), ALL, axis=0, tiled=True)  57.1 us
    all_to_all x12, starting transfers between devices, __call__(): self.last = lax.all_to_all(values, axes, 0, 0, tiled=True)  54 us
    pallas_call x5, Pallas kernels, kernel_call(): pl.pallas_call(body, grid=(steps,), in_specs=[spec(array.shape, block, in...  41.7 us
    dot_general x7, matrix products, rows_dot(): lax.dot_general(left_op, right_op, (((0,), (0,)), ((), ())), preferred_el...  20.5 us
    all_to_all x2, blocking collectives, __call__(): self.last = lax.all_to_all(values, axes, 0, 0, tiled=True)  20.2 us
    pallas_call x1, Pallas kernels, final_update(): pl.pallas_call(final_kernel, grid=(vrows // rows,), in_specs=[fixed(pairs...  16.8 us
    ppermute x2, waiting for transfers between devices, swapped(): theirs = lax.ppermute(part(1 - side).astype(kind), axis, [(0, 1), (1, 0)])  13.2 us
  transfers between devices with their start and end apart: 21, of which 14 were waited for; matrix products, arithmetic and copies ran while one was open for 22% of the time, Pallas kernels for 6%

profile of v13, /device:TPU:0, one launch (start us, length us, event | category | flops | bytes accessed | tf_op | source)
XLA Modules:
  0.0 530.2 jit_solution(8394908945198943728)
XLA Ops:
  19.7 7.3 %all-to-all-start.4 = ((s32[32,1,256]{2,1,0:T(1,128)}), s32[32,1,256]{2,1,0:T(1,128)S(1)}, u32[]{:S(2)}, u32[]{:S(2)}) async-start(s32[32,1,256]{2,1,0:T(1,128)} %copy.290), calls=%async_computation.4 | async-start | bytes 65536 | tf_op jit(solution)/shard_map/all_to_all | solution.py:722
  27.0 7.6 %all-to-all-done.4 = s32[32,1,256]{2,1,0:T(1,128)S(1)} async-done(((s32[32,1,256]{2,1,0:T(1,128)}), s32[32,1,256]{2,1,0:T(1,128)S(1)}, u32[]{:S(2)}, u32[]{:S(2)}) %all-to-all-start.4) | async-done | bytes 32800 | tf_op jit(solution)/shard_map/all_to_all | solution.py:722
  47.9 28.0 %all-to-all-done.5 = bf16[16,32,768]{2,1,0:T(8,128)(2,1)} async-done(((bf16[16,32,768]{2,1,0:T(8,128)(2,1)}), bf16[16,32,768]{2,1,0:T(8,128)(2,1)}, u32[]{:S(2)}, u32[]{:S(2)}) %all-to-all-start.5) | async-done | bytes 786464 | tf_op jit(solution)/shard_map/all_to_all | solution.py:722
  78.4 57.1 %all-gather.7.cloned.1.call-done.shared_ref.weight_ref.up_ref.down_ref = bf16[768,9600]{1,0:T(8,128)(2,1)} async-done(((bf16[24,9600]{1,0:T(8,128)(2,1)}), bf16[768,9600]{1,0:T(8,128)(2,1)}) %all-gather.7.cloned.1.call-update) | async-done | bytes 14745616 | tf_op jit(solution)/shard_map/all_gather | solution.py:816
  135.5 11.5 %attention_forward.1 = (bf16[256,768]{1,0:T(8,128)(2,1)}, bf16[256,768]{1,0:T(8,128)(2,1)}, bf16[64,768]{1,0:T(8,128)(2,1)}, bf16[64,768]{1,0:T(8,128)(2,1)}, f3...) custom-call(f32[256,768]{1,0:T(8,128)} %get-tuple-element.277.embed_, ...), custom_call_target="tpu_custom_call" | custom-call | flops 11010048 | bytes 73728 | tf_op jit(solution)/shard_map/attention_forward/pallas_call | solution.py:167
  147.1 7.2 %feed_forward.1 = (bf16[64,768]{1,0:T(8,128)(2,1)}, f32[64,3072]{1,0:T(8,128)}, bf16[64,3072]{1,0:T(8,128)(2,1)}, bf16[64,768]{1,0:T(8,128)(2,1)}, f32[64,768]{1,0:T(8,128)}, /*index=5*/f32[64,128]{1,0:T(8,128)}) custom-call(f32[64,768]{1,0:T(8,128)} %get-tuple-element.278.middle_ref, f32[14,768]{1,0:T(8,128)} %get-tuple-element.279.small_ref, ...), custom_call_target="tpu_custom_call" | custom-call | flops 9437184 | bytes 147456 | tf_op jit(solution)/shard_map/feed_forward/pallas_call | solution.py:167
  161.1 12.3 %all-to-all-done.6 = bf16[4,64,768]{2,1,0:T(8,128)(2,1)S(1)} async-done(((bf16[4,64,768]{2,1,0:T(8,128)(2,1)}), bf16[4,64,768]{2,1,0:T(8,128)(2,1)S(1)}, u32[]{:S(2)}, u32[]{:S(2)}) %all-to-all-start.6) | async-done | bytes 393248 | tf_op jit(solution)/shard_map/all_to_all | solution.py:722
  179.1 10.4 %all-to-all-done.7 = bf16[2,256,768]{2,1,0:T(8,128)(2,1)} async-done(((bf16[2,256,768]{2,1,0:T(8,128)(2,1)}), bf16[2,256,768]{2,1,0:T(8,128)(2,1)}, u32[]{:S(2)}, u32[]{:S(2)}) %all-to-all-start.7) | async-done | bytes 786464 | tf_op jit(solution)/shard_map/all_to_all | solution.py:722
  207.8 7.6 %all-to-all-done.9 = f32[16,2,1024]{2,1,0:T(2,128)S(1)} async-done(((f32[16,2,1024]{2,1,0:T(2,128)}), f32[16,2,1024]{2,1,0:T(2,128)S(1)}, u32[]{:S(2)}, u32[]{:S(2)}) %all-to-all-start.9) | async-done | bytes 131104 | tf_op jit(solution)/shard_map/all_to_all | solution.py:722
  240.8 11.3 %collective-permute-done.2 = bf16[256,768]{1,0:T(8,128)(2,1)S(1)} collective-permute-done((bf16[256,768]{1,0:T(8,128)(2,1)S(1)}, bf16[256,768]{1,0:T(8,128)(2,1)S(1)}, u32[]{:S(2)}, u32[]{:S(2)}) %collective-permute-start.2) | collective-permute-done | bytes 393248 | tf_op jit(solution)/shard_map/ppermute | solution.py:924
  252.2 15.0 %all_to_all.134.parts_ref = bf16[4,64,768]{2,1,0:T(8,128)(2,1)} all-to-all(bf16[4,64,768]{2,1,0:T(8,128)(2,1)S(1)} %bitcast.186), channel_id=1, replica_groups=mesh['dp'=2,'hi'=4,'mid'=2,'core'=2] {'hi'}, dimensions={0} | all-to-all | bytes 786432 | tf_op jit(solution)/shard_map/all_to_all | solution.py:722
  267.2 7.6 %feed_backward.1 = (bf16[64,768]{1,0:T(8,128)(2,1)}, bf16[64,3072]{1,0:T(8,128)(2,1)}, f32[64,768]{1,0:T(8,128)}, bf16[64,768]{1,0:T(8,128)(2,1)}, f32[16,768]{1,0:T(8,128)}) custom-call(bf16[4,64,768]{2,1,0:T(8,128)(2,1)} %all_to_all.134.parts_ref, f32[64,768]{1,0:T(8,128)} %get-tuple-element.290.normed_ref, f32[64,128]{1,0:T(8,128)} %get-tuple-element.291.inverse_ref, ...), custom_call_target="tpu_custom_call" | custom-call | flops 9437184 | bytes 147456 | tf_op jit(solution)/shard_map/feed_backward/pallas_call | solution.py:167
  282.6 9.5 %attention_backward.1 = (bf16[64,768]{1,0:T(8,128)(2,1)}, bf16[256,768]{1,0:T(8,128)(2,1)}, bf16[256,768]{1,0:T(8,128)(2,1)}) custom-call(bf16[64,768]{1,0:T(8,128)(2,1)} %get-tuple-element.296.d_attend_ref, bf16[256,768]{1,0:T(8,128)(2,1)} %get-tuple-element.297.key_ref, bf16[256,768]{1,0:T(8,128)(2,1)} %get-tuple-element.298.value_ref, ...), custom_call_target="tpu_custom_call" | custom-call | flops 5111808 | bytes 18432 | tf_op jit(solution)/shard_map/attention_backward/pallas_call | solution.py:167
  295.8 7.8 %all-gather.11.cloned.1.call-done.ahead_ref.refs_0_.refs_1_ = bf16[2880,768]{1,0:T(8,128)(2,1)} async-done(((bf16[1440,768]{1,0:T(8,128)(2,1)}), bf16[2880,768]{1,0:T(8,128)(2,1)}) %all-gather.11.cloned.1.call-update) | async-done | bytes 4423696 | tf_op jit(solution)/shard_map/all_gather | solution.py:941
  304.4 5.9 %projection_backward.1 = (bf16[256,768]{1,0:T(8,128)(2,1)S(1)}, f32[256,768]{1,0:T(8,128)}, f32[8,768]{1,0:T(8,128)}) custom-call(f32[64,768]{1,0:T(8,128)} %get-tuple-element.295.d_pre_ref, bf16[64,768]{1,0:T(8,128)(2,1)} %get-tuple-element.300.d_query_ref, bf16[256,768]{1,0:T(8,128)(2,1)} %get-tuple-element.301.d_key_ref, ...), custom_call_target="tpu_custom_call" | custom-call | flops 11796480 | bytes 55296 | tf_op jit(solution)/shard_map/projection_backward/pallas_call | solution.py:167
  317.6 11.2 %all-to-all-done.12 = bf16[4,288,384]{2,1,0:T(8,128)(2,1)S(1)} async-done(((bf16[4,288,384]{2,1,0:T(8,128)(2,1)}), bf16[4,288,384]{2,1,0:T(8,128)(2,1)S(1)}, u32[]{:S(2)}, u32[]{:S(2)}) %all-to-all-start.12) | async-done | bytes 884768 | tf_op jit(solution)/shard_map/all_to_all | solution.py:722
  346.2 8.6 %all-to-all-done.13 = bf16[16,32,768]{2,1,0:T(8,128)(2,1)S(1)} async-done(((bf16[16,32,768]{2,1,0:T(8,128)(2,1)}), bf16[16,32,768]{2,1,0:T(8,128)(2,1)S(1)}, u32[]{:S(2)}, u32[]{:S(2)}) %all-to-all-start.13) | async-done | bytes 786464 | tf_op jit(solution)/shard_map/all_to_all | solution.py:722
  355.6 9.3 %all-to-all-start.14 = ((bf16[32,64,96]{2,1,0:T(8,128)(2,1)}), bf16[32,64,96]{2,1,0:T(8,128)(2,1)}, u32[]{:S(2)}, u32[]{:S(2)}) async-start(bf16[32,64,96]{2,1,0:T(8,128)(2,1)} %bitcast.140), calls=%async_computation.14 | async-start | bytes 1048576 | tf_op jit(solution)/shard_map/all_to_all | solution.py:722
  369.7 12.1 %collective-permute-done.3 = bf16[512,768]{1,0:T(8,128)(2,1)} collective-permute-done((bf16[512,768]{1,0:T(8,128)(2,1)S(1)}, bf16[512,768]{1,0:T(8,128)(2,1)}, u32[]{:S(2)}, u32[]{:S(2)}) %collective-permute-start.3) | collective-permute-done | bytes 786464 | tf_op jit(solution)/shard_map/ppermute | solution.py:1013
  411.7 32.1 %all-to-all-done.15 = bf16[32,24,1062]{2,1,0:T(8,128)(2,1)S(1)} async-done(((bf16[32,24,1062]{2,1,0:T(8,128)(2,1)}), bf16[32,24,1062]{2,1,0:T(8,128)(2,1)S(1)}, u32[]{:S(2)}, u32[]{:S(2)}) %all-to-all-start.15) | async-done | bytes 1631264 | tf_op jit(solution)/shard_map/all_to_all | solution.py:722
  451.1 9.0 %table_gradient.5 = (f32[1920,768]{1,0:T(8,128)}, f32[1,768]{1,0:T(1,128)}) custom-call(bf16[2880,768]{1,0:T(8,128)(2,1)} %all-gather.11.cloned.1.call-done.ahead_ref.refs_0_.refs_1_, bf16[2880,768]{1,0:T(8,128)(2,1)} %all-gather.11.cloned.1.call-done.ahead_ref.refs_0_.refs_1_, bf16[960,768]{1,0:T(8,128)(2,1)} %all-gather.13.cloned.1.call-done.refs_2_.refs_3_, ...), custom_call_target="tpu_custom_call" | custom-call | tf_op jit(solution)/shard_map/table_gradient/pallas_call | solution.py:530
  477.5 10.8 %update_norms.1 = (f32[8,128]{1,0:T(8,128)}, f32[3,24,3072]{2,1,0:T(8,128)}, f32[3,24,3072]{2,1,0:T(8,128)}, f32[3,24,3072]{2,1,0:T(8,128)}, f32[256,24]{1,0:T(8...) custom-call(s32[1]{0:T(128)} %bitcast.72.offset_ref, ...), custom_call_target="tpu_custom_call" | custom-call | tf_op jit(solution)/shard_map/update_norms/pallas_call | solution.py:641
  492.2 8.0 %multiply_add_fusion.first_ref = f32[1920,768]{1,0:T(8,128)} fusion(f32[1920,768]{1,0:T(8,128)} %get-tuple-element.325.refs_4_.grad_ref, f32[1920,768]{1,0:T(8,128)} %refs_2_.1, f32[]{:T(128)S(6)} %min.3), kind=kLoop, calls=%fused_computation.28 | loop fusion | flops 5898240 | bytes 17694724 | tf_op jit(solution)/shard_map/add | solution.py:1149
  502.2 16.8 %final_update.1 = (f32[1920,768]{1,0:T(8,128)}, f32[1920,768]{1,0:T(8,128)}, f32[3,24,3072]{2,1,0:T(8,128)}, f32[256,24]{1,0:T(8,128)}, f32[14,24]{1,0:T(8,128)}) custom-call(f32[32,12]{1,0:T(8,128)} %bitcast.202, f32[32,2]{1,0:T(8,128)} %copy.321.refs_0_.totals_ref, f32[1920,768]{1,0:T(8,128)} %weight_ref.1, f32[1920,768]{1,0:T(8,128)} %multiply_add_fusion.first_ref, ...), custom_call_target="tpu_custom_call" | custom-call | tf_op jit(solution)/shard_map/final_update/pallas_call | solution.py:701
  (279 shorter events, 179.9 us)
Async XLA Ops:
  7.2 128.3 %all-gather.7.cloned.1.call-start = ((), (), s32[]{:S(2)}) async-start(), calls=%async_computation.18 | async-start | bytes 15206400 | tf_op jit(solution)/shard_map/all_gather | solution.py:816
  19.7 14.9 %all-to-all-start.4 = ((s32[32,1,256]{2,1,0:T(1,128)}), s32[32,1,256]{2,1,0:T(1,128)S(1)}, u32[]{:S(2)}, u32[]{:S(2)}) async-start(s32[32,1,256]{2,1,0:T(1,128)} %copy.290), calls=%async_computation.4 | async-start | bytes 65536 | tf_op jit(solution)/shard_map/all_to_all | solution.py:722
  40.2 35.7 %all-to-all-start.5 = ((bf16[16,32,768]{2,1,0:T(8,128)(2,1)}), bf16[16,32,768]{2,1,0:T(8,128)(2,1)}, u32[]{:S(2)}, u32[]{:S(2)}) async-start(bf16[16,32,768]{2,1,0:T(8,128)(2,1)} %broadcast_select_fusion.1), calls=%async_computation.5 | async-start | bytes 1572864 | tf_op jit(solution)/shard_map/all_to_all | solution.py:722
  44.5 179.6 %all-gather.9.cloned.1.call-start = ((), (), s32[]{:S(2)}) async-start(), calls=%async_computation.19 | async-start | bytes 1966080 | tf_op jit(solution)/shard_map/all_gather | solution.py:902
  147.0 120.2 %all-gather.15.cloned.1.call-start = ((), (), s32[]{:S(2)}) async-start(), calls=%async_computation.22 | async-start | bytes 6488064 | tf_op jit(solution)/shard_map/all_gather | solution.py:901
  157.6 15.8 %all-to-all-start.6 = ((bf16[4,64,768]{2,1,0:T(8,128)(2,1)}), bf16[4,64,768]{2,1,0:T(8,128)(2,1)S(1)}, u32[]{:S(2)}, u32[]{:S(2)}) async-start(bf16[4,64,768]{2,1,0:T(8,128)(2,1)} %broadcast_in_dim.352), calls=%async_computation.6 | async-start | bytes 786432 | tf_op jit(solution)/shard_map/all_to_all | solution.py:722
  174.4 15.1 %all-to-all-start.7 = ((bf16[2,256,768]{2,1,0:T(8,128)(2,1)}), bf16[2,256,768]{2,1,0:T(8,128)(2,1)}, u32[]{:S(2)}, u32[]{:S(2)}) async-start(bf16[2,256,768]{2,1,0:T(8,128)(2,1)} %broadcast_in_dim.354), calls=%async_computation.7 | async-start | bytes 1572864 | tf_op jit(solution)/shard_map/all_to_all | solution.py:722
  203.2 12.2 %all-to-all-start.9 = ((f32[16,2,1024]{2,1,0:T(2,128)}), f32[16,2,1024]{2,1,0:T(2,128)S(1)}, u32[]{:S(2)}, u32[]{:S(2)}) async-start(f32[16,2,1024]{2,1,0:T(2,128)} %broadcast_in_dim.357), calls=%async_computation.9 | async-start | bytes 262144 | tf_op jit(solution)/shard_map/all_to_all | solution.py:722
  207.5 96.2 %all-gather.11.cloned.1.call-start = ((), (), s32[]{:S(2)}) async-start(), calls=%async_computation.20 | async-start | bytes 6635520 | tf_op jit(solution)/shard_map/all_gather | solution.py:941
  224.1 3.8 collective-permute-start.1
  240.0 143.6 %all-gather.17.cloned.1.call-start = ((), (), s32[]{:S(2)}) async-start(), calls=%async_computation.23 | async-start | bytes 3244032 | tf_op jit(solution)/shard_map/all_gather | solution.py:967
  240.7 11.4 %collective-permute-start.2 = (bf16[256,768]{1,0:T(8,128)(2,1)S(1)}, bf16[256,768]{1,0:T(8,128)(2,1)S(1)}, u32[]{:S(2)}, u32[]{:S(2)}) collective-permute-start(bf16[256,768]{1,0:T(8,128)(2,1)S(1)} %dynamic-slice_convert_fusion), channel_id=1, source_target_pairs={{0,2},{2,0},{1,3},{3,1},{4,6},{6,4},{5,7},{7,5},{8,10},{10,8},{9,1... | collective-permute-start | bytes 1179656 | tf_op jit(solution)/shard_map/ppermute | solution.py:924
  279.9 31.4 %all-to-all-start.11 = ((bf16[32,64,120]{2,1,0:T(8,128)(2,1)}), bf16[32,64,120]{2,1,0:T(8,128)(2,1)S(1)}, u32[]{:S(2)}, u32[]{:S(2)}) async-start(bf16[32,64,120]{2,1,0:T(8,128)(2,1)} %maximum_bitcast_fusion.1), calls=%async_computation.11 | async-start | bytes 1048576 | tf_op jit(solution)/shard_map/all_to_all | solution.py:722
  312.6 16.2 %all-to-all-start.12 = ((bf16[4,288,384]{2,1,0:T(8,128)(2,1)}), bf16[4,288,384]{2,1,0:T(8,128)(2,1)S(1)}, u32[]{:S(2)}, u32[]{:S(2)}) async-start(bf16[4,288,384]{2,1,0:T(8,128)(2,1)} %copy.302), calls=%async_computation.12 | async-start | bytes 1769472 | tf_op jit(solution)/shard_map/all_to_all | solution.py:722
  317.6 20.9 %copy-start.28 = (f32[8,768]{1,0:T(8,128)S(1)}, f32[8,768]{1,0:T(8,128)}, u32[]{:S(2)}) copy-start(f32[8,768]{1,0:T(8,128)} %get-tuple-element.307) | copy-start | bytes 73732
  317.6 20.9 %copy-start.27 = (f32[16,768]{1,0:T(8,128)S(1)}, f32[16,768]{1,0:T(8,128)}, u32[]{:S(2)}) copy-start(f32[16,768]{1,0:T(8,128)} %get-tuple-element.319) | copy-start | bytes 147460
  328.8 26.0 %all-to-all-start.13 = ((bf16[16,32,768]{2,1,0:T(8,128)(2,1)}), bf16[16,32,768]{2,1,0:T(8,128)(2,1)S(1)}, u32[]{:S(2)}, u32[]{:S(2)}) async-start(bf16[16,32,768]{2,1,0:T(8,128)(2,1)} %select_convert_fusion), calls=%async_computation.13 | async-start | bytes 1572864 | tf_op jit(solution)/shard_map/all_to_all | solution.py:722
  354.8 14.9 %copy-start.4 = (bf16[16,32,768]{2,1,0:T(8,128)(2,1)}, bf16[16,32,768]{2,1,0:T(8,128)(2,1)S(1)}, u32[]{:S(2)}) copy-start(bf16[16,32,768]{2,1,0:T(8,128)(2,1)S(1)} %all-to-all-done.13) | copy-start | bytes 2359300
  354.8 27.0 %collective-permute-start.3 = (bf16[512,768]{1,0:T(8,128)(2,1)S(1)}, bf16[512,768]{1,0:T(8,128)(2,1)}, u32[]{:S(2)}, u32[]{:S(2)}) collective-permute-start(bf16[512,768]{1,0:T(8,128)(2,1)S(1)} %bitcast.171), channel_id=1, source_target_pairs={{0,16},{16,0},{1,17},{17,1},{2,18},{18,2},{3,19},{19,3},{4,20},{20... | collective-permute-start | bytes 2359304 | tf_op jit(solution)/shard_map/ppermute | solution.py:1013
  355.6 32.6 %all-to-all-start.14 = ((bf16[32,64,96]{2,1,0:T(8,128)(2,1)}), bf16[32,64,96]{2,1,0:T(8,128)(2,1)}, u32[]{:S(2)}, u32[]{:S(2)}) async-start(bf16[32,64,96]{2,1,0:T(8,128)(2,1)} %bitcast.140), calls=%async_computation.14 | async-start | bytes 1048576 | tf_op jit(solution)/shard_map/all_to_all | solution.py:722
  395.9 47.9 %all-to-all-start.15 = ((bf16[32,24,1062]{2,1,0:T(8,128)(2,1)}), bf16[32,24,1062]{2,1,0:T(8,128)(2,1)S(1)}, u32[]{:S(2)}, u32[]{:S(2)}) async-start(bf16[32,24,1062]{2,1,0:T(8,128)(2,1)} %broadcast_add_fusion), calls=%async_computation.15 | async-start | bytes 3538944 | tf_op jit(solution)/shard_map/all_to_all | solution.py:722
  400.9 50.3 %all-gather.13.cloned.1.call-start = ((), (), s32[]{:S(2)}) async-start(), calls=%async_computation.21 | async-start | bytes 2211840 | tf_op jit(solution)/shard_map/all_gather | solution.py:941
  465.5 9.8 %all-to-all-start.16 = ((f32[32,1,2]{2,1,0:T(1,128)}), f32[32,1,2]{2,1,0:T(1,128)S(1)}, u32[]{:S(2)}, u32[]{:S(2)}) async-start(f32[32,1,2]{2,1,0:T(1,128)} %copy.312), calls=%async_computation.16 | async-start | bytes 32768 | tf_op jit(solution)/shard_map/all_to_all | solution.py:722
  489.6 11.9 %all-to-all-start.17 = ((f32[32,1,12]{2,1,0:T(1,128)}), f32[32,1,12]{2,1,0:T(1,128)S(1)}, u32[]{:S(2)}, u32[]{:S(2)}) async-start(f32[32,1,12]{2,1,0:T(1,128)} %bitcast.82), calls=%async_computation.17 | async-start | bytes 32768 | tf_op jit(solution)/shard_map/all_to_all | solution.py:722
  (28 other events, 169.6 us)
Sparse Core Ops, SparseCore 0:
  11.5 124.0 all-gather.6
  147.2 17.8 all-gather.8
  167.9 70.2 all-gather.14
  240.2 63.4 all-gather.10
  306.4 63.8 all-gather.16
  406.2 34.6 all-gather.12

commit v14 on v12

--- a/solution.py
+++ b/solution.py
@@ -935,7 +935,7 @@
     grad_head = after(grad_head, d_half, *((stream_all,) if few else ()))
     heads = [
         lax.all_gather(half_b, "dp", axis=0, tiled=True)
-        for half_b in jnp.split(grad_head.astype(bfloat), [vrows * 3 // 4])
+        for half_b in jnp.split(grad_head.astype(bfloat), [vrows // 2])
     ]
     d_output = exchange(d_output.astype(bfloat).reshape(outer, CAP, width), "hi")
     if few:

time: 538 us -> 541 us (level)
  waiting for transfers between devices: 212 us -> 218 us
    all_to_all x12, waiting for transfers between devices: 121 us -> 129 us  [__call__(): self.last = lax.all_to_all(values, axes, 0, 0, tiled=True)]
  transfers between devices with their start and end apart: 21 -> 21, of which waited for: 14 -> 14; matrix products, arithmetic and copies ran while one was open for 23% -> 22% of each run, Pallas kernels for 6% -> 6%
where the time goes in v14:
time: 541 us; the launch traced here: 532 us
  waiting for transfers between devices  218 us (40%)
  Pallas kernels  73.7 us (14%)
  other arithmetic  54.5 us (10%)
  starting transfers between devices  54.4 us (10%)
  local copies, waits for them, and re-layouts  53.5 us (10%)
  matrix products  31.8 us (6%)
  between operations  26.3 us (5%)
  blocking collectives  20.1 us (4%)
    all_to_all x12, waiting for transfers between devices, __call__(): self.last = lax.all_to_all(values, axes, 0, 0, tiled=True)  129 us
    all_gather x1, waiting for transfers between devices, on_device(): shard = lax.all_gather(shard.astype(bfloat), ALL, axis=0, tiled=True)  57.1 us
    all_to_all x12, starting transfers between devices, __call__(): self.last = lax.all_to_all(values, axes, 0, 0, tiled=True)  52.6 us
    pallas_call x5, Pallas kernels, kernel_call(): pl.pallas_call(body, grid=(steps,), in_specs=[spec(array.shape, block, in...  41.6 us
    all_to_all x2, blocking collectives, __call__(): self.last = lax.all_to_all(values, axes, 0, 0, tiled=True)  20.1 us
    dot_general x7, matrix products, rows_dot(): lax.dot_general(left_op, right_op, (((0,), (0,)), ((), ())), preferred_el...  19.8 us
    ppermute x2, waiting for transfers between devices, swapped(): theirs = lax.ppermute(part(1 - side).astype(kind), axis, [(0, 1), (1, 0)])  13.2 us
    ppermute x1, waiting for transfers between devices, of_both(): return jnp.concatenate([rows, lax.ppermute(rows, 'dp', [(0, 1), (1, 0)])])  13 us
  transfers between devices with their start and end apart: 21, of which 14 were waited for; matrix products, arithmetic and copies ran while one was open for 22% of the time, Pallas kernels for 6%

profile of v14, /device:TPU:0, one launch (start us, length us, event | category | flops | bytes accessed | tf_op | source)
XLA Modules:
  0.0 532.1 jit_solution(2214318613758607770)
XLA Ops:
  19.7 7.3 %all-to-all-start.4 = ((s32[32,1,256]{2,1,0:T(1,128)}), s32[32,1,256]{2,1,0:T(1,128)S(1)}, u32[]{:S(2)}, u32[]{:S(2)}) async-start(s32[32,1,256]{2,1,0:T(1,128)} %copy.283), calls=%async_computation.4 | async-start | bytes 65536 | tf_op jit(solution)/shard_map/all_to_all | solution.py:718
  27.0 7.6 %all-to-all-done.4 = s32[32,1,256]{2,1,0:T(1,128)S(1)} async-done(((s32[32,1,256]{2,1,0:T(1,128)}), s32[32,1,256]{2,1,0:T(1,128)S(1)}, u32[]{:S(2)}, u32[]{:S(2)}) %all-to-all-start.4) | async-done | bytes 32800 | tf_op jit(solution)/shard_map/all_to_all | solution.py:718
  47.9 28.0 %all-to-all-done.5 = bf16[16,32,768]{2,1,0:T(8,128)(2,1)} async-done(((bf16[16,32,768]{2,1,0:T(8,128)(2,1)}), bf16[16,32,768]{2,1,0:T(8,128)(2,1)}, u32[]{:S(2)}, u32[]{:S(2)}) %all-to-all-start.5) | async-done | bytes 786464 | tf_op jit(solution)/shard_map/all_to_all | solution.py:718
  78.4 57.1 %all-gather.7.cloned.1.call-done.shared_ref.weight_ref.up_ref.down_ref = bf16[768,9600]{1,0:T(8,128)(2,1)} async-done(((bf16[24,9600]{1,0:T(8,128)(2,1)}), bf16[768,9600]{1,0:T(8,128)(2,1)}) %all-gather.7.cloned.1.call-update) | async-done | bytes 14745616 | tf_op jit(solution)/shard_map/all_gather | solution.py:812
  135.5 11.5 %attention_forward.1 = (bf16[256,768]{1,0:T(8,128)(2,1)}, bf16[256,768]{1,0:T(8,128)(2,1)}, bf16[64,768]{1,0:T(8,128)(2,1)}, bf16[64,768]{1,0:T(8,128)(2,1)}, f3...) custom-call(f32[256,768]{1,0:T(8,128)} %get-tuple-element.276.embed_, ...), custom_call_target="tpu_custom_call" | custom-call | flops 11010048 | bytes 73728 | tf_op jit(solution)/shard_map/attention_forward/pallas_call | solution.py:167
  147.1 7.2 %feed_forward.1 = (bf16[64,768]{1,0:T(8,128)(2,1)}, f32[64,3072]{1,0:T(8,128)}, bf16[64,3072]{1,0:T(8,128)(2,1)}, bf16[64,768]{1,0:T(8,128)(2,1)}, f32[64,768]{1,0:T(8,128)}, /*index=5*/f32[64,128]{1,0:T(8,128)}) custom-call(f32[64,768]{1,0:T(8,128)} %get-tuple-element.277.middle_ref, f32[14,768]{1,0:T(8,128)} %get-tuple-element.278.small_ref, ...), custom_call_target="tpu_custom_call" | custom-call | flops 9437184 | bytes 147456 | tf_op jit(solution)/shard_map/feed_forward/pallas_call | solution.py:167
  161.1 12.3 %all-to-all-done.6 = bf16[4,64,768]{2,1,0:T(8,128)(2,1)S(1)} async-done(((bf16[4,64,768]{2,1,0:T(8,128)(2,1)}), bf16[4,64,768]{2,1,0:T(8,128)(2,1)S(1)}, u32[]{:S(2)}, u32[]{:S(2)}) %all-to-all-start.6) | async-done | bytes 393248 | tf_op jit(solution)/shard_map/all_to_all | solution.py:718
  179.1 10.4 %all-to-all-done.7 = bf16[2,256,768]{2,1,0:T(8,128)(2,1)} async-done(((bf16[2,256,768]{2,1,0:T(8,128)(2,1)}), bf16[2,256,768]{2,1,0:T(8,128)(2,1)}, u32[]{:S(2)}, u32[]{:S(2)}) %all-to-all-start.7) | async-done | bytes 786464 | tf_op jit(solution)/shard_map/all_to_all | solution.py:718
  207.8 7.6 %all-to-all-done.9 = f32[16,2,1024]{2,1,0:T(2,128)S(1)} async-done(((f32[16,2,1024]{2,1,0:T(2,128)}), f32[16,2,1024]{2,1,0:T(2,128)S(1)}, u32[]{:S(2)}, u32[]{:S(2)}) %all-to-all-start.9) | async-done | bytes 131104 | tf_op jit(solution)/shard_map/all_to_all | solution.py:718
  240.0 11.3 %collective-permute-done.2 = bf16[256,768]{1,0:T(8,128)(2,1)S(1)} collective-permute-done((bf16[256,768]{1,0:T(8,128)(2,1)S(1)}, bf16[256,768]{1,0:T(8,128)(2,1)S(1)}, u32[]{:S(2)}, u32[]{:S(2)}) %collective-permute-start.2) | collective-permute-done | bytes 393248 | tf_op jit(solution)/shard_map/ppermute | solution.py:920
  252.4 15.0 %all_to_all.134.parts_ref = bf16[4,64,768]{2,1,0:T(8,128)(2,1)} all-to-all(bf16[4,64,768]{2,1,0:T(8,128)(2,1)S(1)} %bitcast.186), channel_id=1, replica_groups=mesh['dp'=2,'hi'=4,'mid'=2,'core'=2] {'hi'}, dimensions={0} | all-to-all | bytes 786432 | tf_op jit(solution)/shard_map/all_to_all | solution.py:718
  267.4 7.6 %feed_backward.1 = (bf16[64,768]{1,0:T(8,128)(2,1)}, bf16[64,3072]{1,0:T(8,128)(2,1)}, f32[64,768]{1,0:T(8,128)}, bf16[64,768]{1,0:T(8,128)(2,1)}, f32[16,768]{1,0:T(8,128)}) custom-call(bf16[4,64,768]{2,1,0:T(8,128)(2,1)} %all_to_all.134.parts_ref, f32[64,768]{1,0:T(8,128)} %get-tuple-element.289.normed_ref, f32[64,128]{1,0:T(8,128)} %get-tuple-element.290.inverse_ref, ...), custom_call_target="tpu_custom_call" | custom-call | flops 9437184 | bytes 147456 | tf_op jit(solution)/shard_map/feed_backward/pallas_call | solution.py:167
  282.9 9.5 %attention_backward.1 = (bf16[64,768]{1,0:T(8,128)(2,1)}, bf16[256,768]{1,0:T(8,128)(2,1)}, bf16[256,768]{1,0:T(8,128)(2,1)}) custom-call(bf16[64,768]{1,0:T(8,128)(2,1)} %get-tuple-element.295.d_attend_ref, bf16[256,768]{1,0:T(8,128)(2,1)} %get-tuple-element.296.key_ref, bf16[256,768]{1,0:T(8,128)(2,1)} %get-tuple-element.297.value_ref, ...), custom_call_target="tpu_custom_call" | custom-call | flops 5111808 | bytes 18432 | tf_op jit(solution)/shard_map/attention_backward/pallas_call | solution.py:167
  296.9 5.9 %projection_backward.1 = (bf16[256,768]{1,0:T(8,128)(2,1)S(1)}, f32[256,768]{1,0:T(8,128)}, f32[8,768]{1,0:T(8,128)}) custom-call(f32[64,768]{1,0:T(8,128)} %get-tuple-element.294.d_pre_ref, bf16[64,768]{1,0:T(8,128)(2,1)} %get-tuple-element.299.d_query_ref, bf16[256,768]{1,0:T(8,128)(2,1)} %get-tuple-element.300.d_key_ref, ...), custom_call_target="tpu_custom_call" | custom-call | flops 11796480 | bytes 55296 | tf_op jit(solution)/shard_map/projection_backward/pallas_call | solution.py:167
  310.0 12.5 %all-to-all-done.12 = bf16[4,288,384]{2,1,0:T(8,128)(2,1)S(1)} async-done(((bf16[4,288,384]{2,1,0:T(8,128)(2,1)}), bf16[4,288,384]{2,1,0:T(8,128)(2,1)S(1)}, u32[]{:S(2)}, u32[]{:S(2)}) %all-to-all-start.12) | async-done | bytes 884768 | tf_op jit(solution)/shard_map/all_to_all | solution.py:718
  339.5 13.7 %all-to-all-done.13 = bf16[16,32,768]{2,1,0:T(8,128)(2,1)S(1)} async-done(((bf16[16,32,768]{2,1,0:T(8,128)(2,1)}), bf16[16,32,768]{2,1,0:T(8,128)(2,1)S(1)}, u32[]{:S(2)}, u32[]{:S(2)}) %all-to-all-start.13) | async-done | bytes 786464 | tf_op jit(solution)/shard_map/all_to_all | solution.py:718
  354.7 5.3 all-to-all-start.14
  364.6 13.0 %collective-permute-done.3 = bf16[512,768]{1,0:T(8,128)(2,1)} collective-permute-done((bf16[512,768]{1,0:T(8,128)(2,1)S(1)}, bf16[512,768]{1,0:T(8,128)(2,1)}, u32[]{:S(2)}, u32[]{:S(2)}) %collective-permute-start.3) | collective-permute-done | bytes 786464 | tf_op jit(solution)/shard_map/ppermute | solution.py:1009
  391.8 5.8 %all-to-all-start.15 = ((bf16[32,24,1062]{2,1,0:T(8,128)(2,1)}), bf16[32,24,1062]{2,1,0:T(8,128)(2,1)S(1)}, u32[]{:S(2)}, u32[]{:S(2)}) async-start(bf16[32,24,1062]{2,1,0:T(8,128)(2,1)} %broadcast_add_fusion), calls=%async_computation.15 | async-start | bytes 3538944 | tf_op jit(solution)/shard_map/all_to_all | solution.py:718
  406.9 33.7 %all-to-all-done.15 = bf16[32,24,1062]{2,1,0:T(8,128)(2,1)S(1)} async-done(((bf16[32,24,1062]{2,1,0:T(8,128)(2,1)}), bf16[32,24,1062]{2,1,0:T(8,128)(2,1)S(1)}, u32[]{:S(2)}, u32[]{:S(2)}) %all-to-all-start.15) | async-done | bytes 1631264 | tf_op jit(solution)/shard_map/all_to_all | solution.py:718
  452.5 8.9 %table_gradient.5 = (f32[1920,768]{1,0:T(8,128)}, f32[1,768]{1,0:T(1,128)}) custom-call(bf16[1920,768]{1,0:T(8,128)(2,1)} %all-gather.11.cloned.1.call-done.ahead_ref.refs_0_.refs_1_, bf16[1920,768]{1,0:T(8,128)(2,1)} %all-gather.11.cloned.1.call-done.ahead_ref.refs_0_.refs_1_, bf16[1920,768]{1,0:T(8,128)(2,1)} %all-gather.13.cloned.1.call-done.refs_2_.refs_3_, ...), custom_call_target="tpu_custom_call" | custom-call | tf_op jit(solution)/shard_map/table_gradient/pallas_call | solution.py:530
  480.5 10.9 %update_norms.1 = (f32[8,128]{1,0:T(8,128)}, f32[3,24,3072]{2,1,0:T(8,128)}, f32[3,24,3072]{2,1,0:T(8,128)}, f32[3,24,3072]{2,1,0:T(8,128)}, f32[256,24]{1,0:T(8...) custom-call(s32[1]{0:T(128)} %bitcast.72.offset_ref, ...), custom_call_target="tpu_custom_call" | custom-call | tf_op jit(solution)/shard_map/update_norms/pallas_call | solution.py:641
  495.4 11.2 %fusion.5 = (f32[1920,768]{1,0:T(8,128)}, f32[1920,768]{1,0:T(8,128)}) fusion(f32[1920,768]{1,0:T(8,128)} %refs_3_.1, f32[1920,768]{1,0:T(8,128)} %get-tuple-element.324.refs_4_, f32[]{:T(128)S(6)} %min.3, f32[1920,768]{1,0:T(8,128)} %refs_2_.1), kind=kLoop, calls=%fused_computation.29 | loop fusion | flops 11796480 | bytes 29491204 | tf_op jit(solution)/shard_map/add | solution.py:486
  508.6 12.3 %final_update.1 = (f32[1920,768]{1,0:T(8,128)}, f32[3,24,3072]{2,1,0:T(8,128)}, f32[256,24]{1,0:T(8,128)}, f32[14,24]{1,0:T(8,128)}) custom-call(f32[32,12]{1,0:T(8,128)} %bitcast.202, f32[1920,768]{1,0:T(8,128)} %weight_ref.1, f32[1920,768]{1,0:T(8,128)} %get-tuple-element.550.first_ref, f32[1920,768]{1,0:T(8,128)} %get-tuple-element.549.second_ref, ...), custom_call_target="tpu_custom_call" | custom-call | tf_op jit(solution)/shard_map/final_update/pallas_call | solution.py:697
  (270 shorter events, 180.4 us)
Async XLA Ops:
  7.2 128.3 %all-gather.7.cloned.1.call-start = ((), (), s32[]{:S(2)}) async-start(), calls=%async_computation.18 | async-start | bytes 15206400 | tf_op jit(solution)/shard_map/all_gather | solution.py:812
  19.7 14.9 %all-to-all-start.4 = ((s32[32,1,256]{2,1,0:T(1,128)}), s32[32,1,256]{2,1,0:T(1,128)S(1)}, u32[]{:S(2)}, u32[]{:S(2)}) async-start(s32[32,1,256]{2,1,0:T(1,128)} %copy.283), calls=%async_computation.4 | async-start | bytes 65536 | tf_op jit(solution)/shard_map/all_to_all | solution.py:718
  40.2 35.7 %all-to-all-start.5 = ((bf16[16,32,768]{2,1,0:T(8,128)(2,1)}), bf16[16,32,768]{2,1,0:T(8,128)(2,1)}, u32[]{:S(2)}, u32[]{:S(2)}) async-start(bf16[16,32,768]{2,1,0:T(8,128)(2,1)} %broadcast_select_fusion.1), calls=%async_computation.5 | async-start | bytes 1572864 | tf_op jit(solution)/shard_map/all_to_all | solution.py:718
  44.5 179.6 %all-gather.9.cloned.1.call-start = ((), (), s32[]{:S(2)}) async-start(), calls=%async_computation.19 | async-start | bytes 1966080 | tf_op jit(solution)/shard_map/all_gather | solution.py:898
  147.0 120.4 %all-gather.15.cloned.1.call-start = ((), (), s32[]{:S(2)}) async-start(), calls=%async_computation.22 | async-start | bytes 6488064 | tf_op jit(solution)/shard_map/all_gather | solution.py:897
  157.6 15.8 %all-to-all-start.6 = ((bf16[4,64,768]{2,1,0:T(8,128)(2,1)}), bf16[4,64,768]{2,1,0:T(8,128)(2,1)S(1)}, u32[]{:S(2)}, u32[]{:S(2)}) async-start(bf16[4,64,768]{2,1,0:T(8,128)(2,1)} %broadcast_in_dim.352), calls=%async_computation.6 | async-start | bytes 786432 | tf_op jit(solution)/shard_map/all_to_all | solution.py:718
  174.3 15.1 %all-to-all-start.7 = ((bf16[2,256,768]{2,1,0:T(8,128)(2,1)}), bf16[2,256,768]{2,1,0:T(8,128)(2,1)}, u32[]{:S(2)}, u32[]{:S(2)}) async-start(bf16[2,256,768]{2,1,0:T(8,128)(2,1)} %broadcast_in_dim.354), calls=%async_computation.7 | async-start | bytes 1572864 | tf_op jit(solution)/shard_map/all_to_all | solution.py:718
  203.2 12.2 %all-to-all-start.9 = ((f32[16,2,1024]{2,1,0:T(2,128)}), f32[16,2,1024]{2,1,0:T(2,128)S(1)}, u32[]{:S(2)}, u32[]{:S(2)}) async-start(f32[16,2,1024]{2,1,0:T(2,128)} %broadcast_in_dim.357), calls=%async_computation.9 | async-start | bytes 262144 | tf_op jit(solution)/shard_map/all_to_all | solution.py:718
  207.4 88.7 %all-gather.11.cloned.1.call-start = ((), (), s32[]{:S(2)}) async-start(), calls=%async_computation.20 | async-start | bytes 4423680 | tf_op jit(solution)/shard_map/all_gather | solution.py:937
  207.7 13.4 %copy-start.17 = (f32[16,64]{1,0:T(8,128)}, f32[16,64]{1,0:T(8,128)S(1)}, u32[]{:S(2)}) copy-start(f32[16,64]{1,0:T(8,128)S(1)} %fusion.45) | copy-start | bytes 12292
  224.1 3.8 collective-permute-start.1
  238.6 140.9 %all-gather.17.cloned.1.call-start = ((), (), s32[]{:S(2)}) async-start(), calls=%async_computation.23 | async-start | bytes 3244032 | tf_op jit(solution)/shard_map/all_gather | solution.py:963
  239.9 11.4 %collective-permute-start.2 = (bf16[256,768]{1,0:T(8,128)(2,1)S(1)}, bf16[256,768]{1,0:T(8,128)(2,1)S(1)}, u32[]{:S(2)}, u32[]{:S(2)}) collective-permute-start(bf16[256,768]{1,0:T(8,128)(2,1)S(1)} %dynamic-slice_convert_fusion), channel_id=1, source_target_pairs={{0,2},{2,0},{1,3},{3,1},{4,6},{6,4},{5,7},{7,5},{8,10},{10,8},{9,1... | collective-permute-start | bytes 1179656 | tf_op jit(solution)/shard_map/ppermute | solution.py:920
  280.1 23.6 %all-to-all-start.11 = ((bf16[32,64,120]{2,1,0:T(8,128)(2,1)}), bf16[32,64,120]{2,1,0:T(8,128)(2,1)S(1)}, u32[]{:S(2)}, u32[]{:S(2)}) async-start(bf16[32,64,120]{2,1,0:T(8,128)(2,1)} %maximum_bitcast_fusion.1), calls=%async_computation.11 | async-start | bytes 1048576 | tf_op jit(solution)/shard_map/all_to_all | solution.py:718
  305.1 17.4 %all-to-all-start.12 = ((bf16[4,288,384]{2,1,0:T(8,128)(2,1)}), bf16[4,288,384]{2,1,0:T(8,128)(2,1)S(1)}, u32[]{:S(2)}, u32[]{:S(2)}) async-start(bf16[4,288,384]{2,1,0:T(8,128)(2,1)} %copy.295), calls=%async_computation.12 | async-start | bytes 1769472 | tf_op jit(solution)/shard_map/all_to_all | solution.py:718
  310.0 22.1 %copy-start.24 = (f32[8,768]{1,0:T(8,128)S(1)}, f32[8,768]{1,0:T(8,128)}, u32[]{:S(2)}) copy-start(f32[8,768]{1,0:T(8,128)} %get-tuple-element.306) | copy-start | bytes 73732
  310.0 22.1 %copy-start.23 = (f32[16,768]{1,0:T(8,128)S(1)}, f32[16,768]{1,0:T(8,128)}, u32[]{:S(2)}) copy-start(f32[16,768]{1,0:T(8,128)} %get-tuple-element.318) | copy-start | bytes 147460
  322.5 30.7 %all-to-all-start.13 = ((bf16[16,32,768]{2,1,0:T(8,128)(2,1)}), bf16[16,32,768]{2,1,0:T(8,128)(2,1)S(1)}, u32[]{:S(2)}, u32[]{:S(2)}) async-start(bf16[16,32,768]{2,1,0:T(8,128)(2,1)} %select_convert_fusion), calls=%async_computation.13 | async-start | bytes 1572864 | tf_op jit(solution)/shard_map/all_to_all | solution.py:718
  353.2 24.5 %collective-permute-start.3 = (bf16[512,768]{1,0:T(8,128)(2,1)S(1)}, bf16[512,768]{1,0:T(8,128)(2,1)}, u32[]{:S(2)}, u32[]{:S(2)}) collective-permute-start(bf16[512,768]{1,0:T(8,128)(2,1)S(1)} %bitcast.171), channel_id=1, source_target_pairs={{0,16},{16,0},{1,17},{17,1},{2,18},{18,2},{3,19},{19,3},{4,20},{20... | collective-permute-start | bytes 2359304 | tf_op jit(solution)/shard_map/ppermute | solution.py:1009
  354.7 29.5 %all-to-all-start.14 = ((bf16[32,64,96]{2,1,0:T(8,128)(2,1)}), bf16[32,64,96]{2,1,0:T(8,128)(2,1)}, u32[]{:S(2)}, u32[]{:S(2)}) async-start(bf16[32,64,96]{2,1,0:T(8,128)(2,1)} %bitcast.140), calls=%async_computation.14 | async-start | bytes 1048576 | tf_op jit(solution)/shard_map/all_to_all | solution.py:718
  391.8 48.8 %all-to-all-start.15 = ((bf16[32,24,1062]{2,1,0:T(8,128)(2,1)}), bf16[32,24,1062]{2,1,0:T(8,128)(2,1)S(1)}, u32[]{:S(2)}, u32[]{:S(2)}) async-start(bf16[32,24,1062]{2,1,0:T(8,128)(2,1)} %broadcast_add_fusion), calls=%async_computation.15 | async-start | bytes 3538944 | tf_op jit(solution)/shard_map/all_to_all | solution.py:718
  397.6 54.9 %all-gather.13.cloned.1.call-start = ((), (), s32[]{:S(2)}) async-start(), calls=%async_computation.21 | async-start | bytes 4423680 | tf_op jit(solution)/shard_map/all_gather | solution.py:937
  466.8 11.6 %all-to-all-start.16 = ((f32[32,1,2]{2,1,0:T(1,128)}), f32[32,1,2]{2,1,0:T(1,128)S(1)}, u32[]{:S(2)}, u32[]{:S(2)}) async-start(f32[32,1,2]{2,1,0:T(1,128)} %copy.305), calls=%async_computation.16 | async-start | bytes 32768 | tf_op jit(solution)/shard_map/all_to_all | solution.py:718
  492.8 15.2 %all-to-all-start.17 = ((f32[32,1,12]{2,1,0:T(1,128)}), f32[32,1,12]{2,1,0:T(1,128)S(1)}, u32[]{:S(2)}, u32[]{:S(2)}) async-start(f32[32,1,12]{2,1,0:T(1,128)} %bitcast.82), calls=%async_computation.17 | async-start | bytes 32768 | tf_op jit(solution)/shard_map/all_to_all | solution.py:718
  (24 other events, 162.0 us)
Sparse Core Ops, SparseCore 0:
  11.5 124.0 all-gather.6
  147.2 17.8 all-gather.8
  167.9 70.2 all-gather.14
  240.2 41.1 all-gather.10
  284.2 68.5 all-gather.16
  399.6 52.8 all-gather.12
